TPU v7x, 512 devices: a whole 4x8x8 slice. The times are simulated.
512 devices in a mesh: seq: 128 (over x, z, y_hi), tp: 4 (over y_lo, core).
Axes of the slice: x: 4, y: 8 (y_hi: 4, y_lo: 2; y = y_hi * 2 + y_lo), z: 8, core: 2. Of those that a mesh axis runs over, the one named last changes fastest.
Arguments:
- residual_in: float32 [32768, 2048], P('seq', 'tp'), may hold values from -18 to 18
- query_rows: bfloat16 [32768, 2048], P('seq', 'tp'), may hold values from -6 to 6
- key_rows: bfloat16 [32768, 2048], P('seq', 'tp'), may hold values from -6 to 6
- value_rows: bfloat16 [32768, 2048], P('seq', 'tp'), may hold values from -6 to 6
- lengths: int32 [256], P('seq'), may hold values from 0 to 128, as said below
- norm_gain: float32 [2048], P('tp'), may hold values from 0.1 to 1.9
- gate_weight: bfloat16 [2048, 4096], P('seq', 'tp'), may hold values from -0.125 to 0.125
- up_weight: bfloat16 [2048, 4096], P('seq', 'tp'), may hold values from -0.125 to 0.125
- down_weight: bfloat16 [4096, 2048], P('tp', 'seq'), may hold values from -0.375 to 0.375
Outputs:
- attended: bfloat16 [32768, 2048], P('seq', 'tp')
- mixed: float32 [32768, 2048], P('seq', 'tp')
Inputs may be any that keep to these rules, and one draw needn't show every extreme that they name: `lengths`: entry s counts the valid events at the start of segment s, the events s * 128 to s * 128 + 127; the rest of the segment is padding.
All inputs are finite; a program needn't handle non-finite values.
Results may differ from a plain program's by a relative error of at most 0.008.
Values may be sent and summed in bfloat16 or wider, within the bound.
No kernel may reach another device: no remote copies, remote signals or barrier semaphores. Data moves between devices by JAX's collectives and lax.ppermute only.
A program may use at most 64 MiB of HBM per device.

v0:
```python
import math

import jax
import jax.numpy as jnp
from jax import lax
from jax.sharding import PartitionSpec as P

D = 2048
HEAD_DIM = 128
SEG = 128
WINDOW = 512


epsilon = 1e-06


def from_behind(value, axis, by):
    size = lax.axis_size(axis)
    pairs = [(i, i + by) for i in range(size) if 0 <= i + by < size]
    return lax.ppermute(value, axis, pairs)


def on_device(
    residual_in,
    query_rows,
    key_rows,
    value_rows,
    lengths,
    norm_gain,
    gate_weight,
    up_weight,
    down_weight,
):
    row_count = query_rows.shape[0]
    head_local = query_rows.shape[1] // HEAD_DIM
    reach_blocks = (WINDOW + row_count - 2) // row_count
    seq_index = lax.axis_index("seq")
    offsets = jnp.arange(row_count, dtype=jnp.int32) % SEG
    own_valid = (offsets < jnp.repeat(lengths, SEG, total_repeat_length=row_count)).astype(
        jnp.bfloat16
    )
    previous = from_behind((key_rows, value_rows, own_valid), "seq", 1)
    earlier = [previous]
    earlier.append(from_behind((key_rows, value_rows, own_valid), "seq", 2))
    oldest_first = earlier[::-1]
    key_window = jnp.concatenate([block[0] for block in oldest_first] + [key_rows], axis=0)
    value_window = jnp.concatenate([block[1] for block in oldest_first] + [value_rows], axis=0)
    valid_window = jnp.concatenate([block[2] for block in oldest_first] + [own_valid], axis=0)
    key_span = key_window.shape[0]
    query_pos = seq_index * row_count + jnp.arange(row_count, dtype=jnp.int32)
    key_pos = (seq_index - reach_blocks) * row_count + jnp.arange(key_span, dtype=jnp.int32)
    allowed = (key_pos[None, :] <= query_pos[:, None]) & (
        key_pos[None, :] > query_pos[:, None] - WINDOW
    )
    allowed = allowed & (key_pos[None, :] >= 0) & (valid_window[None, :] > 0)
    keep_rows = (own_valid > 0)[:, None]
    score_scale = 1.0 / math.sqrt(HEAD_DIM)
    outputs = []
    for head_index in range(head_local):
        low_col = head_index * HEAD_DIM
        query_head = query_rows[:, low_col : low_col + HEAD_DIM]
        key_head = key_window[:, low_col : low_col + HEAD_DIM]
        value_head = value_window[:, low_col : low_col + HEAD_DIM]
        scores = (
            lax.dot_general(
                query_head, key_head, (((1,), (1,)), ((), ())), preferred_element_type=jnp.float32
            )
            * score_scale
        )
        masked = jnp.where(allowed, scores, -1e30)
        row_max = jnp.max(masked, axis=1, keepdims=True)
        weights = jnp.where(allowed, jnp.exp(masked - row_max), 0.0)
        denominator = jnp.sum(weights, axis=1, keepdims=True)
        numerator = jnp.dot(
            weights.astype(jnp.bfloat16), value_head, preferred_element_type=jnp.float32
        )
        outputs.append(
            jnp.where(keep_rows, numerator / jnp.where(keep_rows, denominator, 1.0), 0.0)
        )
    attended = jnp.concatenate(outputs, axis=1).astype(jnp.bfloat16)
    residual = residual_in + attended.astype(jnp.float32)
    square_sum = lax.psum(jnp.sum(residual * residual, axis=1), "tp")
    inverse = lax.rsqrt(square_sum / D + epsilon)
    normed = (residual * inverse[:, None] * norm_gain[None, :]).astype(jnp.bfloat16)
    normed_full = lax.all_gather(normed, "tp", axis=1, tiled=True)
    gate_full, up_full = (
        lax.all_gather(gate_weight, "seq", axis=0, tiled=True),
        lax.all_gather(up_weight, "seq", axis=0, tiled=True),
    )
    gate_sum = jnp.dot(normed_full, gate_full, preferred_element_type=jnp.float32)
    up_sum = jnp.dot(normed_full, up_full, preferred_element_type=jnp.float32)
    hidden = (jax.nn.silu(gate_sum) * up_sum).astype(jnp.bfloat16)
    down_full = lax.all_gather(down_weight, "seq", axis=1, tiled=True)
    partial_value = jnp.dot(hidden, down_full, preferred_element_type=jnp.float32)
    tp_width = residual_in.shape[1]
    summed = lax.psum(partial_value.astype(jnp.bfloat16), "tp").astype(jnp.float32)
    branch_share = lax.dynamic_slice_in_dim(summed, lax.axis_index("tp") * tp_width, tp_width, 1)
    mixed = residual + branch_share
    return (attended, mixed)


def solution(mesh):
    placed = (
        P("seq", "tp"),
        P("seq", "tp"),
        P("seq", "tp"),
        P("seq", "tp"),
        P("seq"),
        P("tp"),
        P("seq", "tp"),
        P("seq", "tp"),
        P("tp", "seq"),
    )
    return jax.shard_map(
        on_device,
        mesh=mesh,
        in_specs=placed,
        out_specs=(P("seq", "tp"), P("seq", "tp")),
        check_vma=False,
    )
```

profile of v0, /device:TPU:1, one launch (start us, length us, event | category | flops | bytes accessed | tf_op | source)
XLA Modules:
  0.0 574.4 jit_solution(10562217400988549649)
XLA Ops:
  7.2 1.3 fusion.57
  8.6 1.3 compare_select_fusion.1
  9.9 8.3 %collective-permute-start = (bf16[256]{0:T(256)(128)(2,1)S(1)}, bf16[256]{0:T(256)(128)(2,1)S(1)}, u32[]{:S(2)}, u32[]{:S(2)}) collective-permute-start(bf16[256]{0:T(256)(128)(2,1)S(1)} %get-tuple-element.21), channel_id=1, source_target_pairs={{0,8},{4,12},{8,16},{12,20},{16,24},{20,28},{24,32},{28,36},{32,40... | collective-permute-start | bytes 1544 | tf_op jit(solution)/shard_map/ppermute | solution.py:20
  18.2 2.4 collective-permute-start.1
  20.6 5.4 collective-permute-start.2
  26.0 5.4 collective-permute-start.3
  31.4 3.5 collective-permute-start.4
  35.0 1.2 copy.11
  36.3 4.2 collective-permute-start.5
  40.6 2.4 collective-permute-done.3
  43.9 1.3 fusion.59
  46.1 3.1 collective-permute-done.4
  49.6 10.2 %collective-permute-done.5 = bf16[256,512]{1,0:T(8,128)(2,1)S(1)} collective-permute-done((bf16[256,512]{1,0:T(8,128)(2,1)}, bf16[256,512]{1,0:T(8,128)(2,1)S(1)}, u32[]{:S(2)}, u32[]{:S(2)}) %collective-permute-start.5) | collective-permute-done | bytes 262176 | tf_op jit(solution)/shard_map/ppermute | solution.py:20
  59.8 1.0 fusion.17
  63.5 17.3 %psum.14 = f32[256]{0:T(256)S(1)} all-reduce(f32[256]{0:T(256)S(1)} %multiply_reduce_fusion), channel_id=1, replica_groups=mesh['seq'=128,'tp'=4] {'tp'}, use_global_device_ids=true, to_apply=%region_9.10 | all-reduce | flops 256 | bytes 2048 | tf_op jit(solution)/shard_map/psum | solution.py:82
  83.7 29.9 %all-gather.5.cloned.1.call-done = bf16[256,2048]{0,1:T(8,128)(2,1)} async-done(((bf16[256,512]{0,1:T(8,128)(2,1)}), bf16[256,2048]{0,1:T(8,128)(2,1)}) %all-gather.5.cloned.1.call-update) | async-done | bytes 1048592 | tf_op jit(solution)/shard_map/all_gather | solution.py:85
  113.7 132.3 %all-gather.7.cloned.1.call-done = bf16[2048,1024]{1,0:T(8,128)(2,1)} async-done(((bf16[16,1024]{1,0:T(8,128)(2,1)}), bf16[2048,1024]{1,0:T(8,128)(2,1)}) %all-gather.7.cloned.1.call-update) | async-done | bytes 4194320 | tf_op jit(solution)/shard_map/all_gather | solution.py:87
  245.9 3.8 fusion.62
  249.7 127.1 %all-gather.11.cloned.1.call-done = bf16[1024,2048]{0,1:T(8,128)(2,1)} async-done(((bf16[1024,16]{0,1:T(8,128)(2,1)}), bf16[1024,2048]{0,1:T(8,128)(2,1)}) %all-gather.11.cloned.1.call-update) | async-done | bytes 4194320 | tf_op jit(solution)/shard_map/all_gather | solution.py:93
  376.8 130.7 %all-gather.9.cloned.1.call-done = bf16[2048,1024]{1,0:T(8,128)(2,1)} async-done(((bf16[16,1024]{1,0:T(8,128)(2,1)}), bf16[2048,1024]{1,0:T(8,128)(2,1)}) %all-gather.9.cloned.1.call-update) | async-done | bytes 4194320 | tf_op jit(solution)/shard_map/all_gather | solution.py:88
  507.5 7.1 %convolution_convert_fusion = bf16[256,2048]{0,1:T(8,128)(2,1)} fusion(bf16[1024,2048]{0,1:T(8,128)(2,1)} %all-gather.11.cloned.1.call-done, bf16[256,2048]{0,1:T(8,128)(2,1)S(1)} %copy-done.2, bf16[2048,1024]{1,0:T(8,128)(2,1)} %all-gather.9.cloned.1.call-done, f32[256,1024]{1,0:T(8,128)S(1)} %fusion.62), kind=kOutput, calls=%fused_computation | convolution fusion | flops 2149580800 | bytes 11534336 | tf_op jit(solution)/shard_map/dot_general | solution.py:94
  515.5 50.4 %all-reduce.2.cloned.1.call-done = bf16[256,2048]{0,1:T(8,128)(2,1)} async-done(((bf16[256,2048]{0,1:T(8,128)(2,1)}), bf16[256,2048]{0,1:T(8,128)(2,1)}) %all-reduce.2.cloned.1.call-update) | async-done | bytes 1048592 | tf_op jit(solution)/shard_map/psum | solution.py:96
  565.9 1.0 convert_add_fusion
  566.9 1.0 copy.14
  (47 shorter events, 8.8 us)
Async XLA Ops:
  7.2 38.1 %copy-start.3 = (bf16[256,512]{1,0:T(8,128)(2,1)S(1)}, bf16[256,512]{1,0:T(8,128)(2,1)}, u32[]{:S(2)}) copy-start(bf16[256,512]{1,0:T(8,128)(2,1)} %param.12) | copy-start | bytes 786436
  7.2 106.5 %all-gather.5.cloned.1.call-start = ((), (), s32[]{:S(2)}) async-start(), calls=%async_computation | async-start | bytes 1310720 | tf_op jit(solution)/shard_map/all_gather | solution.py:85
  9.9 26.4 %collective-permute-start = (bf16[256]{0:T(256)(128)(2,1)S(1)}, bf16[256]{0:T(256)(128)(2,1)S(1)}, u32[]{:S(2)}, u32[]{:S(2)}) collective-permute-start(bf16[256]{0:T(256)(128)(2,1)S(1)} %get-tuple-element.21), channel_id=1, source_target_pairs={{0,8},{4,12},{8,16},{12,20},{16,24},{20,28},{24,32},{28,36},{32,40... | collective-permute-start | bytes 1544 | tf_op jit(solution)/shard_map/ppermute | solution.py:20
  18.2 22.3 %collective-permute-start.1 = (bf16[256]{0:T(256)(128)(2,1)S(1)}, bf16[256]{0:T(256)(128)(2,1)S(1)}, u32[]{:S(2)}, u32[]{:S(2)}) collective-permute-start(bf16[256]{0:T(256)(128)(2,1)S(1)} %get-tuple-element.21), channel_id=1, source_target_pairs={{0,4},{4,8},{8,12},{12,16},{16,20},{20,24},{24,28},{28,32},{32,36}... | collective-permute-start | bytes 1544 | tf_op jit(solution)/shard_map/ppermute | solution.py:20
  20.6 19.9 %collective-permute-start.2 = (bf16[256,512]{1,0:T(8,128)(2,1)}, bf16[256,512]{1,0:T(8,128)(2,1)S(1)}, u32[]{:S(2)}, u32[]{:S(2)}) collective-permute-start(bf16[256,512]{1,0:T(8,128)(2,1)} %param.13), channel_id=1, source_target_pairs={{0,8},{4,12},{8,16},{12,20},{16,24},{20,28},{24,32},{28,36},{32,40... | collective-permute-start | bytes 786440 | tf_op jit(solution)/shard_map/ppermute | solution.py:20
  26.0 17.0 %collective-permute-start.3 = (bf16[256,512]{1,0:T(8,128)(2,1)}, bf16[256,512]{1,0:T(8,128)(2,1)S(1)}, u32[]{:S(2)}, u32[]{:S(2)}) collective-permute-start(bf16[256,512]{1,0:T(8,128)(2,1)} %param.13), channel_id=1, source_target_pairs={{0,4},{4,8},{8,12},{12,16},{16,20},{20,24},{24,28},{28,32},{32,36}... | collective-permute-start | bytes 786440 | tf_op jit(solution)/shard_map/ppermute | solution.py:20
  31.4 17.8 %collective-permute-start.4 = (bf16[256,512]{1,0:T(8,128)(2,1)}, bf16[256,512]{1,0:T(8,128)(2,1)S(1)}, u32[]{:S(2)}, u32[]{:S(2)}) collective-permute-start(bf16[256,512]{1,0:T(8,128)(2,1)} %param.14), channel_id=1, source_target_pairs={{0,8},{4,12},{8,16},{12,20},{16,24},{20,28},{24,32},{28,36},{32,40... | collective-permute-start | bytes 786440 | tf_op jit(solution)/shard_map/ppermute | solution.py:20
  36.3 23.5 %collective-permute-start.5 = (bf16[256,512]{1,0:T(8,128)(2,1)}, bf16[256,512]{1,0:T(8,128)(2,1)S(1)}, u32[]{:S(2)}, u32[]{:S(2)}) collective-permute-start(bf16[256,512]{1,0:T(8,128)(2,1)} %param.14), channel_id=1, source_target_pairs={{0,4},{4,8},{8,12},{12,16},{16,20},{20,24},{24,28},{28,32},{32,36}... | collective-permute-start | bytes 786440 | tf_op jit(solution)/shard_map/ppermute | solution.py:20
  43.9 15.9 %copy-start = (bf16[256,512]{1,0:T(8,128)(2,1)S(1)}, bf16[256,512]{1,0:T(8,128)(2,1)}, u32[]{:S(2)}) copy-start(bf16[256,512]{1,0:T(8,128)(2,1)} %param.14) | copy-start | bytes 786436
  61.5 19.2 %copy-start.1 = (f32[512]{0:T(512)S(1)}, f32[512]{0:T(512)}, u32[]{:S(2)}) copy-start(f32[512]{0:T(512)} %param.16) | copy-start | bytes 6148
  81.6 164.3 %all-gather.7.cloned.1.call-start = ((), (), s32[]{:S(2)}) async-start(), calls=%async_computation.1 | async-start | bytes 4227072 | tf_op jit(solution)/shard_map/all_gather | solution.py:87
  82.4 294.4 %all-gather.11.cloned.1.call-start = ((), (), s32[]{:S(2)}) async-start(), calls=%async_computation.3 | async-start | bytes 4227072 | tf_op jit(solution)/shard_map/all_gather | solution.py:93
  83.1 424.4 %all-gather.9.cloned.1.call-start = ((), (), s32[]{:S(2)}) async-start(), calls=%async_computation.2 | async-start | bytes 4227072 | tf_op jit(solution)/shard_map/all_gather | solution.py:88
  83.7 482.2 %all-reduce.2.cloned.1.call-start = ((), (), s32[]{:S(2)}) async-start(), calls=%async_computation.4 | async-start | bytes 2097152 | tf_op jit(solution)/shard_map/psum | solution.py:96
  113.7 393.9 %copy-start.2 = (bf16[256,2048]{0,1:T(8,128)(2,1)S(1)}, bf16[256,2048]{0,1:T(8,128)(2,1)}, u32[]{:S(2)}) copy-start(bf16[256,2048]{0,1:T(8,128)(2,1)} %all-gather.5.cloned.1.call-done) | copy-start | bytes 3145732
Sparse Core Ops, SparseCore 0:
  81.7 31.8 all-gather.4
  118.2 127.7 all-gather.6
  250.5 126.2 all-gather.10
  381.2 126.2 all-gather.8
  514.7 51.0 all-reduce.1
where the time goes:
time: 575 us; the launch traced here: 574 us
  waiting for transfers between devices  488 us (85%)
  starting transfers between devices  29.5 us (5%)
  blocking collectives  17.3 us (3%)
  matrix products  15.9 us (3%)
  between operations  14.1 us (2%)
    all_gather x1, waiting for transfers between devices, on_device(): lax.all_gather(gate_weight, 'seq', axis=0, tiled=True)  132 us
    all_gather x1, waiting for transfers between devices, on_device(): lax.all_gather(up_weight, 'seq', axis=0, tiled=True)  131 us
    all_gather x1, waiting for transfers between devices, on_device(): down_full = lax.all_gather(down_weight, 'seq', axis=1, tiled=True)  127 us
    psum x1, waiting for transfers between devices, on_device(): lax.psum(partial_value.astype(jnp.bfloat16), 'tp').astype(jnp.float32)  50.4 us
    all_gather x1, waiting for transfers between devices, on_device(): normed_full = lax.all_gather(normed, 'tp', axis=1, tiled=True)  29.9 us
    ppermute x6, starting transfers between devices, from_behind(): return lax.ppermute(value, axis, pairs)  29.3 us
    psum x1, blocking collectives, on_device(): square_sum = lax.psum(jnp.sum(residual * residual, axis=1), 'tp')  17.3 us
    ppermute x6, waiting for transfers between devices, from_behind(): return lax.ppermute(value, axis, pairs)  15.6 us
  transfers between devices with their start and end apart: 11, of which 8 were waited for; matrix products, arithmetic and copies ran while one was open for 2% of the time, Pallas kernels for 0%

commit v1 on v0

v1 whole, which is shorter than its diff:
```python
import math

import jax
import jax.numpy as jnp
from jax import lax
from jax.experimental import pallas as pl
from jax.experimental.pallas import tpu as pltpu
from jax.sharding import Mesh
from jax.sharding import PartitionSpec as P

D = 2048
HEAD_DIM = 128
SEG = 128
ROWS = 256
TP_WIDTH = 512
UNIT_BLOCK = 256
epsilon = 1e-06

SEQ = ("x", "z", "yh")
TP = ("yl", "c")
F32 = jnp.float32
BF16 = jnp.bfloat16


def from_behind(value, by):
    size = lax.axis_size(SEQ)
    return lax.ppermute(value, SEQ, [(i, i + by) for i in range(size - by)])


def swap(value, axis):
    return lax.ppermute(value, axis, [(0, 1), (1, 0)])


def attention_kernel(
    lengths_ref, q_ref, k0_ref, v0_ref, k1_ref, v1_ref, k2_ref, v2_ref, res_ref, att_ref, send_ref
):
    rows = lax.broadcasted_iota(jnp.int32, (ROWS, ROWS), 0)
    cols = lax.broadcasted_iota(jnp.int32, (ROWS, ROWS), 1)

    def valid(index, block):
        low = index < SEG
        bound = jnp.where(low, lengths_ref[2 * block], lengths_ref[2 * block + 1] + SEG)
        return index < bound

    allowed = (
        valid(cols, 0) & (cols <= rows),
        valid(cols, 1),
        valid(cols, 2) & (cols > rows),
    )
    keep = valid(lax.broadcasted_iota(jnp.int32, (ROWS, 1), 0), 0)
    scale = 1.0 / math.sqrt(HEAD_DIM)
    keys = (k0_ref, k1_ref, k2_ref)
    values = (v0_ref, v1_ref, v2_ref)
    for head in range(TP_WIDTH // HEAD_DIM):
        at = pl.ds(head * HEAD_DIM, HEAD_DIM)
        query = q_ref[:, at]
        masked = []
        for key_ref, allow in zip(keys, allowed):
            scores = lax.dot_general(
                query, key_ref[:, at], (((1,), (1,)), ((), ())), preferred_element_type=F32
            )
            masked.append(jnp.where(allow, scores * scale, -1e30))
        top = jnp.max(jnp.maximum(jnp.maximum(masked[0], masked[1]), masked[2]), axis=1, keepdims=True)
        weights = [jnp.where(a, jnp.exp(m - top), 0.0) for a, m in zip(allowed, masked)]
        denominator = jnp.sum(weights[0] + weights[1] + weights[2], axis=1, keepdims=True)
        numerator = jnp.zeros((ROWS, HEAD_DIM), F32)
        for weight, value_ref in zip(weights, values):
            numerator += jnp.dot(weight.astype(BF16), value_ref[:, at], preferred_element_type=F32)
        out = jnp.where(keep, numerator / jnp.where(keep, denominator, 1.0), 0.0).astype(BF16)
        att_ref[:, at] = out
        send_ref[:, at] = (res_ref[:, at] + out.astype(F32)).astype(BF16)


def attention(lengths, q, k0, v0, k1, v1, k2, v2, residual_in):
    vmem = pl.BlockSpec(memory_space=pltpu.VMEM)
    shape = jax.ShapeDtypeStruct(q.shape, BF16)
    return pl.pallas_call(
        attention_kernel,
        out_shape=(shape, shape),
        in_specs=[pl.BlockSpec(memory_space=pltpu.SMEM)] + [vmem] * 8,
        out_specs=(vmem, vmem),
        compiler_params=pltpu.CompilerParams(vmem_limit_bytes=32 << 20),
        cost_estimate=pl.CostEstimate(
            flops=4 * ROWS * 3 * ROWS * TP_WIDTH, bytes_accessed=3 << 20, transcendentals=3 << 18
        ),
        name="attention",
    )(lengths, q, k0, v0, k1, v1, k2, v2, residual_in)


def feed_forward_kernel(order_ref, r0, r1, r2, r3, gain_ref, w_ref, out_ref, x_ref, acc_ref):
    step = pl.program_id(0)
    parts = (r0, r1, r2, r3)

    @pl.when(step == 0)
    def _():
        square = jnp.zeros((ROWS, 1), F32)
        for ref in parts:
            value = ref[...].astype(F32)
            square += jnp.sum(value * value, axis=1, keepdims=True)
        inverse = lax.rsqrt(square / D + epsilon)
        for p, ref in enumerate(parts):
            gain = gain_ref[pl.ds(order_ref[p], 1), :]
            x_ref[p] = (ref[...].astype(F32) * inverse * gain).astype(BF16)
        acc_ref[...] = jnp.zeros_like(acc_ref)

    span = TP_WIDTH // 16

    def block(p, kind):
        start = order_ref[p] * span
        value = w_ref[pl.ds(start, span), pl.ds(kind * 16, 16), :]
        return value.reshape(TP_WIDTH, UNIT_BLOCK)

    gate = jnp.zeros((ROWS, UNIT_BLOCK), F32)
    up = jnp.zeros((ROWS, UNIT_BLOCK), F32)
    for p in range(4):
        gate += jnp.dot(x_ref[p], block(p, 0), preferred_element_type=F32)
        up += jnp.dot(x_ref[p], block(p, 1), preferred_element_type=F32)
    hidden = (gate / (1.0 + jnp.exp(-gate)) * up).astype(BF16)
    for p in range(4):
        acc_ref[p] += lax.dot_general(
            hidden, block(p, 2), (((1,), (1,)), ((), ())), preferred_element_type=F32
        )

    @pl.when(step == pl.num_programs(0) - 1)
    def _():
        out_ref[...] = acc_ref[...].astype(BF16)


def feed_forward(order, parts, gain, weights):
    whole = pl.BlockSpec((ROWS, TP_WIDTH), lambda i, o: (0, 0))
    units = weights.shape[2]
    return pl.pallas_call(
        feed_forward_kernel,
        out_shape=jax.ShapeDtypeStruct((4, ROWS, TP_WIDTH), BF16),
        grid_spec=pltpu.PrefetchScalarGridSpec(
            num_scalar_prefetch=1,
            grid=(units // UNIT_BLOCK,),
            in_specs=[whole] * 4
            + [
                pl.BlockSpec((4, TP_WIDTH), lambda i, o: (0, 0)),
                pl.BlockSpec((weights.shape[0], 48, UNIT_BLOCK), lambda i, o: (0, 0, i)),
            ],
            out_specs=pl.BlockSpec((4, ROWS, TP_WIDTH), lambda i, o: (0, 0, 0)),
            scratch_shapes=[
                pltpu.VMEM((4, ROWS, TP_WIDTH), BF16),
                pltpu.VMEM((4, ROWS, TP_WIDTH), F32),
            ],
        ),
        compiler_params=pltpu.CompilerParams(vmem_limit_bytes=40 << 20),
        cost_estimate=pl.CostEstimate(
            flops=6 * ROWS * D * units, bytes_accessed=14 << 20, transcendentals=ROWS * units
        ),
        name="feed_forward",
    )(order, *parts, gain, weights)


def on_device(
    residual_in,
    query_rows,
    key_rows,
    value_rows,
    lengths,
    norm_gain,
    gate_weight,
    up_weight,
    down_weight,
):
    packed = jnp.concatenate([gate_weight, up_weight, down_weight.T], axis=0)
    near = lax.all_gather(packed, "yh", axis=0, tiled=True)
    weights = lax.all_gather(near, ("x", "z"), axis=0, tiled=True).reshape(128, 48, -1)

    k1, v1 = from_behind(key_rows, 1), from_behind(value_rows, 1)
    lengths1, lengths2 = from_behind(lengths, 1), from_behind(lengths, 2)
    k2, v2 = from_behind(k1, 1), from_behind(v1, 1)
    gain = lax.all_gather(norm_gain, TP, axis=0)

    attended, sent = attention(
        jnp.concatenate([lengths, lengths1, lengths2]),
        query_rows, key_rows, value_rows, k1, v1, k2, v2, residual_in,
    )

    other_chip = swap(sent, "yl")
    other_core = swap(sent, "c")
    diagonal = swap(other_chip, "c")
    own = 2 * lax.axis_index("yl") + lax.axis_index("c")
    order = jnp.stack([own, own ^ 1, own ^ 2, own ^ 3]).astype(jnp.int32)
    partial = feed_forward(order, (sent, other_core, other_chip, diagonal), gain, weights)

    far = partial[2].astype(F32) + swap(partial[3], "c").astype(F32)
    close = partial[0].astype(F32) + swap(partial[1], "c").astype(F32)
    summed = close + swap(far.astype(BF16), "yl").astype(F32)
    mixed = residual_in + attended.astype(F32) + summed
    return attended, mixed


def solution(mesh):
    fine = Mesh(mesh.devices.reshape(4, 8, 4, 2, 2), SEQ + TP)
    placed = (
        P(SEQ, TP),
        P(SEQ, TP),
        P(SEQ, TP),
        P(SEQ, TP),
        P(SEQ),
        P(TP),
        P(SEQ, TP),
        P(SEQ, TP),
        P(TP, SEQ),
    )
    return jax.shard_map(
        on_device,
        mesh=fine,
        in_specs=placed,
        out_specs=(P(SEQ, TP), P(SEQ, TP)),
        check_vma=False,
    )
```

time: 575 us -> 195 us (0.34)
  waiting for transfers between devices: 488 us -> 82 us
  starting transfers between devices: 29.5 us -> 58 us
  matrix products: 15.9 us -> 0 us
  Pallas kernels: 0 us -> 11.7 us
    all_gather x4 -> x1, waiting for transfers between devices: 420 us -> 61.9 us  [on_device(): lax.all_gather(near, ('x', 'z'), axis=0, tiled=True).reshape(128, 48, -1)]
    psum x1 -> x0, waiting for transfers between devices: 50.4 us -> none  [on_device(): lax.psum(partial_value.astype(jnp.bfloat16), 'tp').astype(jnp.float32)]
    ppermute x6 -> x12, starting transfers between devices: 29.3 us -> 58 us  [the longest x6 29.9 us: from_behind(): return lax.ppermute(value, SEQ, [(i, i + by) for i in range(size - by)])]
    all_gather x0 -> x2, blocking collectives: none -> 21.9 us  [the longest x1 16.8 us: on_device(): near = lax.all_gather(packed, 'yh', axis=0, tiled=True)]
    psum x1 -> x0, blocking collectives: 17.3 us -> none  [on_device(): square_sum = lax.psum(jnp.sum(residual * residual, axis=1), 'tp')]
    dot_general x10 -> x0, matrix products: 15.9 us -> none  [the longest x1 7.08 us: on_device(): jnp.dot(hidden, down_full, preferred_element_type=jnp.float32)]
    pallas_call x0 -> x2, Pallas kernels: none -> 11.7 us  [the longest x1 8.5 us: feed_forward(): pl.pallas_call(feed_forward_kernel, out_shape=jax.ShapeDtypeStruct((4, RO...]
    ppermute x6 -> x12, waiting for transfers between devices: 15.6 us -> 20 us  [the longest x6 13.9 us: from_behind(): return lax.ppermute(value, SEQ, [(i, i + by) for i in range(size - by)])]
  transfers between devices with their start and end apart: 11 -> 13, of which waited for: 8 -> 5; matrix products, arithmetic and copies ran while one was open for 2% -> 0% of each run, Pallas kernels for 0% -> 2%
where the time goes in v1:
time: 195 us; the launch traced here: 194 us
  waiting for transfers between devices  82 us (42%)
  starting transfers between devices  58 us (30%)
  blocking collectives  21.9 us (11%)
  between operations  14.2 us (7%)
  Pallas kernels  11.7 us (6%)
  local copies, waits for them, and re-layouts  3.94 us (2%)
  other arithmetic  2.7 us (1%)
    all_gather x1, waiting for transfers between devices, on_device(): lax.all_gather(near, ('x', 'z'), axis=0, tiled=True).reshape(128, 48, -1)  61.9 us
    ppermute x6, starting transfers between devices, from_behind(): return lax.ppermute(value, SEQ, [(i, i + by) for i in range(size - by)])  29.9 us
    ppermute x6, starting transfers between devices, swap(): return lax.ppermute(value, axis, [(0, 1), (1, 0)])  28.1 us
    all_gather x1, blocking collectives, on_device(): near = lax.all_gather(packed, 'yh', axis=0, tiled=True)  16.8 us
    ppermute x6, waiting for transfers between devices, from_behind(): return lax.ppermute(value, SEQ, [(i, i + by) for i in range(size - by)])  13.9 us
    pallas_call x1, Pallas kernels, feed_forward(): pl.pallas_call(feed_forward_kernel, out_shape=jax.ShapeDtypeStruct((4, RO...  8.5 us
    ppermute x6, waiting for transfers between devices, swap(): return lax.ppermute(value, axis, [(0, 1), (1, 0)])  6.15 us
    all_gather x1, blocking collectives, on_device(): gain = lax.all_gather(norm_gain, TP, axis=0)  5.1 us
  transfers between devices with their start and end apart: 13, of which 5 were waited for; matrix products, arithmetic and copies ran while one was open for 0% of the time, Pallas kernels for 2%

profile of v1, /device:TPU:1, one launch (start us, length us, event | category | flops | bytes accessed | tf_op | source)
XLA Modules:
  0.0 194.4 jit_solution(2297131365752898578)
XLA Ops:
  8.1 16.8 %all_gather.14 = bf16[192,1024]{1,0:T(8,128)(2,1)} all-gather(bf16[48,1024]{1,0:T(8,128)(2,1)S(1)} %pad_maximum_fusion), channel_id=1, replica_groups=mesh['x'=4,'z'=8,'yh'=4,'yl'=2,'c'=2] {'yh'}, dimensions={0}, use_global_device_ids=true | all-gather | bytes 491520 | tf_op jit(solution)/shard_map/all_gather | solution.py:169
  24.9 2.9 %collective-permute-start.2 = (bf16[256,512]{1,0:T(8,128)(2,1)}, bf16[256,512]{1,0:T(8,128)(2,1)S(1)}, u32[]{:S(2)}, u32[]{:S(2)}) collective-permute-start(bf16[256,512]{1,0:T(8,128)(2,1)} %k0_ref.1), channel_id=1, source_target_pairs={{0,4},{4,8},{8,12},{12,16},{16,20},{20,24},{24,28},{28,32},{32,36}... | collective-permute-start | bytes 786440 | tf_op jit(solution)/shard_map/ppermute | solution.py:27
  27.8 3.5 %collective-permute-start.3 = (bf16[256,512]{1,0:T(8,128)(2,1)}, bf16[256,512]{1,0:T(8,128)(2,1)S(1)}, u32[]{:S(2)}, u32[]{:S(2)}) collective-permute-start(bf16[256,512]{1,0:T(8,128)(2,1)} %v0_ref.1), channel_id=1, source_target_pairs={{0,4},{4,8},{8,12},{12,16},{16,20},{20,24},{24,28},{28,32},{32,36}... | collective-permute-start | bytes 786440 | tf_op jit(solution)/shard_map/ppermute | solution.py:27
  31.3 2.3 %collective-permute-done.2.k1_ref = bf16[256,512]{1,0:T(8,128)(2,1)S(1)} collective-permute-done((bf16[256,512]{1,0:T(8,128)(2,1)}, bf16[256,512]{1,0:T(8,128)(2,1)S(1)}, u32[]{:S(2)}, u32[]{:S(2)}) %collective-permute-start.2) | collective-permute-done | bytes 262176 | tf_op jit(solution)/shard_map/ppermute | solution.py:27
  33.6 5.2 %collective-permute-start.4 = (bf16[256,512]{1,0:T(8,128)(2,1)S(1)}, bf16[256,512]{1,0:T(8,128)(2,1)S(1)}, u32[]{:S(2)}, u32[]{:S(2)}) collective-permute-start(bf16[256,512]{1,0:T(8,128)(2,1)S(1)} %collective-permute-done.2.k1_ref), channel_id=1, source_target_pairs={{0,4},{4,8},{8,12},{12,16},{16,20},{20,24},{24,28},{28,32},{32,36}... | collective-permute-start | bytes 786440 | tf_op jit(solution)/shard_map/ppermute | solution.py:27
  38.8 5.9 %collective-permute-done.3.v1_ref = bf16[256,512]{1,0:T(8,128)(2,1)S(1)} collective-permute-done((bf16[256,512]{1,0:T(8,128)(2,1)}, bf16[256,512]{1,0:T(8,128)(2,1)S(1)}, u32[]{:S(2)}, u32[]{:S(2)}) %collective-permute-start.3) | collective-permute-done | bytes 262176 | tf_op jit(solution)/shard_map/ppermute | solution.py:27
  44.7 4.9 %collective-permute-start.5 = (bf16[256,512]{1,0:T(8,128)(2,1)S(1)}, bf16[256,512]{1,0:T(8,128)(2,1)S(1)}, u32[]{:S(2)}, u32[]{:S(2)}) collective-permute-start(bf16[256,512]{1,0:T(8,128)(2,1)S(1)} %collective-permute-done.3.v1_ref), channel_id=1, source_target_pairs={{0,4},{4,8},{8,12},{12,16},{16,20},{20,24},{24,28},{28,32},{32,36}... | collective-permute-start | bytes 786440 | tf_op jit(solution)/shard_map/ppermute | solution.py:27
  49.6 4.7 %collective-permute-start = (s32[2]{0:T(128)}, s32[2]{0:T(128)S(1)}, u32[]{:S(2)}, u32[]{:S(2)}) collective-permute-start(s32[2]{0:T(128)} %param.13), channel_id=1, source_target_pairs={{0,4},{4,8},{8,12},{12,16},{16,20},{20,24},{24,28},{28,32},{32,36}... | collective-permute-start | bytes 32 | tf_op jit(solution)/shard_map/ppermute | solution.py:27
  54.3 8.8 %collective-permute-start.1 = (s32[2]{0:T(128)}, s32[2]{0:T(128)S(1)}, u32[]{:S(2)}, u32[]{:S(2)}) collective-permute-start(s32[2]{0:T(128)} %param.13), channel_id=1, source_target_pairs={{0,8},{4,12},{8,16},{12,20},{16,24},{20,28},{24,32},{28,36},{32,40... | collective-permute-start | bytes 32 | tf_op jit(solution)/shard_map/ppermute | solution.py:27
  63.0 5.6 %collective-permute-done = s32[2]{0:T(128)S(1)} collective-permute-done((s32[2]{0:T(128)}, s32[2]{0:T(128)S(1)}, u32[]{:S(2)}, u32[]{:S(2)}) %collective-permute-start) | collective-permute-done | bytes 40 | tf_op jit(solution)/shard_map/ppermute | solution.py:27
  69.4 1.0 copy-done
  72.4 0.9 copy-done.4
  73.3 3.2 %attention.1 = (bf16[256,512]{1,0:T(8,128)(2,1)}, bf16[256,512]{1,0:T(8,128)(2,1)S(1)}) custom-call(s32[6]{0:T(128)S(1)} %pad_add_fusion.lengths_ref, bf16[256,512]{1,0:T(8,128)(2,1)S(1)} %copy-done.2, bf16[256,512]{1,0:T(8,128)(2,1)S(1)} %copy-done.3, bf16[256,512]{1,0:T(8,128)(2,1)S(1)} %copy-done.4, bf16[256,512]{1,0:T(8,128)(2,1)S(1)} %collective-permute-done.2.k1_ref, ...), custom_call_target="tpu_custom_call" | custom-call | flops 402653184 | bytes 3145728 | tf_op jit(solution)/shard_map/attention/pallas_call | solution.py:77
  76.5 2.0 %collective-permute-start.7 = (bf16[256,512]{1,0:T(8,128)(2,1)S(1)}, bf16[256,512]{1,0:T(8,128)(2,1)S(1)}, u32[]{:S(2)}, u32[]{:S(2)}) collective-permute-start(bf16[256,512]{1,0:T(8,128)(2,1)S(1)} %get-tuple-element.5.r0), channel_id=1, source_target_pairs={{0,2},{2,0},{1,3},{3,1},{4,6},{6,4},{5,7},{7,5},{8,10},{10,8},{9,1... | collective-permute-start | bytes 786440 | tf_op jit(solution)/shard_map/ppermute | solution.py:31
  78.6 11.7 %collective-permute-start.6 = (bf16[256,512]{1,0:T(8,128)(2,1)S(1)}, bf16[256,512]{1,0:T(8,128)(2,1)S(1)}, u32[]{:S(2)}, u32[]{:S(2)}) collective-permute-start(bf16[256,512]{1,0:T(8,128)(2,1)S(1)} %get-tuple-element.5.r0), channel_id=1, source_target_pairs={{0,1},{1,0},{2,3},{3,2},{4,5},{5,4},{6,7},{7,6},{8,9},{9,8},{10,11... | collective-permute-start | bytes 786440 | tf_op jit(solution)/shard_map/ppermute | solution.py:31
  90.3 6.3 %collective-permute-start.8 = (bf16[256,512]{1,0:T(8,128)(2,1)S(1)}, bf16[256,512]{1,0:T(8,128)(2,1)S(1)}, u32[]{:S(2)}, u32[]{:S(2)}) collective-permute-start(bf16[256,512]{1,0:T(8,128)(2,1)S(1)} %collective-permute-done.7.r2), channel_id=1, source_target_pairs={{0,1},{1,0},{2,3},{3,2},{4,5},{5,4},{6,7},{7,6},{8,9},{9,8},{10,11... | collective-permute-start | bytes 786440 | tf_op jit(solution)/shard_map/ppermute | solution.py:31
  96.6 5.1 %all-gather.1 = f32[4,1,512]{2,1,0:T(1,128)S(1)} all-gather(f32[1,1,512]{2,1,0:T(1,128)} %bitcast.27), channel_id=2, replica_groups=mesh['x'=4,'z'=8,'yh'=4,'yl'=2,'c'=2] {'yl','c'}, dimensions={0}, use_global_device_ids=true | all-gather | bytes 10240 | tf_op jit(solution)/shard_map/all_gather | solution.py:175
  101.8 61.9 %all-gather.4.cloned.1.call-done = bf16[6144,1024]{1,0:T(8,128)(2,1)} async-done(((bf16[192,1024]{1,0:T(8,128)(2,1)}), bf16[6144,1024]{1,0:T(8,128)(2,1)}) %all-gather.4.cloned.1.call-update) | async-done | bytes 12582928 | tf_op jit(solution)/shard_map/all_gather | solution.py:170
  163.8 8.5 %feed_forward.1 = bf16[4,256,512]{2,1,0:T(8,128)(2,1)S(1)} custom-call(s32[4]{0:T(128)S(1)} %pad_add_fusion.1.order_ref, bf16[256,512]{1,0:T(8,128)(2,1)S(1)} %get-tuple-element.5.r0, bf16[256,512]{1,0:T(8,128)(2,1)S(1)} %collective-permute-done.6.r1, bf16[256,512]{1,0:T(8,128)(2,1)S(1)} %collective-permute-done.7.r2, ...), custom_call_target="tpu_custom_call" | custom-call | flops 3221225472 | bytes 14680064 | tf_op jit(solution)/shard_map/feed_forward/pallas_call | solution.py:132
  172.3 3.0 %collective-permute-start.10 = (bf16[256,512]{1,0:T(8,128)(2,1)S(1)}, bf16[256,512]{1,0:T(8,128)(2,1)S(1)}, u32[]{:S(2)}, u32[]{:S(2)}) collective-permute-start(bf16[256,512]{1,0:T(8,128)(2,1)S(1)} %get-tuple-element.7), channel_id=1, source_target_pairs={{0,1},{1,0},{2,3},{3,2},{4,5},{5,4},{6,7},{7,6},{8,9},{9,8},{10,11... | collective-permute-start | bytes 786440 | tf_op jit(solution)/shard_map/ppermute | solution.py:31
  175.3 1.9 collective-permute-start.9
  177.3 3.1 %collective-permute-start.11 = (bf16[256,512]{1,0:T(8,128)(2,1)S(1)}, bf16[256,512]{1,0:T(8,128)(2,1)S(1)}, u32[]{:S(2)}, u32[]{:S(2)}) collective-permute-start(bf16[256,512]{1,0:T(8,128)(2,1)S(1)} %fusion), channel_id=1, source_target_pairs={{0,2},{2,0},{1,3},{3,1},{4,6},{6,4},{5,7},{7,5},{8,10},{10,8},{9,1... | collective-permute-start | bytes 786440 | tf_op jit(solution)/shard_map/ppermute | solution.py:31
  180.4 6.1 %collective-permute-done.11 = bf16[256,512]{1,0:T(8,128)(2,1)S(1)} collective-permute-done((bf16[256,512]{1,0:T(8,128)(2,1)S(1)}, bf16[256,512]{1,0:T(8,128)(2,1)S(1)}, u32[]{:S(2)}, u32[]{:S(2)}) %collective-permute-start.11) | collective-permute-done | bytes 262176 | tf_op jit(solution)/shard_map/ppermute | solution.py:31
  186.6 1.0 fusion.2
  (26 shorter events, 3.8 us)
Async XLA Ops:
  7.2 179.4 %copy-start.1 = (f32[256,512]{1,0:T(8,128)S(1)}, f32[256,512]{1,0:T(8,128)}, u32[]{:S(2)}) copy-start(f32[256,512]{1,0:T(8,128)} %res_ref.1) | copy-start | bytes 1572868
  7.2 156.6 %all-gather.4.cloned.1.call-start = ((), (), s32[]{:S(2)}) async-start(), calls=%async_computation | async-start | bytes 12976128 | tf_op jit(solution)/shard_map/all_gather | solution.py:170
  24.9 8.7 %collective-permute-start.2 = (bf16[256,512]{1,0:T(8,128)(2,1)}, bf16[256,512]{1,0:T(8,128)(2,1)S(1)}, u32[]{:S(2)}, u32[]{:S(2)}) collective-permute-start(bf16[256,512]{1,0:T(8,128)(2,1)} %k0_ref.1), channel_id=1, source_target_pairs={{0,4},{4,8},{8,12},{12,16},{16,20},{20,24},{24,28},{28,32},{32,36}... | collective-permute-start | bytes 786440 | tf_op jit(solution)/shard_map/ppermute | solution.py:27
  27.8 16.9 %collective-permute-start.3 = (bf16[256,512]{1,0:T(8,128)(2,1)}, bf16[256,512]{1,0:T(8,128)(2,1)S(1)}, u32[]{:S(2)}, u32[]{:S(2)}) collective-permute-start(bf16[256,512]{1,0:T(8,128)(2,1)} %v0_ref.1), channel_id=1, source_target_pairs={{0,4},{4,8},{8,12},{12,16},{16,20},{20,24},{24,28},{28,32},{32,36}... | collective-permute-start | bytes 786440 | tf_op jit(solution)/shard_map/ppermute | solution.py:27
  33.6 35.8 %collective-permute-start.4 = (bf16[256,512]{1,0:T(8,128)(2,1)S(1)}, bf16[256,512]{1,0:T(8,128)(2,1)S(1)}, u32[]{:S(2)}, u32[]{:S(2)}) collective-permute-start(bf16[256,512]{1,0:T(8,128)(2,1)S(1)} %collective-permute-done.2.k1_ref), channel_id=1, source_target_pairs={{0,4},{4,8},{8,12},{12,16},{16,20},{20,24},{24,28},{28,32},{32,36}... | collective-permute-start | bytes 786440 | tf_op jit(solution)/shard_map/ppermute | solution.py:27
  44.7 24.8 %collective-permute-start.5 = (bf16[256,512]{1,0:T(8,128)(2,1)S(1)}, bf16[256,512]{1,0:T(8,128)(2,1)S(1)}, u32[]{:S(2)}, u32[]{:S(2)}) collective-permute-start(bf16[256,512]{1,0:T(8,128)(2,1)S(1)} %collective-permute-done.3.v1_ref), channel_id=1, source_target_pairs={{0,4},{4,8},{8,12},{12,16},{16,20},{20,24},{24,28},{28,32},{32,36}... | collective-permute-start | bytes 786440 | tf_op jit(solution)/shard_map/ppermute | solution.py:27
  49.6 19.1 %collective-permute-start = (s32[2]{0:T(128)}, s32[2]{0:T(128)S(1)}, u32[]{:S(2)}, u32[]{:S(2)}) collective-permute-start(s32[2]{0:T(128)} %param.13), channel_id=1, source_target_pairs={{0,4},{4,8},{8,12},{12,16},{16,20},{20,24},{24,28},{28,32},{32,36}... | collective-permute-start | bytes 32 | tf_op jit(solution)/shard_map/ppermute | solution.py:27
  54.3 14.4 %collective-permute-start.1 = (s32[2]{0:T(128)}, s32[2]{0:T(128)S(1)}, u32[]{:S(2)}, u32[]{:S(2)}) collective-permute-start(s32[2]{0:T(128)} %param.13), channel_id=1, source_target_pairs={{0,8},{4,12},{8,16},{12,20},{16,24},{20,28},{24,32},{28,36},{32,40... | collective-permute-start | bytes 32 | tf_op jit(solution)/shard_map/ppermute | solution.py:27
  69.4 1.0 copy-start
  70.5 0.9 copy-start.2
  71.4 0.9 copy-start.3
  72.4 1.0 copy-start.4
  76.5 110.1 %copy-start.5 = (bf16[256,512]{1,0:T(8,128)(2,1)S(1)}, bf16[256,512]{1,0:T(8,128)(2,1)}, u32[]{:S(2)}) copy-start(bf16[256,512]{1,0:T(8,128)(2,1)} %get-tuple-element.2) | copy-start | bytes 786436
  76.5 13.8 %collective-permute-start.7 = (bf16[256,512]{1,0:T(8,128)(2,1)S(1)}, bf16[256,512]{1,0:T(8,128)(2,1)S(1)}, u32[]{:S(2)}, u32[]{:S(2)}) collective-permute-start(bf16[256,512]{1,0:T(8,128)(2,1)S(1)} %get-tuple-element.5.r0), channel_id=1, source_target_pairs={{0,2},{2,0},{1,3},{3,1},{4,6},{6,4},{5,7},{7,5},{8,10},{10,8},{9,1... | collective-permute-start | bytes 786440 | tf_op jit(solution)/shard_map/ppermute | solution.py:31
  78.6 23.3 %collective-permute-start.6 = (bf16[256,512]{1,0:T(8,128)(2,1)S(1)}, bf16[256,512]{1,0:T(8,128)(2,1)S(1)}, u32[]{:S(2)}, u32[]{:S(2)}) collective-permute-start(bf16[256,512]{1,0:T(8,128)(2,1)S(1)} %get-tuple-element.5.r0), channel_id=1, source_target_pairs={{0,1},{1,0},{2,3},{3,2},{4,5},{5,4},{6,7},{7,6},{8,9},{9,8},{10,11... | collective-permute-start | bytes 786440 | tf_op jit(solution)/shard_map/ppermute | solution.py:31
  90.3 11.5 %collective-permute-start.8 = (bf16[256,512]{1,0:T(8,128)(2,1)S(1)}, bf16[256,512]{1,0:T(8,128)(2,1)S(1)}, u32[]{:S(2)}, u32[]{:S(2)}) collective-permute-start(bf16[256,512]{1,0:T(8,128)(2,1)S(1)} %collective-permute-done.7.r2), channel_id=1, source_target_pairs={{0,1},{1,0},{2,3},{3,2},{4,5},{5,4},{6,7},{7,6},{8,9},{9,8},{10,11... | collective-permute-start | bytes 786440 | tf_op jit(solution)/shard_map/ppermute | solution.py:31
  172.3 4.9 %collective-permute-start.10 = (bf16[256,512]{1,0:T(8,128)(2,1)S(1)}, bf16[256,512]{1,0:T(8,128)(2,1)S(1)}, u32[]{:S(2)}, u32[]{:S(2)}) collective-permute-start(bf16[256,512]{1,0:T(8,128)(2,1)S(1)} %get-tuple-element.7), channel_id=1, source_target_pairs={{0,1},{1,0},{2,3},{3,2},{4,5},{5,4},{6,7},{7,6},{8,9},{9,8},{10,11... | collective-permute-start | bytes 786440 | tf_op jit(solution)/shard_map/ppermute | solution.py:31
  175.3 5.1 %collective-permute-start.9 = (bf16[256,512]{1,0:T(8,128)(2,1)S(1)}, bf16[256,512]{1,0:T(8,128)(2,1)S(1)}, u32[]{:S(2)}, u32[]{:S(2)}) collective-permute-start(bf16[256,512]{1,0:T(8,128)(2,1)S(1)} %get-tuple-element.6), channel_id=1, source_target_pairs={{0,1},{1,0},{2,3},{3,2},{4,5},{5,4},{6,7},{7,6},{8,9},{9,8},{10,11... | collective-permute-start | bytes 786440 | tf_op jit(solution)/shard_map/ppermute | solution.py:31
  177.3 9.3 %collective-permute-start.11 = (bf16[256,512]{1,0:T(8,128)(2,1)S(1)}, bf16[256,512]{1,0:T(8,128)(2,1)S(1)}, u32[]{:S(2)}, u32[]{:S(2)}) collective-permute-start(bf16[256,512]{1,0:T(8,128)(2,1)S(1)} %fusion), channel_id=1, source_target_pairs={{0,2},{2,0},{1,3},{3,1},{4,6},{6,4},{5,7},{7,5},{8,10},{10,8},{9,1... | collective-permute-start | bytes 786440 | tf_op jit(solution)/shard_map/ppermute | solution.py:31
Sparse Core Ops, SparseCore 0:
  25.0 138.7 all-gather.3

commit v2 on v1

v2 whole, which is shorter than its diff:
```python
import math

import jax
import jax.numpy as jnp
from jax import lax
from jax.experimental import pallas as pl
from jax.experimental.pallas import tpu as pltpu
from jax.sharding import Mesh
from jax.sharding import PartitionSpec as P

D = 2048
HEAD_DIM = 128
SEG = 128
ROWS = 256
TP_WIDTH = 512
UNIT_BLOCK = 256
epsilon = 1e-06

SEQ = ("x", "z", "yh")
TP = ("yl", "c")
F32 = jnp.float32
BF16 = jnp.bfloat16


def from_behind(value, by):
    size = lax.axis_size(SEQ)
    return lax.ppermute(value, SEQ, [(i, i + by) for i in range(size - by)])


def around(value, axis, by):
    size = lax.axis_size(axis)
    return lax.ppermute(value, axis, [(i, (i + by) % size) for i in range(size)])


def swap(value, axis):
    return lax.ppermute(value, axis, [(0, 1), (1, 0)])


def swap_x(value):
    return lax.ppermute(value, "x", [(i, i ^ 1) for i in range(4)])


def attention_kernel(
    lengths_ref, q_ref, k0_ref, v0_ref, k1_ref, v1_ref, k2_ref, v2_ref, res_ref, att_ref, send_ref
):
    rows = lax.broadcasted_iota(jnp.int32, (ROWS, ROWS), 0)
    cols = lax.broadcasted_iota(jnp.int32, (ROWS, ROWS), 1)
    col = lax.broadcasted_iota(jnp.int32, (1, ROWS), 1)

    def valid(key_ref):
        first = key_ref[pl.ds(ROWS, 8), pl.ds(0, ROWS)].astype(F32)[0:1, :].astype(jnp.int32)
        second = key_ref[pl.ds(ROWS + 8, 8), pl.ds(0, ROWS)].astype(F32)[0:1, :].astype(jnp.int32)
        return (col < jnp.where(col < SEG, first, second + SEG)).astype(jnp.int32)

    allowed = (
        (valid(k0_ref) > 0) & (cols <= rows),
        (valid(k1_ref) + jnp.zeros_like(cols)) > 0,
        (valid(k2_ref) > 0) & (cols > rows),
    )
    row = lax.broadcasted_iota(jnp.int32, (ROWS, 1), 0)
    keep = row < jnp.where(row < SEG, lengths_ref[0], lengths_ref[1] + SEG)
    scale = 1.0 / math.sqrt(HEAD_DIM)
    keys = (k0_ref, k1_ref, k2_ref)
    values = (v0_ref, v1_ref, v2_ref)
    for head in range(TP_WIDTH // HEAD_DIM):
        at = pl.ds(head * HEAD_DIM, HEAD_DIM)
        query = q_ref[:, at]
        masked = []
        for key_ref, allow in zip(keys, allowed):
            scores = lax.dot_general(
                query,
                key_ref[pl.ds(0, ROWS), at],
                (((1,), (1,)), ((), ())),
                preferred_element_type=F32,
            )
            masked.append(jnp.where(allow, scores * scale, -1e30))
        top = jnp.max(jnp.maximum(jnp.maximum(masked[0], masked[1]), masked[2]), axis=1, keepdims=True)
        weights = [jnp.where(a, jnp.exp(m - top), 0.0) for a, m in zip(allowed, masked)]
        denominator = jnp.sum(weights[0] + weights[1] + weights[2], axis=1, keepdims=True)
        numerator = jnp.zeros((ROWS, HEAD_DIM), F32)
        for weight, value_ref in zip(weights, values):
            numerator += jnp.dot(weight.astype(BF16), value_ref[:, at], preferred_element_type=F32)
        out = jnp.where(keep, numerator / jnp.where(keep, denominator, 1.0), 0.0).astype(BF16)
        att_ref[:, at] = out
        send_ref[:, at] = (res_ref[:, at] + out.astype(F32)).astype(BF16)


def attention(lengths, q, k0, v0, k1, v1, k2, v2, residual_in):
    shape = jax.ShapeDtypeStruct(q.shape, BF16)
    return pl.pallas_call(
        attention_kernel,
        out_shape=(shape, shape),
        in_specs=[pl.BlockSpec(memory_space=pltpu.SMEM)] + [pl.BlockSpec()] * 8,
        out_specs=(pl.BlockSpec(), pl.BlockSpec()),
        compiler_params=pltpu.CompilerParams(vmem_limit_bytes=32 << 20),
        cost_estimate=pl.CostEstimate(
            flops=4 * ROWS * 3 * ROWS * TP_WIDTH, bytes_accessed=3 << 20, transcendentals=3 << 18
        ),
        name="attention",
    )(lengths, q, k0, v0, k1, v1, k2, v2, residual_in)


def feed_forward_kernel(place_ref, *refs):
    parts, gain_ref, w_ref, outs, x_ref, acc_ref = (
        refs[:8], refs[8], refs[9], refs[10:18], refs[18], refs[19],
    )
    step = pl.program_id(0)

    @pl.when(step == 0)
    def _():
        for g in range(2):
            square = jnp.zeros((ROWS, 1), F32)
            for p in range(4):
                value = parts[4 * g + p][...].astype(F32)
                square += jnp.sum(value * value, axis=1, keepdims=True)
            inverse = lax.rsqrt(square / D + epsilon)
            for p in range(4):
                gain = gain_ref[pl.ds(place_ref[p], 1), :]
                value = parts[4 * g + p][...].astype(F32)
                x_ref[p, pl.ds(g * ROWS, ROWS), :] = (value * inverse * gain).astype(BF16)
        acc_ref[...] = jnp.zeros_like(acc_ref)

    def block(p, kind):
        pieces = [
            w_ref[:, pl.ds(place_ref[4 + p], 1), pl.ds(place_ref[8 + y], 1), pl.ds(kind * 16, 16), :]
            for y in range(4)
        ]
        return jnp.concatenate(pieces, axis=2).reshape(TP_WIDTH, UNIT_BLOCK)

    gate = jnp.zeros((2 * ROWS, UNIT_BLOCK), F32)
    up = jnp.zeros((2 * ROWS, UNIT_BLOCK), F32)
    for p in range(4):
        gate += jnp.dot(x_ref[p], block(p, 0), preferred_element_type=F32)
        up += jnp.dot(x_ref[p], block(p, 1), preferred_element_type=F32)
    hidden = (gate / (1.0 + jnp.exp(-gate)) * up).astype(BF16)
    for p in range(4):
        acc_ref[p] += lax.dot_general(
            hidden, block(p, 2), (((1,), (1,)), ((), ())), preferred_element_type=F32
        )

    @pl.when(step == pl.num_programs(0) - 1)
    def _():
        for g in range(2):
            for p in range(4):
                outs[4 * g + p][...] = acc_ref[p, pl.ds(g * ROWS, ROWS), :].astype(BF16)


def feed_forward(place, parts, gain, weights):
    whole = pl.BlockSpec((ROWS, TP_WIDTH), lambda i, o: (0, 0))
    units = weights.shape[4]
    return pl.pallas_call(
        feed_forward_kernel,
        out_shape=[jax.ShapeDtypeStruct((ROWS, TP_WIDTH), BF16)] * 8,
        grid_spec=pltpu.PrefetchScalarGridSpec(
            num_scalar_prefetch=1,
            grid=(units // UNIT_BLOCK,),
            in_specs=[whole] * 8
            + [
                pl.BlockSpec((4, TP_WIDTH), lambda i, o: (0, 0)),
                pl.BlockSpec((8, 4, 4, 48, UNIT_BLOCK), lambda i, o: (0, 0, 0, 0, i)),
            ],
            out_specs=[whole] * 8,
            scratch_shapes=[
                pltpu.VMEM((4, 2 * ROWS, TP_WIDTH), BF16),
                pltpu.VMEM((4, 2 * ROWS, TP_WIDTH), F32),
            ],
        ),
        compiler_params=pltpu.CompilerParams(vmem_limit_bytes=48 << 20),
        cost_estimate=pl.CostEstimate(
            flops=12 * ROWS * D * units, bytes_accessed=10 << 20, transcendentals=2 * ROWS * units
        ),
        name="feed_forward",
    )(place, *parts, gain, weights)


def on_device(
    residual_in,
    query_rows,
    key_rows,
    value_rows,
    lengths,
    norm_gain,
    gate_weight,
    up_weight,
    down_weight,
):
    x, yh = lax.axis_index("x"), lax.axis_index("yh")
    half = gate_weight.shape[1] // 2

    packed = jnp.concatenate([gate_weight, up_weight, down_weight.T], axis=0)
    near = [packed] + [around(packed, "yh", by) for by in (1, 2, 3)]
    parity = x & 1
    mine = jnp.stack([lax.dynamic_slice_in_dim(w, parity * half, half, 1) for w in near])
    other = jnp.stack([lax.dynamic_slice_in_dim(w, (1 - parity) * half, half, 1) for w in near])
    plane = jnp.stack([mine, around(other, "x", 1), around(mine, "x", 2), around(other, "x", 3)])
    weights = lax.all_gather(plane, "z", axis=0)

    tail = jnp.broadcast_to(
        jnp.repeat(lengths.astype(BF16), 8)[:, None], (16, key_rows.shape[1])
    )
    k0 = jnp.concatenate([key_rows, tail], axis=0)
    k1, v1 = from_behind(k0, 1), from_behind(value_rows, 1)
    k2, v2 = from_behind(k1, 1), from_behind(v1, 1)
    gain = lax.all_gather(norm_gain, TP, axis=0)
    residual_in, gain = lax.optimization_barrier((residual_in, gain))

    attended, sent = attention(
        lengths, query_rows, k0, value_rows, k1, v1, k2, v2, residual_in
    )

    partner = swap_x(sent)
    parts = []
    for start in (sent, partner):
        chip = swap(start, "yl")
        parts += [start, swap(start, "c"), chip, swap(chip, "c")]
    own = 2 * lax.axis_index("yl") + lax.axis_index("c")
    order = [own, own ^ 1, own ^ 2, own ^ 3]
    place = order + [(x - t) & 3 for t in order] + [(yh - y) & 3 for y in range(4)]
    outs = feed_forward(jnp.stack(place).astype(jnp.int32), parts, gain, weights)

    def add(left, right):
        return left.astype(F32) + right.astype(F32)

    def cores(g, p):
        return add(outs[4 * g + p], swap(outs[4 * g + p + 1], "c"))

    far = cores(0, 2) + swap_x(cores(1, 2).astype(BF16)).astype(F32)
    close = cores(0, 0) + swap_x(cores(1, 0).astype(BF16)).astype(F32)
    summed = close + swap(far.astype(BF16), "yl").astype(F32)
    mixed = residual_in + attended.astype(F32) + summed
    return attended, mixed


def solution(mesh):
    fine = Mesh(mesh.devices.reshape(4, 8, 4, 2, 2), SEQ + TP)
    placed = (
        P(SEQ, TP),
        P(SEQ, TP),
        P(SEQ, TP),
        P(SEQ, TP),
        P(SEQ),
        P(TP),
        P(SEQ, TP),
        P(SEQ, TP),
        P(TP, SEQ),
    )
    return jax.shard_map(
        on_device,
        mesh=fine,
        in_specs=placed,
        out_specs=(P(SEQ, TP), P(SEQ, TP)),
        check_vma=False,
    )
```

time: 195 us -> 192 us (0.985)
  waiting for transfers between devices: 82 us -> 27.2 us
  starting transfers between devices: 58 us -> 99 us
  blocking collectives: 21.9 us -> 30.3 us
  other arithmetic: 2.7 us -> 4.79 us
    all_gather x1, waiting for transfers between devices: 61.9 us -> 7 us  [on_device(): weights = lax.all_gather(plane, 'z', axis=0)]
    ppermute x0 -> x9, starting transfers between devices: none -> 34.9 us  [the longest x6 24.3 us: around(): lax.ppermute(value, axis, [(i, (i + by) % size) for i in range(size)])]
    all_gather x1, blocking collectives: 5.1 us -> 30.3 us  [on_device(): gain = lax.all_gather(norm_gain, TP, axis=0)]
    ppermute x6 -> x11, starting transfers between devices: 28.1 us -> 45.9 us  [swap(): return lax.ppermute(value, axis, [(0, 1), (1, 0)])]
    all_gather x1 -> x0, blocking collectives: 16.8 us -> none  [on_device(): near = lax.all_gather(packed, 'yh', axis=0, tiled=True)]
    ppermute x6 -> x4, waiting for transfers between devices: 13.9 us -> 1.04 us  [from_behind(): return lax.ppermute(value, SEQ, [(i, i + by) for i in range(size - by)])]
    ppermute x0 -> x9, waiting for transfers between devices: none -> 12.1 us  [the longest x6 9.95 us: around(): lax.ppermute(value, axis, [(i, (i + by) % size) for i in range(size)])]
    ppermute x6 -> x4, starting transfers between devices: 29.9 us -> 18.2 us  [from_behind(): return lax.ppermute(value, SEQ, [(i, i + by) for i in range(size - by)])]
  transfers between devices with their start and end apart: 13 -> 25, of which waited for: 5 -> 9; matrix products, arithmetic and copies ran while one was open for 0% -> 1% of each run, Pallas kernels for 2% -> 2%
where the time goes in v2:
time: 192 us; the launch traced here: 190 us
  starting transfers between devices  99 us (52%)
  blocking collectives  30.3 us (16%)
  waiting for transfers between devices  27.2 us (14%)
  between operations  14.5 us (8%)
  Pallas kernels  10.7 us (6%)
  other arithmetic  4.79 us (2%)
  local copies, waits for them, and re-layouts  3.9 us (2%)
    ppermute x11, starting transfers between devices, swap(): return lax.ppermute(value, axis, [(0, 1), (1, 0)])  45.9 us
    all_gather x1, blocking collectives, on_device(): gain = lax.all_gather(norm_gain, TP, axis=0)  30.3 us
    ppermute x6, starting transfers between devices, around(): lax.ppermute(value, axis, [(i, (i + by) % size) for i in range(size)])  24.3 us
    ppermute x4, starting transfers between devices, from_behind(): return lax.ppermute(value, SEQ, [(i, i + by) for i in range(size - by)])  18.2 us
    ppermute x3, starting transfers between devices, swap_x(): return lax.ppermute(value, 'x', [(i, i ^ 1) for i in range(4)])  10.6 us
    ppermute x6, waiting for transfers between devices, around(): lax.ppermute(value, axis, [(i, (i + by) % size) for i in range(size)])  9.95 us
    pallas_call x1, Pallas kernels, feed_forward(): pl.pallas_call(feed_forward_kernel, out_shape=[jax.ShapeDtypeStruct((ROWS...  7.52 us
    ppermute x11, waiting for transfers between devices, swap(): return lax.ppermute(value, axis, [(0, 1), (1, 0)])  7.02 us
  transfers between devices with their start and end apart: 25, of which 9 were waited for; matrix products, arithmetic and copies ran while one was open for 1% of the time, Pallas kernels for 2%

profile of v2, /device:TPU:1, one launch (start us, length us, event | category | flops | bytes accessed | tf_op | source)
XLA Modules:
  0.0 190.3 jit_solution(10625255478543705810)
XLA Ops:
  8.0 6.7 %collective-permute-start.13 = (bf16[48,1024]{1,0:T(8,128)(2,1)S(1)}, bf16[48,1024]{1,0:T(8,128)(2,1)S(1)}, u32[]{:S(2)}, u32[]{:S(2)}) collective-permute-start(bf16[48,1024]{1,0:T(8,128)(2,1)S(1)} %pad_maximum_fusion.4), channel_id=1, source_target_pairs={{0,12},{4,0},{8,4},{12,8},{1,13},{5,1},{9,5},{13,9},{2,14},{6,2},{... | collective-permute-start | bytes 294920 | tf_op jit(solution)/shard_map/ppermute | solution.py:32
  14.7 3.5 %collective-permute-start.12 = (bf16[48,1024]{1,0:T(8,128)(2,1)S(1)}, bf16[48,1024]{1,0:T(8,128)(2,1)S(1)}, u32[]{:S(2)}, u32[]{:S(2)}) collective-permute-start(bf16[48,1024]{1,0:T(8,128)(2,1)S(1)} %pad_maximum_fusion.4), channel_id=1, source_target_pairs={{0,8},{4,12},{8,0},{12,4},{1,9},{5,13},{9,1},{13,5},{2,10},{6,14},... | collective-permute-start | bytes 294920 | tf_op jit(solution)/shard_map/ppermute | solution.py:32
  18.3 4.2 %collective-permute-start.11 = (bf16[48,1024]{1,0:T(8,128)(2,1)S(1)}, bf16[48,1024]{1,0:T(8,128)(2,1)S(1)}, u32[]{:S(2)}, u32[]{:S(2)}) collective-permute-start(bf16[48,1024]{1,0:T(8,128)(2,1)S(1)} %pad_maximum_fusion.4), channel_id=1, source_target_pairs={{0,4},{4,8},{8,12},{12,0},{1,5},{5,9},{9,13},{13,1},{2,6},{6,10},{... | collective-permute-start | bytes 294920 | tf_op jit(solution)/shard_map/ppermute | solution.py:32
  26.2 4.6 %collective-permute-start.15 = (bf16[4,48,512]{2,1,0:T(8,128)(2,1)S(1)}, bf16[4,48,512]{2,1,0:T(8,128)(2,1)S(1)}, u32[]{:S(2)}, u32[]{:S(2)}) collective-permute-start(bf16[4,48,512]{2,1,0:T(8,128)(2,1)S(1)} %get-tuple-element.27), channel_id=1, source_target_pairs={{0,256},{128,384},{256,0},{384,128},{1,257},{129,385},{257,1},{385... | collective-permute-start | bytes 589832 | tf_op jit(solution)/shard_map/ppermute | solution.py:32
  30.9 2.8 %collective-permute-start.16 = (bf16[4,48,512]{2,1,0:T(8,128)(2,1)S(1)}, bf16[4,48,512]{2,1,0:T(8,128)(2,1)S(1)}, u32[]{:S(2)}, u32[]{:S(2)}) collective-permute-start(bf16[4,48,512]{2,1,0:T(8,128)(2,1)S(1)} %pad_maximum_fusion.3), channel_id=1, source_target_pairs={{0,384},{128,0},{256,128},{384,256},{1,385},{129,1},{257,129},{385... | collective-permute-start | bytes 589832 | tf_op jit(solution)/shard_map/ppermute | solution.py:32
  33.6 2.5 %collective-permute-start.14 = (bf16[4,48,512]{2,1,0:T(8,128)(2,1)S(1)}, bf16[4,48,512]{2,1,0:T(8,128)(2,1)S(1)}, u32[]{:S(2)}, u32[]{:S(2)}) collective-permute-start(bf16[4,48,512]{2,1,0:T(8,128)(2,1)S(1)} %pad_maximum_fusion.3), channel_id=1, source_target_pairs={{0,128},{128,256},{256,384},{384,0},{1,129},{129,257},{257,385},{3... | collective-permute-start | bytes 589832 | tf_op jit(solution)/shard_map/ppermute | solution.py:32
  36.2 3.5 %collective-permute-done.16 = bf16[4,48,512]{2,1,0:T(8,128)(2,1)S(1)} collective-permute-done((bf16[4,48,512]{2,1,0:T(8,128)(2,1)S(1)}, bf16[4,48,512]{2,1,0:T(8,128)(2,1)S(1)}, u32[]{:S(2)}, u32[]{:S(2)}) %collective-permute-start.16) | collective-permute-done | bytes 196640 | tf_op jit(solution)/shard_map/ppermute | solution.py:32
  39.6 2.9 %collective-permute-done.14 = bf16[4,48,512]{2,1,0:T(8,128)(2,1)S(1)} collective-permute-done((bf16[4,48,512]{2,1,0:T(8,128)(2,1)S(1)}, bf16[4,48,512]{2,1,0:T(8,128)(2,1)S(1)}, u32[]{:S(2)}, u32[]{:S(2)}) %collective-permute-start.14) | collective-permute-done | bytes 196640 | tf_op jit(solution)/shard_map/ppermute | solution.py:32
  47.5 6.2 %collective-permute-start.1 = (bf16[256,512]{1,0:T(8,128)(2,1)}, bf16[256,512]{1,0:T(8,128)(2,1)S(1)}, u32[]{:S(2)}, u32[]{:S(2)}) collective-permute-start(bf16[256,512]{1,0:T(8,128)(2,1)} %v0_ref.1), channel_id=1, source_target_pairs={{0,4},{4,8},{8,12},{12,16},{16,20},{20,24},{24,28},{28,32},{32,36}... | collective-permute-start | bytes 786440 | tf_op jit(solution)/shard_map/ppermute | solution.py:27
  53.7 4.8 %collective-permute-start.2 = (bf16[272,512]{1,0:T(8,128)(2,1)S(1)}, bf16[272,512]{1,0:T(8,128)(2,1)S(1)}, u32[]{:S(2)}, u32[]{:S(2)}) collective-permute-start(bf16[272,512]{1,0:T(8,128)(2,1)S(1)} %collective-permute-done.k1_ref), channel_id=1, source_target_pairs={{0,4},{4,8},{8,12},{12,16},{16,20},{20,24},{24,28},{28,32},{32,36}... | collective-permute-start | bytes 835592 | tf_op jit(solution)/shard_map/ppermute | solution.py:27
  59.5 5.1 %collective-permute-start.3 = (bf16[256,512]{1,0:T(8,128)(2,1)S(1)}, bf16[256,512]{1,0:T(8,128)(2,1)S(1)}, u32[]{:S(2)}, u32[]{:S(2)}) collective-permute-start(bf16[256,512]{1,0:T(8,128)(2,1)S(1)} %collective-permute-done.1.v1_ref), channel_id=1, source_target_pairs={{0,4},{4,8},{8,12},{12,16},{16,20},{20,24},{24,28},{28,32},{32,36}... | collective-permute-start | bytes 786440 | tf_op jit(solution)/shard_map/ppermute | solution.py:27
  64.6 30.3 %all-gather.2 = f32[4,1,512]{2,1,0:T(1,128)S(1)} all-gather(f32[1,1,512]{2,1,0:T(1,128)} %bitcast.44), channel_id=2, replica_groups=mesh['x'=4,'z'=8,'yh'=4,'yl'=2,'c'=2] {'yl','c'}, dimensions={0}, use_global_device_ids=true | all-gather | bytes 10240 | tf_op jit(solution)/shard_map/all_gather | solution.py:204
  98.5 3.2 %attention.1 = (bf16[256,512]{1,0:T(8,128)(2,1)}, bf16[256,512]{1,0:T(8,128)(2,1)S(1)}) custom-call(s32[2]{0:T(128)S(1)} %copy-done.4, bf16[256,512]{1,0:T(8,128)(2,1)S(1)} %copy-done.2, bf16[272,512]{1,0:T(8,128)(2,1)S(1)} %pad_maximum_fusion.1.k0_ref, bf16[256,512]{1,0:T(8,128)(2,1)S(1)} %copy-done.3, bf16[272,512]{1,0:T(8,128)(2,1)S(1)} %collective-permute-done.k1_ref, ...), custom_call_target="tpu_custom_call" | custom-call | flops 402653184 | bytes 3145728 | tf_op jit(solution)/shard_map/attention/pallas_call | solution.py:90
  101.7 5.1 %collective-permute-start.7 = (bf16[256,512]{1,0:T(8,128)(2,1)S(1)}, bf16[256,512]{1,0:T(8,128)(2,1)S(1)}, u32[]{:S(2)}, u32[]{:S(2)}) collective-permute-start(bf16[256,512]{1,0:T(8,128)(2,1)S(1)} %get-tuple-element.16.refs_0_), channel_id=1, source_target_pairs={{0,128},{128,0},{256,384},{384,256},{1,129},{129,1},{257,385},{385... | collective-permute-start | bytes 786440 | tf_op jit(solution)/shard_map/ppermute | solution.py:40
  106.8 11.4 %collective-permute-start.5 = (bf16[256,512]{1,0:T(8,128)(2,1)S(1)}, bf16[256,512]{1,0:T(8,128)(2,1)S(1)}, u32[]{:S(2)}, u32[]{:S(2)}) collective-permute-start(bf16[256,512]{1,0:T(8,128)(2,1)S(1)} %get-tuple-element.16.refs_0_), channel_id=1, source_target_pairs={{0,2},{2,0},{1,3},{3,1},{4,6},{6,4},{5,7},{7,5},{8,10},{10,8},{9,1... | collective-permute-start | bytes 786440 | tf_op jit(solution)/shard_map/ppermute | solution.py:36
  118.2 5.5 %collective-permute-start.9 = (bf16[256,512]{1,0:T(8,128)(2,1)S(1)}, bf16[256,512]{1,0:T(8,128)(2,1)S(1)}, u32[]{:S(2)}, u32[]{:S(2)}) collective-permute-start(bf16[256,512]{1,0:T(8,128)(2,1)S(1)} %collective-permute-done.7.refs_4_), channel_id=1, source_target_pairs={{0,2},{2,0},{1,3},{3,1},{4,6},{6,4},{5,7},{7,5},{8,10},{10,8},{9,1... | collective-permute-start | bytes 786440 | tf_op jit(solution)/shard_map/ppermute | solution.py:36
  123.7 3.9 %collective-permute-start.4 = (bf16[256,512]{1,0:T(8,128)(2,1)S(1)}, bf16[256,512]{1,0:T(8,128)(2,1)S(1)}, u32[]{:S(2)}, u32[]{:S(2)}) collective-permute-start(bf16[256,512]{1,0:T(8,128)(2,1)S(1)} %get-tuple-element.16.refs_0_), channel_id=1, source_target_pairs={{0,1},{1,0},{2,3},{3,2},{4,5},{5,4},{6,7},{7,6},{8,9},{9,8},{10,11... | collective-permute-start | bytes 786440 | tf_op jit(solution)/shard_map/ppermute | solution.py:36
  129.6 2.4 %collective-permute-start.6 = (bf16[256,512]{1,0:T(8,128)(2,1)S(1)}, bf16[256,512]{1,0:T(8,128)(2,1)S(1)}, u32[]{:S(2)}, u32[]{:S(2)}) collective-permute-start(bf16[256,512]{1,0:T(8,128)(2,1)S(1)} %collective-permute-done.5.refs_2_), channel_id=1, source_target_pairs={{0,1},{1,0},{2,3},{3,2},{4,5},{5,4},{6,7},{7,6},{8,9},{9,8},{10,11... | collective-permute-start | bytes 786440 | tf_op jit(solution)/shard_map/ppermute | solution.py:36
  135.5 7.0 %all-gather.5.cloned.1.call-done = bf16[32,4,48,512]{3,2,1,0:T(8,128)(2,1)} async-done(((bf16[4,4,48,512]{3,2,1,0:T(8,128)(2,1)}), bf16[32,4,48,512]{3,2,1,0:T(8,128)(2,1)}) %all-gather.5.cloned.1.call-update) | async-done | bytes 6291472 | tf_op jit(solution)/shard_map/all_gather | solution.py:196
  142.5 7.5 %feed_forward.1 = (bf16[256,512]{1,0:T(8,128)(2,1)S(1)}, bf16[256,512]{1,0:T(8,128)(2,1)S(1)}, bf16[256,512]{1,0:T(8,128)(2,1)S(1)}, bf16[256,512]{1,0:T(8,128)(...) custom-call(s32[12]{0:T(128)S(1)} %stack.96.place_ref, ...), custom_call_target="tpu_custom_call" | custom-call | flops 3221225472 | bytes 10485760 | tf_op jit(solution)/shard_map/feed_forward/pallas_call | solution.py:151
  150.0 2.4 %collective-permute-start.21 = (bf16[256,512]{1,0:T(8,128)(2,1)S(1)}, bf16[256,512]{1,0:T(8,128)(2,1)S(1)}, u32[]{:S(2)}, u32[]{:S(2)}) collective-permute-start(bf16[256,512]{1,0:T(8,128)(2,1)S(1)} %get-tuple-element.25), channel_id=1, source_target_pairs={{0,1},{1,0},{2,3},{3,2},{4,5},{5,4},{6,7},{7,6},{8,9},{9,8},{10,11... | collective-permute-start | bytes 786440 | tf_op jit(solution)/shard_map/ppermute | solution.py:36
  160.8 3.6 %collective-permute-start.19 = (bf16[256,512]{1,0:T(8,128)(2,1)S(1)}, bf16[256,512]{1,0:T(8,128)(2,1)S(1)}, u32[]{:S(2)}, u32[]{:S(2)}) collective-permute-start(bf16[256,512]{1,0:T(8,128)(2,1)S(1)} %add_convert_fusion.2), channel_id=1, source_target_pairs={{0,128},{128,0},{256,384},{384,256},{1,129},{129,1},{257,385},{385... | collective-permute-start | bytes 786440 | tf_op jit(solution)/shard_map/ppermute | solution.py:40
  166.7 10.1 %collective-permute-start.23 = (bf16[256,512]{1,0:T(8,128)(2,1)S(1)}, bf16[256,512]{1,0:T(8,128)(2,1)S(1)}, u32[]{:S(2)}, u32[]{:S(2)}) collective-permute-start(bf16[256,512]{1,0:T(8,128)(2,1)S(1)} %add_convert_fusion), channel_id=1, source_target_pairs={{0,2},{2,0},{1,3},{3,1},{4,6},{6,4},{5,7},{7,5},{8,10},{10,8},{9,1... | collective-permute-start | bytes 786440 | tf_op jit(solution)/shard_map/ppermute | solution.py:36
  176.8 5.6 %collective-permute-done.23 = bf16[256,512]{1,0:T(8,128)(2,1)S(1)} collective-permute-done((bf16[256,512]{1,0:T(8,128)(2,1)S(1)}, bf16[256,512]{1,0:T(8,128)(2,1)S(1)}, u32[]{:S(2)}, u32[]{:S(2)}) %collective-permute-start.23) | collective-permute-done | bytes 262176 | tf_op jit(solution)/shard_map/ppermute | solution.py:36
  (61 shorter events, 31.1 us)
Async XLA Ops:
  7.2 135.3 %all-gather.5.cloned.1.call-start = ((), (), s32[]{:S(2)}) async-start(), calls=%async_computation | async-start | bytes 7077888 | tf_op jit(solution)/shard_map/all_gather | solution.py:196
  8.0 14.5 %collective-permute-start.13 = (bf16[48,1024]{1,0:T(8,128)(2,1)S(1)}, bf16[48,1024]{1,0:T(8,128)(2,1)S(1)}, u32[]{:S(2)}, u32[]{:S(2)}) collective-permute-start(bf16[48,1024]{1,0:T(8,128)(2,1)S(1)} %pad_maximum_fusion.4), channel_id=1, source_target_pairs={{0,12},{4,0},{8,4},{12,8},{1,13},{5,1},{9,5},{13,9},{2,14},{6,2},{... | collective-permute-start | bytes 294920 | tf_op jit(solution)/shard_map/ppermute | solution.py:32
  14.7 9.3 %collective-permute-start.12 = (bf16[48,1024]{1,0:T(8,128)(2,1)S(1)}, bf16[48,1024]{1,0:T(8,128)(2,1)S(1)}, u32[]{:S(2)}, u32[]{:S(2)}) collective-permute-start(bf16[48,1024]{1,0:T(8,128)(2,1)S(1)} %pad_maximum_fusion.4), channel_id=1, source_target_pairs={{0,8},{4,12},{8,0},{12,4},{1,9},{5,13},{9,1},{13,5},{2,10},{6,14},... | collective-permute-start | bytes 294920 | tf_op jit(solution)/shard_map/ppermute | solution.py:32
  18.3 7.9 %collective-permute-start.11 = (bf16[48,1024]{1,0:T(8,128)(2,1)S(1)}, bf16[48,1024]{1,0:T(8,128)(2,1)S(1)}, u32[]{:S(2)}, u32[]{:S(2)}) collective-permute-start(bf16[48,1024]{1,0:T(8,128)(2,1)S(1)} %pad_maximum_fusion.4), channel_id=1, source_target_pairs={{0,4},{4,8},{8,12},{12,0},{1,5},{5,9},{9,13},{13,1},{2,6},{6,10},{... | collective-permute-start | bytes 294920 | tf_op jit(solution)/shard_map/ppermute | solution.py:32
  26.2 9.9 %collective-permute-start.15 = (bf16[4,48,512]{2,1,0:T(8,128)(2,1)S(1)}, bf16[4,48,512]{2,1,0:T(8,128)(2,1)S(1)}, u32[]{:S(2)}, u32[]{:S(2)}) collective-permute-start(bf16[4,48,512]{2,1,0:T(8,128)(2,1)S(1)} %get-tuple-element.27), channel_id=1, source_target_pairs={{0,256},{128,384},{256,0},{384,128},{1,257},{129,385},{257,1},{385... | collective-permute-start | bytes 589832 | tf_op jit(solution)/shard_map/ppermute | solution.py:32
  30.9 8.8 %collective-permute-start.16 = (bf16[4,48,512]{2,1,0:T(8,128)(2,1)S(1)}, bf16[4,48,512]{2,1,0:T(8,128)(2,1)S(1)}, u32[]{:S(2)}, u32[]{:S(2)}) collective-permute-start(bf16[4,48,512]{2,1,0:T(8,128)(2,1)S(1)} %pad_maximum_fusion.3), channel_id=1, source_target_pairs={{0,384},{128,0},{256,128},{384,256},{1,385},{129,1},{257,129},{385... | collective-permute-start | bytes 589832 | tf_op jit(solution)/shard_map/ppermute | solution.py:32
  33.6 8.9 %collective-permute-start.14 = (bf16[4,48,512]{2,1,0:T(8,128)(2,1)S(1)}, bf16[4,48,512]{2,1,0:T(8,128)(2,1)S(1)}, u32[]{:S(2)}, u32[]{:S(2)}) collective-permute-start(bf16[4,48,512]{2,1,0:T(8,128)(2,1)S(1)} %pad_maximum_fusion.3), channel_id=1, source_target_pairs={{0,128},{128,256},{256,384},{384,0},{1,129},{129,257},{257,385},{3... | collective-permute-start | bytes 589832 | tf_op jit(solution)/shard_map/ppermute | solution.py:32
  45.4 8.3 %collective-permute-start = (bf16[272,512]{1,0:T(8,128)(2,1)S(1)}, bf16[272,512]{1,0:T(8,128)(2,1)S(1)}, u32[]{:S(2)}, u32[]{:S(2)}) collective-permute-start(bf16[272,512]{1,0:T(8,128)(2,1)S(1)} %pad_maximum_fusion.1.k0_ref), channel_id=1, source_target_pairs={{0,4},{4,8},{8,12},{12,16},{16,20},{20,24},{24,28},{28,32},{32,36}... | collective-permute-start | bytes 835592 | tf_op jit(solution)/shard_map/ppermute | solution.py:27
  47.5 12.0 %collective-permute-start.1 = (bf16[256,512]{1,0:T(8,128)(2,1)}, bf16[256,512]{1,0:T(8,128)(2,1)S(1)}, u32[]{:S(2)}, u32[]{:S(2)}) collective-permute-start(bf16[256,512]{1,0:T(8,128)(2,1)} %v0_ref.1), channel_id=1, source_target_pairs={{0,4},{4,8},{8,12},{12,16},{16,20},{20,24},{24,28},{28,32},{32,36}... | collective-permute-start | bytes 786440 | tf_op jit(solution)/shard_map/ppermute | solution.py:27
  53.7 41.2 %collective-permute-start.2 = (bf16[272,512]{1,0:T(8,128)(2,1)S(1)}, bf16[272,512]{1,0:T(8,128)(2,1)S(1)}, u32[]{:S(2)}, u32[]{:S(2)}) collective-permute-start(bf16[272,512]{1,0:T(8,128)(2,1)S(1)} %collective-permute-done.k1_ref), channel_id=1, source_target_pairs={{0,4},{4,8},{8,12},{12,16},{16,20},{20,24},{24,28},{28,32},{32,36}... | collective-permute-start | bytes 835592 | tf_op jit(solution)/shard_map/ppermute | solution.py:27
  59.5 35.4 %collective-permute-start.3 = (bf16[256,512]{1,0:T(8,128)(2,1)S(1)}, bf16[256,512]{1,0:T(8,128)(2,1)S(1)}, u32[]{:S(2)}, u32[]{:S(2)}) collective-permute-start(bf16[256,512]{1,0:T(8,128)(2,1)S(1)} %collective-permute-done.1.v1_ref), channel_id=1, source_target_pairs={{0,4},{4,8},{8,12},{12,16},{16,20},{20,24},{24,28},{28,32},{32,36}... | collective-permute-start | bytes 786440 | tf_op jit(solution)/shard_map/ppermute | solution.py:27
  101.7 16.5 %collective-permute-start.7 = (bf16[256,512]{1,0:T(8,128)(2,1)S(1)}, bf16[256,512]{1,0:T(8,128)(2,1)S(1)}, u32[]{:S(2)}, u32[]{:S(2)}) collective-permute-start(bf16[256,512]{1,0:T(8,128)(2,1)S(1)} %get-tuple-element.16.refs_0_), channel_id=1, source_target_pairs={{0,128},{128,0},{256,384},{384,256},{1,129},{129,1},{257,385},{385... | collective-permute-start | bytes 786440 | tf_op jit(solution)/shard_map/ppermute | solution.py:40
  106.8 22.8 %collective-permute-start.5 = (bf16[256,512]{1,0:T(8,128)(2,1)S(1)}, bf16[256,512]{1,0:T(8,128)(2,1)S(1)}, u32[]{:S(2)}, u32[]{:S(2)}) collective-permute-start(bf16[256,512]{1,0:T(8,128)(2,1)S(1)} %get-tuple-element.16.refs_0_), channel_id=1, source_target_pairs={{0,2},{2,0},{1,3},{3,1},{4,6},{6,4},{5,7},{7,5},{8,10},{10,8},{9,1... | collective-permute-start | bytes 786440 | tf_op jit(solution)/shard_map/ppermute | solution.py:36
  118.2 13.8 %collective-permute-start.9 = (bf16[256,512]{1,0:T(8,128)(2,1)S(1)}, bf16[256,512]{1,0:T(8,128)(2,1)S(1)}, u32[]{:S(2)}, u32[]{:S(2)}) collective-permute-start(bf16[256,512]{1,0:T(8,128)(2,1)S(1)} %collective-permute-done.7.refs_4_), channel_id=1, source_target_pairs={{0,2},{2,0},{1,3},{3,1},{4,6},{6,4},{5,7},{7,5},{8,10},{10,8},{9,1... | collective-permute-start | bytes 786440 | tf_op jit(solution)/shard_map/ppermute | solution.py:36
  123.7 10.3 %collective-permute-start.4 = (bf16[256,512]{1,0:T(8,128)(2,1)S(1)}, bf16[256,512]{1,0:T(8,128)(2,1)S(1)}, u32[]{:S(2)}, u32[]{:S(2)}) collective-permute-start(bf16[256,512]{1,0:T(8,128)(2,1)S(1)} %get-tuple-element.16.refs_0_), channel_id=1, source_target_pairs={{0,1},{1,0},{2,3},{3,2},{4,5},{5,4},{6,7},{7,6},{8,9},{9,8},{10,11... | collective-permute-start | bytes 786440 | tf_op jit(solution)/shard_map/ppermute | solution.py:36
  127.7 6.4 %collective-permute-start.8 = (bf16[256,512]{1,0:T(8,128)(2,1)S(1)}, bf16[256,512]{1,0:T(8,128)(2,1)S(1)}, u32[]{:S(2)}, u32[]{:S(2)}) collective-permute-start(bf16[256,512]{1,0:T(8,128)(2,1)S(1)} %collective-permute-done.7.refs_4_), channel_id=1, source_target_pairs={{0,1},{1,0},{2,3},{3,2},{4,5},{5,4},{6,7},{7,6},{8,9},{9,8},{10,11... | collective-permute-start | bytes 786440 | tf_op jit(solution)/shard_map/ppermute | solution.py:36
  129.6 4.5 %collective-permute-start.6 = (bf16[256,512]{1,0:T(8,128)(2,1)S(1)}, bf16[256,512]{1,0:T(8,128)(2,1)S(1)}, u32[]{:S(2)}, u32[]{:S(2)}) collective-permute-start(bf16[256,512]{1,0:T(8,128)(2,1)S(1)} %collective-permute-done.5.refs_2_), channel_id=1, source_target_pairs={{0,1},{1,0},{2,3},{3,2},{4,5},{5,4},{6,7},{7,6},{8,9},{9,8},{10,11... | collective-permute-start | bytes 786440 | tf_op jit(solution)/shard_map/ppermute | solution.py:36
  150.0 6.7 %collective-permute-start.21 = (bf16[256,512]{1,0:T(8,128)(2,1)S(1)}, bf16[256,512]{1,0:T(8,128)(2,1)S(1)}, u32[]{:S(2)}, u32[]{:S(2)}) collective-permute-start(bf16[256,512]{1,0:T(8,128)(2,1)S(1)} %get-tuple-element.25), channel_id=1, source_target_pairs={{0,1},{1,0},{2,3},{3,2},{4,5},{5,4},{6,7},{7,6},{8,9},{9,8},{10,11... | collective-permute-start | bytes 786440 | tf_op jit(solution)/shard_map/ppermute | solution.py:36
  152.4 8.3 %collective-permute-start.18 = (bf16[256,512]{1,0:T(8,128)(2,1)S(1)}, bf16[256,512]{1,0:T(8,128)(2,1)S(1)}, u32[]{:S(2)}, u32[]{:S(2)}) collective-permute-start(bf16[256,512]{1,0:T(8,128)(2,1)S(1)} %get-tuple-element.21), channel_id=1, source_target_pairs={{0,1},{1,0},{2,3},{3,2},{4,5},{5,4},{6,7},{7,6},{8,9},{9,8},{10,11... | collective-permute-start | bytes 786440 | tf_op jit(solution)/shard_map/ppermute | solution.py:36
  154.3 10.1 %collective-permute-start.20 = (bf16[256,512]{1,0:T(8,128)(2,1)S(1)}, bf16[256,512]{1,0:T(8,128)(2,1)S(1)}, u32[]{:S(2)}, u32[]{:S(2)}) collective-permute-start(bf16[256,512]{1,0:T(8,128)(2,1)S(1)} %get-tuple-element.23), channel_id=1, source_target_pairs={{0,1},{1,0},{2,3},{3,2},{4,5},{5,4},{6,7},{7,6},{8,9},{9,8},{10,11... | collective-permute-start | bytes 786440 | tf_op jit(solution)/shard_map/ppermute | solution.py:36
  156.8 9.8 %collective-permute-start.22 = (bf16[256,512]{1,0:T(8,128)(2,1)S(1)}, bf16[256,512]{1,0:T(8,128)(2,1)S(1)}, u32[]{:S(2)}, u32[]{:S(2)}) collective-permute-start(bf16[256,512]{1,0:T(8,128)(2,1)S(1)} %add_convert_fusion.1), channel_id=1, source_target_pairs={{0,128},{128,0},{256,384},{384,256},{1,129},{129,1},{257,385},{385... | collective-permute-start | bytes 786440 | tf_op jit(solution)/shard_map/ppermute | solution.py:40
  158.7 18.1 %collective-permute-start.17 = (bf16[256,512]{1,0:T(8,128)(2,1)S(1)}, bf16[256,512]{1,0:T(8,128)(2,1)S(1)}, u32[]{:S(2)}, u32[]{:S(2)}) collective-permute-start(bf16[256,512]{1,0:T(8,128)(2,1)S(1)} %get-tuple-element.19), channel_id=1, source_target_pairs={{0,1},{1,0},{2,3},{3,2},{4,5},{5,4},{6,7},{7,6},{8,9},{9,8},{10,11... | collective-permute-start | bytes 786440 | tf_op jit(solution)/shard_map/ppermute | solution.py:36
  160.8 16.1 %collective-permute-start.19 = (bf16[256,512]{1,0:T(8,128)(2,1)S(1)}, bf16[256,512]{1,0:T(8,128)(2,1)S(1)}, u32[]{:S(2)}, u32[]{:S(2)}) collective-permute-start(bf16[256,512]{1,0:T(8,128)(2,1)S(1)} %add_convert_fusion.2), channel_id=1, source_target_pairs={{0,128},{128,0},{256,384},{384,256},{1,129},{129,1},{257,385},{385... | collective-permute-start | bytes 786440 | tf_op jit(solution)/shard_map/ppermute | solution.py:40
  166.7 15.8 %collective-permute-start.23 = (bf16[256,512]{1,0:T(8,128)(2,1)S(1)}, bf16[256,512]{1,0:T(8,128)(2,1)S(1)}, u32[]{:S(2)}, u32[]{:S(2)}) collective-permute-start(bf16[256,512]{1,0:T(8,128)(2,1)S(1)} %add_convert_fusion), channel_id=1, source_target_pairs={{0,2},{2,0},{1,3},{3,1},{4,6},{6,4},{5,7},{7,5},{8,10},{10,8},{9,1... | collective-permute-start | bytes 786440 | tf_op jit(solution)/shard_map/ppermute | solution.py:36
  (7 other events, 87.1 us)
Sparse Core Ops, SparseCore 0:
  43.6 98.8 all-gather.4

commit v3 on v2

v3 whole, which is shorter than its diff:
```python
import math

import jax
import jax.numpy as jnp
from jax import lax
from jax.experimental import pallas as pl
from jax.experimental.pallas import tpu as pltpu
from jax.sharding import Mesh
from jax.sharding import PartitionSpec as P

D = 2048
HEAD_DIM = 128
SEG = 128
ROWS = 256
TP_WIDTH = 512
UNIT_BLOCK = 256
UNITS = 512
EXTRA = 16
epsilon = 1e-06

SEQ = ("x", "z", "yh")
TP = ("yl", "c")
F32 = jnp.float32
BF16 = jnp.bfloat16


def from_behind(value, by):
    size = lax.axis_size(SEQ)
    return lax.ppermute(value, SEQ, [(i, i + by) for i in range(size - by)])


def around(value, axis, by):
    size = lax.axis_size(axis)
    return lax.ppermute(value, axis, [(i, (i + by) % size) for i in range(size)])


def swap(value, axis):
    return lax.ppermute(value, axis, [(0, 1), (1, 0)])


def attention_kernel(
    lengths_ref, gain_ref, *refs
):
    outside, (att_ref, send_ref), inside, sems = refs[:8], refs[8:10], refs[10:18], refs[18]
    copies = [
        pltpu.make_async_copy(src, dst, sems.at[i])
        for i, (src, dst) in enumerate(zip(outside, inside))
    ]
    for copy in copies:
        copy.start()
    q_ref, k0_ref, v0_ref, k1_ref, v1_ref, k2_ref, v2_ref, res_ref = inside
    gain = gain_ref[...]
    high = gain.astype(BF16).astype(F32)
    middle = (gain - high).astype(BF16).astype(F32)
    low = gain - high - middle
    extra = lax.broadcasted_iota(jnp.int32, (EXTRA, TP_WIDTH), 0)
    extra = jnp.where(extra == 0, high, jnp.where(extra == 1, middle, jnp.where(extra == 2, low, 0.0)))
    send_ref[pl.ds(ROWS, EXTRA), :] = extra.astype(BF16)
    for copy in copies:
        copy.wait()
    rows = lax.broadcasted_iota(jnp.int32, (ROWS, ROWS), 0)
    cols = lax.broadcasted_iota(jnp.int32, (ROWS, ROWS), 1)
    col = lax.broadcasted_iota(jnp.int32, (1, ROWS), 1)

    def valid(key_ref):
        first = key_ref[pl.ds(ROWS, 8), pl.ds(0, ROWS)].astype(F32)[0:1, :].astype(jnp.int32)
        second = key_ref[pl.ds(ROWS + 8, 8), pl.ds(0, ROWS)].astype(F32)[0:1, :].astype(jnp.int32)
        return (col < jnp.where(col < SEG, first, second + SEG)).astype(jnp.int32)

    allowed = (
        (valid(k0_ref) > 0) & (cols <= rows),
        (valid(k1_ref) + jnp.zeros_like(cols)) > 0,
        (valid(k2_ref) > 0) & (cols > rows),
    )
    row = lax.broadcasted_iota(jnp.int32, (ROWS, 1), 0)
    keep = row < jnp.where(row < SEG, lengths_ref[0], lengths_ref[1] + SEG)
    scale = 1.0 / math.sqrt(HEAD_DIM)
    keys = (k0_ref, k1_ref, k2_ref)
    values = (v0_ref, v1_ref, v2_ref)
    for head in range(TP_WIDTH // HEAD_DIM):
        at = pl.ds(head * HEAD_DIM, HEAD_DIM)
        query = q_ref[:, at]
        masked = []
        for key_ref, allow in zip(keys, allowed):
            scores = lax.dot_general(
                query,
                key_ref[pl.ds(0, ROWS), at],
                (((1,), (1,)), ((), ())),
                preferred_element_type=F32,
            )
            masked.append(jnp.where(allow, scores * scale, -1e30))
        top = jnp.max(jnp.maximum(jnp.maximum(masked[0], masked[1]), masked[2]), axis=1, keepdims=True)
        weights = [jnp.where(a, jnp.exp(m - top), 0.0) for a, m in zip(allowed, masked)]
        denominator = jnp.sum(weights[0] + weights[1] + weights[2], axis=1, keepdims=True)
        numerator = jnp.zeros((ROWS, HEAD_DIM), F32)
        for weight, value_ref in zip(weights, values):
            numerator += jnp.dot(weight.astype(BF16), value_ref[:, at], preferred_element_type=F32)
        out = jnp.where(keep, numerator / jnp.where(keep, denominator, 1.0), 0.0).astype(BF16)
        att_ref[:, at] = out
        send_ref[pl.ds(0, ROWS), at] = (res_ref[:, at] + out.astype(F32)).astype(BF16)


def attention(lengths, gain, q, k0, v0, k1, v1, k2, v2, residual_in):
    return pl.pallas_call(
        attention_kernel,
        out_shape=(
            jax.ShapeDtypeStruct((ROWS, TP_WIDTH), BF16),
            jax.ShapeDtypeStruct((ROWS + EXTRA, TP_WIDTH), BF16),
        ),
        in_specs=[SMEM, pl.BlockSpec()] + [HBM] * 8,
        out_specs=(pl.BlockSpec(), pl.BlockSpec()),
        scratch_shapes=[
            pltpu.VMEM(a.shape, a.dtype) for a in (q, k0, v0, k1, v1, k2, v2, residual_in)
        ]
        + [pltpu.SemaphoreType.DMA((8,))],
        compiler_params=pltpu.CompilerParams(vmem_limit_bytes=60 << 20),
        cost_estimate=pl.CostEstimate(
            flops=4 * ROWS * 3 * ROWS * TP_WIDTH, bytes_accessed=3 << 20, transcendentals=3 << 18
        ),
        name="attention",
    )(lengths, gain, q, k0, v0, k1, v1, k2, v2, residual_in)


def through_units(x_ref, acc_ref, load):
    for low in range(0, UNITS, UNIT_BLOCK):
        gate = jnp.zeros((ROWS, UNIT_BLOCK), F32)
        up = jnp.zeros((ROWS, UNIT_BLOCK), F32)
        for p in range(4):
            gate += jnp.dot(x_ref[p], load(p, 0, low), preferred_element_type=F32)
            up += jnp.dot(x_ref[p], load(p, 1, low), preferred_element_type=F32)
        hidden = (gate / (1.0 + jnp.exp(-gate)) * up).astype(BF16)
        for p in range(4):
            acc_ref[p] += lax.dot_general(
                hidden, load(p, 2, low), (((1,), (1,)), ((), ())), preferred_element_type=F32
            )


def first_units_kernel(place_ref, *refs):
    parts, blocks, halves = refs[:4], refs[4:11], refs[11:13]
    x_ref, acc_ref, w_ref, sems = refs[13:]
    copies = [
        pltpu.make_async_copy(block, w_ref.at[place_ref[12 + i]], sems.at[i])
        for i, block in enumerate(blocks)
    ] + [
        pltpu.make_async_copy(half, w_ref.at[place_ref[19], pl.ds(2 * i, 2)], sems.at[7 + i])
        for i, half in enumerate(halves)
    ]
    for copy in copies:
        copy.start()
    square = jnp.zeros((ROWS, 1), F32)
    for ref in parts:
        value = ref[pl.ds(0, ROWS), :].astype(F32)
        square += jnp.sum(value * value, axis=1, keepdims=True)
    inverse = lax.rsqrt(square / D + epsilon)
    for p, ref in enumerate(parts):
        extra = ref[pl.ds(ROWS, EXTRA), :].astype(F32)
        gain = extra[0:1] + extra[1:2] + extra[2:3]
        x_ref[p] = (ref[pl.ds(0, ROWS), :].astype(F32) * inverse * gain).astype(BF16)
    acc_ref[...] = jnp.zeros_like(acc_ref)
    for copy in copies:
        copy.wait()

    def load(p, kind, low):
        pieces = [
            w_ref[
                :,
                pl.ds(place_ref[4 + p], 1),
                pl.ds(place_ref[8 + y], 1),
                pl.ds(kind * 16, 16),
                pl.ds(low, UNIT_BLOCK),
            ]
            for y in range(4)
        ]
        return jnp.concatenate(pieces, axis=2).reshape(TP_WIDTH, UNIT_BLOCK)

    through_units(x_ref, acc_ref, load)


def last_units_kernel(place_ref, x_ref, acc_in, *refs):
    blocks, halves, outs, acc_ref, w_ref, sems = (
        refs[:3], refs[3:5], refs[5:9], refs[9], refs[10], refs[11],
    )
    copies = [
        pltpu.make_async_copy(block, w_ref.at[place_ref[20 + i]], sems.at[i])
        for i, block in enumerate(blocks)
    ] + [
        pltpu.make_async_copy(half, w_ref.at[place_ref[23], pl.ds(4 * i, 4)], sems.at[3 + i])
        for i, half in enumerate(halves)
    ]
    for copy in copies:
        copy.start()
    acc_ref[...] = acc_in[...]
    for copy in copies:
        copy.wait()

    def load(p, kind, low):
        pieces = [
            w_ref[
                pl.ds(place_ref[p], 1),
                :,
                pl.ds(place_ref[8 + y], 1),
                pl.ds(kind * 16, 16),
                pl.ds(low, UNIT_BLOCK),
            ]
            for y in range(4)
        ]
        return jnp.concatenate(pieces, axis=2).reshape(TP_WIDTH, UNIT_BLOCK)

    through_units(x_ref, acc_ref, load)
    for p in range(4):
        outs[p][...] = acc_ref[p].astype(BF16)


HBM = pl.BlockSpec(memory_space=pltpu.HBM)
SMEM = pl.BlockSpec(memory_space=pltpu.SMEM)


def units_cost():
    return pl.CostEstimate(
        flops=6 * ROWS * D * UNITS, bytes_accessed=10 << 20, transcendentals=ROWS * UNITS
    )


def first_units(place, parts, blocks, halves):
    return pl.pallas_call(
        first_units_kernel,
        out_shape=(
            jax.ShapeDtypeStruct((4, ROWS, TP_WIDTH), BF16),
            jax.ShapeDtypeStruct((4, ROWS, TP_WIDTH), F32),
        ),
        in_specs=[SMEM] + [pl.BlockSpec()] * 4 + [HBM] * 9,
        out_specs=(pl.BlockSpec(), pl.BlockSpec()),
        scratch_shapes=[pltpu.VMEM((8, 4, 4, 48, UNITS), BF16), pltpu.SemaphoreType.DMA((9,))],
        compiler_params=pltpu.CompilerParams(vmem_limit_bytes=60 << 20),
        cost_estimate=units_cost(),
        name="first_units",
    )(place, *parts, *blocks, *halves)


def last_units(place, x, acc, blocks, halves):
    return pl.pallas_call(
        last_units_kernel,
        out_shape=[jax.ShapeDtypeStruct((ROWS, TP_WIDTH), BF16)] * 4,
        in_specs=[SMEM] + [pl.BlockSpec()] * 2 + [HBM] * 5,
        out_specs=[pl.BlockSpec()] * 4,
        scratch_shapes=[
            pltpu.VMEM((4, ROWS, TP_WIDTH), F32),
            pltpu.VMEM((4, 8, 4, 48, UNITS), BF16),
            pltpu.SemaphoreType.DMA((5,)),
        ],
        compiler_params=pltpu.CompilerParams(vmem_limit_bytes=60 << 20),
        cost_estimate=units_cost(),
        name="last_units",
    )(place, x, acc, *blocks, *halves)


def on_device(
    residual_in,
    query_rows,
    key_rows,
    value_rows,
    lengths,
    norm_gain,
    gate_weight,
    up_weight,
    down_weight,
):
    x, z, yh = (lax.axis_index(axis) for axis in SEQ)

    packed = jnp.concatenate([gate_weight, up_weight, down_weight.T], axis=0)
    near = [packed] + [around(packed, "yh", by) for by in (1, 2, 3)]
    first = jnp.stack([w[:, :UNITS] for w in near])
    second = jnp.stack([w[:, UNITS:] for w in near])
    line = lax.all_gather(second, "z", axis=0)
    plane = jnp.stack([first] + [around(first, "x", by) for by in (1, 2, 3)])

    tail = jnp.broadcast_to(
        jnp.repeat(lengths.astype(BF16), 8)[:, None], (16, key_rows.shape[1])
    )
    k0 = jnp.concatenate([key_rows, tail], axis=0)
    k1, v1 = from_behind(k0, 1), from_behind(value_rows, 1)

    plane, k1, v1 = lax.optimization_barrier((plane, k1, v1))
    k2, v2 = from_behind(k1, 1), from_behind(v1, 1)
    line, k2, v2 = lax.optimization_barrier((line, k2, v2))

    attended, sent = attention(
        lengths, norm_gain[None, :], query_rows, k0, value_rows, k1, v1, k2, v2, residual_in
    )

    forward, backward = [plane], [plane]
    for by in range(3):
        if by == 2:
            forward[2], backward[2], sent = lax.optimization_barrier((forward[2], backward[2], sent))
        forward.append(around(forward[-1], "z", 1))
        backward.append(around(backward[-1], "z", -1))
    z_blocks = forward + backward[1:]
    z_halves = [around(forward[3][:2], "z", 1), around(backward[3][2:], "z", -1)]
    z_place = [z, z - 1, z - 2, z - 3, z + 1, z + 2, z + 3, z + 4]

    x_blocks = [line, around(line, "x", 1), around(line, "x", -1)]
    x_halves = [around(x_blocks[1][:4], "x", 1), around(x_blocks[2][4:], "x", -1)]
    x_place = [x, x - 1, x + 1, x + 2]

    chip = swap(sent, "yl")
    parts = [sent, swap(sent, "c"), chip, swap(chip, "c")]
    own = 2 * lax.axis_index("yl") + lax.axis_index("c")
    order = [own, own ^ 1, own ^ 2, own ^ 3]
    place = (
        order
        + [(x - t) & 3 for t in order]
        + [(yh - y) & 3 for y in range(4)]
        + [at & 7 for at in z_place]
        + [at & 3 for at in x_place]
    )
    place = jnp.stack(place).astype(jnp.int32)
    normed, acc = first_units(place, parts, z_blocks, z_halves)
    outs = last_units(place, normed, acc, x_blocks, x_halves)

    def add(left, right):
        return left.astype(F32) + right.astype(F32)

    far = add(outs[2], swap(outs[3], "c"))
    close = add(outs[0], swap(outs[1], "c"))
    summed = close + swap(far.astype(BF16), "yl").astype(F32)
    mixed = residual_in + attended.astype(F32) + summed
    return attended, mixed


def solution(mesh):
    fine = Mesh(mesh.devices.reshape(4, 8, 4, 2, 2), SEQ + TP)
    placed = (
        P(SEQ, TP),
        P(SEQ, TP),
        P(SEQ, TP),
        P(SEQ, TP),
        P(SEQ),
        P(TP),
        P(SEQ, TP),
        P(SEQ, TP),
        P(TP, SEQ),
    )
    return jax.shard_map(
        on_device,
        mesh=fine,
        in_specs=placed,
        out_specs=(P(SEQ, TP), P(SEQ, TP)),
        check_vma=False,
    )
```

time: 192 us -> 222 us (1.16)
  blocking collectives: 30.3 us -> 0 us
  starting transfers between devices: 99 us -> 125 us
  waiting for transfers between devices: 27.2 us -> 47.2 us
  Pallas kernels: 10.7 us -> 20.2 us
    ppermute x6 -> x18, starting transfers between devices: 24.3 us -> 70.5 us  [around(): lax.ppermute(value, axis, [(i, (i + by) % size) for i in range(size)])]
    all_gather x1 -> x0, blocking collectives: 30.3 us -> none  [on_device(): gain = lax.all_gather(norm_gain, TP, axis=0)]
    ppermute x11 -> x6, starting transfers between devices: 45.9 us -> 34.2 us  [swap(): return lax.ppermute(value, axis, [(0, 1), (1, 0)])]
    all_gather x1, waiting for transfers between devices: 7 us -> 18.6 us  [on_device(): line = lax.all_gather(second, 'z', axis=0)]
    ppermute x3 -> x0, starting transfers between devices: 10.6 us -> none  [swap_x(): return lax.ppermute(value, 'x', [(i, i ^ 1) for i in range(4)])]
    pallas_call x2 -> x3, Pallas kernels: 10.7 us -> 20.2 us  [the longest x1 7.56 us: last_units(): pl.pallas_call(last_units_kernel, out_shape=[jax.ShapeDtypeStruct((ROWS,...]
    ppermute x4, waiting for transfers between devices: 1.04 us -> 6.83 us  [from_behind(): return lax.ppermute(value, SEQ, [(i, i + by) for i in range(size - by)])]
    ppermute x6 -> x18, waiting for transfers between devices: 9.95 us -> 14.8 us  [around(): lax.ppermute(value, axis, [(i, (i + by) % size) for i in range(size)])]
  transfers between devices with their start and end apart: 25 -> 29, of which waited for: 9 -> 10; matrix products, arithmetic and copies ran while one was open for 1% -> 2% of each run, Pallas kernels for 2% -> 6%
where the time goes in v3:
time: 222 us; the launch traced here: 218 us
  starting transfers between devices  125 us (56%)
  waiting for transfers between devices  47.2 us (21%)
  Pallas kernels  20.2 us (9%)
  between operations  14.7 us (7%)
  other arithmetic  5.62 us (3%)
  local copies, waits for them, and re-layouts  5.38 us (2%)
    ppermute x18, starting transfers between devices, around(): lax.ppermute(value, axis, [(i, (i + by) % size) for i in range(size)])  70.5 us
    ppermute x6, starting transfers between devices, swap(): return lax.ppermute(value, axis, [(0, 1), (1, 0)])  34.2 us
    ppermute x4, starting transfers between devices, from_behind(): return lax.ppermute(value, SEQ, [(i, i + by) for i in range(size - by)])  20.3 us
    all_gather x1, waiting for transfers between devices, on_device(): line = lax.all_gather(second, 'z', axis=0)  18.6 us
    ppermute x18, waiting for transfers between devices, around(): lax.ppermute(value, axis, [(i, (i + by) % size) for i in range(size)])  14.8 us
    pallas_call x1, Pallas kernels, last_units(): pl.pallas_call(last_units_kernel, out_shape=[jax.ShapeDtypeStruct((ROWS,...  7.56 us
    pallas_call x1, Pallas kernels, first_units(): pl.pallas_call(first_units_kernel, out_shape=(jax.ShapeDtypeStruct((4, RO...  7.54 us
    ppermute x6, waiting for transfers between devices, swap(): return lax.ppermute(value, axis, [(0, 1), (1, 0)])  6.96 us
  transfers between devices with their start and end apart: 29, of which 10 were waited for; matrix products, arithmetic and copies ran while one was open for 2% of the time, Pallas kernels for 6%

profile of v3, /device:TPU:1, one launch (start us, length us, event | category | flops | bytes accessed | tf_op | source)
XLA Modules:
  0.0 218.1 jit_solution(4522991163653670190)
XLA Ops:
  8.1 6.7 %collective-permute-start.2 = (bf16[48,1024]{1,0:T(8,128)(2,1)S(1)}, bf16[48,1024]{1,0:T(8,128)(2,1)S(1)}, u32[]{:S(2)}, u32[]{:S(2)}) collective-permute-start(bf16[48,1024]{1,0:T(8,128)(2,1)S(1)} %pad_maximum_fusion.4), channel_id=1, source_target_pairs={{0,12},{4,0},{8,4},{12,8},{1,13},{5,1},{9,5},{13,9},{2,14},{6,2},{... | collective-permute-start | bytes 294920 | tf_op jit(solution)/shard_map/ppermute | solution.py:34
  14.8 3.5 %collective-permute-start.1 = (bf16[48,1024]{1,0:T(8,128)(2,1)S(1)}, bf16[48,1024]{1,0:T(8,128)(2,1)S(1)}, u32[]{:S(2)}, u32[]{:S(2)}) collective-permute-start(bf16[48,1024]{1,0:T(8,128)(2,1)S(1)} %pad_maximum_fusion.4), channel_id=1, source_target_pairs={{0,8},{4,12},{8,0},{12,4},{1,9},{5,13},{9,1},{13,5},{2,10},{6,14},... | collective-permute-start | bytes 294920 | tf_op jit(solution)/shard_map/ppermute | solution.py:34
  18.3 4.2 %collective-permute-start = (bf16[48,1024]{1,0:T(8,128)(2,1)S(1)}, bf16[48,1024]{1,0:T(8,128)(2,1)S(1)}, u32[]{:S(2)}, u32[]{:S(2)}) collective-permute-start(bf16[48,1024]{1,0:T(8,128)(2,1)S(1)} %pad_maximum_fusion.4), channel_id=1, source_target_pairs={{0,4},{4,8},{8,12},{12,0},{1,5},{5,9},{9,13},{13,1},{2,6},{6,10},{... | collective-permute-start | bytes 294920 | tf_op jit(solution)/shard_map/ppermute | solution.py:34
  27.2 4.6 %collective-permute-start.4 = (bf16[4,48,512]{2,1,0:T(8,128)(2,1)S(1)}, bf16[4,48,512]{2,1,0:T(8,128)(2,1)S(1)}, u32[]{:S(2)}, u32[]{:S(2)}) collective-permute-start(bf16[4,48,512]{2,1,0:T(8,128)(2,1)S(1)} %get-tuple-element.37), channel_id=1, source_target_pairs={{0,256},{128,384},{256,0},{384,128},{1,257},{129,385},{257,1},{385... | collective-permute-start | bytes 589832 | tf_op jit(solution)/shard_map/ppermute | solution.py:34
  34.0 4.3 %collective-permute-start.5 = (bf16[4,48,512]{2,1,0:T(8,128)(2,1)S(1)}, bf16[4,48,512]{2,1,0:T(8,128)(2,1)S(1)}, u32[]{:S(2)}, u32[]{:S(2)}) collective-permute-start(bf16[4,48,512]{2,1,0:T(8,128)(2,1)S(1)} %get-tuple-element.37), channel_id=1, source_target_pairs={{0,384},{128,0},{256,128},{384,256},{1,385},{129,1},{257,129},{385... | collective-permute-start | bytes 589832 | tf_op jit(solution)/shard_map/ppermute | solution.py:34
  41.6 6.4 %collective-permute-start.7 = (bf16[256,512]{1,0:T(8,128)(2,1)S(1)}, bf16[256,512]{1,0:T(8,128)(2,1)S(1)}, u32[]{:S(2)}, u32[]{:S(2)}) collective-permute-start(bf16[256,512]{1,0:T(8,128)(2,1)S(1)} %copy-done.14), channel_id=1, source_target_pairs={{0,4},{4,8},{8,12},{12,16},{16,20},{20,24},{24,28},{28,32},{32,36}... | collective-permute-start | bytes 786440 | tf_op jit(solution)/shard_map/ppermute | solution.py:29
  49.0 3.5 %collective-permute-done.7.refs_4_ = bf16[256,512]{1,0:T(8,128)(2,1)S(1)} collective-permute-done((bf16[256,512]{1,0:T(8,128)(2,1)S(1)}, bf16[256,512]{1,0:T(8,128)(2,1)S(1)}, u32[]{:S(2)}, u32[]{:S(2)}) %collective-permute-start.7) | collective-permute-done | bytes 262176 | tf_op jit(solution)/shard_map/ppermute | solution.py:29
  52.6 12.6 %collective-permute-start.12 = (bf16[4,4,48,512]{3,2,1,0:T(8,128)(2,1)}, bf16[4,4,48,512]{3,2,1,0:T(8,128)(2,1)}, u32[]{:S(2)}, u32[]{:S(2)}) collective-permute-start(bf16[4,4,48,512]{3,2,1,0:T(8,128)(2,1)} %pad_maximum_fusion.refs_4_), channel_id=1, source_target_pairs={{0,112},{16,0},{32,16},{48,32},{64,48},{80,64},{96,80},{112,96},{1... | collective-permute-start | bytes 2359304 | tf_op jit(solution)/shard_map/ppermute | solution.py:34
  67.1 4.5 %collective-permute-start.8 = (bf16[272,512]{1,0:T(8,128)(2,1)S(1)}, bf16[272,512]{1,0:T(8,128)(2,1)S(1)}, u32[]{:S(2)}, u32[]{:S(2)}) collective-permute-start(bf16[272,512]{1,0:T(8,128)(2,1)S(1)} %collective-permute-done.6.refs_3_), channel_id=1, source_target_pairs={{0,4},{4,8},{8,12},{12,16},{16,20},{20,24},{24,28},{28,32},{32,36}... | collective-permute-start | bytes 835592 | tf_op jit(solution)/shard_map/ppermute | solution.py:29
  71.6 6.2 %collective-permute-start.9 = (bf16[256,512]{1,0:T(8,128)(2,1)S(1)}, bf16[256,512]{1,0:T(8,128)(2,1)S(1)}, u32[]{:S(2)}, u32[]{:S(2)}) collective-permute-start(bf16[256,512]{1,0:T(8,128)(2,1)S(1)} %collective-permute-done.7.refs_4_), channel_id=1, source_target_pairs={{0,4},{4,8},{8,12},{12,16},{16,20},{20,24},{24,28},{28,32},{32,36}... | collective-permute-start | bytes 786440 | tf_op jit(solution)/shard_map/ppermute | solution.py:29
  77.9 3.3 %collective-permute-done.9.refs_6_ = bf16[256,512]{1,0:T(8,128)(2,1)S(1)} collective-permute-done((bf16[256,512]{1,0:T(8,128)(2,1)S(1)}, bf16[256,512]{1,0:T(8,128)(2,1)S(1)}, u32[]{:S(2)}, u32[]{:S(2)}) %collective-permute-start.9) | collective-permute-done | bytes 262176 | tf_op jit(solution)/shard_map/ppermute | solution.py:29
  81.2 18.6 %all-gather.3.cloned.1.call-done = bf16[32,48,512]{2,1,0:T(8,128)(2,1)} async-done(((bf16[4,48,512]{2,1,0:T(8,128)(2,1)}), bf16[32,48,512]{2,1,0:T(8,128)(2,1)}) %all-gather.3.cloned.1.call-update) | async-done | bytes 1572880 | tf_op jit(solution)/shard_map/all_gather | solution.py:274
  99.8 3.7 %collective-permute-start.22 = (bf16[8,4,48,512]{3,2,1,0:T(8,128)(2,1)}, bf16[8,4,48,512]{3,2,1,0:T(8,128)(2,1)S(1)}, u32[]{:S(2)}, u32[]{:S(2)}) collective-permute-start(bf16[8,4,48,512]{3,2,1,0:T(8,128)(2,1)} %bitcast.48), channel_id=1, source_target_pairs={{0,384},{128,0},{256,128},{384,256},{1,385},{129,1},{257,129},{385... | collective-permute-start | bytes 4718600 | tf_op jit(solution)/shard_map/ppermute | solution.py:34
  111.5 5.1 %attention.1 = (bf16[256,512]{1,0:T(8,128)(2,1)}, bf16[272,512]{1,0:T(8,128)(2,1)}) custom-call(s32[2]{0:T(128)} %lengths_ref.1, f32[1,512]{1,0:T(1,128)} %bitcast.55, bf16[256,512]{1,0:T(8,128)(2,1)} %refs_0_.1, bf16[272,512]{1,0:T(8,128)(2,1)} %copy-done.5, bf16[256,512]{1,0:T(8,128)(2,1)} %refs_2_.1, bf16[272,512]{1,0:T(8,128)(2,1)} %copy-done.9, ...), custom_call_target="tpu_custom_call" | custom-call | flops 402653184 | bytes 3145728 | tf_op jit(solution)/shard_map/attention/pallas_call | solution.py:104
  116.6 7.2 %collective-permute-done.13.refs_9_ = bf16[4,4,48,512]{3,2,1,0:T(8,128)(2,1)} collective-permute-done((bf16[4,4,48,512]{3,2,1,0:T(8,128)(2,1)}, bf16[4,4,48,512]{3,2,1,0:T(8,128)(2,1)}, u32[]{:S(2)}, u32[]{:S(2)}) %collective-permute-start.13) | collective-permute-done | bytes 786464 | tf_op jit(solution)/shard_map/ppermute | solution.py:34
  123.8 5.2 %collective-permute-start.17 = (bf16[4,4,48,512]{3,2,1,0:T(8,128)(2,1)}, bf16[4,4,48,512]{3,2,1,0:T(8,128)(2,1)S(1)}, u32[]{:S(2)}, u32[]{:S(2)}) collective-permute-start(bf16[4,4,48,512]{3,2,1,0:T(8,128)(2,1)} %collective-permute-done.11.refs_6_), channel_id=1, source_target_pairs={{0,16},{16,32},{32,48},{48,64},{64,80},{80,96},{96,112},{112,0},{1... | collective-permute-start | bytes 2359304 | tf_op jit(solution)/shard_map/ppermute | solution.py:34
  130.9 15.8 %collective-permute-start.15 = (bf16[272,512]{1,0:T(8,128)(2,1)}, bf16[272,512]{1,0:T(8,128)(2,1)}, u32[]{:S(2)}, u32[]{:S(2)}) collective-permute-start(bf16[272,512]{1,0:T(8,128)(2,1)} %get-tuple-element.26.refs_0_), channel_id=1, source_target_pairs={{0,2},{2,0},{1,3},{3,1},{4,6},{6,4},{5,7},{7,5},{8,10},{10,8},{9,1... | collective-permute-start | bytes 835592 | tf_op jit(solution)/shard_map/ppermute | solution.py:38
  150.8 3.4 %collective-permute-start.23 = (bf16[4,4,48,512]{3,2,1,0:T(8,128)(2,1)}, bf16[4,4,48,512]{3,2,1,0:T(8,128)(2,1)}, u32[]{:S(2)}, u32[]{:S(2)}) collective-permute-start(bf16[4,4,48,512]{3,2,1,0:T(8,128)(2,1)} %slice.58), channel_id=1, source_target_pairs={{0,128},{128,256},{256,384},{384,0},{1,129},{129,257},{257,385},{3... | collective-permute-start | bytes 2359304 | tf_op jit(solution)/shard_map/ppermute | solution.py:34
  154.2 5.1 %collective-permute-start.14 = (bf16[272,512]{1,0:T(8,128)(2,1)S(1)}, bf16[272,512]{1,0:T(8,128)(2,1)S(1)}, u32[]{:S(2)}, u32[]{:S(2)}) collective-permute-start(bf16[272,512]{1,0:T(8,128)(2,1)S(1)} %copy-done.11), channel_id=1, source_target_pairs={{0,1},{1,0},{2,3},{3,2},{4,5},{5,4},{6,7},{7,6},{8,9},{9,8},{10,11... | collective-permute-start | bytes 835592 | tf_op jit(solution)/shard_map/ppermute | solution.py:38
  161.3 4.6 %collective-permute-start.20 = (bf16[2,4,48,512]{3,2,1,0:T(8,128)(2,1)S(1)}, bf16[2,4,48,512]{3,2,1,0:T(8,128)(2,1)S(1)}, u32[]{:S(2)}, u32[]{:S(2)}) collective-permute-start(bf16[2,4,48,512]{3,2,1,0:T(8,128)(2,1)S(1)} %slice.57), channel_id=1, source_target_pairs={{0,112},{16,0},{32,16},{48,32},{64,48},{80,64},{96,80},{112,96},{1... | collective-permute-start | bytes 1179656 | tf_op jit(solution)/shard_map/ppermute | solution.py:34
  175.2 7.5 %first_units.1 = (bf16[4,256,512]{2,1,0:T(8,128)(2,1)}, f32[4,256,512]{2,1,0:T(8,128)}) custom-call(s32[24]{0:T(128)} %stack.159.place_ref, bf16[272,512]{1,0:T(8,128)(2,1)} %get-tuple-element.26.refs_0_, bf16[272,512]{1,0:T(8,128)(2,1)} %copy-done.12, bf16[272,512]{1,0:T(8,128)(2,1)} %collective-permute-done.15.refs_2_, bf16[272,512]{1,0:T(8,128)(2,1)} %copy-done.13, ...), custom_call_target="tpu_custom_call" | custom-call | flops 1610612736 | bytes 10485760 | tf_op jit(solution)/shard_map/first_units/pallas_call | solution.py:225
  183.7 7.6 %last_units.1 = (bf16[256,512]{1,0:T(8,128)(2,1)}, bf16[256,512]{1,0:T(8,128)(2,1)}, bf16[256,512]{1,0:T(8,128)(2,1)}, bf16[256,512]{1,0:T(8,128)(2,1)}) custom-call(s32[24]{0:T(128)} %stack.159.place_ref, bf16[4,256,512]{2,1,0:T(8,128)(2,1)} %get-tuple-element.29.x_ref, f32[4,256,512]{2,1,0:T(8,128)} %get-tuple-element.30.acc_in, ...), custom_call_target="tpu_custom_call" | custom-call | flops 1610612736 | bytes 10485760 | tf_op jit(solution)/shard_map/last_units/pallas_call | solution.py:241
  196.9 6.2 %collective-permute-start.27 = (bf16[256,512]{1,0:T(8,128)(2,1)S(1)}, bf16[256,512]{1,0:T(8,128)(2,1)S(1)}, u32[]{:S(2)}, u32[]{:S(2)}) collective-permute-start(bf16[256,512]{1,0:T(8,128)(2,1)S(1)} %add_convert_fusion), channel_id=1, source_target_pairs={{0,2},{2,0},{1,3},{3,1},{4,6},{6,4},{5,7},{7,5},{8,10},{10,8},{9,1... | collective-permute-start | bytes 786440 | tf_op jit(solution)/shard_map/ppermute | solution.py:38
  203.1 6.2 %collective-permute-done.27 = bf16[256,512]{1,0:T(8,128)(2,1)S(1)} collective-permute-done((bf16[256,512]{1,0:T(8,128)(2,1)S(1)}, bf16[256,512]{1,0:T(8,128)(2,1)S(1)}, u32[]{:S(2)}, u32[]{:S(2)}) %collective-permute-start.27) | collective-permute-done | bytes 262176 | tf_op jit(solution)/shard_map/ppermute | solution.py:38
  (98 shorter events, 47.5 us)
Async XLA Ops:
  7.2 92.6 %all-gather.3.cloned.1.call-start = ((), (), s32[]{:S(2)}) async-start(), calls=%async_computation | async-start | bytes 1769472 | tf_op jit(solution)/shard_map/all_gather | solution.py:274
  8.1 14.5 %collective-permute-start.2 = (bf16[48,1024]{1,0:T(8,128)(2,1)S(1)}, bf16[48,1024]{1,0:T(8,128)(2,1)S(1)}, u32[]{:S(2)}, u32[]{:S(2)}) collective-permute-start(bf16[48,1024]{1,0:T(8,128)(2,1)S(1)} %pad_maximum_fusion.4), channel_id=1, source_target_pairs={{0,12},{4,0},{8,4},{12,8},{1,13},{5,1},{9,5},{13,9},{2,14},{6,2},{... | collective-permute-start | bytes 294920 | tf_op jit(solution)/shard_map/ppermute | solution.py:34
  27.2 20.8 %collective-permute-start.4 = (bf16[4,48,512]{2,1,0:T(8,128)(2,1)S(1)}, bf16[4,48,512]{2,1,0:T(8,128)(2,1)S(1)}, u32[]{:S(2)}, u32[]{:S(2)}) collective-permute-start(bf16[4,48,512]{2,1,0:T(8,128)(2,1)S(1)} %get-tuple-element.37), channel_id=1, source_target_pairs={{0,256},{128,384},{256,0},{384,128},{1,257},{129,385},{257,1},{385... | collective-permute-start | bytes 589832 | tf_op jit(solution)/shard_map/ppermute | solution.py:34
  31.8 16.2 %collective-permute-start.3 = (bf16[4,48,512]{2,1,0:T(8,128)(2,1)S(1)}, bf16[4,48,512]{2,1,0:T(8,128)(2,1)S(1)}, u32[]{:S(2)}, u32[]{:S(2)}) collective-permute-start(bf16[4,48,512]{2,1,0:T(8,128)(2,1)S(1)} %get-tuple-element.37), channel_id=1, source_target_pairs={{0,128},{128,256},{256,384},{384,0},{1,129},{129,257},{257,385},{3... | collective-permute-start | bytes 589832 | tf_op jit(solution)/shard_map/ppermute | solution.py:34
  34.0 14.0 %collective-permute-start.5 = (bf16[4,48,512]{2,1,0:T(8,128)(2,1)S(1)}, bf16[4,48,512]{2,1,0:T(8,128)(2,1)S(1)}, u32[]{:S(2)}, u32[]{:S(2)}) collective-permute-start(bf16[4,48,512]{2,1,0:T(8,128)(2,1)S(1)} %get-tuple-element.37), channel_id=1, source_target_pairs={{0,384},{128,0},{256,128},{384,256},{1,385},{129,1},{257,129},{385... | collective-permute-start | bytes 589832 | tf_op jit(solution)/shard_map/ppermute | solution.py:34
  38.5 14.1 %collective-permute-start.6 = (bf16[272,512]{1,0:T(8,128)(2,1)S(1)}, bf16[272,512]{1,0:T(8,128)(2,1)S(1)}, u32[]{:S(2)}, u32[]{:S(2)}) collective-permute-start(bf16[272,512]{1,0:T(8,128)(2,1)S(1)} %pad_maximum_fusion.1.refs_1_), channel_id=1, source_target_pairs={{0,4},{4,8},{8,12},{12,16},{16,20},{20,24},{24,28},{28,32},{32,36}... | collective-permute-start | bytes 835592 | tf_op jit(solution)/shard_map/ppermute | solution.py:29
  41.6 10.9 %collective-permute-start.7 = (bf16[256,512]{1,0:T(8,128)(2,1)S(1)}, bf16[256,512]{1,0:T(8,128)(2,1)S(1)}, u32[]{:S(2)}, u32[]{:S(2)}) collective-permute-start(bf16[256,512]{1,0:T(8,128)(2,1)S(1)} %copy-done.14), channel_id=1, source_target_pairs={{0,4},{4,8},{8,12},{12,16},{16,20},{20,24},{24,28},{28,32},{32,36}... | collective-permute-start | bytes 786440 | tf_op jit(solution)/shard_map/ppermute | solution.py:29
  52.6 53.4 %collective-permute-start.12 = (bf16[4,4,48,512]{3,2,1,0:T(8,128)(2,1)}, bf16[4,4,48,512]{3,2,1,0:T(8,128)(2,1)}, u32[]{:S(2)}, u32[]{:S(2)}) collective-permute-start(bf16[4,4,48,512]{3,2,1,0:T(8,128)(2,1)} %pad_maximum_fusion.refs_4_), channel_id=1, source_target_pairs={{0,112},{16,0},{32,16},{48,32},{64,48},{80,64},{96,80},{112,96},{1... | collective-permute-start | bytes 2359304 | tf_op jit(solution)/shard_map/ppermute | solution.py:34
  65.2 43.7 %collective-permute-start.10 = (bf16[4,4,48,512]{3,2,1,0:T(8,128)(2,1)}, bf16[4,4,48,512]{3,2,1,0:T(8,128)(2,1)}, u32[]{:S(2)}, u32[]{:S(2)}) collective-permute-start(bf16[4,4,48,512]{3,2,1,0:T(8,128)(2,1)} %pad_maximum_fusion.refs_4_), channel_id=1, source_target_pairs={{0,16},{16,32},{32,48},{48,64},{64,80},{80,96},{96,112},{112,0},{1... | collective-permute-start | bytes 2359304 | tf_op jit(solution)/shard_map/ppermute | solution.py:34
  67.1 14.1 %collective-permute-start.8 = (bf16[272,512]{1,0:T(8,128)(2,1)S(1)}, bf16[272,512]{1,0:T(8,128)(2,1)S(1)}, u32[]{:S(2)}, u32[]{:S(2)}) collective-permute-start(bf16[272,512]{1,0:T(8,128)(2,1)S(1)} %collective-permute-done.6.refs_3_), channel_id=1, source_target_pairs={{0,4},{4,8},{8,12},{12,16},{16,20},{20,24},{24,28},{28,32},{32,36}... | collective-permute-start | bytes 835592 | tf_op jit(solution)/shard_map/ppermute | solution.py:29
  71.6 9.5 %collective-permute-start.9 = (bf16[256,512]{1,0:T(8,128)(2,1)S(1)}, bf16[256,512]{1,0:T(8,128)(2,1)S(1)}, u32[]{:S(2)}, u32[]{:S(2)}) collective-permute-start(bf16[256,512]{1,0:T(8,128)(2,1)S(1)} %collective-permute-done.7.refs_4_), channel_id=1, source_target_pairs={{0,4},{4,8},{8,12},{12,16},{16,20},{20,24},{24,28},{28,32},{32,36}... | collective-permute-start | bytes 786440 | tf_op jit(solution)/shard_map/ppermute | solution.py:29
  99.8 46.9 %collective-permute-start.22 = (bf16[8,4,48,512]{3,2,1,0:T(8,128)(2,1)}, bf16[8,4,48,512]{3,2,1,0:T(8,128)(2,1)S(1)}, u32[]{:S(2)}, u32[]{:S(2)}) collective-permute-start(bf16[8,4,48,512]{3,2,1,0:T(8,128)(2,1)} %bitcast.48), channel_id=1, source_target_pairs={{0,384},{128,0},{256,128},{384,256},{1,385},{129,1},{257,129},{385... | collective-permute-start | bytes 4718600 | tf_op jit(solution)/shard_map/ppermute | solution.py:34
  103.6 46.2 %collective-permute-start.21 = (bf16[8,4,48,512]{3,2,1,0:T(8,128)(2,1)}, bf16[8,4,48,512]{3,2,1,0:T(8,128)(2,1)S(1)}, u32[]{:S(2)}, u32[]{:S(2)}) collective-permute-start(bf16[8,4,48,512]{3,2,1,0:T(8,128)(2,1)} %bitcast.49), channel_id=1, source_target_pairs={{0,128},{128,256},{256,384},{384,0},{1,129},{129,257},{257,385},{3... | collective-permute-start | bytes 4718600 | tf_op jit(solution)/shard_map/ppermute | solution.py:34
  106.0 17.8 %collective-permute-start.13 = (bf16[4,4,48,512]{3,2,1,0:T(8,128)(2,1)}, bf16[4,4,48,512]{3,2,1,0:T(8,128)(2,1)}, u32[]{:S(2)}, u32[]{:S(2)}) collective-permute-start(bf16[4,4,48,512]{3,2,1,0:T(8,128)(2,1)} %collective-permute-done.12.refs_8_), channel_id=1, source_target_pairs={{0,112},{16,0},{32,16},{48,32},{64,48},{80,64},{96,80},{112,96},{1... | collective-permute-start | bytes 2359304 | tf_op jit(solution)/shard_map/ppermute | solution.py:34
  108.9 14.9 %collective-permute-start.11 = (bf16[4,4,48,512]{3,2,1,0:T(8,128)(2,1)}, bf16[4,4,48,512]{3,2,1,0:T(8,128)(2,1)}, u32[]{:S(2)}, u32[]{:S(2)}) collective-permute-start(bf16[4,4,48,512]{3,2,1,0:T(8,128)(2,1)} %collective-permute-done.10.refs_5_), channel_id=1, source_target_pairs={{0,16},{16,32},{32,48},{48,64},{64,80},{80,96},{96,112},{112,0},{1... | collective-permute-start | bytes 2359304 | tf_op jit(solution)/shard_map/ppermute | solution.py:34
  123.8 30.4 %collective-permute-start.17 = (bf16[4,4,48,512]{3,2,1,0:T(8,128)(2,1)}, bf16[4,4,48,512]{3,2,1,0:T(8,128)(2,1)S(1)}, u32[]{:S(2)}, u32[]{:S(2)}) collective-permute-start(bf16[4,4,48,512]{3,2,1,0:T(8,128)(2,1)} %collective-permute-done.11.refs_6_), channel_id=1, source_target_pairs={{0,16},{16,32},{32,48},{48,64},{64,80},{80,96},{96,112},{112,0},{1... | collective-permute-start | bytes 2359304 | tf_op jit(solution)/shard_map/ppermute | solution.py:34
  129.0 30.4 %collective-permute-start.18 = (bf16[4,4,48,512]{3,2,1,0:T(8,128)(2,1)}, bf16[4,4,48,512]{3,2,1,0:T(8,128)(2,1)S(1)}, u32[]{:S(2)}, u32[]{:S(2)}) collective-permute-start(bf16[4,4,48,512]{3,2,1,0:T(8,128)(2,1)} %collective-permute-done.13.refs_9_), channel_id=1, source_target_pairs={{0,112},{16,0},{32,16},{48,32},{64,48},{80,64},{96,80},{112,96},{1... | collective-permute-start | bytes 2359304 | tf_op jit(solution)/shard_map/ppermute | solution.py:34
  130.9 30.4 %collective-permute-start.15 = (bf16[272,512]{1,0:T(8,128)(2,1)}, bf16[272,512]{1,0:T(8,128)(2,1)}, u32[]{:S(2)}, u32[]{:S(2)}) collective-permute-start(bf16[272,512]{1,0:T(8,128)(2,1)} %get-tuple-element.26.refs_0_), channel_id=1, source_target_pairs={{0,2},{2,0},{1,3},{3,1},{4,6},{6,4},{5,7},{7,5},{8,10},{10,8},{9,1... | collective-permute-start | bytes 835592 | tf_op jit(solution)/shard_map/ppermute | solution.py:38
  147.8 35.0 %collective-permute-start.24 = (bf16[4,4,48,512]{3,2,1,0:T(8,128)(2,1)}, bf16[4,4,48,512]{3,2,1,0:T(8,128)(2,1)S(1)}, u32[]{:S(2)}, u32[]{:S(2)}) collective-permute-start(bf16[4,4,48,512]{3,2,1,0:T(8,128)(2,1)} %slice.59), channel_id=1, source_target_pairs={{0,384},{128,0},{256,128},{384,256},{1,385},{129,1},{257,129},{385... | collective-permute-start | bytes 2359304 | tf_op jit(solution)/shard_map/ppermute | solution.py:34
  150.8 32.0 %collective-permute-start.23 = (bf16[4,4,48,512]{3,2,1,0:T(8,128)(2,1)}, bf16[4,4,48,512]{3,2,1,0:T(8,128)(2,1)}, u32[]{:S(2)}, u32[]{:S(2)}) collective-permute-start(bf16[4,4,48,512]{3,2,1,0:T(8,128)(2,1)} %slice.58), channel_id=1, source_target_pairs={{0,128},{128,256},{256,384},{384,0},{1,129},{129,257},{257,385},{3... | collective-permute-start | bytes 2359304 | tf_op jit(solution)/shard_map/ppermute | solution.py:34
  154.2 11.8 %collective-permute-start.14 = (bf16[272,512]{1,0:T(8,128)(2,1)S(1)}, bf16[272,512]{1,0:T(8,128)(2,1)S(1)}, u32[]{:S(2)}, u32[]{:S(2)}) collective-permute-start(bf16[272,512]{1,0:T(8,128)(2,1)S(1)} %copy-done.11), channel_id=1, source_target_pairs={{0,1},{1,0},{2,3},{3,2},{4,5},{5,4},{6,7},{7,6},{8,9},{9,8},{10,11... | collective-permute-start | bytes 835592 | tf_op jit(solution)/shard_map/ppermute | solution.py:38
  159.3 13.9 %collective-permute-start.19 = (bf16[2,4,48,512]{3,2,1,0:T(8,128)(2,1)S(1)}, bf16[2,4,48,512]{3,2,1,0:T(8,128)(2,1)S(1)}, u32[]{:S(2)}, u32[]{:S(2)}) collective-permute-start(bf16[2,4,48,512]{3,2,1,0:T(8,128)(2,1)S(1)} %slice.56), channel_id=1, source_target_pairs={{0,16},{16,32},{32,48},{48,64},{64,80},{80,96},{96,112},{112,0},{1... | collective-permute-start | bytes 1179656 | tf_op jit(solution)/shard_map/ppermute | solution.py:34
  161.3 13.1 %collective-permute-start.20 = (bf16[2,4,48,512]{3,2,1,0:T(8,128)(2,1)S(1)}, bf16[2,4,48,512]{3,2,1,0:T(8,128)(2,1)S(1)}, u32[]{:S(2)}, u32[]{:S(2)}) collective-permute-start(bf16[2,4,48,512]{3,2,1,0:T(8,128)(2,1)S(1)} %slice.57), channel_id=1, source_target_pairs={{0,112},{16,0},{32,16},{48,32},{64,48},{80,64},{96,80},{112,96},{1... | collective-permute-start | bytes 1179656 | tf_op jit(solution)/shard_map/ppermute | solution.py:34
  196.9 12.4 %collective-permute-start.27 = (bf16[256,512]{1,0:T(8,128)(2,1)S(1)}, bf16[256,512]{1,0:T(8,128)(2,1)S(1)}, u32[]{:S(2)}, u32[]{:S(2)}) collective-permute-start(bf16[256,512]{1,0:T(8,128)(2,1)S(1)} %add_convert_fusion), channel_id=1, source_target_pairs={{0,2},{2,0},{1,3},{3,1},{4,6},{6,4},{5,7},{7,5},{8,10},{10,8},{9,1... | collective-permute-start | bytes 786440 | tf_op jit(solution)/shard_map/ppermute | solution.py:38
  (25 other events, 467.1 us)
Sparse Core Ops, SparseCore 0:
  27.1 72.6 all-gather.2

commit v4 on v2

v4 whole, which is shorter than its diff:
```python
import math

import jax
import jax.numpy as jnp
from jax import lax
from jax.experimental import pallas as pl
from jax.experimental.pallas import tpu as pltpu
from jax.sharding import Mesh
from jax.sharding import PartitionSpec as P

D = 2048
HEAD_DIM = 128
SEG = 128
ROWS = 256
TP_WIDTH = 512
UNIT_BLOCK = 256
EXTRA = 16
epsilon = 1e-06

SEQ = ("x", "z", "yh")
TP = ("yl", "c")
F32 = jnp.float32
BF16 = jnp.bfloat16


def from_behind(value, by):
    size = lax.axis_size(SEQ)
    return lax.ppermute(value, SEQ, [(i, i + by) for i in range(size - by)])


def around(value, axis, by):
    size = lax.axis_size(axis)
    return lax.ppermute(value, axis, [(i, (i + by) % size) for i in range(size)])


def swap(value, axis):
    size = lax.axis_size(axis)
    return lax.ppermute(value, axis, [(i, i ^ 1) for i in range(size)])


def attention_kernel(
    lengths_ref, gain_ref, *refs
):
    outside, (att_ref, send_ref), inside, sems = refs[:8], refs[8:10], refs[10:18], refs[18]
    copies = [
        pltpu.make_async_copy(src, dst, sems.at[i])
        for i, (src, dst) in enumerate(zip(outside, inside))
    ]
    for copy in copies:
        copy.start()
    q_ref, k0_ref, v0_ref, k1_ref, v1_ref, k2_ref, v2_ref, res_ref = inside
    gain = gain_ref[...]
    high = gain.astype(BF16).astype(F32)
    middle = (gain - high).astype(BF16).astype(F32)
    low = gain - high - middle
    extra = lax.broadcasted_iota(jnp.int32, (EXTRA, TP_WIDTH), 0)
    extra = jnp.where(extra == 0, high, jnp.where(extra == 1, middle, jnp.where(extra == 2, low, 0.0)))
    send_ref[pl.ds(ROWS, EXTRA), :] = extra.astype(BF16)
    for copy in copies:
        copy.wait()
    rows = lax.broadcasted_iota(jnp.int32, (ROWS, ROWS), 0)
    cols = lax.broadcasted_iota(jnp.int32, (ROWS, ROWS), 1)
    col = lax.broadcasted_iota(jnp.int32, (1, ROWS), 1)

    def valid(key_ref):
        first = key_ref[pl.ds(ROWS, 8), pl.ds(0, ROWS)].astype(F32)[0:1, :].astype(jnp.int32)
        second = key_ref[pl.ds(ROWS + 8, 8), pl.ds(0, ROWS)].astype(F32)[0:1, :].astype(jnp.int32)
        return (col < jnp.where(col < SEG, first, second + SEG)).astype(jnp.int32)

    allowed = (
        (valid(k0_ref) > 0) & (cols <= rows),
        (valid(k1_ref) + jnp.zeros_like(cols)) > 0,
        (valid(k2_ref) > 0) & (cols > rows),
    )
    row = lax.broadcasted_iota(jnp.int32, (ROWS, 1), 0)
    keep = row < jnp.where(row < SEG, lengths_ref[0], lengths_ref[1] + SEG)
    scale = 1.0 / math.sqrt(HEAD_DIM)
    keys = (k0_ref, k1_ref, k2_ref)
    values = (v0_ref, v1_ref, v2_ref)
    for head in range(TP_WIDTH // HEAD_DIM):
        at = pl.ds(head * HEAD_DIM, HEAD_DIM)
        query = q_ref[:, at]
        masked = []
        for key_ref, allow in zip(keys, allowed):
            scores = lax.dot_general(
                query,
                key_ref[pl.ds(0, ROWS), at],
                (((1,), (1,)), ((), ())),
                preferred_element_type=F32,
            )
            masked.append(jnp.where(allow, scores * scale, -1e30))
        top = jnp.max(jnp.maximum(jnp.maximum(masked[0], masked[1]), masked[2]), axis=1, keepdims=True)
        weights = [jnp.where(a, jnp.exp(m - top), 0.0) for a, m in zip(allowed, masked)]
        denominator = jnp.sum(weights[0] + weights[1] + weights[2], axis=1, keepdims=True)
        numerator = jnp.zeros((ROWS, HEAD_DIM), F32)
        for weight, value_ref in zip(weights, values):
            numerator += jnp.dot(weight.astype(BF16), value_ref[:, at], preferred_element_type=F32)
        out = jnp.where(keep, numerator / jnp.where(keep, denominator, 1.0), 0.0).astype(BF16)
        att_ref[:, at] = out
        send_ref[pl.ds(0, ROWS), at] = (res_ref[:, at] + out.astype(F32)).astype(BF16)


HBM = pl.BlockSpec(memory_space=pltpu.HBM)
SMEM = pl.BlockSpec(memory_space=pltpu.SMEM)


def attention(lengths, gain, q, k0, v0, k1, v1, k2, v2, residual_in):
    return pl.pallas_call(
        attention_kernel,
        out_shape=(
            jax.ShapeDtypeStruct((ROWS, TP_WIDTH), BF16),
            jax.ShapeDtypeStruct((ROWS + EXTRA, TP_WIDTH), BF16),
        ),
        in_specs=[SMEM, pl.BlockSpec()] + [HBM] * 8,
        out_specs=(pl.BlockSpec(), pl.BlockSpec()),
        scratch_shapes=[
            pltpu.VMEM(a.shape, a.dtype) for a in (q, k0, v0, k1, v1, k2, v2, residual_in)
        ]
        + [pltpu.SemaphoreType.DMA((8,))],
        compiler_params=pltpu.CompilerParams(vmem_limit_bytes=60 << 20),
        cost_estimate=pl.CostEstimate(
            flops=4 * ROWS * 3 * ROWS * TP_WIDTH, bytes_accessed=3 << 20, transcendentals=3 << 18
        ),
        name="attention",
    )(lengths, gain, q, k0, v0, k1, v1, k2, v2, residual_in)


def feed_forward_kernel(place_ref, *refs):
    parts, w_ref, outs, x_ref, acc_ref = refs[:8], refs[8], refs[9:13], refs[13], refs[14]
    step = pl.program_id(0)

    @pl.when(step == 0)
    def _():
        for g in range(2):
            square = jnp.zeros((ROWS, 1), F32)
            for p in range(4):
                value = parts[4 * g + p][pl.ds(0, ROWS), :].astype(F32)
                square += jnp.sum(value * value, axis=1, keepdims=True)
            inverse = lax.rsqrt(square / D + epsilon)
            for p in range(4):
                extra = parts[4 * g + p][pl.ds(ROWS, EXTRA), :].astype(F32)
                gain = extra[0:1] + extra[1:2] + extra[2:3]
                value = parts[4 * g + p][pl.ds(0, ROWS), :].astype(F32)
                x_ref[p, pl.ds(g * ROWS, ROWS), :] = (value * inverse * gain).astype(BF16)
        acc_ref[...] = jnp.zeros_like(acc_ref)

    def block(p, kind):
        pieces = [
            w_ref[
                pl.ds(place_ref[p] * 8, 8),
                pl.ds(place_ref[4 + y], 1),
                pl.ds(kind * 16, 16),
                :,
            ]
            for y in range(4)
        ]
        return jnp.concatenate(pieces, axis=1).reshape(TP_WIDTH, UNIT_BLOCK)

    gate = jnp.zeros((2 * ROWS, UNIT_BLOCK), F32)
    up = jnp.zeros((2 * ROWS, UNIT_BLOCK), F32)
    for p in range(4):
        gate += jnp.dot(x_ref[p], block(p, 0), preferred_element_type=F32)
        up += jnp.dot(x_ref[p], block(p, 1), preferred_element_type=F32)
    hidden = (gate / (1.0 + jnp.exp(-gate)) * up).astype(BF16)
    for p in range(4):
        acc_ref[p] += lax.dot_general(
            hidden, block(p, 2), (((1,), (1,)), ((), ())), preferred_element_type=F32
        )

    @pl.when(step == pl.num_programs(0) - 1)
    def _():
        for g in range(2):
            for i, p in enumerate((2, 0)):
                outs[2 * g][i] = acc_ref[p, pl.ds(g * ROWS, ROWS), :].astype(BF16)
                outs[2 * g + 1][i] = acc_ref[p + 1, pl.ds(g * ROWS, ROWS), :].astype(BF16)


def feed_forward(place, parts, weights):
    whole = pl.BlockSpec((ROWS + EXTRA, TP_WIDTH), lambda i, o: (0, 0))
    pair = pl.BlockSpec((2, ROWS, TP_WIDTH), lambda i, o: (0, 0, 0))
    units = weights.shape[3]
    return pl.pallas_call(
        feed_forward_kernel,
        out_shape=[jax.ShapeDtypeStruct((2, ROWS, TP_WIDTH), BF16)] * 4,
        grid_spec=pltpu.PrefetchScalarGridSpec(
            num_scalar_prefetch=1,
            grid=(units // UNIT_BLOCK,),
            in_specs=[whole] * 8
            + [pl.BlockSpec((32, 4, 48, UNIT_BLOCK), lambda i, o: (0, 0, 0, i))],
            out_specs=[pair] * 4,
            scratch_shapes=[
                pltpu.VMEM((4, 2 * ROWS, TP_WIDTH), BF16),
                pltpu.VMEM((4, 2 * ROWS, TP_WIDTH), F32),
            ],
        ),
        compiler_params=pltpu.CompilerParams(vmem_limit_bytes=48 << 20),
        cost_estimate=pl.CostEstimate(
            flops=12 * ROWS * D * units, bytes_accessed=10 << 20, transcendentals=2 * ROWS * units
        ),
        name="feed_forward",
    )(place, *parts, weights)


def on_device(
    residual_in,
    query_rows,
    key_rows,
    value_rows,
    lengths,
    norm_gain,
    gate_weight,
    up_weight,
    down_weight,
):
    yh = lax.axis_index("yh")
    half = gate_weight.shape[1] // 2

    packed = jnp.concatenate([gate_weight, up_weight, down_weight.T], axis=0)
    parity = yh & 1
    mine = lax.dynamic_slice_in_dim(packed, parity * half, half, 1)
    other = lax.dynamic_slice_in_dim(packed, (1 - parity) * half, half, 1)
    near = jnp.stack(
        [mine, around(other, "yh", 1), around(mine, "yh", 2), around(other, "yh", 3)]
    )
    weights = lax.all_gather(near, ("x", "z"), axis=0)

    tail = jnp.broadcast_to(
        jnp.repeat(lengths.astype(BF16), 8)[:, None], (16, key_rows.shape[1])
    )
    k0 = jnp.concatenate([key_rows, tail], axis=0)
    k1, v1 = from_behind(k0, 1), from_behind(value_rows, 1)
    k2, v2 = from_behind(k1, 1), from_behind(v1, 1)

    attended, sent = attention(
        lengths, norm_gain[None, :], query_rows, k0, value_rows, k1, v1, k2, v2, residual_in
    )

    partner = swap(sent, "yh")
    parts = []
    for start in (sent, partner):
        chip = swap(start, "yl")
        parts += [start, swap(start, "c"), chip, swap(chip, "c")]
    own = 2 * lax.axis_index("yl") + lax.axis_index("c")
    place = [own, own ^ 1, own ^ 2, own ^ 3] + [(yh - y) & 3 for y in range(4)]
    place = jnp.stack(place).astype(jnp.int32)
    own_keep, own_send, partner_keep, partner_send = feed_forward(place, parts, weights)

    def add(left, right):
        return left.astype(F32) + right.astype(F32)

    partner_got = swap(partner_send, "c")
    own_got = swap(own_send, "c")
    partner_far = swap(add(partner_keep[0], partner_got[0]).astype(BF16), "yl")
    own_far = swap(add(own_keep[0], own_got[0]).astype(BF16), "yl")
    back = swap((add(partner_keep[1], partner_got[1]) + partner_far.astype(F32)).astype(BF16), "yh")
    summed = add(own_keep[1], own_got[1]) + own_far.astype(F32) + back.astype(F32)
    mixed = residual_in + attended.astype(F32) + summed
    return attended, mixed


def solution(mesh):
    fine = Mesh(mesh.devices.reshape(4, 8, 4, 2, 2), SEQ + TP)
    placed = (
        P(SEQ, TP),
        P(SEQ, TP),
        P(SEQ, TP),
        P(SEQ, TP),
        P(SEQ),
        P(TP),
        P(SEQ, TP),
        P(SEQ, TP),
        P(TP, SEQ),
    )
    return jax.shard_map(
        on_device,
        mesh=fine,
        in_specs=placed,
        out_specs=(P(SEQ, TP), P(SEQ, TP)),
        check_vma=False,
    )
```

time: 192 us -> 185 us (0.964)
  waiting for transfers between devices: 27.2 us -> 67.3 us
  blocking collectives: 30.3 us -> 0 us
  starting transfers between devices: 99 us -> 82.1 us
    all_gather x1 -> x0, blocking collectives: 30.3 us -> none  [on_device(): gain = lax.all_gather(norm_gain, TP, axis=0)]
    all_gather x1, waiting for transfers between devices: 7 us -> 27.6 us  [on_device(): weights = lax.all_gather(near, ('x', 'z'), axis=0)]
    ppermute x4, waiting for transfers between devices: 1.04 us -> 21.4 us  [from_behind(): return lax.ppermute(value, SEQ, [(i, i + by) for i in range(size - by)])]
    ppermute x6 -> x3, starting transfers between devices: 24.3 us -> 14.5 us  [around(): lax.ppermute(value, axis, [(i, (i + by) % size) for i in range(size)])]
    ppermute x6 -> x3, waiting for transfers between devices: 9.95 us -> 2.75 us  [around(): lax.ppermute(value, axis, [(i, (i + by) % size) for i in range(size)])]
    ppermute x14 -> x12, waiting for transfers between devices: 9.16 us -> 15.5 us  [swap(): return lax.ppermute(value, axis, [(i, i ^ 1) for i in range(size)])]
    ppermute x14 -> x12, starting transfers between devices: 56.5 us -> 50.9 us  [swap(): return lax.ppermute(value, axis, [(i, i ^ 1) for i in range(size)])]
    pallas_call x2, Pallas kernels: 10.7 us -> 12.6 us  [the longest x1 7.54 us: feed_forward(): pl.pallas_call(feed_forward_kernel, out_shape=[jax.ShapeDtypeStruct((2, R...]
  transfers between devices with their start and end apart: 25 -> 20, of which waited for: 9 -> 9; matrix products, arithmetic and copies ran while one was open for 1% -> 1% of each run, Pallas kernels for 2% -> 3%
where the time goes in v4:
time: 185 us; the launch traced here: 183 us
  starting transfers between devices  82.1 us (44%)
  waiting for transfers between devices  67.3 us (36%)
  between operations  14.4 us (8%)
  Pallas kernels  12.6 us (7%)
  other arithmetic  4.47 us (2%)
  local copies, waits for them, and re-layouts  2.01 us (1%)
    ppermute x12, starting transfers between devices, swap(): return lax.ppermute(value, axis, [(i, i ^ 1) for i in range(size)])  50.9 us
    all_gather x1, waiting for transfers between devices, on_device(): weights = lax.all_gather(near, ('x', 'z'), axis=0)  27.6 us
    ppermute x4, waiting for transfers between devices, from_behind(): return lax.ppermute(value, SEQ, [(i, i + by) for i in range(size - by)])  21.4 us
    ppermute x4, starting transfers between devices, from_behind(): return lax.ppermute(value, SEQ, [(i, i + by) for i in range(size - by)])  16.7 us
    ppermute x12, waiting for transfers between devices, swap(): return lax.ppermute(value, axis, [(i, i ^ 1) for i in range(size)])  15.5 us
    ppermute x3, starting transfers between devices, around(): lax.ppermute(value, axis, [(i, (i + by) % size) for i in range(size)])  14.5 us
    pallas_call x1, Pallas kernels, feed_forward(): pl.pallas_call(feed_forward_kernel, out_shape=[jax.ShapeDtypeStruct((2, R...  7.54 us
    pallas_call x1, Pallas kernels, attention(): pl.pallas_call(attention_kernel, out_shape=(jax.ShapeDtypeStruct((ROWS, T...  5.08 us
  transfers between devices with their start and end apart: 20, of which 9 were waited for; matrix products, arithmetic and copies ran while one was open for 1% of the time, Pallas kernels for 3%

profile of v4, /device:TPU:1, one launch (start us, length us, event | category | flops | bytes accessed | tf_op | source)
XLA Modules:
  0.0 182.8 jit_solution(14805938043341349855)
XLA Ops:
  8.0 8.3 %collective-permute-start.12 = (bf16[48,512]{1,0:T(8,128)(2,1)S(1)}, bf16[48,512]{1,0:T(8,128)(2,1)S(1)}, u32[]{:S(2)}, u32[]{:S(2)}) collective-permute-start(bf16[48,512]{1,0:T(8,128)(2,1)S(1)} %get-tuple-element.14), channel_id=1, source_target_pairs={{0,8},{4,12},{8,0},{12,4},{1,9},{5,13},{9,1},{13,5},{2,10},{6,14},... | collective-permute-start | bytes 147464 | tf_op jit(solution)/shard_map/ppermute | solution.py:33
  18.3 4.2 %collective-permute-start.11 = (bf16[48,512]{1,0:T(8,128)(2,1)S(1)}, bf16[48,512]{1,0:T(8,128)(2,1)S(1)}, u32[]{:S(2)}, u32[]{:S(2)}) collective-permute-start(bf16[48,512]{1,0:T(8,128)(2,1)S(1)} %get-tuple-element.15), channel_id=1, source_target_pairs={{0,4},{4,8},{8,12},{12,0},{1,5},{5,9},{9,13},{13,1},{2,6},{6,10},{... | collective-permute-start | bytes 147464 | tf_op jit(solution)/shard_map/ppermute | solution.py:33
  22.7 2.6 %collective-permute-done.11 = bf16[48,512]{1,0:T(8,128)(2,1)S(1)} collective-permute-done((bf16[48,512]{1,0:T(8,128)(2,1)S(1)}, bf16[48,512]{1,0:T(8,128)(2,1)S(1)}, u32[]{:S(2)}, u32[]{:S(2)}) %collective-permute-start.11) | collective-permute-done | bytes 49184 | tf_op jit(solution)/shard_map/ppermute | solution.py:33
  27.9 3.3 %collective-permute-start = (bf16[272,512]{1,0:T(8,128)(2,1)S(1)}, bf16[272,512]{1,0:T(8,128)(2,1)S(1)}, u32[]{:S(2)}, u32[]{:S(2)}) collective-permute-start(bf16[272,512]{1,0:T(8,128)(2,1)S(1)} %pad_maximum_fusion.refs_1_), channel_id=1, source_target_pairs={{0,4},{4,8},{8,12},{12,16},{16,20},{20,24},{24,28},{28,32},{32,36}... | collective-permute-start | bytes 835592 | tf_op jit(solution)/shard_map/ppermute | solution.py:28
  31.2 4.7 %collective-permute-start.1 = (bf16[256,512]{1,0:T(8,128)(2,1)}, bf16[256,512]{1,0:T(8,128)(2,1)S(1)}, u32[]{:S(2)}, u32[]{:S(2)}) collective-permute-start(bf16[256,512]{1,0:T(8,128)(2,1)} %refs_2_.1), channel_id=1, source_target_pairs={{0,4},{4,8},{8,12},{12,16},{16,20},{20,24},{24,28},{28,32},{32,36}... | collective-permute-start | bytes 786440 | tf_op jit(solution)/shard_map/ppermute | solution.py:28
  35.9 3.9 %collective-permute-start.2 = (bf16[272,512]{1,0:T(8,128)(2,1)S(1)}, bf16[272,512]{1,0:T(8,128)(2,1)S(1)}, u32[]{:S(2)}, u32[]{:S(2)}) collective-permute-start(bf16[272,512]{1,0:T(8,128)(2,1)S(1)} %collective-permute-done.refs_3_), channel_id=1, source_target_pairs={{0,4},{4,8},{8,12},{12,16},{16,20},{20,24},{24,28},{28,32},{32,36}... | collective-permute-start | bytes 835592 | tf_op jit(solution)/shard_map/ppermute | solution.py:28
  39.8 6.9 %collective-permute-done.1.refs_4_ = bf16[256,512]{1,0:T(8,128)(2,1)S(1)} collective-permute-done((bf16[256,512]{1,0:T(8,128)(2,1)}, bf16[256,512]{1,0:T(8,128)(2,1)S(1)}, u32[]{:S(2)}, u32[]{:S(2)}) %collective-permute-start.1) | collective-permute-done | bytes 262176 | tf_op jit(solution)/shard_map/ppermute | solution.py:28
  46.7 4.9 %collective-permute-start.3 = (bf16[256,512]{1,0:T(8,128)(2,1)S(1)}, bf16[256,512]{1,0:T(8,128)(2,1)S(1)}, u32[]{:S(2)}, u32[]{:S(2)}) collective-permute-start(bf16[256,512]{1,0:T(8,128)(2,1)S(1)} %collective-permute-done.1.refs_4_), channel_id=1, source_target_pairs={{0,4},{4,8},{8,12},{12,16},{16,20},{20,24},{24,28},{28,32},{32,36}... | collective-permute-start | bytes 786440 | tf_op jit(solution)/shard_map/ppermute | solution.py:28
  51.6 14.4 %collective-permute-done.3.refs_6_ = bf16[256,512]{1,0:T(8,128)(2,1)S(1)} collective-permute-done((bf16[256,512]{1,0:T(8,128)(2,1)S(1)}, bf16[256,512]{1,0:T(8,128)(2,1)S(1)}, u32[]{:S(2)}, u32[]{:S(2)}) %collective-permute-start.3) | collective-permute-done | bytes 262176 | tf_op jit(solution)/shard_map/ppermute | solution.py:28
  66.9 5.1 %attention.1 = (bf16[256,512]{1,0:T(8,128)(2,1)}, bf16[272,512]{1,0:T(8,128)(2,1)}) custom-call(s32[2]{0:T(128)} %lengths_ref.1, f32[1,512]{1,0:T(1,128)} %bitcast.34, bf16[256,512]{1,0:T(8,128)(2,1)} %refs_0_.1, bf16[272,512]{1,0:T(8,128)(2,1)} %copy-done.2, bf16[256,512]{1,0:T(8,128)(2,1)} %refs_2_.1, bf16[272,512]{1,0:T(8,128)(2,1)} %copy-done.3, ...), custom_call_target="tpu_custom_call" | custom-call | flops 402653184 | bytes 3145728 | tf_op jit(solution)/shard_map/attention/pallas_call | solution.py:108
  72.0 7.3 %collective-permute-start.7 = (bf16[272,512]{1,0:T(8,128)(2,1)}, bf16[272,512]{1,0:T(8,128)(2,1)S(1)}, u32[]{:S(2)}, u32[]{:S(2)}) collective-permute-start(bf16[272,512]{1,0:T(8,128)(2,1)} %get-tuple-element.9.refs_0_), channel_id=1, source_target_pairs={{0,4},{4,0},{8,12},{12,8},{1,5},{5,1},{9,13},{13,9},{2,6},{6,2},{1... | collective-permute-start | bytes 835592 | tf_op jit(solution)/shard_map/ppermute | solution.py:38
  79.3 10.5 %collective-permute-start.5 = (bf16[272,512]{1,0:T(8,128)(2,1)}, bf16[272,512]{1,0:T(8,128)(2,1)S(1)}, u32[]{:S(2)}, u32[]{:S(2)}) collective-permute-start(bf16[272,512]{1,0:T(8,128)(2,1)} %get-tuple-element.9.refs_0_), channel_id=1, source_target_pairs={{0,2},{2,0},{1,3},{3,1},{4,6},{6,4},{5,7},{7,5},{8,10},{10,8},{9,1... | collective-permute-start | bytes 835592 | tf_op jit(solution)/shard_map/ppermute | solution.py:38
  89.8 7.4 %collective-permute-start.9 = (bf16[272,512]{1,0:T(8,128)(2,1)S(1)}, bf16[272,512]{1,0:T(8,128)(2,1)S(1)}, u32[]{:S(2)}, u32[]{:S(2)}) collective-permute-start(bf16[272,512]{1,0:T(8,128)(2,1)S(1)} %collective-permute-done.7.refs_4_), channel_id=1, source_target_pairs={{0,2},{2,0},{1,3},{3,1},{4,6},{6,4},{5,7},{7,5},{8,10},{10,8},{9,1... | collective-permute-start | bytes 835592 | tf_op jit(solution)/shard_map/ppermute | solution.py:38
  97.2 5.1 %collective-permute-start.4 = (bf16[272,512]{1,0:T(8,128)(2,1)}, bf16[272,512]{1,0:T(8,128)(2,1)S(1)}, u32[]{:S(2)}, u32[]{:S(2)}) collective-permute-start(bf16[272,512]{1,0:T(8,128)(2,1)} %get-tuple-element.9.refs_0_), channel_id=1, source_target_pairs={{0,1},{1,0},{2,3},{3,2},{4,5},{5,4},{6,7},{7,6},{8,9},{9,8},{10,11... | collective-permute-start | bytes 835592 | tf_op jit(solution)/shard_map/ppermute | solution.py:38
  104.3 2.4 %collective-permute-start.6 = (bf16[272,512]{1,0:T(8,128)(2,1)S(1)}, bf16[272,512]{1,0:T(8,128)(2,1)S(1)}, u32[]{:S(2)}, u32[]{:S(2)}) collective-permute-start(bf16[272,512]{1,0:T(8,128)(2,1)S(1)} %collective-permute-done.5.refs_2_), channel_id=1, source_target_pairs={{0,1},{1,0},{2,3},{3,2},{4,5},{5,4},{6,7},{7,6},{8,9},{9,8},{10,11... | collective-permute-start | bytes 835592 | tf_op jit(solution)/shard_map/ppermute | solution.py:38
  106.7 2.1 %collective-permute-start.10 = (bf16[272,512]{1,0:T(8,128)(2,1)S(1)}, bf16[272,512]{1,0:T(8,128)(2,1)S(1)}, u32[]{:S(2)}, u32[]{:S(2)}) collective-permute-start(bf16[272,512]{1,0:T(8,128)(2,1)S(1)} %collective-permute-done.9.refs_6_), channel_id=1, source_target_pairs={{0,1},{1,0},{2,3},{3,2},{4,5},{5,4},{6,7},{7,6},{8,9},{9,8},{10,11... | collective-permute-start | bytes 835592 | tf_op jit(solution)/shard_map/ppermute | solution.py:38
  110.1 27.6 %all-gather.3.cloned.1.call-done = bf16[128,48,512]{2,1,0:T(8,128)(2,1)} async-done(((bf16[4,48,512]{2,1,0:T(8,128)(2,1)}), bf16[128,48,512]{2,1,0:T(8,128)(2,1)}) %all-gather.3.cloned.1.call-update) | async-done | bytes 6291472 | tf_op jit(solution)/shard_map/all_gather | solution.py:225
  138.7 7.5 %feed_forward.1 = (bf16[2,256,512]{2,1,0:T(8,128)(2,1)S(1)}, bf16[2,256,512]{2,1,0:T(8,128)(2,1)S(1)}, bf16[2,256,512]{2,1,0:T(8,128)(2,1)S(1)}, bf16[2,256,512]{2,1,0:T(8,128)(2,1)S(1)}) custom-call(s32[8]{0:T(128)S(1)} %stack.50.place_ref, bf16[272,512]{1,0:T(8,128)(2,1)S(1)} %copy-done, bf16[272,512]{1,0:T(8,128)(2,1)S(1)} %collective-permute-done.4.refs_1_, ...), custom_call_target="tpu_custom_call" | custom-call | flops 3221225472 | bytes 10485760 | tf_op jit(solution)/shard_map/feed_forward/pallas_call | solution.py:182
  146.3 2.9 %collective-permute-start.16 = (bf16[2,256,512]{2,1,0:T(8,128)(2,1)S(1)}, bf16[2,256,512]{2,1,0:T(8,128)(2,1)S(1)}, u32[]{:S(2)}, u32[]{:S(2)}) collective-permute-start(bf16[2,256,512]{2,1,0:T(8,128)(2,1)S(1)} %get-tuple-element.13), channel_id=1, source_target_pairs={{0,1},{1,0},{2,3},{3,2},{4,5},{5,4},{6,7},{7,6},{8,9},{9,8},{10,11... | collective-permute-start | bytes 1572872 | tf_op jit(solution)/shard_map/ppermute | solution.py:38
  151.2 3.1 %collective-permute-start.17 = (bf16[256,512]{1,0:T(8,128)(2,1)S(1)}, bf16[256,512]{1,0:T(8,128)(2,1)S(1)}, u32[]{:S(2)}, u32[]{:S(2)}) collective-permute-start(bf16[256,512]{1,0:T(8,128)(2,1)S(1)} %fusion.4), channel_id=1, source_target_pairs={{0,2},{2,0},{1,3},{3,1},{4,6},{6,4},{5,7},{7,5},{8,10},{10,8},{9,1... | collective-permute-start | bytes 786440 | tf_op jit(solution)/shard_map/ppermute | solution.py:38
  154.4 2.2 %collective-permute-start.15 = (bf16[256,512]{1,0:T(8,128)(2,1)S(1)}, bf16[256,512]{1,0:T(8,128)(2,1)S(1)}, u32[]{:S(2)}, u32[]{:S(2)}) collective-permute-start(bf16[256,512]{1,0:T(8,128)(2,1)S(1)} %fusion.3), channel_id=1, source_target_pairs={{0,2},{2,0},{1,3},{3,1},{4,6},{6,4},{5,7},{7,5},{8,10},{10,8},{9,1... | collective-permute-start | bytes 786440 | tf_op jit(solution)/shard_map/ppermute | solution.py:38
  156.5 3.9 %collective-permute-done.17 = bf16[256,512]{1,0:T(8,128)(2,1)S(1)} collective-permute-done((bf16[256,512]{1,0:T(8,128)(2,1)S(1)}, bf16[256,512]{1,0:T(8,128)(2,1)S(1)}, u32[]{:S(2)}, u32[]{:S(2)}) %collective-permute-start.17) | collective-permute-done | bytes 262176 | tf_op jit(solution)/shard_map/ppermute | solution.py:38
  160.5 4.0 %collective-permute-start.18 = (bf16[256,512]{1,0:T(8,128)(2,1)S(1)}, bf16[256,512]{1,0:T(8,128)(2,1)S(1)}, u32[]{:S(2)}, u32[]{:S(2)}) collective-permute-start(bf16[256,512]{1,0:T(8,128)(2,1)S(1)} %fusion), channel_id=1, source_target_pairs={{0,4},{4,0},{8,12},{12,8},{1,5},{5,1},{9,13},{13,9},{2,6},{6,2},{1... | collective-permute-start | bytes 786440 | tf_op jit(solution)/shard_map/ppermute | solution.py:38
  166.0 8.9 %collective-permute-done.18 = bf16[256,512]{1,0:T(8,128)(2,1)S(1)} collective-permute-done((bf16[256,512]{1,0:T(8,128)(2,1)S(1)}, bf16[256,512]{1,0:T(8,128)(2,1)S(1)}, u32[]{:S(2)}, u32[]{:S(2)}) %collective-permute-start.18) | collective-permute-done | bytes 262176 | tf_op jit(solution)/shard_map/ppermute | solution.py:38
  (48 shorter events, 15.2 us)
Async XLA Ops:
  7.2 130.6 %all-gather.3.cloned.1.call-start = ((), (), s32[]{:S(2)}) async-start(), calls=%async_computation | async-start | bytes 6488064 | tf_op jit(solution)/shard_map/all_gather | solution.py:225
  8.0 14.5 %collective-permute-start.12 = (bf16[48,512]{1,0:T(8,128)(2,1)S(1)}, bf16[48,512]{1,0:T(8,128)(2,1)S(1)}, u32[]{:S(2)}, u32[]{:S(2)}) collective-permute-start(bf16[48,512]{1,0:T(8,128)(2,1)S(1)} %get-tuple-element.14), channel_id=1, source_target_pairs={{0,8},{4,12},{8,0},{12,4},{1,9},{5,13},{9,1},{13,5},{2,10},{6,14},... | collective-permute-start | bytes 147464 | tf_op jit(solution)/shard_map/ppermute | solution.py:33
  16.3 6.4 %collective-permute-start.13 = (bf16[48,512]{1,0:T(8,128)(2,1)S(1)}, bf16[48,512]{1,0:T(8,128)(2,1)S(1)}, u32[]{:S(2)}, u32[]{:S(2)}) collective-permute-start(bf16[48,512]{1,0:T(8,128)(2,1)S(1)} %get-tuple-element.15), channel_id=1, source_target_pairs={{0,12},{4,0},{8,4},{12,8},{1,13},{5,1},{9,5},{13,9},{2,14},{6,2},{... | collective-permute-start | bytes 147464 | tf_op jit(solution)/shard_map/ppermute | solution.py:33
  18.3 7.0 %collective-permute-start.11 = (bf16[48,512]{1,0:T(8,128)(2,1)S(1)}, bf16[48,512]{1,0:T(8,128)(2,1)S(1)}, u32[]{:S(2)}, u32[]{:S(2)}) collective-permute-start(bf16[48,512]{1,0:T(8,128)(2,1)S(1)} %get-tuple-element.15), channel_id=1, source_target_pairs={{0,4},{4,8},{8,12},{12,0},{1,5},{5,9},{9,13},{13,1},{2,6},{6,10},{... | collective-permute-start | bytes 147464 | tf_op jit(solution)/shard_map/ppermute | solution.py:33
  27.9 38.2 %copy-start.2 = (bf16[272,512]{1,0:T(8,128)(2,1)}, bf16[272,512]{1,0:T(8,128)(2,1)S(1)}, u32[]{:S(2)}) copy-start(bf16[272,512]{1,0:T(8,128)(2,1)S(1)} %pad_maximum_fusion.refs_1_) | copy-start | bytes 835588
  27.9 7.9 %collective-permute-start = (bf16[272,512]{1,0:T(8,128)(2,1)S(1)}, bf16[272,512]{1,0:T(8,128)(2,1)S(1)}, u32[]{:S(2)}, u32[]{:S(2)}) collective-permute-start(bf16[272,512]{1,0:T(8,128)(2,1)S(1)} %pad_maximum_fusion.refs_1_), channel_id=1, source_target_pairs={{0,4},{4,8},{8,12},{12,16},{16,20},{20,24},{24,28},{28,32},{32,36}... | collective-permute-start | bytes 835592 | tf_op jit(solution)/shard_map/ppermute | solution.py:28
  31.2 15.5 %collective-permute-start.1 = (bf16[256,512]{1,0:T(8,128)(2,1)}, bf16[256,512]{1,0:T(8,128)(2,1)S(1)}, u32[]{:S(2)}, u32[]{:S(2)}) collective-permute-start(bf16[256,512]{1,0:T(8,128)(2,1)} %refs_2_.1), channel_id=1, source_target_pairs={{0,4},{4,8},{8,12},{12,16},{16,20},{20,24},{24,28},{28,32},{32,36}... | collective-permute-start | bytes 786440 | tf_op jit(solution)/shard_map/ppermute | solution.py:28
  35.9 30.2 %copy-start.3 = (bf16[272,512]{1,0:T(8,128)(2,1)}, bf16[272,512]{1,0:T(8,128)(2,1)S(1)}, u32[]{:S(2)}) copy-start(bf16[272,512]{1,0:T(8,128)(2,1)S(1)} %collective-permute-done.refs_3_) | copy-start | bytes 835588
  35.9 30.2 %collective-permute-start.2 = (bf16[272,512]{1,0:T(8,128)(2,1)S(1)}, bf16[272,512]{1,0:T(8,128)(2,1)S(1)}, u32[]{:S(2)}, u32[]{:S(2)}) collective-permute-start(bf16[272,512]{1,0:T(8,128)(2,1)S(1)} %collective-permute-done.refs_3_), channel_id=1, source_target_pairs={{0,4},{4,8},{8,12},{12,16},{16,20},{20,24},{24,28},{28,32},{32,36}... | collective-permute-start | bytes 835592 | tf_op jit(solution)/shard_map/ppermute | solution.py:28
  46.7 19.4 %collective-permute-start.3 = (bf16[256,512]{1,0:T(8,128)(2,1)S(1)}, bf16[256,512]{1,0:T(8,128)(2,1)S(1)}, u32[]{:S(2)}, u32[]{:S(2)}) collective-permute-start(bf16[256,512]{1,0:T(8,128)(2,1)S(1)} %collective-permute-done.1.refs_4_), channel_id=1, source_target_pairs={{0,4},{4,8},{8,12},{12,16},{16,20},{20,24},{24,28},{28,32},{32,36}... | collective-permute-start | bytes 786440 | tf_op jit(solution)/shard_map/ppermute | solution.py:28
  72.0 17.8 %collective-permute-start.7 = (bf16[272,512]{1,0:T(8,128)(2,1)}, bf16[272,512]{1,0:T(8,128)(2,1)S(1)}, u32[]{:S(2)}, u32[]{:S(2)}) collective-permute-start(bf16[272,512]{1,0:T(8,128)(2,1)} %get-tuple-element.9.refs_0_), channel_id=1, source_target_pairs={{0,4},{4,0},{8,12},{12,8},{1,5},{5,1},{9,13},{13,9},{2,6},{6,2},{1... | collective-permute-start | bytes 835592 | tf_op jit(solution)/shard_map/ppermute | solution.py:38
  79.3 25.0 %collective-permute-start.5 = (bf16[272,512]{1,0:T(8,128)(2,1)}, bf16[272,512]{1,0:T(8,128)(2,1)S(1)}, u32[]{:S(2)}, u32[]{:S(2)}) collective-permute-start(bf16[272,512]{1,0:T(8,128)(2,1)} %get-tuple-element.9.refs_0_), channel_id=1, source_target_pairs={{0,2},{2,0},{1,3},{3,1},{4,6},{6,4},{5,7},{7,5},{8,10},{10,8},{9,1... | collective-permute-start | bytes 835592 | tf_op jit(solution)/shard_map/ppermute | solution.py:38
  89.8 16.9 %collective-permute-start.9 = (bf16[272,512]{1,0:T(8,128)(2,1)S(1)}, bf16[272,512]{1,0:T(8,128)(2,1)S(1)}, u32[]{:S(2)}, u32[]{:S(2)}) collective-permute-start(bf16[272,512]{1,0:T(8,128)(2,1)S(1)} %collective-permute-done.7.refs_4_), channel_id=1, source_target_pairs={{0,2},{2,0},{1,3},{3,1},{4,6},{6,4},{5,7},{7,5},{8,10},{10,8},{9,1... | collective-permute-start | bytes 835592 | tf_op jit(solution)/shard_map/ppermute | solution.py:38
  97.2 11.7 %collective-permute-start.4 = (bf16[272,512]{1,0:T(8,128)(2,1)}, bf16[272,512]{1,0:T(8,128)(2,1)S(1)}, u32[]{:S(2)}, u32[]{:S(2)}) collective-permute-start(bf16[272,512]{1,0:T(8,128)(2,1)} %get-tuple-element.9.refs_0_), channel_id=1, source_target_pairs={{0,1},{1,0},{2,3},{3,2},{4,5},{5,4},{6,7},{7,6},{8,9},{9,8},{10,11... | collective-permute-start | bytes 835592 | tf_op jit(solution)/shard_map/ppermute | solution.py:38
  102.3 6.6 %collective-permute-start.8 = (bf16[272,512]{1,0:T(8,128)(2,1)S(1)}, bf16[272,512]{1,0:T(8,128)(2,1)S(1)}, u32[]{:S(2)}, u32[]{:S(2)}) collective-permute-start(bf16[272,512]{1,0:T(8,128)(2,1)S(1)} %collective-permute-done.7.refs_4_), channel_id=1, source_target_pairs={{0,1},{1,0},{2,3},{3,2},{4,5},{5,4},{6,7},{7,6},{8,9},{9,8},{10,11... | collective-permute-start | bytes 835592 | tf_op jit(solution)/shard_map/ppermute | solution.py:38
  104.3 4.7 %collective-permute-start.6 = (bf16[272,512]{1,0:T(8,128)(2,1)S(1)}, bf16[272,512]{1,0:T(8,128)(2,1)S(1)}, u32[]{:S(2)}, u32[]{:S(2)}) collective-permute-start(bf16[272,512]{1,0:T(8,128)(2,1)S(1)} %collective-permute-done.5.refs_2_), channel_id=1, source_target_pairs={{0,1},{1,0},{2,3},{3,2},{4,5},{5,4},{6,7},{7,6},{8,9},{9,8},{10,11... | collective-permute-start | bytes 835592 | tf_op jit(solution)/shard_map/ppermute | solution.py:38
  106.7 3.5 %collective-permute-start.10 = (bf16[272,512]{1,0:T(8,128)(2,1)S(1)}, bf16[272,512]{1,0:T(8,128)(2,1)S(1)}, u32[]{:S(2)}, u32[]{:S(2)}) collective-permute-start(bf16[272,512]{1,0:T(8,128)(2,1)S(1)} %collective-permute-done.9.refs_6_), channel_id=1, source_target_pairs={{0,1},{1,0},{2,3},{3,2},{4,5},{5,4},{6,7},{7,6},{8,9},{9,8},{10,11... | collective-permute-start | bytes 835592 | tf_op jit(solution)/shard_map/ppermute | solution.py:38
  138.7 36.3 %copy-start.1 = (f32[256,512]{1,0:T(8,128)S(1)}, f32[256,512]{1,0:T(8,128)}, u32[]{:S(2)}) copy-start(f32[256,512]{1,0:T(8,128)} %refs_7_.1) | copy-start | bytes 1572868
  138.7 36.3 %copy-start.5 = (bf16[256,512]{1,0:T(8,128)(2,1)S(1)}, bf16[256,512]{1,0:T(8,128)(2,1)}, u32[]{:S(2)}) copy-start(bf16[256,512]{1,0:T(8,128)(2,1)} %get-tuple-element.6) | copy-start | bytes 786436
  146.3 4.8 %collective-permute-start.16 = (bf16[2,256,512]{2,1,0:T(8,128)(2,1)S(1)}, bf16[2,256,512]{2,1,0:T(8,128)(2,1)S(1)}, u32[]{:S(2)}, u32[]{:S(2)}) collective-permute-start(bf16[2,256,512]{2,1,0:T(8,128)(2,1)S(1)} %get-tuple-element.13), channel_id=1, source_target_pairs={{0,1},{1,0},{2,3},{3,2},{4,5},{5,4},{6,7},{7,6},{8,9},{9,8},{10,11... | collective-permute-start | bytes 1572872 | tf_op jit(solution)/shard_map/ppermute | solution.py:38
  149.1 5.1 %collective-permute-start.14 = (bf16[2,256,512]{2,1,0:T(8,128)(2,1)S(1)}, bf16[2,256,512]{2,1,0:T(8,128)(2,1)S(1)}, u32[]{:S(2)}, u32[]{:S(2)}) collective-permute-start(bf16[2,256,512]{2,1,0:T(8,128)(2,1)S(1)} %get-tuple-element.11), channel_id=1, source_target_pairs={{0,1},{1,0},{2,3},{3,2},{4,5},{5,4},{6,7},{7,6},{8,9},{9,8},{10,11... | collective-permute-start | bytes 1572872 | tf_op jit(solution)/shard_map/ppermute | solution.py:38
  151.2 9.3 %collective-permute-start.17 = (bf16[256,512]{1,0:T(8,128)(2,1)S(1)}, bf16[256,512]{1,0:T(8,128)(2,1)S(1)}, u32[]{:S(2)}, u32[]{:S(2)}) collective-permute-start(bf16[256,512]{1,0:T(8,128)(2,1)S(1)} %fusion.4), channel_id=1, source_target_pairs={{0,2},{2,0},{1,3},{3,1},{4,6},{6,4},{5,7},{7,5},{8,10},{10,8},{9,1... | collective-permute-start | bytes 786440 | tf_op jit(solution)/shard_map/ppermute | solution.py:38
  154.4 11.7 %collective-permute-start.15 = (bf16[256,512]{1,0:T(8,128)(2,1)S(1)}, bf16[256,512]{1,0:T(8,128)(2,1)S(1)}, u32[]{:S(2)}, u32[]{:S(2)}) collective-permute-start(bf16[256,512]{1,0:T(8,128)(2,1)S(1)} %fusion.3), channel_id=1, source_target_pairs={{0,2},{2,0},{1,3},{3,1},{4,6},{6,4},{5,7},{7,5},{8,10},{10,8},{9,1... | collective-permute-start | bytes 786440 | tf_op jit(solution)/shard_map/ppermute | solution.py:38
  160.5 14.5 %collective-permute-start.18 = (bf16[256,512]{1,0:T(8,128)(2,1)S(1)}, bf16[256,512]{1,0:T(8,128)(2,1)S(1)}, u32[]{:S(2)}, u32[]{:S(2)}) collective-permute-start(bf16[256,512]{1,0:T(8,128)(2,1)S(1)} %fusion), channel_id=1, source_target_pairs={{0,4},{4,0},{8,12},{12,8},{1,5},{5,1},{9,13},{13,9},{2,6},{6,2},{1... | collective-permute-start | bytes 786440 | tf_op jit(solution)/shard_map/ppermute | solution.py:38
  (4 other events, 21.8 us)
Sparse Core Ops, SparseCore 0:
  26.1 111.5 all-gather.2

commit v5 on v4

--- a/solution.py
+++ b/solution.py
@@ -125,24 +125,33 @@
     )(lengths, gain, q, k0, v0, k1, v1, k2, v2, residual_in)
 
 
-def feed_forward_kernel(place_ref, *refs):
-    parts, w_ref, outs, x_ref, acc_ref = refs[:8], refs[8], refs[9:13], refs[13], refs[14]
+def normalize_kernel(*refs):
+    parts, outs = refs[:8], refs[8:]
+    for g in range(2):
+        square = jnp.zeros((ROWS, 1), F32)
+        for p in range(4):
+            value = parts[4 * g + p][pl.ds(0, ROWS), :].astype(F32)
+            square += jnp.sum(value * value, axis=1, keepdims=True)
+        inverse = lax.rsqrt(square / D + epsilon)
+        for p in range(4):
+            extra = parts[4 * g + p][pl.ds(ROWS, EXTRA), :].astype(F32)
+            gain = extra[0:1] + extra[1:2] + extra[2:3]
+            value = parts[4 * g + p][pl.ds(0, ROWS), :].astype(F32)
+            outs[g][p] = (value * inverse * gain).astype(BF16)
+
+
+def normalize(parts):
+    return pl.pallas_call(
+        normalize_kernel,
+        out_shape=[jax.ShapeDtypeStruct((4, ROWS, TP_WIDTH), BF16)] * 2,
+        compiler_params=pltpu.CompilerParams(vmem_limit_bytes=32 << 20),
+        cost_estimate=pl.CostEstimate(flops=8 * ROWS * D, bytes_accessed=4 << 20, transcendentals=0),
+        name="normalize",
+    )(*parts)
+
+
+def feed_forward_kernel(place_ref, x_ref, w_ref, keep_ref, send_ref, acc_ref):
     step = pl.program_id(0)
-
-    @pl.when(step == 0)
-    def _():
-        for g in range(2):
-            square = jnp.zeros((ROWS, 1), F32)
-            for p in range(4):
-                value = parts[4 * g + p][pl.ds(0, ROWS), :].astype(F32)
-                square += jnp.sum(value * value, axis=1, keepdims=True)
-            inverse = lax.rsqrt(square / D + epsilon)
-            for p in range(4):
-                extra = parts[4 * g + p][pl.ds(ROWS, EXTRA), :].astype(F32)
-                gain = extra[0:1] + extra[1:2] + extra[2:3]
-                value = parts[4 * g + p][pl.ds(0, ROWS), :].astype(F32)
-                x_ref[p, pl.ds(g * ROWS, ROWS), :] = (value * inverse * gain).astype(BF16)
-        acc_ref[...] = jnp.zeros_like(acc_ref)
 
     def block(p, kind):
         pieces = [
@@ -156,49 +165,53 @@
         ]
         return jnp.concatenate(pieces, axis=1).reshape(TP_WIDTH, UNIT_BLOCK)
 
-    gate = jnp.zeros((2 * ROWS, UNIT_BLOCK), F32)
-    up = jnp.zeros((2 * ROWS, UNIT_BLOCK), F32)
+    gate = jnp.zeros((ROWS, UNIT_BLOCK), F32)
+    up = jnp.zeros((ROWS, UNIT_BLOCK), F32)
     for p in range(4):
         gate += jnp.dot(x_ref[p], block(p, 0), preferred_element_type=F32)
         up += jnp.dot(x_ref[p], block(p, 1), preferred_element_type=F32)
     hidden = (gate / (1.0 + jnp.exp(-gate)) * up).astype(BF16)
-    for p in range(4):
-        acc_ref[p] += lax.dot_general(
+
+    def down(p):
+        return lax.dot_general(
             hidden, block(p, 2), (((1,), (1,)), ((), ())), preferred_element_type=F32
         )
 
-    @pl.when(step == pl.num_programs(0) - 1)
+    @pl.when(step == 0)
     def _():
-        for g in range(2):
-            for i, p in enumerate((2, 0)):
-                outs[2 * g][i] = acc_ref[p, pl.ds(g * ROWS, ROWS), :].astype(BF16)
-                outs[2 * g + 1][i] = acc_ref[p + 1, pl.ds(g * ROWS, ROWS), :].astype(BF16)
-
-
-def feed_forward(place, parts, weights):
-    whole = pl.BlockSpec((ROWS + EXTRA, TP_WIDTH), lambda i, o: (0, 0))
+        for p in range(4):
+            acc_ref[p] = down(p)
+
+    @pl.when(step == 1)
+    def _():
+        for i, p in enumerate((2, 0)):
+            send_ref[i] = (acc_ref[p + 1] + down(p + 1)).astype(BF16)
+            keep_ref[i] = (acc_ref[p] + down(p)).astype(BF16)
+
+
+def feed_forward(place, x, weights):
     pair = pl.BlockSpec((2, ROWS, TP_WIDTH), lambda i, o: (0, 0, 0))
     units = weights.shape[3]
+    assert units == 2 * UNIT_BLOCK
     return pl.pallas_call(
         feed_forward_kernel,
-        out_shape=[jax.ShapeDtypeStruct((2, ROWS, TP_WIDTH), BF16)] * 4,
+        out_shape=[jax.ShapeDtypeStruct((2, ROWS, TP_WIDTH), BF16)] * 2,
         grid_spec=pltpu.PrefetchScalarGridSpec(
             num_scalar_prefetch=1,
-            grid=(units // UNIT_BLOCK,),
-            in_specs=[whole] * 8
-            + [pl.BlockSpec((32, 4, 48, UNIT_BLOCK), lambda i, o: (0, 0, 0, i))],
-            out_specs=[pair] * 4,
-            scratch_shapes=[
-                pltpu.VMEM((4, 2 * ROWS, TP_WIDTH), BF16),
-                pltpu.VMEM((4, 2 * ROWS, TP_WIDTH), F32),
+            grid=(2,),
+            in_specs=[
+                pl.BlockSpec((4, ROWS, TP_WIDTH), lambda i, o: (0, 0, 0)),
+                pl.BlockSpec((32, 4, 48, UNIT_BLOCK), lambda i, o: (0, 0, 0, i)),
             ],
-        ),
-        compiler_params=pltpu.CompilerParams(vmem_limit_bytes=48 << 20),
+            out_specs=[pair] * 2,
+            scratch_shapes=[pltpu.VMEM((4, ROWS, TP_WIDTH), F32)],
+        ),
+        compiler_params=pltpu.CompilerParams(vmem_limit_bytes=58 << 20),
         cost_estimate=pl.CostEstimate(
-            flops=12 * ROWS * D * units, bytes_accessed=10 << 20, transcendentals=2 * ROWS * units
+            flops=6 * ROWS * D * units, bytes_accessed=8 << 20, transcendentals=ROWS * units
         ),
         name="feed_forward",
-    )(place, *parts, weights)
+    )(place, x, weights)
 
 
 def on_device(
@@ -243,7 +256,10 @@
     own = 2 * lax.axis_index("yl") + lax.axis_index("c")
     place = [own, own ^ 1, own ^ 2, own ^ 3] + [(yh - y) & 3 for y in range(4)]
     place = jnp.stack(place).astype(jnp.int32)
-    own_keep, own_send, partner_keep, partner_send = feed_forward(place, parts, weights)
+    own_x, partner_x = normalize(parts)
+    partner_keep, partner_send = feed_forward(place, partner_x, weights)
+    own_x, partner_send = lax.optimization_barrier((own_x, partner_send))
+    own_keep, own_send = feed_forward(place, own_x, weights)
 
     def add(left, right):
         return left.astype(F32) + right.astype(F32)

time: 185 us -> 191 us (1.032)
  starting transfers between devices: 82.1 us -> 65.6 us
  waiting for transfers between devices: 67.3 us -> 80.1 us
  Pallas kernels: 12.6 us -> 18.7 us
  local copies, waits for them, and re-layouts: 2.01 us -> 4.57 us
    ppermute x12, starting transfers between devices: 50.9 us -> 34 us  [swap(): return lax.ppermute(value, axis, [(i, i ^ 1) for i in range(size)])]
    ppermute x4, waiting for transfers between devices: 21.4 us -> 30.9 us  [from_behind(): return lax.ppermute(value, SEQ, [(i, i + by) for i in range(size - by)])]
    ppermute x12, waiting for transfers between devices: 15.5 us -> 23.3 us  [swap(): return lax.ppermute(value, axis, [(i, i ^ 1) for i in range(size)])]
    pallas_call x1 -> x2, Pallas kernels: 7.54 us -> 12.7 us  [feed_forward(): pl.pallas_call(feed_forward_kernel, out_shape=[jax.ShapeDtypeStruct((2, R...]
    all_gather x1, waiting for transfers between devices: 27.6 us -> 23.1 us  [on_device(): weights = lax.all_gather(near, ('x', 'z'), axis=0)]
    unnamed x16 -> x22, local copies, waits for them, and re-layouts: 1.75 us -> 3.78 us
  transfers between devices with their start and end apart: 20 -> 20, of which waited for: 9 -> 10; matrix products, arithmetic and copies ran while one was open for 1% -> 2% of each run, Pallas kernels for 3% -> 7%
where the time goes in v5:
time: 191 us; the launch traced here: 190 us
  waiting for transfers between devices  80.1 us (42%)
  starting transfers between devices  65.6 us (34%)
  Pallas kernels  18.7 us (10%)
  between operations  14.4 us (8%)
  other arithmetic  6.35 us (3%)
  local copies, waits for them, and re-layouts  4.57 us (2%)
    ppermute x12, starting transfers between devices, swap(): return lax.ppermute(value, axis, [(i, i ^ 1) for i in range(size)])  34 us
    ppermute x4, waiting for transfers between devices, from_behind(): return lax.ppermute(value, SEQ, [(i, i + by) for i in range(size - by)])  30.9 us
    ppermute x12, waiting for transfers between devices, swap(): return lax.ppermute(value, axis, [(i, i ^ 1) for i in range(size)])  23.3 us
    all_gather x1, waiting for transfers between devices, on_device(): weights = lax.all_gather(near, ('x', 'z'), axis=0)  23.1 us
    ppermute x4, starting transfers between devices, from_behind(): return lax.ppermute(value, SEQ, [(i, i + by) for i in range(size - by)])  17.1 us
    ppermute x3, starting transfers between devices, around(): lax.ppermute(value, axis, [(i, (i + by) % size) for i in range(size)])  14.5 us
    pallas_call x2, Pallas kernels, feed_forward(): pl.pallas_call(feed_forward_kernel, out_shape=[jax.ShapeDtypeStruct((2, R...  12.7 us
    pallas_call x1, Pallas kernels, attention(): pl.pallas_call(attention_kernel, out_shape=(jax.ShapeDtypeStruct((ROWS, T...  5.05 us
  transfers between devices with their start and end apart: 20, of which 10 were waited for; matrix products, arithmetic and copies ran while one was open for 2% of the time, Pallas kernels for 7%

profile of v5, /device:TPU:1, one launch (start us, length us, event | category | flops | bytes accessed | tf_op | source)
XLA Modules:
  0.0 189.6 jit_solution(14328977254144642292)
XLA Ops:
  8.0 6.7 %collective-permute-start.13 = (bf16[48,512]{1,0:T(8,128)(2,1)S(1)}, bf16[48,512]{1,0:T(8,128)(2,1)S(1)}, u32[]{:S(2)}, u32[]{:S(2)}) collective-permute-start(bf16[48,512]{1,0:T(8,128)(2,1)S(1)} %get-tuple-element.23), channel_id=1, source_target_pairs={{0,12},{4,0},{8,4},{12,8},{1,13},{5,1},{9,5},{13,9},{2,14},{6,2},{... | collective-permute-start | bytes 147464 | tf_op jit(solution)/shard_map/ppermute | solution.py:33
  14.7 3.5 %collective-permute-start.12 = (bf16[48,512]{1,0:T(8,128)(2,1)S(1)}, bf16[48,512]{1,0:T(8,128)(2,1)S(1)}, u32[]{:S(2)}, u32[]{:S(2)}) collective-permute-start(bf16[48,512]{1,0:T(8,128)(2,1)S(1)} %get-tuple-element.22), channel_id=1, source_target_pairs={{0,8},{4,12},{8,0},{12,4},{1,9},{5,13},{9,1},{13,5},{2,10},{6,14},... | collective-permute-start | bytes 147464 | tf_op jit(solution)/shard_map/ppermute | solution.py:33
  18.3 4.2 %collective-permute-start.11 = (bf16[48,512]{1,0:T(8,128)(2,1)S(1)}, bf16[48,512]{1,0:T(8,128)(2,1)S(1)}, u32[]{:S(2)}, u32[]{:S(2)}) collective-permute-start(bf16[48,512]{1,0:T(8,128)(2,1)S(1)} %get-tuple-element.23), channel_id=1, source_target_pairs={{0,4},{4,8},{8,12},{12,0},{1,5},{5,9},{9,13},{13,1},{2,6},{6,10},{... | collective-permute-start | bytes 147464 | tf_op jit(solution)/shard_map/ppermute | solution.py:33
  27.9 3.0 %collective-permute-start = (bf16[272,512]{1,0:T(8,128)(2,1)S(1)}, bf16[272,512]{1,0:T(8,128)(2,1)S(1)}, u32[]{:S(2)}, u32[]{:S(2)}) collective-permute-start(bf16[272,512]{1,0:T(8,128)(2,1)S(1)} %pad_maximum_fusion.refs_1_), channel_id=1, source_target_pairs={{0,4},{4,8},{8,12},{12,16},{16,20},{20,24},{24,28},{28,32},{32,36}... | collective-permute-start | bytes 835592 | tf_op jit(solution)/shard_map/ppermute | solution.py:28
  30.9 4.9 %collective-permute-start.1 = (bf16[256,512]{1,0:T(8,128)(2,1)}, bf16[256,512]{1,0:T(8,128)(2,1)S(1)}, u32[]{:S(2)}, u32[]{:S(2)}) collective-permute-start(bf16[256,512]{1,0:T(8,128)(2,1)} %refs_2_.1), channel_id=1, source_target_pairs={{0,4},{4,8},{8,12},{12,16},{16,20},{20,24},{24,28},{28,32},{32,36}... | collective-permute-start | bytes 786440 | tf_op jit(solution)/shard_map/ppermute | solution.py:28
  35.9 4.2 %collective-permute-start.2 = (bf16[272,512]{1,0:T(8,128)(2,1)S(1)}, bf16[272,512]{1,0:T(8,128)(2,1)S(1)}, u32[]{:S(2)}, u32[]{:S(2)}) collective-permute-start(bf16[272,512]{1,0:T(8,128)(2,1)S(1)} %collective-permute-done.refs_3_), channel_id=1, source_target_pairs={{0,4},{4,8},{8,12},{12,16},{16,20},{20,24},{24,28},{28,32},{32,36}... | collective-permute-start | bytes 835592 | tf_op jit(solution)/shard_map/ppermute | solution.py:28
  40.1 10.6 %collective-permute-done.1.refs_4_ = bf16[256,512]{1,0:T(8,128)(2,1)S(1)} collective-permute-done((bf16[256,512]{1,0:T(8,128)(2,1)}, bf16[256,512]{1,0:T(8,128)(2,1)S(1)}, u32[]{:S(2)}, u32[]{:S(2)}) %collective-permute-start.1) | collective-permute-done | bytes 262176 | tf_op jit(solution)/shard_map/ppermute | solution.py:28
  50.7 5.0 %collective-permute-start.3 = (bf16[256,512]{1,0:T(8,128)(2,1)S(1)}, bf16[256,512]{1,0:T(8,128)(2,1)S(1)}, u32[]{:S(2)}, u32[]{:S(2)}) collective-permute-start(bf16[256,512]{1,0:T(8,128)(2,1)S(1)} %collective-permute-done.1.refs_4_), channel_id=1, source_target_pairs={{0,4},{4,8},{8,12},{12,16},{16,20},{20,24},{24,28},{28,32},{32,36}... | collective-permute-start | bytes 786440 | tf_op jit(solution)/shard_map/ppermute | solution.py:28
  55.7 20.3 %collective-permute-done.3.refs_6_ = bf16[256,512]{1,0:T(8,128)(2,1)S(1)} collective-permute-done((bf16[256,512]{1,0:T(8,128)(2,1)S(1)}, bf16[256,512]{1,0:T(8,128)(2,1)S(1)}, u32[]{:S(2)}, u32[]{:S(2)}) %collective-permute-start.3) | collective-permute-done | bytes 262176 | tf_op jit(solution)/shard_map/ppermute | solution.py:28
  76.8 5.1 %attention.1 = (bf16[256,512]{1,0:T(8,128)(2,1)}, bf16[272,512]{1,0:T(8,128)(2,1)}) custom-call(s32[2]{0:T(128)} %lengths_ref.1, f32[1,512]{1,0:T(1,128)} %bitcast.36, bf16[256,512]{1,0:T(8,128)(2,1)} %refs_0_.1, bf16[272,512]{1,0:T(8,128)(2,1)} %copy-done.4, bf16[256,512]{1,0:T(8,128)(2,1)} %refs_2_.1, bf16[272,512]{1,0:T(8,128)(2,1)} %copy-done.6, ...), custom_call_target="tpu_custom_call" | custom-call | flops 402653184 | bytes 3145728 | tf_op jit(solution)/shard_map/attention/pallas_call | solution.py:108
  81.9 5.0 %collective-permute-start.7 = (bf16[272,512]{1,0:T(8,128)(2,1)}, bf16[272,512]{1,0:T(8,128)(2,1)S(1)}, u32[]{:S(2)}, u32[]{:S(2)}) collective-permute-start(bf16[272,512]{1,0:T(8,128)(2,1)} %get-tuple-element.13.refs_0_), channel_id=1, source_target_pairs={{0,4},{4,0},{8,12},{12,8},{1,5},{5,1},{9,13},{13,9},{2,6},{6,2},{1... | collective-permute-start | bytes 835592 | tf_op jit(solution)/shard_map/ppermute | solution.py:38
  88.8 9.4 %collective-permute-done.7.refs_4_ = bf16[272,512]{1,0:T(8,128)(2,1)S(1)} collective-permute-done((bf16[272,512]{1,0:T(8,128)(2,1)}, bf16[272,512]{1,0:T(8,128)(2,1)S(1)}, u32[]{:S(2)}, u32[]{:S(2)}) %collective-permute-start.7) | collective-permute-done | bytes 278560 | tf_op jit(solution)/shard_map/ppermute | solution.py:38
  100.1 3.0 %collective-permute-start.4 = (bf16[272,512]{1,0:T(8,128)(2,1)}, bf16[272,512]{1,0:T(8,128)(2,1)S(1)}, u32[]{:S(2)}, u32[]{:S(2)}) collective-permute-start(bf16[272,512]{1,0:T(8,128)(2,1)} %get-tuple-element.13.refs_0_), channel_id=1, source_target_pairs={{0,1},{1,0},{2,3},{3,2},{4,5},{5,4},{6,7},{7,6},{8,9},{9,8},{10,11... | collective-permute-start | bytes 835592 | tf_op jit(solution)/shard_map/ppermute | solution.py:38
  105.1 2.4 %collective-permute-start.6 = (bf16[272,512]{1,0:T(8,128)(2,1)S(1)}, bf16[272,512]{1,0:T(8,128)(2,1)S(1)}, u32[]{:S(2)}, u32[]{:S(2)}) collective-permute-start(bf16[272,512]{1,0:T(8,128)(2,1)S(1)} %collective-permute-done.5.refs_2_), channel_id=1, source_target_pairs={{0,1},{1,0},{2,3},{3,2},{4,5},{5,4},{6,7},{7,6},{8,9},{9,8},{10,11... | collective-permute-start | bytes 835592 | tf_op jit(solution)/shard_map/ppermute | solution.py:38
  107.5 3.6 %collective-permute-start.10 = (bf16[272,512]{1,0:T(8,128)(2,1)S(1)}, bf16[272,512]{1,0:T(8,128)(2,1)S(1)}, u32[]{:S(2)}, u32[]{:S(2)}) collective-permute-start(bf16[272,512]{1,0:T(8,128)(2,1)S(1)} %collective-permute-done.9.refs_6_), channel_id=1, source_target_pairs={{0,1},{1,0},{2,3},{3,2},{4,5},{5,4},{6,7},{7,6},{8,9},{9,8},{10,11... | collective-permute-start | bytes 835592 | tf_op jit(solution)/shard_map/ppermute | solution.py:38
  116.2 23.1 %all-gather.3.cloned.1.call-done = bf16[128,48,512]{2,1,0:T(8,128)(2,1)} async-done(((bf16[4,48,512]{2,1,0:T(8,128)(2,1)}), bf16[128,48,512]{2,1,0:T(8,128)(2,1)}) %all-gather.3.cloned.1.call-update) | async-done | bytes 6291472 | tf_op jit(solution)/shard_map/all_gather | solution.py:238
  139.3 6.3 %feed_forward.2 = (bf16[2,256,512]{2,1,0:T(8,128)(2,1)}, bf16[2,256,512]{2,1,0:T(8,128)(2,1)}) custom-call(s32[8]{0:T(128)} %stack.50.place_ref, bf16[4,256,512]{2,1,0:T(8,128)(2,1)} %copy-done.1, bf16[32,4,48,512]{3,2,1,0:T(8,128)(2,1)} %bitcast.29), custom_call_target="tpu_custom_call" | custom-call | flops 1610612736 | bytes 8388608 | tf_op jit(solution)/shard_map/feed_forward/pallas_call | solution.py:196
  145.6 3.0 %collective-permute-start.16 = (bf16[2,256,512]{2,1,0:T(8,128)(2,1)}, bf16[2,256,512]{2,1,0:T(8,128)(2,1)S(1)}, u32[]{:S(2)}, u32[]{:S(2)}) collective-permute-start(bf16[2,256,512]{2,1,0:T(8,128)(2,1)} %get-tuple-element.21), channel_id=1, source_target_pairs={{0,1},{1,0},{2,3},{3,2},{4,5},{5,4},{6,7},{7,6},{8,9},{9,8},{10,11... | collective-permute-start | bytes 1572872 | tf_op jit(solution)/shard_map/ppermute | solution.py:38
  148.6 6.4 %feed_forward.3 = (bf16[2,256,512]{2,1,0:T(8,128)(2,1)}, bf16[2,256,512]{2,1,0:T(8,128)(2,1)}) custom-call(s32[8]{0:T(128)} %stack.50.place_ref, bf16[4,256,512]{2,1,0:T(8,128)(2,1)} %copy-done, bf16[32,4,48,512]{3,2,1,0:T(8,128)(2,1)} %bitcast.30), custom_call_target="tpu_custom_call" | custom-call | flops 1610612736 | bytes 8388608 | tf_op jit(solution)/shard_map/feed_forward/pallas_call | solution.py:196
  157.0 3.1 %collective-permute-start.17 = (bf16[256,512]{1,0:T(8,128)(2,1)S(1)}, bf16[256,512]{1,0:T(8,128)(2,1)S(1)}, u32[]{:S(2)}, u32[]{:S(2)}) collective-permute-start(bf16[256,512]{1,0:T(8,128)(2,1)S(1)} %fusion.4), channel_id=1, source_target_pairs={{0,2},{2,0},{1,3},{3,1},{4,6},{6,4},{5,7},{7,5},{8,10},{10,8},{9,1... | collective-permute-start | bytes 786440 | tf_op jit(solution)/shard_map/ppermute | solution.py:38
  161.1 2.2 %collective-permute-start.15 = (bf16[256,512]{1,0:T(8,128)(2,1)S(1)}, bf16[256,512]{1,0:T(8,128)(2,1)S(1)}, u32[]{:S(2)}, u32[]{:S(2)}) collective-permute-start(bf16[256,512]{1,0:T(8,128)(2,1)S(1)} %fusion.3), channel_id=1, source_target_pairs={{0,2},{2,0},{1,3},{3,1},{4,6},{6,4},{5,7},{7,5},{8,10},{10,8},{9,1... | collective-permute-start | bytes 786440 | tf_op jit(solution)/shard_map/ppermute | solution.py:38
  163.3 2.9 %collective-permute-done.17 = bf16[256,512]{1,0:T(8,128)(2,1)S(1)} collective-permute-done((bf16[256,512]{1,0:T(8,128)(2,1)S(1)}, bf16[256,512]{1,0:T(8,128)(2,1)S(1)}, u32[]{:S(2)}, u32[]{:S(2)}) %collective-permute-start.17) | collective-permute-done | bytes 262176 | tf_op jit(solution)/shard_map/ppermute | solution.py:38
  166.3 4.0 %collective-permute-start.18 = (bf16[256,512]{1,0:T(8,128)(2,1)S(1)}, bf16[256,512]{1,0:T(8,128)(2,1)S(1)}, u32[]{:S(2)}, u32[]{:S(2)}) collective-permute-start(bf16[256,512]{1,0:T(8,128)(2,1)S(1)} %fusion), channel_id=1, source_target_pairs={{0,4},{4,0},{8,12},{12,8},{1,5},{5,1},{9,13},{13,9},{2,6},{6,2},{1... | collective-permute-start | bytes 786440 | tf_op jit(solution)/shard_map/ppermute | solution.py:38
  171.9 8.9 %collective-permute-done.18 = bf16[256,512]{1,0:T(8,128)(2,1)S(1)} collective-permute-done((bf16[256,512]{1,0:T(8,128)(2,1)S(1)}, bf16[256,512]{1,0:T(8,128)(2,1)S(1)}, u32[]{:S(2)}, u32[]{:S(2)}) %collective-permute-start.18) | collective-permute-done | bytes 262176 | tf_op jit(solution)/shard_map/ppermute | solution.py:38
  (56 shorter events, 24.4 us)
Async XLA Ops:
  7.2 132.1 %all-gather.3.cloned.1.call-start = ((), (), s32[]{:S(2)}) async-start(), calls=%async_computation | async-start | bytes 6488064 | tf_op jit(solution)/shard_map/all_gather | solution.py:238
  8.0 14.5 %collective-permute-start.13 = (bf16[48,512]{1,0:T(8,128)(2,1)S(1)}, bf16[48,512]{1,0:T(8,128)(2,1)S(1)}, u32[]{:S(2)}, u32[]{:S(2)}) collective-permute-start(bf16[48,512]{1,0:T(8,128)(2,1)S(1)} %get-tuple-element.23), channel_id=1, source_target_pairs={{0,12},{4,0},{8,4},{12,8},{1,13},{5,1},{9,5},{13,9},{2,14},{6,2},{... | collective-permute-start | bytes 147464 | tf_op jit(solution)/shard_map/ppermute | solution.py:33
  14.7 8.7 %collective-permute-start.12 = (bf16[48,512]{1,0:T(8,128)(2,1)S(1)}, bf16[48,512]{1,0:T(8,128)(2,1)S(1)}, u32[]{:S(2)}, u32[]{:S(2)}) collective-permute-start(bf16[48,512]{1,0:T(8,128)(2,1)S(1)} %get-tuple-element.22), channel_id=1, source_target_pairs={{0,8},{4,12},{8,0},{12,4},{1,9},{5,13},{9,1},{13,5},{2,10},{6,14},... | collective-permute-start | bytes 147464 | tf_op jit(solution)/shard_map/ppermute | solution.py:33
  18.3 7.0 %collective-permute-start.11 = (bf16[48,512]{1,0:T(8,128)(2,1)S(1)}, bf16[48,512]{1,0:T(8,128)(2,1)S(1)}, u32[]{:S(2)}, u32[]{:S(2)}) collective-permute-start(bf16[48,512]{1,0:T(8,128)(2,1)S(1)} %get-tuple-element.23), channel_id=1, source_target_pairs={{0,4},{4,8},{8,12},{12,0},{1,5},{5,9},{9,13},{13,1},{2,6},{6,10},{... | collective-permute-start | bytes 147464 | tf_op jit(solution)/shard_map/ppermute | solution.py:33
  27.9 48.1 %copy-start.4 = (bf16[272,512]{1,0:T(8,128)(2,1)}, bf16[272,512]{1,0:T(8,128)(2,1)S(1)}, u32[]{:S(2)}) copy-start(bf16[272,512]{1,0:T(8,128)(2,1)S(1)} %pad_maximum_fusion.refs_1_) | copy-start | bytes 835588
  27.9 7.9 %collective-permute-start = (bf16[272,512]{1,0:T(8,128)(2,1)S(1)}, bf16[272,512]{1,0:T(8,128)(2,1)S(1)}, u32[]{:S(2)}, u32[]{:S(2)}) collective-permute-start(bf16[272,512]{1,0:T(8,128)(2,1)S(1)} %pad_maximum_fusion.refs_1_), channel_id=1, source_target_pairs={{0,4},{4,8},{8,12},{12,16},{16,20},{20,24},{24,28},{28,32},{32,36}... | collective-permute-start | bytes 835592 | tf_op jit(solution)/shard_map/ppermute | solution.py:28
  30.9 19.7 %collective-permute-start.1 = (bf16[256,512]{1,0:T(8,128)(2,1)}, bf16[256,512]{1,0:T(8,128)(2,1)S(1)}, u32[]{:S(2)}, u32[]{:S(2)}) collective-permute-start(bf16[256,512]{1,0:T(8,128)(2,1)} %refs_2_.1), channel_id=1, source_target_pairs={{0,4},{4,8},{8,12},{12,16},{16,20},{20,24},{24,28},{28,32},{32,36}... | collective-permute-start | bytes 786440 | tf_op jit(solution)/shard_map/ppermute | solution.py:28
  35.9 40.2 %copy-start.6 = (bf16[272,512]{1,0:T(8,128)(2,1)}, bf16[272,512]{1,0:T(8,128)(2,1)S(1)}, u32[]{:S(2)}) copy-start(bf16[272,512]{1,0:T(8,128)(2,1)S(1)} %collective-permute-done.refs_3_) | copy-start | bytes 835588
  35.9 40.1 %collective-permute-start.2 = (bf16[272,512]{1,0:T(8,128)(2,1)S(1)}, bf16[272,512]{1,0:T(8,128)(2,1)S(1)}, u32[]{:S(2)}, u32[]{:S(2)}) collective-permute-start(bf16[272,512]{1,0:T(8,128)(2,1)S(1)} %collective-permute-done.refs_3_), channel_id=1, source_target_pairs={{0,4},{4,8},{8,12},{12,16},{16,20},{20,24},{24,28},{28,32},{32,36}... | collective-permute-start | bytes 835592 | tf_op jit(solution)/shard_map/ppermute | solution.py:28
  50.7 25.4 %collective-permute-start.3 = (bf16[256,512]{1,0:T(8,128)(2,1)S(1)}, bf16[256,512]{1,0:T(8,128)(2,1)S(1)}, u32[]{:S(2)}, u32[]{:S(2)}) collective-permute-start(bf16[256,512]{1,0:T(8,128)(2,1)S(1)} %collective-permute-done.1.refs_4_), channel_id=1, source_target_pairs={{0,4},{4,8},{8,12},{12,16},{16,20},{20,24},{24,28},{28,32},{32,36}... | collective-permute-start | bytes 786440 | tf_op jit(solution)/shard_map/ppermute | solution.py:28
  81.9 16.3 %collective-permute-start.7 = (bf16[272,512]{1,0:T(8,128)(2,1)}, bf16[272,512]{1,0:T(8,128)(2,1)S(1)}, u32[]{:S(2)}, u32[]{:S(2)}) collective-permute-start(bf16[272,512]{1,0:T(8,128)(2,1)} %get-tuple-element.13.refs_0_), channel_id=1, source_target_pairs={{0,4},{4,0},{8,12},{12,8},{1,5},{5,1},{9,13},{13,9},{2,6},{6,2},{1... | collective-permute-start | bytes 835592 | tf_op jit(solution)/shard_map/ppermute | solution.py:38
  86.9 18.2 %collective-permute-start.5 = (bf16[272,512]{1,0:T(8,128)(2,1)}, bf16[272,512]{1,0:T(8,128)(2,1)S(1)}, u32[]{:S(2)}, u32[]{:S(2)}) collective-permute-start(bf16[272,512]{1,0:T(8,128)(2,1)} %get-tuple-element.13.refs_0_), channel_id=1, source_target_pairs={{0,2},{2,0},{1,3},{3,1},{4,6},{6,4},{5,7},{7,5},{8,10},{10,8},{9,1... | collective-permute-start | bytes 835592 | tf_op jit(solution)/shard_map/ppermute | solution.py:38
  98.2 9.3 %collective-permute-start.9 = (bf16[272,512]{1,0:T(8,128)(2,1)S(1)}, bf16[272,512]{1,0:T(8,128)(2,1)S(1)}, u32[]{:S(2)}, u32[]{:S(2)}) collective-permute-start(bf16[272,512]{1,0:T(8,128)(2,1)S(1)} %collective-permute-done.7.refs_4_), channel_id=1, source_target_pairs={{0,2},{2,0},{1,3},{3,1},{4,6},{6,4},{5,7},{7,5},{8,10},{10,8},{9,1... | collective-permute-start | bytes 835592 | tf_op jit(solution)/shard_map/ppermute | solution.py:38
  100.1 11.6 %collective-permute-start.4 = (bf16[272,512]{1,0:T(8,128)(2,1)}, bf16[272,512]{1,0:T(8,128)(2,1)S(1)}, u32[]{:S(2)}, u32[]{:S(2)}) collective-permute-start(bf16[272,512]{1,0:T(8,128)(2,1)} %get-tuple-element.13.refs_0_), channel_id=1, source_target_pairs={{0,1},{1,0},{2,3},{3,2},{4,5},{5,4},{6,7},{7,6},{8,9},{9,8},{10,11... | collective-permute-start | bytes 835592 | tf_op jit(solution)/shard_map/ppermute | solution.py:38
  103.2 8.6 %collective-permute-start.8 = (bf16[272,512]{1,0:T(8,128)(2,1)S(1)}, bf16[272,512]{1,0:T(8,128)(2,1)S(1)}, u32[]{:S(2)}, u32[]{:S(2)}) collective-permute-start(bf16[272,512]{1,0:T(8,128)(2,1)S(1)} %collective-permute-done.7.refs_4_), channel_id=1, source_target_pairs={{0,1},{1,0},{2,3},{3,2},{4,5},{5,4},{6,7},{7,6},{8,9},{9,8},{10,11... | collective-permute-start | bytes 835592 | tf_op jit(solution)/shard_map/ppermute | solution.py:38
  105.1 6.6 %collective-permute-start.6 = (bf16[272,512]{1,0:T(8,128)(2,1)S(1)}, bf16[272,512]{1,0:T(8,128)(2,1)S(1)}, u32[]{:S(2)}, u32[]{:S(2)}) collective-permute-start(bf16[272,512]{1,0:T(8,128)(2,1)S(1)} %collective-permute-done.5.refs_2_), channel_id=1, source_target_pairs={{0,1},{1,0},{2,3},{3,2},{4,5},{5,4},{6,7},{7,6},{8,9},{9,8},{10,11... | collective-permute-start | bytes 835592 | tf_op jit(solution)/shard_map/ppermute | solution.py:38
  107.5 4.7 %collective-permute-start.10 = (bf16[272,512]{1,0:T(8,128)(2,1)S(1)}, bf16[272,512]{1,0:T(8,128)(2,1)S(1)}, u32[]{:S(2)}, u32[]{:S(2)}) collective-permute-start(bf16[272,512]{1,0:T(8,128)(2,1)S(1)} %collective-permute-done.9.refs_6_), channel_id=1, source_target_pairs={{0,1},{1,0},{2,3},{3,2},{4,5},{5,4},{6,7},{7,6},{8,9},{9,8},{10,11... | collective-permute-start | bytes 835592 | tf_op jit(solution)/shard_map/ppermute | solution.py:38
  145.6 35.2 %copy-start.3 = (f32[256,512]{1,0:T(8,128)S(1)}, f32[256,512]{1,0:T(8,128)}, u32[]{:S(2)}) copy-start(f32[256,512]{1,0:T(8,128)} %refs_7_.1) | copy-start | bytes 1572868
  145.6 35.2 %copy-start.8 = (bf16[256,512]{1,0:T(8,128)(2,1)S(1)}, bf16[256,512]{1,0:T(8,128)(2,1)}, u32[]{:S(2)}) copy-start(bf16[256,512]{1,0:T(8,128)(2,1)} %get-tuple-element.10) | copy-start | bytes 786436
  145.6 11.3 %collective-permute-start.16 = (bf16[2,256,512]{2,1,0:T(8,128)(2,1)}, bf16[2,256,512]{2,1,0:T(8,128)(2,1)S(1)}, u32[]{:S(2)}, u32[]{:S(2)}) collective-permute-start(bf16[2,256,512]{2,1,0:T(8,128)(2,1)} %get-tuple-element.21), channel_id=1, source_target_pairs={{0,1},{1,0},{2,3},{3,2},{4,5},{5,4},{6,7},{7,6},{8,9},{9,8},{10,11... | collective-permute-start | bytes 1572872 | tf_op jit(solution)/shard_map/ppermute | solution.py:38
  154.9 5.1 %collective-permute-start.14 = (bf16[2,256,512]{2,1,0:T(8,128)(2,1)}, bf16[2,256,512]{2,1,0:T(8,128)(2,1)S(1)}, u32[]{:S(2)}, u32[]{:S(2)}) collective-permute-start(bf16[2,256,512]{2,1,0:T(8,128)(2,1)} %get-tuple-element.19), channel_id=1, source_target_pairs={{0,1},{1,0},{2,3},{3,2},{4,5},{5,4},{6,7},{7,6},{8,9},{9,8},{10,11... | collective-permute-start | bytes 1572872 | tf_op jit(solution)/shard_map/ppermute | solution.py:38
  157.0 9.3 %collective-permute-start.17 = (bf16[256,512]{1,0:T(8,128)(2,1)S(1)}, bf16[256,512]{1,0:T(8,128)(2,1)S(1)}, u32[]{:S(2)}, u32[]{:S(2)}) collective-permute-start(bf16[256,512]{1,0:T(8,128)(2,1)S(1)} %fusion.4), channel_id=1, source_target_pairs={{0,2},{2,0},{1,3},{3,1},{4,6},{6,4},{5,7},{7,5},{8,10},{10,8},{9,1... | collective-permute-start | bytes 786440 | tf_op jit(solution)/shard_map/ppermute | solution.py:38
  161.1 10.7 %collective-permute-start.15 = (bf16[256,512]{1,0:T(8,128)(2,1)S(1)}, bf16[256,512]{1,0:T(8,128)(2,1)S(1)}, u32[]{:S(2)}, u32[]{:S(2)}) collective-permute-start(bf16[256,512]{1,0:T(8,128)(2,1)S(1)} %fusion.3), channel_id=1, source_target_pairs={{0,2},{2,0},{1,3},{3,1},{4,6},{6,4},{5,7},{7,5},{8,10},{10,8},{9,1... | collective-permute-start | bytes 786440 | tf_op jit(solution)/shard_map/ppermute | solution.py:38
  166.3 14.5 %collective-permute-start.18 = (bf16[256,512]{1,0:T(8,128)(2,1)S(1)}, bf16[256,512]{1,0:T(8,128)(2,1)S(1)}, u32[]{:S(2)}, u32[]{:S(2)}) collective-permute-start(bf16[256,512]{1,0:T(8,128)(2,1)S(1)} %fusion), channel_id=1, source_target_pairs={{0,4},{4,0},{8,12},{12,8},{1,5},{5,1},{9,13},{13,9},{2,6},{6,2},{1... | collective-permute-start | bytes 786440 | tf_op jit(solution)/shard_map/ppermute | solution.py:38
  (7 other events, 41.2 us)
Sparse Core Ops, SparseCore 0:
  26.1 113.0 all-gather.2

commit v6 on v5

--- a/solution.py
+++ b/solution.py
@@ -17,7 +17,7 @@
 EXTRA = 16
 epsilon = 1e-06
 
-SEQ = ("x", "z", "yh")
+SEQ = ("xh", "xl", "z", "yh")
 TP = ("yl", "c")
 F32 = jnp.float32
 BF16 = jnp.bfloat16
@@ -126,7 +126,7 @@
 
 
 def normalize_kernel(*refs):
-    parts, outs = refs[:8], refs[8:]
+    parts, out = refs[:8], refs[8]
     for g in range(2):
         square = jnp.zeros((ROWS, 1), F32)
         for p in range(4):
@@ -137,78 +137,88 @@
             extra = parts[4 * g + p][pl.ds(ROWS, EXTRA), :].astype(F32)
             gain = extra[0:1] + extra[1:2] + extra[2:3]
             value = parts[4 * g + p][pl.ds(0, ROWS), :].astype(F32)
-            outs[g][p] = (value * inverse * gain).astype(BF16)
+            out[p, pl.ds(g * ROWS, ROWS), :] = (value * inverse * gain).astype(BF16)
 
 
 def normalize(parts):
     return pl.pallas_call(
         normalize_kernel,
-        out_shape=[jax.ShapeDtypeStruct((4, ROWS, TP_WIDTH), BF16)] * 2,
+        out_shape=jax.ShapeDtypeStruct((4, 2 * ROWS, TP_WIDTH), BF16),
         compiler_params=pltpu.CompilerParams(vmem_limit_bytes=32 << 20),
         cost_estimate=pl.CostEstimate(flops=8 * ROWS * D, bytes_accessed=4 << 20, transcendentals=0),
         name="normalize",
     )(*parts)
 
 
-def feed_forward_kernel(place_ref, x_ref, w_ref, keep_ref, send_ref, acc_ref):
-    step = pl.program_id(0)
-
-    def block(p, kind):
+def feed_forward_kernel(place_ref, x_hbm, w_hbm, *refs):
+    outs, (x_ref, w_ref, gate_ref, up_ref, hidden_ref, sems) = refs[:4], refs[4:]
+    copies = [pltpu.make_async_copy(x_hbm, x_ref, sems.at[2])] + [
+        pltpu.make_async_copy(w_hbm.at[pl.ds(place_ref[j] * 8, 8)], w_ref.at[j], sems.at[j])
+        for j in range(2)
+    ]
+    for copy in copies:
+        copy.start()
+
+    def block(p, kind, low, width):
         pieces = [
             w_ref[
-                pl.ds(place_ref[p] * 8, 8),
-                pl.ds(place_ref[4 + y], 1),
+                p % 2,
+                :,
+                pl.ds(place_ref[6 + y], 1),
+                pl.ds(place_ref[2 + p], 1),
                 pl.ds(kind * 16, 16),
-                :,
+                pl.ds(low, width),
             ]
             for y in range(4)
         ]
-        return jnp.concatenate(pieces, axis=1).reshape(TP_WIDTH, UNIT_BLOCK)
-
-    gate = jnp.zeros((ROWS, UNIT_BLOCK), F32)
-    up = jnp.zeros((ROWS, UNIT_BLOCK), F32)
-    for p in range(4):
-        gate += jnp.dot(x_ref[p], block(p, 0), preferred_element_type=F32)
-        up += jnp.dot(x_ref[p], block(p, 1), preferred_element_type=F32)
-    hidden = (gate / (1.0 + jnp.exp(-gate)) * up).astype(BF16)
-
-    def down(p):
-        return lax.dot_general(
-            hidden, block(p, 2), (((1,), (1,)), ((), ())), preferred_element_type=F32
-        )
-
-    @pl.when(step == 0)
-    def _():
-        for p in range(4):
-            acc_ref[p] = down(p)
-
-    @pl.when(step == 1)
-    def _():
-        for i, p in enumerate((2, 0)):
-            send_ref[i] = (acc_ref[p + 1] + down(p + 1)).astype(BF16)
-            keep_ref[i] = (acc_ref[p] + down(p)).astype(BF16)
+        return jnp.concatenate(pieces, axis=1).reshape(TP_WIDTH, width)
+
+    units = w_ref.shape[5]
+    copies[0].wait()
+    for j in range(2):
+        copies[1 + j].wait()
+        for low in range(0, units, UNIT_BLOCK):
+            at = pl.ds(low, UNIT_BLOCK)
+            for kind, total_ref in ((0, gate_ref), (1, up_ref)):
+                total = jnp.dot(
+                    x_ref[j], block(j, kind, low, UNIT_BLOCK), preferred_element_type=F32
+                ) + jnp.dot(
+                    x_ref[j + 2], block(j + 2, kind, low, UNIT_BLOCK), preferred_element_type=F32
+                )
+                total_ref[:, at] = total if j == 0 else total_ref[:, at] + total
+    for low in range(0, units, UNIT_BLOCK):
+        at = pl.ds(low, UNIT_BLOCK)
+        gate = gate_ref[:, at]
+        hidden_ref[:, at] = (gate / (1.0 + jnp.exp(-gate)) * up_ref[:, at]).astype(BF16)
+    for i, p in enumerate((2, 0)):
+        for away in (1, 0):
+            product = lax.dot_general(
+                hidden_ref[...],
+                block(p + away, 2, 0, units),
+                (((1,), (1,)), ((), ())),
+                preferred_element_type=F32,
+            ).astype(BF16)
+            for g in range(2):
+                outs[2 * g + away][i] = product[g * ROWS : (g + 1) * ROWS]
 
 
 def feed_forward(place, x, weights):
-    pair = pl.BlockSpec((2, ROWS, TP_WIDTH), lambda i, o: (0, 0, 0))
-    units = weights.shape[3]
-    assert units == 2 * UNIT_BLOCK
+    units = weights.shape[4]
     return pl.pallas_call(
         feed_forward_kernel,
-        out_shape=[jax.ShapeDtypeStruct((2, ROWS, TP_WIDTH), BF16)] * 2,
-        grid_spec=pltpu.PrefetchScalarGridSpec(
-            num_scalar_prefetch=1,
-            grid=(2,),
-            in_specs=[
-                pl.BlockSpec((4, ROWS, TP_WIDTH), lambda i, o: (0, 0, 0)),
-                pl.BlockSpec((32, 4, 48, UNIT_BLOCK), lambda i, o: (0, 0, 0, i)),
-            ],
-            out_specs=[pair] * 2,
-            scratch_shapes=[pltpu.VMEM((4, ROWS, TP_WIDTH), F32)],
-        ),
+        out_shape=[jax.ShapeDtypeStruct((2, ROWS, TP_WIDTH), BF16)] * 4,
+        in_specs=[SMEM, HBM, HBM],
+        scratch_shapes=[
+            pltpu.VMEM((4, 2 * ROWS, TP_WIDTH), BF16),
+            pltpu.VMEM((2, 8, 4, 2, 48, units), BF16),
+            pltpu.VMEM((2 * ROWS, units), F32),
+            pltpu.VMEM((2 * ROWS, units), F32),
+            pltpu.VMEM((2 * ROWS, units), BF16),
+            pltpu.SemaphoreType.DMA((3,)),
+        ],
         compiler_params=pltpu.CompilerParams(vmem_limit_bytes=58 << 20),
         cost_estimate=pl.CostEstimate(
-            flops=6 * ROWS * D * units, bytes_accessed=8 << 20, transcendentals=ROWS * units
+            flops=12 * ROWS * D * units, bytes_accessed=10 << 20, transcendentals=2 * ROWS * units
         ),
         name="feed_forward",
     )(place, x, weights)
@@ -225,17 +235,15 @@
     up_weight,
     down_weight,
 ):
-    yh = lax.axis_index("yh")
+    xh, yh = lax.axis_index("xh"), lax.axis_index("yh")
     half = gate_weight.shape[1] // 2
 
     packed = jnp.concatenate([gate_weight, up_weight, down_weight.T], axis=0)
-    parity = yh & 1
-    mine = lax.dynamic_slice_in_dim(packed, parity * half, half, 1)
-    other = lax.dynamic_slice_in_dim(packed, (1 - parity) * half, half, 1)
-    near = jnp.stack(
-        [mine, around(other, "yh", 1), around(mine, "yh", 2), around(other, "yh", 3)]
-    )
-    weights = lax.all_gather(near, ("x", "z"), axis=0)
+    mine = lax.dynamic_slice_in_dim(packed, xh * half, half, 1)
+    other = lax.dynamic_slice_in_dim(packed, (1 - xh) * half, half, 1)
+    pair = jnp.stack([mine, swap(other, "xh")])
+    near = jnp.stack([pair] + [around(pair, "yh", by) for by in (1, 2, 3)])
+    weights = lax.all_gather(near, ("xl", "z"), axis=0)
 
     tail = jnp.broadcast_to(
         jnp.repeat(lengths.astype(BF16), 8)[:, None], (16, key_rows.shape[1])
@@ -248,18 +256,16 @@
         lengths, norm_gain[None, :], query_rows, k0, value_rows, k1, v1, k2, v2, residual_in
     )
 
-    partner = swap(sent, "yh")
+    partner = swap(sent, "xh")
     parts = []
     for start in (sent, partner):
         chip = swap(start, "yl")
         parts += [start, swap(start, "c"), chip, swap(chip, "c")]
     own = 2 * lax.axis_index("yl") + lax.axis_index("c")
-    place = [own, own ^ 1, own ^ 2, own ^ 3] + [(yh - y) & 3 for y in range(4)]
+    order = [own, own ^ 1, own ^ 2, own ^ 3]
+    place = [own & 1, (own & 1) ^ 1] + [(t >> 1) ^ xh for t in order] + [(yh - y) & 3 for y in range(4)]
     place = jnp.stack(place).astype(jnp.int32)
-    own_x, partner_x = normalize(parts)
-    partner_keep, partner_send = feed_forward(place, partner_x, weights)
-    own_x, partner_send = lax.optimization_barrier((own_x, partner_send))
-    own_keep, own_send = feed_forward(place, own_x, weights)
+    own_keep, own_send, partner_keep, partner_send = feed_forward(place, normalize(parts), weights)
 
     def add(left, right):
         return left.astype(F32) + right.astype(F32)
@@ -268,14 +274,14 @@
     own_got = swap(own_send, "c")
     partner_far = swap(add(partner_keep[0], partner_got[0]).astype(BF16), "yl")
     own_far = swap(add(own_keep[0], own_got[0]).astype(BF16), "yl")
-    back = swap((add(partner_keep[1], partner_got[1]) + partner_far.astype(F32)).astype(BF16), "yh")
+    back = swap((add(partner_keep[1], partner_got[1]) + partner_far.astype(F32)).astype(BF16), "xh")
     summed = add(own_keep[1], own_got[1]) + own_far.astype(F32) + back.astype(F32)
     mixed = residual_in + attended.astype(F32) + summed
     return attended, mixed
 
 
 def solution(mesh):
-    fine = Mesh(mesh.devices.reshape(4, 8, 4, 2, 2), SEQ + TP)
+    fine = Mesh(mesh.devices.reshape(2, 2, 8, 4, 2, 2), SEQ + TP)
     placed = (
         P(SEQ, TP),
         P(SEQ, TP),

time: 191 us -> 213 us (1.12)
  starting transfers between devices: 65.6 us -> 111 us
  waiting for transfers between devices: 80.1 us -> 59.2 us
  Pallas kernels: 18.7 us -> 13.8 us
    ppermute x12 -> x13, starting transfers between devices: 34 us -> 61.1 us  [swap(): return lax.ppermute(value, axis, [(i, i ^ 1) for i in range(size)])]
    ppermute x12 -> x13, waiting for transfers between devices: 23.3 us -> 48.1 us  [swap(): return lax.ppermute(value, axis, [(i, i ^ 1) for i in range(size)])]
    ppermute x4, waiting for transfers between devices: 30.9 us -> 7.74 us  [from_behind(): return lax.ppermute(value, SEQ, [(i, i + by) for i in range(size - by)])]
    all_gather x1, waiting for transfers between devices: 23.1 us -> 0.01 us  [on_device(): weights = lax.all_gather(near, ('xl', 'z'), axis=0)]
    ppermute x4, starting transfers between devices: 17.1 us -> 36.2 us  [from_behind(): return lax.ppermute(value, SEQ, [(i, i + by) for i in range(size - by)])]
    pallas_call x2 -> x1, Pallas kernels: 12.7 us -> 7.78 us  [feed_forward(): pl.pallas_call(feed_forward_kernel, out_shape=[jax.ShapeDtypeStruct((2, R...]
  transfers between devices with their start and end apart: 20 -> 21, of which waited for: 10 -> 10; matrix products, arithmetic and copies ran while one was open for 2% -> 3% of each run, Pallas kernels for 7% -> 3%
where the time goes in v6:
time: 213 us; the launch traced here: 211 us
  starting transfers between devices  111 us (52%)
  waiting for transfers between devices  59.2 us (28%)
  between operations  14.4 us (7%)
  Pallas kernels  13.8 us (6%)
  other arithmetic  8.35 us (4%)
  local copies, waits for them, and re-layouts  3.97 us (2%)
    ppermute x13, starting transfers between devices, swap(): return lax.ppermute(value, axis, [(i, i ^ 1) for i in range(size)])  61.1 us
    ppermute x13, waiting for transfers between devices, swap(): return lax.ppermute(value, axis, [(i, i ^ 1) for i in range(size)])  48.1 us
    ppermute x4, starting transfers between devices, from_behind(): return lax.ppermute(value, SEQ, [(i, i + by) for i in range(size - by)])  36.2 us
    ppermute x3, starting transfers between devices, around(): lax.ppermute(value, axis, [(i, (i + by) % size) for i in range(size)])  13.8 us
    pallas_call x1, Pallas kernels, feed_forward(): pl.pallas_call(feed_forward_kernel, out_shape=[jax.ShapeDtypeStruct((2, R...  7.78 us
    ppermute x4, waiting for transfers between devices, from_behind(): return lax.ppermute(value, SEQ, [(i, i + by) for i in range(size - by)])  7.74 us
    pallas_call x1, Pallas kernels, attention(): pl.pallas_call(attention_kernel, out_shape=(jax.ShapeDtypeStruct((ROWS, T...  5.06 us
  transfers between devices with their start and end apart: 21, of which 10 were waited for; matrix products, arithmetic and copies ran while one was open for 3% of the time, Pallas kernels for 3%

profile of v6, /device:TPU:1, one launch (start us, length us, event | category | flops | bytes accessed | tf_op | source)
XLA Modules:
  0.0 210.9 jit_solution(14567516051515340643)
XLA Ops:
  8.0 5.5 %collective-permute-start.11 = (bf16[48,512]{1,0:T(8,128)(2,1)S(1)}, bf16[48,512]{1,0:T(8,128)(2,1)S(1)}, u32[]{:S(2)}, u32[]{:S(2)}) collective-permute-start(bf16[48,512]{1,0:T(8,128)(2,1)S(1)} %get-tuple-element.17), channel_id=1, source_target_pairs={{0,256},{256,0},{1,257},{257,1},{2,258},{258,2},{3,259},{259,3},{4... | collective-permute-start | bytes 147464 | tf_op jit(solution)/shard_map/ppermute | solution.py:38
  15.0 6.1 %collective-permute-start.14 = (bf16[2,48,512]{2,1,0:T(8,128)(2,1)S(1)}, bf16[2,48,512]{2,1,0:T(8,128)(2,1)S(1)}, u32[]{:S(2)}, u32[]{:S(2)}) collective-permute-start(bf16[2,48,512]{2,1,0:T(8,128)(2,1)S(1)} %get-tuple-element.15), channel_id=1, source_target_pairs={{0,12},{4,0},{8,4},{12,8},{1,13},{5,1},{9,5},{13,9},{2,14},{6,2},{... | collective-permute-start | bytes 294920 | tf_op jit(solution)/shard_map/ppermute | solution.py:33
  21.1 3.5 %collective-permute-start.13 = (bf16[2,48,512]{2,1,0:T(8,128)(2,1)S(1)}, bf16[2,48,512]{2,1,0:T(8,128)(2,1)S(1)}, u32[]{:S(2)}, u32[]{:S(2)}) collective-permute-start(bf16[2,48,512]{2,1,0:T(8,128)(2,1)S(1)} %get-tuple-element.15), channel_id=1, source_target_pairs={{0,8},{4,12},{8,0},{12,4},{1,9},{5,13},{9,1},{13,5},{2,10},{6,14},... | collective-permute-start | bytes 294920 | tf_op jit(solution)/shard_map/ppermute | solution.py:33
  24.6 4.2 %collective-permute-start.12 = (bf16[2,48,512]{2,1,0:T(8,128)(2,1)S(1)}, bf16[2,48,512]{2,1,0:T(8,128)(2,1)S(1)}, u32[]{:S(2)}, u32[]{:S(2)}) collective-permute-start(bf16[2,48,512]{2,1,0:T(8,128)(2,1)S(1)} %get-tuple-element.15), channel_id=1, source_target_pairs={{0,4},{4,8},{8,12},{12,0},{1,5},{5,9},{9,13},{13,1},{2,6},{6,10},{... | collective-permute-start | bytes 294920 | tf_op jit(solution)/shard_map/ppermute | solution.py:33
  34.9 4.8 %collective-permute-start = (bf16[272,512]{1,0:T(8,128)(2,1)S(1)}, bf16[272,512]{1,0:T(8,128)(2,1)S(1)}, u32[]{:S(2)}, u32[]{:S(2)}) collective-permute-start(bf16[272,512]{1,0:T(8,128)(2,1)S(1)} %pad_maximum_fusion.1.refs_1_), channel_id=1, source_target_pairs={{0,4},{4,8},{8,12},{12,16},{16,20},{20,24},{24,28},{28,32},{32,36}... | collective-permute-start | bytes 835592 | tf_op jit(solution)/shard_map/ppermute | solution.py:28
  39.7 5.9 %collective-permute-start.1 = (bf16[256,512]{1,0:T(8,128)(2,1)}, bf16[256,512]{1,0:T(8,128)(2,1)S(1)}, u32[]{:S(2)}, u32[]{:S(2)}) collective-permute-start(bf16[256,512]{1,0:T(8,128)(2,1)} %refs_2_.1), channel_id=1, source_target_pairs={{0,4},{4,8},{8,12},{12,16},{16,20},{20,24},{24,28},{28,32},{32,36}... | collective-permute-start | bytes 786440 | tf_op jit(solution)/shard_map/ppermute | solution.py:28
  45.7 17.0 %collective-permute-start.2 = (bf16[272,512]{1,0:T(8,128)(2,1)S(1)}, bf16[272,512]{1,0:T(8,128)(2,1)S(1)}, u32[]{:S(2)}, u32[]{:S(2)}) collective-permute-start(bf16[272,512]{1,0:T(8,128)(2,1)S(1)} %collective-permute-done.refs_3_), channel_id=1, source_target_pairs={{0,4},{4,8},{8,12},{12,16},{16,20},{20,24},{24,28},{28,32},{32,36}... | collective-permute-start | bytes 835592 | tf_op jit(solution)/shard_map/ppermute | solution.py:28
  62.8 8.5 %collective-permute-start.3 = (bf16[256,512]{1,0:T(8,128)(2,1)S(1)}, bf16[256,512]{1,0:T(8,128)(2,1)S(1)}, u32[]{:S(2)}, u32[]{:S(2)}) collective-permute-start(bf16[256,512]{1,0:T(8,128)(2,1)S(1)} %collective-permute-done.1.refs_4_), channel_id=1, source_target_pairs={{0,4},{4,8},{8,12},{12,16},{16,20},{20,24},{24,28},{28,32},{32,36}... | collective-permute-start | bytes 786440 | tf_op jit(solution)/shard_map/ppermute | solution.py:28
  71.3 7.7 %collective-permute-done.3.refs_6_ = bf16[256,512]{1,0:T(8,128)(2,1)S(1)} collective-permute-done((bf16[256,512]{1,0:T(8,128)(2,1)S(1)}, bf16[256,512]{1,0:T(8,128)(2,1)S(1)}, u32[]{:S(2)}, u32[]{:S(2)}) %collective-permute-start.3) | collective-permute-done | bytes 262176 | tf_op jit(solution)/shard_map/ppermute | solution.py:28
  79.8 5.1 %attention.1 = (bf16[256,512]{1,0:T(8,128)(2,1)}, bf16[272,512]{1,0:T(8,128)(2,1)}) custom-call(s32[2]{0:T(128)} %lengths_ref.1, f32[1,512]{1,0:T(1,128)} %bitcast.40, bf16[256,512]{1,0:T(8,128)(2,1)} %refs_0_.1, bf16[272,512]{1,0:T(8,128)(2,1)} %copy-done.3, bf16[256,512]{1,0:T(8,128)(2,1)} %refs_2_.1, bf16[272,512]{1,0:T(8,128)(2,1)} %copy-done.4, ...), custom_call_target="tpu_custom_call" | custom-call | flops 402653184 | bytes 3145728 | tf_op jit(solution)/shard_map/attention/pallas_call | solution.py:108
  84.9 9.8 %collective-permute-start.7 = (bf16[272,512]{1,0:T(8,128)(2,1)}, bf16[272,512]{1,0:T(8,128)(2,1)S(1)}, u32[]{:S(2)}, u32[]{:S(2)}) collective-permute-start(bf16[272,512]{1,0:T(8,128)(2,1)} %get-tuple-element.9.refs_0_), channel_id=1, source_target_pairs={{0,256},{256,0},{1,257},{257,1},{2,258},{258,2},{3,259},{259,3},{4... | collective-permute-start | bytes 835592 | tf_op jit(solution)/shard_map/ppermute | solution.py:38
  94.7 16.0 %collective-permute-start.5 = (bf16[272,512]{1,0:T(8,128)(2,1)}, bf16[272,512]{1,0:T(8,128)(2,1)S(1)}, u32[]{:S(2)}, u32[]{:S(2)}) collective-permute-start(bf16[272,512]{1,0:T(8,128)(2,1)} %get-tuple-element.9.refs_0_), channel_id=1, source_target_pairs={{0,2},{2,0},{1,3},{3,1},{4,6},{6,4},{5,7},{7,5},{8,10},{10,8},{9,1... | collective-permute-start | bytes 835592 | tf_op jit(solution)/shard_map/ppermute | solution.py:38
  110.7 36.1 %collective-permute-done.7.refs_4_ = bf16[272,512]{1,0:T(8,128)(2,1)S(1)} collective-permute-done((bf16[272,512]{1,0:T(8,128)(2,1)}, bf16[272,512]{1,0:T(8,128)(2,1)S(1)}, u32[]{:S(2)}, u32[]{:S(2)}) %collective-permute-start.7) | collective-permute-done | bytes 278560 | tf_op jit(solution)/shard_map/ppermute | solution.py:38
  146.8 8.5 %collective-permute-start.9 = (bf16[272,512]{1,0:T(8,128)(2,1)S(1)}, bf16[272,512]{1,0:T(8,128)(2,1)S(1)}, u32[]{:S(2)}, u32[]{:S(2)}) collective-permute-start(bf16[272,512]{1,0:T(8,128)(2,1)S(1)} %collective-permute-done.7.refs_4_), channel_id=1, source_target_pairs={{0,2},{2,0},{1,3},{3,1},{4,6},{6,4},{5,7},{7,5},{8,10},{10,8},{9,1... | collective-permute-start | bytes 835592 | tf_op jit(solution)/shard_map/ppermute | solution.py:38
  155.3 2.7 %collective-permute-start.4 = (bf16[272,512]{1,0:T(8,128)(2,1)}, bf16[272,512]{1,0:T(8,128)(2,1)S(1)}, u32[]{:S(2)}, u32[]{:S(2)}) collective-permute-start(bf16[272,512]{1,0:T(8,128)(2,1)} %get-tuple-element.9.refs_0_), channel_id=1, source_target_pairs={{0,1},{1,0},{2,3},{3,2},{4,5},{5,4},{6,7},{7,6},{8,9},{9,8},{10,11... | collective-permute-start | bytes 835592 | tf_op jit(solution)/shard_map/ppermute | solution.py:38
  160.0 2.4 %collective-permute-start.6 = (bf16[272,512]{1,0:T(8,128)(2,1)S(1)}, bf16[272,512]{1,0:T(8,128)(2,1)S(1)}, u32[]{:S(2)}, u32[]{:S(2)}) collective-permute-start(bf16[272,512]{1,0:T(8,128)(2,1)S(1)} %collective-permute-done.5.refs_2_), channel_id=1, source_target_pairs={{0,1},{1,0},{2,3},{3,2},{4,5},{5,4},{6,7},{7,6},{8,9},{9,8},{10,11... | collective-permute-start | bytes 835592 | tf_op jit(solution)/shard_map/ppermute | solution.py:38
  162.4 2.4 %collective-permute-start.10 = (bf16[272,512]{1,0:T(8,128)(2,1)S(1)}, bf16[272,512]{1,0:T(8,128)(2,1)S(1)}, u32[]{:S(2)}, u32[]{:S(2)}) collective-permute-start(bf16[272,512]{1,0:T(8,128)(2,1)S(1)} %collective-permute-done.9.refs_6_), channel_id=1, source_target_pairs={{0,1},{1,0},{2,3},{3,2},{4,5},{5,4},{6,7},{7,6},{8,9},{9,8},{10,11... | collective-permute-start | bytes 835592 | tf_op jit(solution)/shard_map/ppermute | solution.py:38
  169.3 7.8 %feed_forward.1 = (bf16[2,256,512]{2,1,0:T(8,128)(2,1)}, bf16[2,256,512]{2,1,0:T(8,128)(2,1)}, bf16[2,256,512]{2,1,0:T(8,128)(2,1)}, bf16[2,256,512]{2,1,0:T(8,128)(2,1)}) custom-call(s32[10]{0:T(128)} %stack.67.place_ref, bf16[4,512,512]{2,1,0:T(8,128)(2,1)} %copy-done, bf16[16,4,2,48,512]{4,3,2,1,0:T(8,128)(2,1)} %bitcast.41), custom_call_target="tpu_custom_call" | custom-call | flops 3221225472 | bytes 10485760 | tf_op jit(solution)/shard_map/feed_forward/pallas_call | solution.py:207
  177.1 2.3 %collective-permute-start.17 = (bf16[2,256,512]{2,1,0:T(8,128)(2,1)}, bf16[2,256,512]{2,1,0:T(8,128)(2,1)S(1)}, u32[]{:S(2)}, u32[]{:S(2)}) collective-permute-start(bf16[2,256,512]{2,1,0:T(8,128)(2,1)} %get-tuple-element.13), channel_id=1, source_target_pairs={{0,1},{1,0},{2,3},{3,2},{4,5},{5,4},{6,7},{7,6},{8,9},{9,8},{10,11... | collective-permute-start | bytes 1572872 | tf_op jit(solution)/shard_map/ppermute | solution.py:38
  182.5 3.4 %collective-permute-start.18 = (bf16[256,512]{1,0:T(8,128)(2,1)S(1)}, bf16[256,512]{1,0:T(8,128)(2,1)S(1)}, u32[]{:S(2)}, u32[]{:S(2)}) collective-permute-start(bf16[256,512]{1,0:T(8,128)(2,1)S(1)} %fusion.4), channel_id=1, source_target_pairs={{0,2},{2,0},{1,3},{3,1},{4,6},{6,4},{5,7},{7,5},{8,10},{10,8},{9,1... | collective-permute-start | bytes 786440 | tf_op jit(solution)/shard_map/ppermute | solution.py:38
  188.8 3.1 %collective-permute-done.18 = bf16[256,512]{1,0:T(8,128)(2,1)S(1)} collective-permute-done((bf16[256,512]{1,0:T(8,128)(2,1)S(1)}, bf16[256,512]{1,0:T(8,128)(2,1)S(1)}, u32[]{:S(2)}, u32[]{:S(2)}) %collective-permute-start.18) | collective-permute-done | bytes 262176 | tf_op jit(solution)/shard_map/ppermute | solution.py:38
  192.9 2.2 %collective-permute-start.19 = (bf16[256,512]{1,0:T(8,128)(2,1)S(1)}, bf16[256,512]{1,0:T(8,128)(2,1)S(1)}, u32[]{:S(2)}, u32[]{:S(2)}) collective-permute-start(bf16[256,512]{1,0:T(8,128)(2,1)S(1)} %fusion), channel_id=1, source_target_pairs={{0,256},{256,0},{1,257},{257,1},{2,258},{258,2},{3,259},{259,3},{4... | collective-permute-start | bytes 786440 | tf_op jit(solution)/shard_map/ppermute | solution.py:38
  195.1 2.4 %collective-permute-done.16 = bf16[256,512]{1,0:T(8,128)(2,1)S(1)} collective-permute-done((bf16[256,512]{1,0:T(8,128)(2,1)S(1)}, bf16[256,512]{1,0:T(8,128)(2,1)S(1)}, u32[]{:S(2)}, u32[]{:S(2)}) %collective-permute-start.16) | collective-permute-done | bytes 262176 | tf_op jit(solution)/shard_map/ppermute | solution.py:38
  197.5 4.6 %collective-permute-done.19 = bf16[256,512]{1,0:T(8,128)(2,1)S(1)} collective-permute-done((bf16[256,512]{1,0:T(8,128)(2,1)S(1)}, bf16[256,512]{1,0:T(8,128)(2,1)S(1)}, u32[]{:S(2)}, u32[]{:S(2)}) %collective-permute-start.19) | collective-permute-done | bytes 262176 | tf_op jit(solution)/shard_map/ppermute | solution.py:38
  (54 shorter events, 24.6 us)
Async XLA Ops:
  7.2 162.1 %all-gather.3.cloned.1.call-start = ((), (), s32[]{:S(2)}) async-start(), calls=%async_computation | async-start | bytes 6684672 | tf_op jit(solution)/shard_map/all_gather | solution.py:246
  8.0 7.0 %collective-permute-start.11 = (bf16[48,512]{1,0:T(8,128)(2,1)S(1)}, bf16[48,512]{1,0:T(8,128)(2,1)S(1)}, u32[]{:S(2)}, u32[]{:S(2)}) collective-permute-start(bf16[48,512]{1,0:T(8,128)(2,1)S(1)} %get-tuple-element.17), channel_id=1, source_target_pairs={{0,256},{256,0},{1,257},{257,1},{2,258},{258,2},{3,259},{259,3},{4... | collective-permute-start | bytes 147464 | tf_op jit(solution)/shard_map/ppermute | solution.py:38
  15.0 13.9 %collective-permute-start.14 = (bf16[2,48,512]{2,1,0:T(8,128)(2,1)S(1)}, bf16[2,48,512]{2,1,0:T(8,128)(2,1)S(1)}, u32[]{:S(2)}, u32[]{:S(2)}) collective-permute-start(bf16[2,48,512]{2,1,0:T(8,128)(2,1)S(1)} %get-tuple-element.15), channel_id=1, source_target_pairs={{0,12},{4,0},{8,4},{12,8},{1,13},{5,1},{9,5},{13,9},{2,14},{6,2},{... | collective-permute-start | bytes 294920 | tf_op jit(solution)/shard_map/ppermute | solution.py:33
  21.1 9.3 %collective-permute-start.13 = (bf16[2,48,512]{2,1,0:T(8,128)(2,1)S(1)}, bf16[2,48,512]{2,1,0:T(8,128)(2,1)S(1)}, u32[]{:S(2)}, u32[]{:S(2)}) collective-permute-start(bf16[2,48,512]{2,1,0:T(8,128)(2,1)S(1)} %get-tuple-element.15), channel_id=1, source_target_pairs={{0,8},{4,12},{8,0},{12,4},{1,9},{5,13},{9,1},{13,5},{2,10},{6,14},... | collective-permute-start | bytes 294920 | tf_op jit(solution)/shard_map/ppermute | solution.py:33
  24.6 7.6 %collective-permute-start.12 = (bf16[2,48,512]{2,1,0:T(8,128)(2,1)S(1)}, bf16[2,48,512]{2,1,0:T(8,128)(2,1)S(1)}, u32[]{:S(2)}, u32[]{:S(2)}) collective-permute-start(bf16[2,48,512]{2,1,0:T(8,128)(2,1)S(1)} %get-tuple-element.15), channel_id=1, source_target_pairs={{0,4},{4,8},{8,12},{12,0},{1,5},{5,9},{9,13},{13,1},{2,6},{6,10},{... | collective-permute-start | bytes 294920 | tf_op jit(solution)/shard_map/ppermute | solution.py:33
  34.9 44.0 %copy-start.3 = (bf16[272,512]{1,0:T(8,128)(2,1)}, bf16[272,512]{1,0:T(8,128)(2,1)S(1)}, u32[]{:S(2)}) copy-start(bf16[272,512]{1,0:T(8,128)(2,1)S(1)} %pad_maximum_fusion.1.refs_1_) | copy-start | bytes 835588
  34.9 10.7 %collective-permute-start = (bf16[272,512]{1,0:T(8,128)(2,1)S(1)}, bf16[272,512]{1,0:T(8,128)(2,1)S(1)}, u32[]{:S(2)}, u32[]{:S(2)}) collective-permute-start(bf16[272,512]{1,0:T(8,128)(2,1)S(1)} %pad_maximum_fusion.1.refs_1_), channel_id=1, source_target_pairs={{0,4},{4,8},{8,12},{12,16},{16,20},{20,24},{24,28},{28,32},{32,36}... | collective-permute-start | bytes 835592 | tf_op jit(solution)/shard_map/ppermute | solution.py:28
  39.7 23.1 %collective-permute-start.1 = (bf16[256,512]{1,0:T(8,128)(2,1)}, bf16[256,512]{1,0:T(8,128)(2,1)S(1)}, u32[]{:S(2)}, u32[]{:S(2)}) collective-permute-start(bf16[256,512]{1,0:T(8,128)(2,1)} %refs_2_.1), channel_id=1, source_target_pairs={{0,4},{4,8},{8,12},{12,16},{16,20},{20,24},{24,28},{28,32},{32,36}... | collective-permute-start | bytes 786440 | tf_op jit(solution)/shard_map/ppermute | solution.py:28
  45.6 33.3 %copy-start.4 = (bf16[272,512]{1,0:T(8,128)(2,1)}, bf16[272,512]{1,0:T(8,128)(2,1)S(1)}, u32[]{:S(2)}) copy-start(bf16[272,512]{1,0:T(8,128)(2,1)S(1)} %collective-permute-done.refs_3_) | copy-start | bytes 835588
  45.7 33.3 %collective-permute-start.2 = (bf16[272,512]{1,0:T(8,128)(2,1)S(1)}, bf16[272,512]{1,0:T(8,128)(2,1)S(1)}, u32[]{:S(2)}, u32[]{:S(2)}) collective-permute-start(bf16[272,512]{1,0:T(8,128)(2,1)S(1)} %collective-permute-done.refs_3_), channel_id=1, source_target_pairs={{0,4},{4,8},{8,12},{12,16},{16,20},{20,24},{24,28},{28,32},{32,36}... | collective-permute-start | bytes 835592 | tf_op jit(solution)/shard_map/ppermute | solution.py:28
  62.8 16.2 %collective-permute-start.3 = (bf16[256,512]{1,0:T(8,128)(2,1)S(1)}, bf16[256,512]{1,0:T(8,128)(2,1)S(1)}, u32[]{:S(2)}, u32[]{:S(2)}) collective-permute-start(bf16[256,512]{1,0:T(8,128)(2,1)S(1)} %collective-permute-done.1.refs_4_), channel_id=1, source_target_pairs={{0,4},{4,8},{8,12},{12,16},{16,20},{20,24},{24,28},{28,32},{32,36}... | collective-permute-start | bytes 786440 | tf_op jit(solution)/shard_map/ppermute | solution.py:28
  84.9 61.9 %collective-permute-start.7 = (bf16[272,512]{1,0:T(8,128)(2,1)}, bf16[272,512]{1,0:T(8,128)(2,1)S(1)}, u32[]{:S(2)}, u32[]{:S(2)}) collective-permute-start(bf16[272,512]{1,0:T(8,128)(2,1)} %get-tuple-element.9.refs_0_), channel_id=1, source_target_pairs={{0,256},{256,0},{1,257},{257,1},{2,258},{258,2},{3,259},{259,3},{4... | collective-permute-start | bytes 835592 | tf_op jit(solution)/shard_map/ppermute | solution.py:38
  94.7 65.3 %collective-permute-start.5 = (bf16[272,512]{1,0:T(8,128)(2,1)}, bf16[272,512]{1,0:T(8,128)(2,1)S(1)}, u32[]{:S(2)}, u32[]{:S(2)}) collective-permute-start(bf16[272,512]{1,0:T(8,128)(2,1)} %get-tuple-element.9.refs_0_), channel_id=1, source_target_pairs={{0,2},{2,0},{1,3},{3,1},{4,6},{6,4},{5,7},{7,5},{8,10},{10,8},{9,1... | collective-permute-start | bytes 835592 | tf_op jit(solution)/shard_map/ppermute | solution.py:38
  146.8 15.6 %collective-permute-start.9 = (bf16[272,512]{1,0:T(8,128)(2,1)S(1)}, bf16[272,512]{1,0:T(8,128)(2,1)S(1)}, u32[]{:S(2)}, u32[]{:S(2)}) collective-permute-start(bf16[272,512]{1,0:T(8,128)(2,1)S(1)} %collective-permute-done.7.refs_4_), channel_id=1, source_target_pairs={{0,2},{2,0},{1,3},{3,1},{4,6},{6,4},{5,7},{7,5},{8,10},{10,8},{9,1... | collective-permute-start | bytes 835592 | tf_op jit(solution)/shard_map/ppermute | solution.py:38
  155.3 10.2 %collective-permute-start.4 = (bf16[272,512]{1,0:T(8,128)(2,1)}, bf16[272,512]{1,0:T(8,128)(2,1)S(1)}, u32[]{:S(2)}, u32[]{:S(2)}) collective-permute-start(bf16[272,512]{1,0:T(8,128)(2,1)} %get-tuple-element.9.refs_0_), channel_id=1, source_target_pairs={{0,1},{1,0},{2,3},{3,2},{4,5},{5,4},{6,7},{7,6},{8,9},{9,8},{10,11... | collective-permute-start | bytes 835592 | tf_op jit(solution)/shard_map/ppermute | solution.py:38
  158.0 7.5 %collective-permute-start.8 = (bf16[272,512]{1,0:T(8,128)(2,1)S(1)}, bf16[272,512]{1,0:T(8,128)(2,1)S(1)}, u32[]{:S(2)}, u32[]{:S(2)}) collective-permute-start(bf16[272,512]{1,0:T(8,128)(2,1)S(1)} %collective-permute-done.7.refs_4_), channel_id=1, source_target_pairs={{0,1},{1,0},{2,3},{3,2},{4,5},{5,4},{6,7},{7,6},{8,9},{9,8},{10,11... | collective-permute-start | bytes 835592 | tf_op jit(solution)/shard_map/ppermute | solution.py:38
  160.0 5.5 %collective-permute-start.6 = (bf16[272,512]{1,0:T(8,128)(2,1)S(1)}, bf16[272,512]{1,0:T(8,128)(2,1)S(1)}, u32[]{:S(2)}, u32[]{:S(2)}) collective-permute-start(bf16[272,512]{1,0:T(8,128)(2,1)S(1)} %collective-permute-done.5.refs_2_), channel_id=1, source_target_pairs={{0,1},{1,0},{2,3},{3,2},{4,5},{5,4},{6,7},{7,6},{8,9},{9,8},{10,11... | collective-permute-start | bytes 835592 | tf_op jit(solution)/shard_map/ppermute | solution.py:38
  162.4 3.6 %collective-permute-start.10 = (bf16[272,512]{1,0:T(8,128)(2,1)S(1)}, bf16[272,512]{1,0:T(8,128)(2,1)S(1)}, u32[]{:S(2)}, u32[]{:S(2)}) collective-permute-start(bf16[272,512]{1,0:T(8,128)(2,1)S(1)} %collective-permute-done.9.refs_6_), channel_id=1, source_target_pairs={{0,1},{1,0},{2,3},{3,2},{4,5},{5,4},{6,7},{7,6},{8,9},{9,8},{10,11... | collective-permute-start | bytes 835592 | tf_op jit(solution)/shard_map/ppermute | solution.py:38
  169.3 32.8 %copy-start.6 = (bf16[256,512]{1,0:T(8,128)(2,1)S(1)}, bf16[256,512]{1,0:T(8,128)(2,1)}, u32[]{:S(2)}) copy-start(bf16[256,512]{1,0:T(8,128)(2,1)} %get-tuple-element.6) | copy-start | bytes 786436
  177.1 4.3 %collective-permute-start.17 = (bf16[2,256,512]{2,1,0:T(8,128)(2,1)}, bf16[2,256,512]{2,1,0:T(8,128)(2,1)S(1)}, u32[]{:S(2)}, u32[]{:S(2)}) collective-permute-start(bf16[2,256,512]{2,1,0:T(8,128)(2,1)} %get-tuple-element.13), channel_id=1, source_target_pairs={{0,1},{1,0},{2,3},{3,2},{4,5},{5,4},{6,7},{7,6},{8,9},{9,8},{10,11... | collective-permute-start | bytes 1572872 | tf_op jit(solution)/shard_map/ppermute | solution.py:38
  179.4 6.5 %collective-permute-start.15 = (bf16[2,256,512]{2,1,0:T(8,128)(2,1)}, bf16[2,256,512]{2,1,0:T(8,128)(2,1)S(1)}, u32[]{:S(2)}, u32[]{:S(2)}) collective-permute-start(bf16[2,256,512]{2,1,0:T(8,128)(2,1)} %get-tuple-element.11), channel_id=1, source_target_pairs={{0,1},{1,0},{2,3},{3,2},{4,5},{5,4},{6,7},{7,6},{8,9},{9,8},{10,11... | collective-permute-start | bytes 1572872 | tf_op jit(solution)/shard_map/ppermute | solution.py:38
  182.5 9.4 %collective-permute-start.18 = (bf16[256,512]{1,0:T(8,128)(2,1)S(1)}, bf16[256,512]{1,0:T(8,128)(2,1)S(1)}, u32[]{:S(2)}, u32[]{:S(2)}) collective-permute-start(bf16[256,512]{1,0:T(8,128)(2,1)S(1)} %fusion.4), channel_id=1, source_target_pairs={{0,2},{2,0},{1,3},{3,1},{4,6},{6,4},{5,7},{7,5},{8,10},{10,8},{9,1... | collective-permute-start | bytes 786440 | tf_op jit(solution)/shard_map/ppermute | solution.py:38
  186.9 10.6 %collective-permute-start.16 = (bf16[256,512]{1,0:T(8,128)(2,1)S(1)}, bf16[256,512]{1,0:T(8,128)(2,1)S(1)}, u32[]{:S(2)}, u32[]{:S(2)}) collective-permute-start(bf16[256,512]{1,0:T(8,128)(2,1)S(1)} %fusion.3), channel_id=1, source_target_pairs={{0,2},{2,0},{1,3},{3,1},{4,6},{6,4},{5,7},{7,5},{8,10},{10,8},{9,1... | collective-permute-start | bytes 786440 | tf_op jit(solution)/shard_map/ppermute | solution.py:38
  192.9 9.2 %collective-permute-start.19 = (bf16[256,512]{1,0:T(8,128)(2,1)S(1)}, bf16[256,512]{1,0:T(8,128)(2,1)S(1)}, u32[]{:S(2)}, u32[]{:S(2)}) collective-permute-start(bf16[256,512]{1,0:T(8,128)(2,1)S(1)} %fusion), channel_id=1, source_target_pairs={{0,256},{256,0},{1,257},{257,1},{2,258},{258,2},{3,259},{259,3},{4... | collective-permute-start | bytes 786440 | tf_op jit(solution)/shard_map/ppermute | solution.py:38
  (6 other events, 53.0 us)
Sparse Core Ops, SparseCore 0:
  33.2 108.3 all-gather.2

commit v7 on v6

--- a/solution.py
+++ b/solution.py
@@ -17,7 +17,7 @@
 EXTRA = 16
 epsilon = 1e-06
 
-SEQ = ("xh", "xl", "z", "yh")
+SEQ = ("x", "z", "yh")
 TP = ("yl", "c")
 F32 = jnp.float32
 BF16 = jnp.bfloat16
@@ -150,51 +150,47 @@
     )(*parts)
 
 
-def feed_forward_kernel(place_ref, x_hbm, w_hbm, *refs):
-    outs, (x_ref, w_ref, gate_ref, up_ref, hidden_ref, sems) = refs[:4], refs[4:]
-    copies = [pltpu.make_async_copy(x_hbm, x_ref, sems.at[2])] + [
-        pltpu.make_async_copy(w_hbm.at[pl.ds(place_ref[j] * 8, 8)], w_ref.at[j], sems.at[j])
-        for j in range(2)
-    ]
+def feed_forward_kernel(place_ref, x_hbm, *refs):
+    blocks, halves, plane, outs = refs[:3], refs[3:5], refs[5], refs[6:10]
+    x_ref, wide_ref, down_ref, hidden_ref, sems = refs[10:]
+    pairs = [(x_hbm, x_ref)]
+    pairs += [(block, wide_ref.at[place_ref[8 + i]]) for i, block in enumerate(blocks)]
+    pairs += [(half, wide_ref.at[place_ref[11], pl.ds(4 * i, 4)]) for i, half in enumerate(halves)]
+    pairs += [(plane.at[:, i], down_ref.at[place_ref[12 + i]]) for i in range(4)]
+    copies = [pltpu.make_async_copy(src, dst, sems.at[i]) for i, (src, dst) in enumerate(pairs)]
     for copy in copies:
         copy.start()
 
-    def block(p, kind, low, width):
+    def load(w_ref, p, low_row, low, width):
         pieces = [
             w_ref[
-                p % 2,
+                pl.ds(place_ref[p], 1),
                 :,
-                pl.ds(place_ref[6 + y], 1),
-                pl.ds(place_ref[2 + p], 1),
-                pl.ds(kind * 16, 16),
+                pl.ds(place_ref[4 + y], 1),
+                pl.ds(low_row, 16),
                 pl.ds(low, width),
             ]
             for y in range(4)
         ]
-        return jnp.concatenate(pieces, axis=1).reshape(TP_WIDTH, width)
-
-    units = w_ref.shape[5]
-    copies[0].wait()
-    for j in range(2):
-        copies[1 + j].wait()
-        for low in range(0, units, UNIT_BLOCK):
-            at = pl.ds(low, UNIT_BLOCK)
-            for kind, total_ref in ((0, gate_ref), (1, up_ref)):
-                total = jnp.dot(
-                    x_ref[j], block(j, kind, low, UNIT_BLOCK), preferred_element_type=F32
-                ) + jnp.dot(
-                    x_ref[j + 2], block(j + 2, kind, low, UNIT_BLOCK), preferred_element_type=F32
-                )
-                total_ref[:, at] = total if j == 0 else total_ref[:, at] + total
+        return jnp.concatenate(pieces, axis=2).reshape(TP_WIDTH, width)
+
+    units = down_ref.shape[4]
+    for copy in copies[:6]:
+        copy.wait()
     for low in range(0, units, UNIT_BLOCK):
-        at = pl.ds(low, UNIT_BLOCK)
-        gate = gate_ref[:, at]
-        hidden_ref[:, at] = (gate / (1.0 + jnp.exp(-gate)) * up_ref[:, at]).astype(BF16)
+        gate = jnp.zeros((2 * ROWS, UNIT_BLOCK), F32)
+        up = jnp.zeros((2 * ROWS, UNIT_BLOCK), F32)
+        for p in range(4):
+            gate += jnp.dot(x_ref[p], load(wide_ref, p, 0, low, UNIT_BLOCK), preferred_element_type=F32)
+            up += jnp.dot(x_ref[p], load(wide_ref, p, 16, low, UNIT_BLOCK), preferred_element_type=F32)
+        hidden_ref[:, pl.ds(low, UNIT_BLOCK)] = (gate / (1.0 + jnp.exp(-gate)) * up).astype(BF16)
+    for copy in copies[6:]:
+        copy.wait()
     for i, p in enumerate((2, 0)):
         for away in (1, 0):
             product = lax.dot_general(
                 hidden_ref[...],
-                block(p + away, 2, 0, units),
+                load(down_ref, p + away, 0, 0, units),
                 (((1,), (1,)), ((), ())),
                 preferred_element_type=F32,
             ).astype(BF16)
@@ -202,26 +198,25 @@
                 outs[2 * g + away][i] = product[g * ROWS : (g + 1) * ROWS]
 
 
-def feed_forward(place, x, weights):
-    units = weights.shape[4]
+def feed_forward(place, x, blocks, halves, plane):
+    units = plane.shape[4]
     return pl.pallas_call(
         feed_forward_kernel,
         out_shape=[jax.ShapeDtypeStruct((2, ROWS, TP_WIDTH), BF16)] * 4,
-        in_specs=[SMEM, HBM, HBM],
+        in_specs=[SMEM] + [HBM] * 7,
         scratch_shapes=[
             pltpu.VMEM((4, 2 * ROWS, TP_WIDTH), BF16),
-            pltpu.VMEM((2, 8, 4, 2, 48, units), BF16),
-            pltpu.VMEM((2 * ROWS, units), F32),
-            pltpu.VMEM((2 * ROWS, units), F32),
+            pltpu.VMEM((4, 8, 4, 32, units), BF16),
+            pltpu.VMEM((4, 8, 4, 16, units), BF16),
             pltpu.VMEM((2 * ROWS, units), BF16),
-            pltpu.SemaphoreType.DMA((3,)),
+            pltpu.SemaphoreType.DMA((10,)),
         ],
         compiler_params=pltpu.CompilerParams(vmem_limit_bytes=58 << 20),
         cost_estimate=pl.CostEstimate(
             flops=12 * ROWS * D * units, bytes_accessed=10 << 20, transcendentals=2 * ROWS * units
         ),
         name="feed_forward",
-    )(place, x, weights)
+    )(place, x, *blocks, *halves, plane)
 
 
 def on_device(
@@ -235,37 +230,48 @@
     up_weight,
     down_weight,
 ):
-    xh, yh = lax.axis_index("xh"), lax.axis_index("yh")
+    x, yh = lax.axis_index("x"), lax.axis_index("yh")
     half = gate_weight.shape[1] // 2
 
     packed = jnp.concatenate([gate_weight, up_weight, down_weight.T], axis=0)
-    mine = lax.dynamic_slice_in_dim(packed, xh * half, half, 1)
-    other = lax.dynamic_slice_in_dim(packed, (1 - xh) * half, half, 1)
-    pair = jnp.stack([mine, swap(other, "xh")])
-    near = jnp.stack([pair] + [around(pair, "yh", by) for by in (1, 2, 3)])
-    weights = lax.all_gather(near, ("xl", "z"), axis=0)
+    parity = yh & 1
+    mine = lax.dynamic_slice_in_dim(packed, parity * half, half, 1)
+    other = lax.dynamic_slice_in_dim(packed, (1 - parity) * half, half, 1)
+    near = jnp.stack(
+        [mine, around(other, "yh", 1), around(mine, "yh", 2), around(other, "yh", 3)]
+    )
+    line = lax.all_gather(near[:, :32], "z", axis=0)
+    down = near[:, 32:]
+    down = jnp.stack([down] + [around(down, "x", by) for by in (1, 2, 3)])
 
     tail = jnp.broadcast_to(
         jnp.repeat(lengths.astype(BF16), 8)[:, None], (16, key_rows.shape[1])
     )
     k0 = jnp.concatenate([key_rows, tail], axis=0)
     k1, v1 = from_behind(k0, 1), from_behind(value_rows, 1)
+    down, k1, v1 = lax.optimization_barrier((down, k1, v1))
     k2, v2 = from_behind(k1, 1), from_behind(v1, 1)
+    line, k2, v2 = lax.optimization_barrier((line, k2, v2))
+    plane = lax.all_gather(down, "z", axis=0)
+    blocks = [line, around(line, "x", 1), around(line, "x", -1)]
+    halves = [around(blocks[1][:4], "x", 1), around(blocks[2][4:], "x", -1)]
 
     attended, sent = attention(
         lengths, norm_gain[None, :], query_rows, k0, value_rows, k1, v1, k2, v2, residual_in
     )
 
-    partner = swap(sent, "xh")
+    partner = swap(sent, "yh")
     parts = []
     for start in (sent, partner):
         chip = swap(start, "yl")
         parts += [start, swap(start, "c"), chip, swap(chip, "c")]
     own = 2 * lax.axis_index("yl") + lax.axis_index("c")
-    order = [own, own ^ 1, own ^ 2, own ^ 3]
-    place = [own & 1, (own & 1) ^ 1] + [(t >> 1) ^ xh for t in order] + [(yh - y) & 3 for y in range(4)]
+    place = [own, own ^ 1, own ^ 2, own ^ 3] + [(yh - y) & 3 for y in range(4)]
+    place += [(x - by) & 3 for by in (0, 1, 3, 2)] + [(x - by) & 3 for by in range(4)]
     place = jnp.stack(place).astype(jnp.int32)
-    own_keep, own_send, partner_keep, partner_send = feed_forward(place, normalize(parts), weights)
+    own_keep, own_send, partner_keep, partner_send = feed_forward(
+        place, normalize(parts), blocks, halves, plane
+    )
 
     def add(left, right):
         return left.astype(F32) + right.astype(F32)
@@ -274,14 +280,14 @@
     own_got = swap(own_send, "c")
     partner_far = swap(add(partner_keep[0], partner_got[0]).astype(BF16), "yl")
     own_far = swap(add(own_keep[0], own_got[0]).astype(BF16), "yl")
-    back = swap((add(partner_keep[1], partner_got[1]) + partner_far.astype(F32)).astype(BF16), "xh")
+    back = swap((add(partner_keep[1], partner_got[1]) + partner_far.astype(F32)).astype(BF16), "yh")
     summed = add(own_keep[1], own_got[1]) + own_far.astype(F32) + back.astype(F32)
     mixed = residual_in + attended.astype(F32) + summed
     return attended, mixed
 
 
 def solution(mesh):
-    fine = Mesh(mesh.devices.reshape(2, 2, 8, 4, 2, 2), SEQ + TP)
+    fine = Mesh(mesh.devices.reshape(4, 8, 4, 2, 2), SEQ + TP)
     placed = (
         P(SEQ, TP),
         P(SEQ, TP),

time: 213 us -> 187 us (0.88)
  waiting for transfers between devices: 59.2 us -> 43.5 us
  starting transfers between devices: 111 us -> 101 us
    ppermute x13 -> x12, waiting for transfers between devices: 48.1 us -> 17.6 us  [swap(): return lax.ppermute(value, axis, [(i, i ^ 1) for i in range(size)])]
    ppermute x3 -> x10, starting transfers between devices: 13.8 us -> 37.5 us  [around(): lax.ppermute(value, axis, [(i, (i + by) % size) for i in range(size)])]
    ppermute x4, starting transfers between devices: 36.2 us -> 17.8 us  [from_behind(): return lax.ppermute(value, SEQ, [(i, i + by) for i in range(size - by)])]
    ppermute x13 -> x12, starting transfers between devices: 61.1 us -> 45.9 us  [swap(): return lax.ppermute(value, axis, [(i, i ^ 1) for i in range(size)])]
    ppermute x4, waiting for transfers between devices: 7.74 us -> 16.7 us  [from_behind(): return lax.ppermute(value, SEQ, [(i, i + by) for i in range(size - by)])]
    all_gather x1 -> x2, waiting for transfers between devices: 0.01 us -> 5.22 us  [the longest x1 5.21 us: on_device(): line = lax.all_gather(near[:, :32], 'z', axis=0)]
    slice x0 -> x2, local copies, waits for them, and re-layouts: none -> 2.18 us  [on_device(): halves = [around(blocks[1][:4], 'x', 1), around(blocks[2][4:], 'x', -1)]]
  transfers between devices with their start and end apart: 21 -> 28, of which waited for: 10 -> 11; matrix products, arithmetic and copies ran while one was open for 3% -> 5% of each run, Pallas kernels for 3% -> 3%
where the time goes in v7:
time: 187 us; the launch traced here: 186 us
  starting transfers between devices  101 us (54%)
  waiting for transfers between devices  43.5 us (23%)
  between operations  14.5 us (8%)
  Pallas kernels  14.2 us (8%)
  other arithmetic  8.02 us (4%)
  local copies, waits for them, and re-layouts  4.35 us (2%)
    ppermute x12, starting transfers between devices, swap(): return lax.ppermute(value, axis, [(i, i ^ 1) for i in range(size)])  45.9 us
    ppermute x10, starting transfers between devices, around(): lax.ppermute(value, axis, [(i, (i + by) % size) for i in range(size)])  37.5 us
    ppermute x4, starting transfers between devices, from_behind(): return lax.ppermute(value, SEQ, [(i, i + by) for i in range(size - by)])  17.8 us
    ppermute x12, waiting for transfers between devices, swap(): return lax.ppermute(value, axis, [(i, i ^ 1) for i in range(size)])  17.6 us
    ppermute x4, waiting for transfers between devices, from_behind(): return lax.ppermute(value, SEQ, [(i, i + by) for i in range(size - by)])  16.7 us
    pallas_call x1, Pallas kernels, feed_forward(): pl.pallas_call(feed_forward_kernel, out_shape=[jax.ShapeDtypeStruct((2, R...  8.16 us
    all_gather x1, waiting for transfers between devices, on_device(): line = lax.all_gather(near[:, :32], 'z', axis=0)  5.21 us
    pallas_call x1, Pallas kernels, attention(): pl.pallas_call(attention_kernel, out_shape=(jax.ShapeDtypeStruct((ROWS, T...  5.09 us
  transfers between devices with their start and end apart: 28, of which 11 were waited for; matrix products, arithmetic and copies ran while one was open for 5% of the time, Pallas kernels for 3%

profile of v7, /device:TPU:1, one launch (start us, length us, event | category | flops | bytes accessed | tf_op | source)
XLA Modules:
  0.0 185.9 jit_solution(9966878561553711532)
XLA Ops:
  8.0 8.3 %collective-permute-start.1 = (bf16[48,512]{1,0:T(8,128)(2,1)S(1)}, bf16[48,512]{1,0:T(8,128)(2,1)S(1)}, u32[]{:S(2)}, u32[]{:S(2)}) collective-permute-start(bf16[48,512]{1,0:T(8,128)(2,1)S(1)} %get-tuple-element.26), channel_id=1, source_target_pairs={{0,8},{4,12},{8,0},{12,4},{1,9},{5,13},{9,1},{13,5},{2,10},{6,14},... | collective-permute-start | bytes 147464 | tf_op jit(solution)/shard_map/ppermute | solution.py:33
  18.3 4.2 %collective-permute-start = (bf16[48,512]{1,0:T(8,128)(2,1)S(1)}, bf16[48,512]{1,0:T(8,128)(2,1)S(1)}, u32[]{:S(2)}, u32[]{:S(2)}) collective-permute-start(bf16[48,512]{1,0:T(8,128)(2,1)S(1)} %get-tuple-element.27), channel_id=1, source_target_pairs={{0,4},{4,8},{8,12},{12,0},{1,5},{5,9},{9,13},{13,1},{2,6},{6,10},{... | collective-permute-start | bytes 147464 | tf_op jit(solution)/shard_map/ppermute | solution.py:33
  22.7 2.6 %collective-permute-done = bf16[48,512]{1,0:T(8,128)(2,1)S(1)} collective-permute-done((bf16[48,512]{1,0:T(8,128)(2,1)S(1)}, bf16[48,512]{1,0:T(8,128)(2,1)S(1)}, u32[]{:S(2)}, u32[]{:S(2)}) %collective-permute-start) | collective-permute-done | bytes 49184 | tf_op jit(solution)/shard_map/ppermute | solution.py:33
  26.0 3.3 %collective-permute-start.7 = (bf16[256,512]{1,0:T(8,128)(2,1)}, bf16[256,512]{1,0:T(8,128)(2,1)S(1)}, u32[]{:S(2)}, u32[]{:S(2)}) collective-permute-start(bf16[256,512]{1,0:T(8,128)(2,1)} %refs_2_.1), channel_id=1, source_target_pairs={{0,4},{4,8},{8,12},{12,16},{16,20},{20,24},{24,28},{28,32},{32,36}... | collective-permute-start | bytes 786440 | tf_op jit(solution)/shard_map/ppermute | solution.py:28
  31.2 4.7 %collective-permute-start.6 = (bf16[272,512]{1,0:T(8,128)(2,1)S(1)}, bf16[272,512]{1,0:T(8,128)(2,1)S(1)}, u32[]{:S(2)}, u32[]{:S(2)}) collective-permute-start(bf16[272,512]{1,0:T(8,128)(2,1)S(1)} %pad_maximum_fusion.refs_1_), channel_id=1, source_target_pairs={{0,4},{4,8},{8,12},{12,16},{16,20},{20,24},{24,28},{28,32},{32,36}... | collective-permute-start | bytes 835592 | tf_op jit(solution)/shard_map/ppermute | solution.py:28
  35.9 4.6 %collective-permute-start.4 = (bf16[4,16,512]{2,1,0:T(8,128)(2,1)S(1)}, bf16[4,16,512]{2,1,0:T(8,128)(2,1)S(1)}, u32[]{:S(2)}, u32[]{:S(2)}) collective-permute-start(bf16[4,16,512]{2,1,0:T(8,128)(2,1)S(1)} %pad_maximum_fusion.6), channel_id=1, source_target_pairs={{0,256},{128,384},{256,0},{384,128},{1,257},{129,385},{257,1},{385... | collective-permute-start | bytes 196616 | tf_op jit(solution)/shard_map/ppermute | solution.py:33
  42.8 4.3 %collective-permute-start.5 = (bf16[4,16,512]{2,1,0:T(8,128)(2,1)S(1)}, bf16[4,16,512]{2,1,0:T(8,128)(2,1)S(1)}, u32[]{:S(2)}, u32[]{:S(2)}) collective-permute-start(bf16[4,16,512]{2,1,0:T(8,128)(2,1)S(1)} %pad_maximum_fusion.6), channel_id=1, source_target_pairs={{0,384},{128,0},{256,128},{384,256},{1,385},{129,1},{257,129},{385... | collective-permute-start | bytes 196616 | tf_op jit(solution)/shard_map/ppermute | solution.py:33
  50.0 6.2 %collective-permute-start.8 = (bf16[272,512]{1,0:T(8,128)(2,1)S(1)}, bf16[272,512]{1,0:T(8,128)(2,1)S(1)}, u32[]{:S(2)}, u32[]{:S(2)}) collective-permute-start(bf16[272,512]{1,0:T(8,128)(2,1)S(1)} %collective-permute-done.6.refs_3_), channel_id=1, source_target_pairs={{0,4},{4,8},{8,12},{12,16},{16,20},{20,24},{24,28},{28,32},{32,36}... | collective-permute-start | bytes 835592 | tf_op jit(solution)/shard_map/ppermute | solution.py:28
  56.2 3.6 %collective-permute-start.9 = (bf16[256,512]{1,0:T(8,128)(2,1)S(1)}, bf16[256,512]{1,0:T(8,128)(2,1)S(1)}, u32[]{:S(2)}, u32[]{:S(2)}) collective-permute-start(bf16[256,512]{1,0:T(8,128)(2,1)S(1)} %collective-permute-done.7.refs_4_), channel_id=1, source_target_pairs={{0,4},{4,8},{8,12},{12,16},{16,20},{20,24},{24,28},{28,32},{32,36}... | collective-permute-start | bytes 786440 | tf_op jit(solution)/shard_map/ppermute | solution.py:28
  59.9 15.8 %collective-permute-done.9.refs_6_ = bf16[256,512]{1,0:T(8,128)(2,1)S(1)} collective-permute-done((bf16[256,512]{1,0:T(8,128)(2,1)S(1)}, bf16[256,512]{1,0:T(8,128)(2,1)S(1)}, u32[]{:S(2)}, u32[]{:S(2)}) %collective-permute-start.9) | collective-permute-done | bytes 262176 | tf_op jit(solution)/shard_map/ppermute | solution.py:28
  75.7 5.2 %all-gather.5.cloned.1.call-done = bf16[32,32,512]{2,1,0:T(8,128)(2,1)} async-done(((bf16[4,32,512]{2,1,0:T(8,128)(2,1)}), bf16[32,32,512]{2,1,0:T(8,128)(2,1)}) %all-gather.5.cloned.1.call-update) | async-done | bytes 1048592 | tf_op jit(solution)/shard_map/all_gather | solution.py:243
  82.8 3.4 %collective-permute-start.17 = (bf16[8,4,32,512]{3,2,1,0:T(8,128)(2,1)}, bf16[8,4,32,512]{3,2,1,0:T(8,128)(2,1)}, u32[]{:S(2)}, u32[]{:S(2)}) collective-permute-start(bf16[8,4,32,512]{3,2,1,0:T(8,128)(2,1)} %bitcast.58), channel_id=1, source_target_pairs={{0,128},{128,256},{256,384},{384,0},{1,129},{129,257},{257,385},{3... | collective-permute-start | bytes 3145736 | tf_op jit(solution)/shard_map/ppermute | solution.py:33
  86.2 5.1 %attention.1 = (bf16[256,512]{1,0:T(8,128)(2,1)}, bf16[272,512]{1,0:T(8,128)(2,1)}) custom-call(s32[2]{0:T(128)} %lengths_ref.1, f32[1,512]{1,0:T(1,128)} %bitcast.55, bf16[256,512]{1,0:T(8,128)(2,1)} %refs_0_.1, bf16[272,512]{1,0:T(8,128)(2,1)} %copy-done.3, bf16[256,512]{1,0:T(8,128)(2,1)} %refs_2_.1, bf16[272,512]{1,0:T(8,128)(2,1)} %copy-done.5, ...), custom_call_target="tpu_custom_call" | custom-call | flops 402653184 | bytes 3145728 | tf_op jit(solution)/shard_map/attention/pallas_call | solution.py:108
  93.9 10.0 %collective-permute-start.11 = (bf16[272,512]{1,0:T(8,128)(2,1)}, bf16[272,512]{1,0:T(8,128)(2,1)S(1)}, u32[]{:S(2)}, u32[]{:S(2)}) collective-permute-start(bf16[272,512]{1,0:T(8,128)(2,1)} %get-tuple-element.19.refs_0_), channel_id=1, source_target_pairs={{0,2},{2,0},{1,3},{3,1},{4,6},{6,4},{5,7},{7,5},{8,10},{10,8},{9,1... | collective-permute-start | bytes 835592 | tf_op jit(solution)/shard_map/ppermute | solution.py:38
  103.9 3.6 %collective-permute-start.10 = (bf16[272,512]{1,0:T(8,128)(2,1)}, bf16[272,512]{1,0:T(8,128)(2,1)S(1)}, u32[]{:S(2)}, u32[]{:S(2)}) collective-permute-start(bf16[272,512]{1,0:T(8,128)(2,1)} %get-tuple-element.19.refs_0_), channel_id=1, source_target_pairs={{0,1},{1,0},{2,3},{3,2},{4,5},{5,4},{6,7},{7,6},{8,9},{9,8},{10,11... | collective-permute-start | bytes 835592 | tf_op jit(solution)/shard_map/ppermute | solution.py:38
  107.6 4.2 %collective-permute-start.15 = (bf16[272,512]{1,0:T(8,128)(2,1)S(1)}, bf16[272,512]{1,0:T(8,128)(2,1)S(1)}, u32[]{:S(2)}, u32[]{:S(2)}) collective-permute-start(bf16[272,512]{1,0:T(8,128)(2,1)S(1)} %collective-permute-done.13.refs_4_), channel_id=1, source_target_pairs={{0,2},{2,0},{1,3},{3,1},{4,6},{6,4},{5,7},{7,5},{8,10},{10,8},{9,1... | collective-permute-start | bytes 835592 | tf_op jit(solution)/shard_map/ppermute | solution.py:38
  112.9 4.7 %collective-permute-start.20 = (bf16[4,4,32,512]{3,2,1,0:T(8,128)(2,1)S(1)}, bf16[4,4,32,512]{3,2,1,0:T(8,128)(2,1)}, u32[]{:S(2)}, u32[]{:S(2)}) collective-permute-start(bf16[4,4,32,512]{3,2,1,0:T(8,128)(2,1)S(1)} %slice.49), channel_id=1, source_target_pairs={{0,384},{128,0},{256,128},{384,256},{1,385},{129,1},{257,129},{385... | collective-permute-start | bytes 1572872 | tf_op jit(solution)/shard_map/ppermute | solution.py:33
  120.6 6.5 %collective-permute-start.14 = (bf16[272,512]{1,0:T(8,128)(2,1)S(1)}, bf16[272,512]{1,0:T(8,128)(2,1)S(1)}, u32[]{:S(2)}, u32[]{:S(2)}) collective-permute-start(bf16[272,512]{1,0:T(8,128)(2,1)S(1)} %collective-permute-done.13.refs_4_), channel_id=1, source_target_pairs={{0,1},{1,0},{2,3},{3,2},{4,5},{5,4},{6,7},{7,6},{8,9},{9,8},{10,11... | collective-permute-start | bytes 835592 | tf_op jit(solution)/shard_map/ppermute | solution.py:38
  134.9 8.2 %feed_forward.1 = (bf16[2,256,512]{2,1,0:T(8,128)(2,1)}, bf16[2,256,512]{2,1,0:T(8,128)(2,1)}, bf16[2,256,512]{2,1,0:T(8,128)(2,1)}, bf16[2,256,512]{2,1,0:T(8,128)(2,1)}) custom-call(s32[16]{0:T(128)} %stack.95.place_ref, bf16[4,512,512]{2,1,0:T(8,128)(2,1)} %copy-done, bf16[8,4,32,512]{3,2,1,0:T(8,128)(2,1)} %bitcast.59, ...), custom_call_target="tpu_custom_call" | custom-call | flops 3221225472 | bytes 10485760 | tf_op jit(solution)/shard_map/feed_forward/pallas_call | solution.py:203
  143.1 3.4 %collective-permute-start.23 = (bf16[2,256,512]{2,1,0:T(8,128)(2,1)}, bf16[2,256,512]{2,1,0:T(8,128)(2,1)S(1)}, u32[]{:S(2)}, u32[]{:S(2)}) collective-permute-start(bf16[2,256,512]{2,1,0:T(8,128)(2,1)} %get-tuple-element.25), channel_id=1, source_target_pairs={{0,1},{1,0},{2,3},{3,2},{4,5},{5,4},{6,7},{7,6},{8,9},{9,8},{10,11... | collective-permute-start | bytes 1572872 | tf_op jit(solution)/shard_map/ppermute | solution.py:38
  149.5 5.6 %collective-permute-start.24 = (bf16[256,512]{1,0:T(8,128)(2,1)S(1)}, bf16[256,512]{1,0:T(8,128)(2,1)S(1)}, u32[]{:S(2)}, u32[]{:S(2)}) collective-permute-start(bf16[256,512]{1,0:T(8,128)(2,1)S(1)} %fusion.4), channel_id=1, source_target_pairs={{0,2},{2,0},{1,3},{3,1},{4,6},{6,4},{5,7},{7,5},{8,10},{10,8},{9,1... | collective-permute-start | bytes 786440 | tf_op jit(solution)/shard_map/ppermute | solution.py:38
  158.0 3.3 %collective-permute-done.24 = bf16[256,512]{1,0:T(8,128)(2,1)S(1)} collective-permute-done((bf16[256,512]{1,0:T(8,128)(2,1)S(1)}, bf16[256,512]{1,0:T(8,128)(2,1)S(1)}, u32[]{:S(2)}, u32[]{:S(2)}) %collective-permute-start.24) | collective-permute-done | bytes 262176 | tf_op jit(solution)/shard_map/ppermute | solution.py:38
  164.3 2.6 %collective-permute-done.22 = bf16[256,512]{1,0:T(8,128)(2,1)S(1)} collective-permute-done((bf16[256,512]{1,0:T(8,128)(2,1)S(1)}, bf16[256,512]{1,0:T(8,128)(2,1)S(1)}, u32[]{:S(2)}, u32[]{:S(2)}) %collective-permute-start.22) | collective-permute-done | bytes 262176 | tf_op jit(solution)/shard_map/ppermute | solution.py:38
  166.9 11.2 %collective-permute-done.25 = bf16[256,512]{1,0:T(8,128)(2,1)S(1)} collective-permute-done((bf16[256,512]{1,0:T(8,128)(2,1)S(1)}, bf16[256,512]{1,0:T(8,128)(2,1)S(1)}, u32[]{:S(2)}, u32[]{:S(2)}) %collective-permute-start.25) | collective-permute-done | bytes 262176 | tf_op jit(solution)/shard_map/ppermute | solution.py:38
  (75 shorter events, 36.9 us)
Async XLA Ops:
  7.2 73.7 %all-gather.5.cloned.1.call-start = ((), (), s32[]{:S(2)}) async-start(), calls=%async_computation | async-start | bytes 1179648 | tf_op jit(solution)/shard_map/all_gather | solution.py:243
  8.0 14.5 %collective-permute-start.1 = (bf16[48,512]{1,0:T(8,128)(2,1)S(1)}, bf16[48,512]{1,0:T(8,128)(2,1)S(1)}, u32[]{:S(2)}, u32[]{:S(2)}) collective-permute-start(bf16[48,512]{1,0:T(8,128)(2,1)S(1)} %get-tuple-element.26), channel_id=1, source_target_pairs={{0,8},{4,12},{8,0},{12,4},{1,9},{5,13},{9,1},{13,5},{2,10},{6,14},... | collective-permute-start | bytes 147464 | tf_op jit(solution)/shard_map/ppermute | solution.py:33
  16.3 6.4 %collective-permute-start.2 = (bf16[48,512]{1,0:T(8,128)(2,1)S(1)}, bf16[48,512]{1,0:T(8,128)(2,1)S(1)}, u32[]{:S(2)}, u32[]{:S(2)}) collective-permute-start(bf16[48,512]{1,0:T(8,128)(2,1)S(1)} %get-tuple-element.27), channel_id=1, source_target_pairs={{0,12},{4,0},{8,4},{12,8},{1,13},{5,1},{9,5},{13,9},{2,14},{6,2},{... | collective-permute-start | bytes 147464 | tf_op jit(solution)/shard_map/ppermute | solution.py:33
  18.3 7.0 %collective-permute-start = (bf16[48,512]{1,0:T(8,128)(2,1)S(1)}, bf16[48,512]{1,0:T(8,128)(2,1)S(1)}, u32[]{:S(2)}, u32[]{:S(2)}) collective-permute-start(bf16[48,512]{1,0:T(8,128)(2,1)S(1)} %get-tuple-element.27), channel_id=1, source_target_pairs={{0,4},{4,8},{8,12},{12,0},{1,5},{5,9},{9,13},{13,1},{2,6},{6,10},{... | collective-permute-start | bytes 147464 | tf_op jit(solution)/shard_map/ppermute | solution.py:33
  26.0 109.0 %all-gather.7.cloned.1.call-start = ((), (), s32[]{:S(2)}) async-start(), calls=%async_computation.1 | async-start | bytes 2359296 | tf_op jit(solution)/shard_map/all_gather | solution.py:255
  26.0 23.1 %collective-permute-start.7 = (bf16[256,512]{1,0:T(8,128)(2,1)}, bf16[256,512]{1,0:T(8,128)(2,1)S(1)}, u32[]{:S(2)}, u32[]{:S(2)}) collective-permute-start(bf16[256,512]{1,0:T(8,128)(2,1)} %refs_2_.1), channel_id=1, source_target_pairs={{0,4},{4,8},{8,12},{12,16},{16,20},{20,24},{24,28},{28,32},{32,36}... | collective-permute-start | bytes 786440 | tf_op jit(solution)/shard_map/ppermute | solution.py:28
  31.2 18.8 %collective-permute-start.6 = (bf16[272,512]{1,0:T(8,128)(2,1)S(1)}, bf16[272,512]{1,0:T(8,128)(2,1)S(1)}, u32[]{:S(2)}, u32[]{:S(2)}) collective-permute-start(bf16[272,512]{1,0:T(8,128)(2,1)S(1)} %pad_maximum_fusion.refs_1_), channel_id=1, source_target_pairs={{0,4},{4,8},{8,12},{12,16},{16,20},{20,24},{24,28},{28,32},{32,36}... | collective-permute-start | bytes 835592 | tf_op jit(solution)/shard_map/ppermute | solution.py:28
  35.9 11.2 %collective-permute-start.4 = (bf16[4,16,512]{2,1,0:T(8,128)(2,1)S(1)}, bf16[4,16,512]{2,1,0:T(8,128)(2,1)S(1)}, u32[]{:S(2)}, u32[]{:S(2)}) collective-permute-start(bf16[4,16,512]{2,1,0:T(8,128)(2,1)S(1)} %pad_maximum_fusion.6), channel_id=1, source_target_pairs={{0,256},{128,384},{256,0},{384,128},{1,257},{129,385},{257,1},{385... | collective-permute-start | bytes 196616 | tf_op jit(solution)/shard_map/ppermute | solution.py:33
  40.5 6.7 %collective-permute-start.3 = (bf16[4,16,512]{2,1,0:T(8,128)(2,1)S(1)}, bf16[4,16,512]{2,1,0:T(8,128)(2,1)S(1)}, u32[]{:S(2)}, u32[]{:S(2)}) collective-permute-start(bf16[4,16,512]{2,1,0:T(8,128)(2,1)S(1)} %pad_maximum_fusion.6), channel_id=1, source_target_pairs={{0,128},{128,256},{256,384},{384,0},{1,129},{129,257},{257,385},{3... | collective-permute-start | bytes 196616 | tf_op jit(solution)/shard_map/ppermute | solution.py:33
  50.0 25.7 %collective-permute-start.8 = (bf16[272,512]{1,0:T(8,128)(2,1)S(1)}, bf16[272,512]{1,0:T(8,128)(2,1)S(1)}, u32[]{:S(2)}, u32[]{:S(2)}) collective-permute-start(bf16[272,512]{1,0:T(8,128)(2,1)S(1)} %collective-permute-done.6.refs_3_), channel_id=1, source_target_pairs={{0,4},{4,8},{8,12},{12,16},{16,20},{20,24},{24,28},{28,32},{32,36}... | collective-permute-start | bytes 835592 | tf_op jit(solution)/shard_map/ppermute | solution.py:28
  56.2 19.5 %collective-permute-start.9 = (bf16[256,512]{1,0:T(8,128)(2,1)S(1)}, bf16[256,512]{1,0:T(8,128)(2,1)S(1)}, u32[]{:S(2)}, u32[]{:S(2)}) collective-permute-start(bf16[256,512]{1,0:T(8,128)(2,1)S(1)} %collective-permute-done.7.refs_4_), channel_id=1, source_target_pairs={{0,4},{4,8},{8,12},{12,16},{16,20},{20,24},{24,28},{28,32},{32,36}... | collective-permute-start | bytes 786440 | tf_op jit(solution)/shard_map/ppermute | solution.py:28
  80.9 30.9 %collective-permute-start.18 = (bf16[8,4,32,512]{3,2,1,0:T(8,128)(2,1)}, bf16[8,4,32,512]{3,2,1,0:T(8,128)(2,1)}, u32[]{:S(2)}, u32[]{:S(2)}) collective-permute-start(bf16[8,4,32,512]{3,2,1,0:T(8,128)(2,1)} %bitcast.57), channel_id=1, source_target_pairs={{0,384},{128,0},{256,128},{384,256},{1,385},{129,1},{257,129},{385... | collective-permute-start | bytes 3145736 | tf_op jit(solution)/shard_map/ppermute | solution.py:33
  82.8 34.8 %collective-permute-start.17 = (bf16[8,4,32,512]{3,2,1,0:T(8,128)(2,1)}, bf16[8,4,32,512]{3,2,1,0:T(8,128)(2,1)}, u32[]{:S(2)}, u32[]{:S(2)}) collective-permute-start(bf16[8,4,32,512]{3,2,1,0:T(8,128)(2,1)} %bitcast.58), channel_id=1, source_target_pairs={{0,128},{128,256},{256,384},{384,0},{1,129},{129,257},{257,385},{3... | collective-permute-start | bytes 3145736 | tf_op jit(solution)/shard_map/ppermute | solution.py:33
  91.3 16.2 %collective-permute-start.13 = (bf16[272,512]{1,0:T(8,128)(2,1)}, bf16[272,512]{1,0:T(8,128)(2,1)S(1)}, u32[]{:S(2)}, u32[]{:S(2)}) collective-permute-start(bf16[272,512]{1,0:T(8,128)(2,1)} %get-tuple-element.19.refs_0_), channel_id=1, source_target_pairs={{0,4},{4,0},{8,12},{12,8},{1,5},{5,1},{9,13},{13,9},{2,6},{6,2},{1... | collective-permute-start | bytes 835592 | tf_op jit(solution)/shard_map/ppermute | solution.py:38
  93.9 26.7 %collective-permute-start.11 = (bf16[272,512]{1,0:T(8,128)(2,1)}, bf16[272,512]{1,0:T(8,128)(2,1)S(1)}, u32[]{:S(2)}, u32[]{:S(2)}) collective-permute-start(bf16[272,512]{1,0:T(8,128)(2,1)} %get-tuple-element.19.refs_0_), channel_id=1, source_target_pairs={{0,2},{2,0},{1,3},{3,1},{4,6},{6,4},{5,7},{7,5},{8,10},{10,8},{9,1... | collective-permute-start | bytes 835592 | tf_op jit(solution)/shard_map/ppermute | solution.py:38
  103.9 23.2 %collective-permute-start.10 = (bf16[272,512]{1,0:T(8,128)(2,1)}, bf16[272,512]{1,0:T(8,128)(2,1)S(1)}, u32[]{:S(2)}, u32[]{:S(2)}) collective-permute-start(bf16[272,512]{1,0:T(8,128)(2,1)} %get-tuple-element.19.refs_0_), channel_id=1, source_target_pairs={{0,1},{1,0},{2,3},{3,2},{4,5},{5,4},{6,7},{7,6},{8,9},{9,8},{10,11... | collective-permute-start | bytes 835592 | tf_op jit(solution)/shard_map/ppermute | solution.py:38
  107.6 21.5 %collective-permute-start.15 = (bf16[272,512]{1,0:T(8,128)(2,1)S(1)}, bf16[272,512]{1,0:T(8,128)(2,1)S(1)}, u32[]{:S(2)}, u32[]{:S(2)}) collective-permute-start(bf16[272,512]{1,0:T(8,128)(2,1)S(1)} %collective-permute-done.13.refs_4_), channel_id=1, source_target_pairs={{0,2},{2,0},{1,3},{3,1},{4,6},{6,4},{5,7},{7,5},{8,10},{10,8},{9,1... | collective-permute-start | bytes 835592 | tf_op jit(solution)/shard_map/ppermute | solution.py:38
  112.9 22.0 %collective-permute-start.20 = (bf16[4,4,32,512]{3,2,1,0:T(8,128)(2,1)S(1)}, bf16[4,4,32,512]{3,2,1,0:T(8,128)(2,1)}, u32[]{:S(2)}, u32[]{:S(2)}) collective-permute-start(bf16[4,4,32,512]{3,2,1,0:T(8,128)(2,1)S(1)} %slice.49), channel_id=1, source_target_pairs={{0,384},{128,0},{256,128},{384,256},{1,385},{129,1},{257,129},{385... | collective-permute-start | bytes 1572872 | tf_op jit(solution)/shard_map/ppermute | solution.py:33
  118.7 16.2 %collective-permute-start.19 = (bf16[4,4,32,512]{3,2,1,0:T(8,128)(2,1)S(1)}, bf16[4,4,32,512]{3,2,1,0:T(8,128)(2,1)}, u32[]{:S(2)}, u32[]{:S(2)}) collective-permute-start(bf16[4,4,32,512]{3,2,1,0:T(8,128)(2,1)S(1)} %slice.48), channel_id=1, source_target_pairs={{0,128},{128,256},{256,384},{384,0},{1,129},{129,257},{257,385},{3... | collective-permute-start | bytes 1572872 | tf_op jit(solution)/shard_map/ppermute | solution.py:33
  120.6 11.5 %collective-permute-start.14 = (bf16[272,512]{1,0:T(8,128)(2,1)S(1)}, bf16[272,512]{1,0:T(8,128)(2,1)S(1)}, u32[]{:S(2)}, u32[]{:S(2)}) collective-permute-start(bf16[272,512]{1,0:T(8,128)(2,1)S(1)} %collective-permute-done.13.refs_4_), channel_id=1, source_target_pairs={{0,1},{1,0},{2,3},{3,2},{4,5},{5,4},{6,7},{7,6},{8,9},{9,8},{10,11... | collective-permute-start | bytes 835592 | tf_op jit(solution)/shard_map/ppermute | solution.py:38
  146.5 8.6 %collective-permute-start.21 = (bf16[2,256,512]{2,1,0:T(8,128)(2,1)}, bf16[2,256,512]{2,1,0:T(8,128)(2,1)S(1)}, u32[]{:S(2)}, u32[]{:S(2)}) collective-permute-start(bf16[2,256,512]{2,1,0:T(8,128)(2,1)} %get-tuple-element.23), channel_id=1, source_target_pairs={{0,1},{1,0},{2,3},{3,2},{4,5},{5,4},{6,7},{7,6},{8,9},{9,8},{10,11... | collective-permute-start | bytes 1572872 | tf_op jit(solution)/shard_map/ppermute | solution.py:38
  149.5 11.8 %collective-permute-start.24 = (bf16[256,512]{1,0:T(8,128)(2,1)S(1)}, bf16[256,512]{1,0:T(8,128)(2,1)S(1)}, u32[]{:S(2)}, u32[]{:S(2)}) collective-permute-start(bf16[256,512]{1,0:T(8,128)(2,1)S(1)} %fusion.4), channel_id=1, source_target_pairs={{0,2},{2,0},{1,3},{3,1},{4,6},{6,4},{5,7},{7,5},{8,10},{10,8},{9,1... | collective-permute-start | bytes 786440 | tf_op jit(solution)/shard_map/ppermute | solution.py:38
  156.1 10.8 %collective-permute-start.22 = (bf16[256,512]{1,0:T(8,128)(2,1)S(1)}, bf16[256,512]{1,0:T(8,128)(2,1)S(1)}, u32[]{:S(2)}, u32[]{:S(2)}) collective-permute-start(bf16[256,512]{1,0:T(8,128)(2,1)S(1)} %fusion.3), channel_id=1, source_target_pairs={{0,2},{2,0},{1,3},{3,1},{4,6},{6,4},{5,7},{7,5},{8,10},{10,8},{9,1... | collective-permute-start | bytes 786440 | tf_op jit(solution)/shard_map/ppermute | solution.py:38
  162.4 15.7 %collective-permute-start.25 = (bf16[256,512]{1,0:T(8,128)(2,1)S(1)}, bf16[256,512]{1,0:T(8,128)(2,1)S(1)}, u32[]{:S(2)}, u32[]{:S(2)}) collective-permute-start(bf16[256,512]{1,0:T(8,128)(2,1)S(1)} %fusion), channel_id=1, source_target_pairs={{0,4},{4,0},{8,12},{12,8},{1,5},{5,1},{9,13},{13,9},{2,6},{6,2},{1... | collective-permute-start | bytes 786440 | tf_op jit(solution)/shard_map/ppermute | solution.py:38
  (14 other events, 316.5 us)
Sparse Core Ops, SparseCore 0:
  26.1 54.7 all-gather.4
  83.0 43.9 all-gather.6

commit v8 on v5

--- a/solution.py
+++ b/solution.py
@@ -126,7 +126,7 @@
 
 
 def normalize_kernel(*refs):
-    parts, outs = refs[:8], refs[8:]
+    parts, out = refs[:8], refs[8]
     for g in range(2):
         square = jnp.zeros((ROWS, 1), F32)
         for p in range(4):
@@ -137,81 +137,119 @@
             extra = parts[4 * g + p][pl.ds(ROWS, EXTRA), :].astype(F32)
             gain = extra[0:1] + extra[1:2] + extra[2:3]
             value = parts[4 * g + p][pl.ds(0, ROWS), :].astype(F32)
-            outs[g][p] = (value * inverse * gain).astype(BF16)
+            at = pl.ds(p % 2 * TP_WIDTH, TP_WIDTH)
+            out[p // 2, pl.ds(g * ROWS, ROWS), at] = (value * inverse * gain).astype(BF16)
 
 
 def normalize(parts):
     return pl.pallas_call(
         normalize_kernel,
-        out_shape=[jax.ShapeDtypeStruct((4, ROWS, TP_WIDTH), BF16)] * 2,
+        out_shape=jax.ShapeDtypeStruct((2, 2 * ROWS, 2 * TP_WIDTH), BF16),
         compiler_params=pltpu.CompilerParams(vmem_limit_bytes=32 << 20),
         cost_estimate=pl.CostEstimate(flops=8 * ROWS * D, bytes_accessed=4 << 20, transcendentals=0),
         name="normalize",
     )(*parts)
 
 
-def feed_forward_kernel(place_ref, x_ref, w_ref, keep_ref, send_ref, acc_ref):
-    step = pl.program_id(0)
-
-    def block(p, kind):
-        pieces = [
-            w_ref[
-                pl.ds(place_ref[p] * 8, 8),
-                pl.ds(place_ref[4 + y], 1),
-                pl.ds(kind * 16, 16),
-                :,
-            ]
-            for y in range(4)
-        ]
-        return jnp.concatenate(pieces, axis=1).reshape(TP_WIDTH, UNIT_BLOCK)
-
-    gate = jnp.zeros((ROWS, UNIT_BLOCK), F32)
-    up = jnp.zeros((ROWS, UNIT_BLOCK), F32)
-    for p in range(4):
-        gate += jnp.dot(x_ref[p], block(p, 0), preferred_element_type=F32)
-        up += jnp.dot(x_ref[p], block(p, 1), preferred_element_type=F32)
-    hidden = (gate / (1.0 + jnp.exp(-gate)) * up).astype(BF16)
-
-    def down(p):
-        return lax.dot_general(
-            hidden, block(p, 2), (((1,), (1,)), ((), ())), preferred_element_type=F32
-        )
-
-    @pl.when(step == 0)
-    def _():
-        for p in range(4):
-            acc_ref[p] = down(p)
-
-    @pl.when(step == 1)
-    def _():
-        for i, p in enumerate((2, 0)):
-            send_ref[i] = (acc_ref[p + 1] + down(p + 1)).astype(BF16)
-            keep_ref[i] = (acc_ref[p] + down(p)).astype(BF16)
+def pieces_of(w_ref, p, place_ref, low_row, low, width):
+    pieces = [
+        w_ref[p, :, pl.ds(place_ref[4 + y], 1), pl.ds(low_row, 16), pl.ds(low, width)]
+        for y in range(4)
+    ]
+    return jnp.concatenate(pieces, axis=1).reshape(TP_WIDTH, width)
+
+
+def down_projection(hidden_ref, rows, out_own, out_partner, i):
+    product = lax.dot_general(
+        hidden_ref[...], rows, (((1,), (1,)), ((), ())), preferred_element_type=F32
+    ).astype(BF16)
+    out_own[i] = product[:ROWS]
+    out_partner[i] = product[ROWS:]
+
+
+def hidden_kernel(place_ref, x_hbm, w_hbm, hidden_ref, own_ref, partner_ref, x_ref, w_ref, gate_ref, up_ref, sems):
+    copies = []
+    for j in range(2):
+        copies.append(pltpu.make_async_copy(x_hbm.at[j], x_ref.at[j], sems.at[3 * j]))
+        for p in (2 * j, 2 * j + 1):
+            source = w_hbm.at[pl.ds(place_ref[p] * 8, 8)]
+            copies.append(pltpu.make_async_copy(source, w_ref.at[p], sems.at[3 * j + 1 + p % 2]))
+    for copy in copies:
+        copy.start()
+    units = w_ref.shape[4]
+    for j in range(2):
+        for copy in copies[3 * j : 3 * j + 3]:
+            copy.wait()
+        for low in range(0, units, UNIT_BLOCK):
+            at = pl.ds(low, UNIT_BLOCK)
+            totals = []
+            for kind, total_ref in ((0, gate_ref), (1, up_ref)):
+                rows = jnp.concatenate(
+                    [pieces_of(w_ref, 2 * j + i, place_ref, 16 * kind, low, UNIT_BLOCK) for i in range(2)],
+                    axis=0,
+                )
+                total = jnp.dot(x_ref[j], rows, preferred_element_type=F32)
+                if j == 0:
+                    total_ref[:, at] = total
+                else:
+                    totals.append(total_ref[:, at] + total)
+            if j == 1:
+                gate, up = totals
+                hidden_ref[:, at] = (gate / (1.0 + jnp.exp(-gate)) * up).astype(BF16)
+    for i, p in enumerate((3, 1)):
+        rows = pieces_of(w_ref, p, place_ref, 32, 0, units)
+        down_projection(hidden_ref, rows, own_ref, partner_ref, i)
+
+
+def keep_kernel(place_ref, hidden_hbm, w_hbm, own_ref, partner_ref, hidden_ref, w_ref, sems):
+    copies = [pltpu.make_async_copy(hidden_hbm, hidden_ref, sems.at[2])]
+    for i, p in enumerate((2, 0)):
+        source = w_hbm.at[pl.ds(place_ref[p] * 8, 8), :, pl.ds(32, 16)]
+        copies.append(pltpu.make_async_copy(source, w_ref.at[i], sems.at[i]))
+    for copy in copies:
+        copy.start()
+    for copy in copies:
+        copy.wait()
+    for i in range(2):
+        rows = pieces_of(w_ref, i, place_ref, 0, 0, w_ref.shape[4])
+        down_projection(hidden_ref, rows, own_ref, partner_ref, i)
 
 
 def feed_forward(place, x, weights):
-    pair = pl.BlockSpec((2, ROWS, TP_WIDTH), lambda i, o: (0, 0, 0))
     units = weights.shape[3]
-    assert units == 2 * UNIT_BLOCK
-    return pl.pallas_call(
-        feed_forward_kernel,
-        out_shape=[jax.ShapeDtypeStruct((2, ROWS, TP_WIDTH), BF16)] * 2,
-        grid_spec=pltpu.PrefetchScalarGridSpec(
-            num_scalar_prefetch=1,
-            grid=(2,),
-            in_specs=[
-                pl.BlockSpec((4, ROWS, TP_WIDTH), lambda i, o: (0, 0, 0)),
-                pl.BlockSpec((32, 4, 48, UNIT_BLOCK), lambda i, o: (0, 0, 0, i)),
-            ],
-            out_specs=[pair] * 2,
-            scratch_shapes=[pltpu.VMEM((4, ROWS, TP_WIDTH), F32)],
-        ),
+    pair = jax.ShapeDtypeStruct((2, ROWS, TP_WIDTH), BF16)
+    flops = 4 * ROWS * D * units
+    hidden, own_send, partner_send = pl.pallas_call(
+        hidden_kernel,
+        out_shape=(jax.ShapeDtypeStruct((2 * ROWS, units), BF16), pair, pair),
+        in_specs=[SMEM, HBM, HBM],
+        scratch_shapes=[
+            pltpu.VMEM((2, 2 * ROWS, 2 * TP_WIDTH), BF16),
+            pltpu.VMEM((4, 8, 4, 48, units), BF16),
+            pltpu.VMEM((2 * ROWS, units), F32),
+            pltpu.VMEM((2 * ROWS, units), F32),
+            pltpu.SemaphoreType.DMA((6,)),
+        ],
         compiler_params=pltpu.CompilerParams(vmem_limit_bytes=58 << 20),
         cost_estimate=pl.CostEstimate(
-            flops=6 * ROWS * D * units, bytes_accessed=8 << 20, transcendentals=ROWS * units
+            flops=5 * flops // 2, bytes_accessed=10 << 20, transcendentals=2 * ROWS * units
         ),
-        name="feed_forward",
+        name="hidden",
     )(place, x, weights)
+    own_keep, partner_keep = pl.pallas_call(
+        keep_kernel,
+        out_shape=(pair, pair),
+        in_specs=[SMEM, HBM, HBM],
+        scratch_shapes=[
+            pltpu.VMEM((2 * ROWS, units), BF16),
+            pltpu.VMEM((2, 8, 4, 16, units), BF16),
+            pltpu.SemaphoreType.DMA((3,)),
+        ],
+        compiler_params=pltpu.CompilerParams(vmem_limit_bytes=58 << 20),
+        cost_estimate=pl.CostEstimate(flops=flops // 2, bytes_accessed=3 << 20, transcendentals=0),
+        name="keep",
+    )(place, hidden, weights)
+    return own_keep, own_send, partner_keep, partner_send
 
 
 def on_device(
@@ -256,10 +294,9 @@
     own = 2 * lax.axis_index("yl") + lax.axis_index("c")
     place = [own, own ^ 1, own ^ 2, own ^ 3] + [(yh - y) & 3 for y in range(4)]
     place = jnp.stack(place).astype(jnp.int32)
-    own_x, partner_x = normalize(parts)
-    partner_keep, partner_send = feed_forward(place, partner_x, weights)
-    own_x, partner_send = lax.optimization_barrier((own_x, partner_send))
-    own_keep, own_send = feed_forward(place, own_x, weights)
+    own_keep, own_send, partner_keep, partner_send = feed_forward(
+        place, normalize(parts), weights
+    )
 
     def add(left, right):
         return left.astype(F32) + right.astype(F32)

time: 191 us -> 191 us (level)
  Pallas kernels: 18.7 us -> 16.5 us
    pallas_call x3, Pallas kernels: 13.6 us -> 11.5 us  [the longest x1 6.85 us: feed_forward(): pl.pallas_call(hidden_kernel, out_shape=(jax.ShapeDtypeStruct((2 * ROWS,...]
  transfers between devices with their start and end apart: 20 -> 20, of which waited for: 10 -> 10; matrix products, arithmetic and copies ran while one was open for 2% -> 3% of each run, Pallas kernels for 7% -> 5%
where the time goes in v8:
time: 191 us; the launch traced here: 190 us
  waiting for transfers between devices  81 us (42%)
  starting transfers between devices  65.6 us (34%)
  Pallas kernels  16.5 us (9%)
  between operations  14.4 us (8%)
  other arithmetic  8.25 us (4%)
  local copies, waits for them, and re-layouts  3.93 us (2%)
    ppermute x12, starting transfers between devices, swap(): return lax.ppermute(value, axis, [(i, i ^ 1) for i in range(size)])  34 us
    ppermute x4, waiting for transfers between devices, from_behind(): return lax.ppermute(value, SEQ, [(i, i + by) for i in range(size - by)])  30.9 us
    all_gather x1, waiting for transfers between devices, on_device(): weights = lax.all_gather(near, ('x', 'z'), axis=0)  23.7 us
    ppermute x12, waiting for transfers between devices, swap(): return lax.ppermute(value, axis, [(i, i ^ 1) for i in range(size)])  23.6 us
    ppermute x4, starting transfers between devices, from_behind(): return lax.ppermute(value, SEQ, [(i, i + by) for i in range(size - by)])  17.1 us
    ppermute x3, starting transfers between devices, around(): lax.ppermute(value, axis, [(i, (i + by) % size) for i in range(size)])  14.5 us
    pallas_call x1, Pallas kernels, feed_forward(): pl.pallas_call(hidden_kernel, out_shape=(jax.ShapeDtypeStruct((2 * ROWS,...  6.85 us
    pallas_call x1, Pallas kernels, attention(): pl.pallas_call(attention_kernel, out_shape=(jax.ShapeDtypeStruct((ROWS, T...  5.07 us
  transfers between devices with their start and end apart: 20, of which 10 were waited for; matrix products, arithmetic and copies ran while one was open for 3% of the time, Pallas kernels for 5%

profile of v8, /device:TPU:1, one launch (start us, length us, event | category | flops | bytes accessed | tf_op | source)
XLA Modules:
  0.0 189.7 jit_solution(10192061365126685546)
XLA Ops:
  8.0 6.7 %collective-permute-start.13 = (bf16[48,512]{1,0:T(8,128)(2,1)S(1)}, bf16[48,512]{1,0:T(8,128)(2,1)S(1)}, u32[]{:S(2)}, u32[]{:S(2)}) collective-permute-start(bf16[48,512]{1,0:T(8,128)(2,1)S(1)} %get-tuple-element.17), channel_id=1, source_target_pairs={{0,12},{4,0},{8,4},{12,8},{1,13},{5,1},{9,5},{13,9},{2,14},{6,2},{... | collective-permute-start | bytes 147464 | tf_op jit(solution)/shard_map/ppermute | solution.py:33
  14.7 3.5 %collective-permute-start.12 = (bf16[48,512]{1,0:T(8,128)(2,1)S(1)}, bf16[48,512]{1,0:T(8,128)(2,1)S(1)}, u32[]{:S(2)}, u32[]{:S(2)}) collective-permute-start(bf16[48,512]{1,0:T(8,128)(2,1)S(1)} %get-tuple-element.16), channel_id=1, source_target_pairs={{0,8},{4,12},{8,0},{12,4},{1,9},{5,13},{9,1},{13,5},{2,10},{6,14},... | collective-permute-start | bytes 147464 | tf_op jit(solution)/shard_map/ppermute | solution.py:33
  18.3 4.2 %collective-permute-start.11 = (bf16[48,512]{1,0:T(8,128)(2,1)S(1)}, bf16[48,512]{1,0:T(8,128)(2,1)S(1)}, u32[]{:S(2)}, u32[]{:S(2)}) collective-permute-start(bf16[48,512]{1,0:T(8,128)(2,1)S(1)} %get-tuple-element.17), channel_id=1, source_target_pairs={{0,4},{4,8},{8,12},{12,0},{1,5},{5,9},{9,13},{13,1},{2,6},{6,10},{... | collective-permute-start | bytes 147464 | tf_op jit(solution)/shard_map/ppermute | solution.py:33
  27.9 3.0 %collective-permute-start = (bf16[272,512]{1,0:T(8,128)(2,1)S(1)}, bf16[272,512]{1,0:T(8,128)(2,1)S(1)}, u32[]{:S(2)}, u32[]{:S(2)}) collective-permute-start(bf16[272,512]{1,0:T(8,128)(2,1)S(1)} %pad_maximum_fusion.refs_1_), channel_id=1, source_target_pairs={{0,4},{4,8},{8,12},{12,16},{16,20},{20,24},{24,28},{28,32},{32,36}... | collective-permute-start | bytes 835592 | tf_op jit(solution)/shard_map/ppermute | solution.py:28
  30.9 4.9 %collective-permute-start.1 = (bf16[256,512]{1,0:T(8,128)(2,1)}, bf16[256,512]{1,0:T(8,128)(2,1)S(1)}, u32[]{:S(2)}, u32[]{:S(2)}) collective-permute-start(bf16[256,512]{1,0:T(8,128)(2,1)} %refs_2_.1), channel_id=1, source_target_pairs={{0,4},{4,8},{8,12},{12,16},{16,20},{20,24},{24,28},{28,32},{32,36}... | collective-permute-start | bytes 786440 | tf_op jit(solution)/shard_map/ppermute | solution.py:28
  35.9 4.2 %collective-permute-start.2 = (bf16[272,512]{1,0:T(8,128)(2,1)S(1)}, bf16[272,512]{1,0:T(8,128)(2,1)S(1)}, u32[]{:S(2)}, u32[]{:S(2)}) collective-permute-start(bf16[272,512]{1,0:T(8,128)(2,1)S(1)} %collective-permute-done.refs_3_), channel_id=1, source_target_pairs={{0,4},{4,8},{8,12},{12,16},{16,20},{20,24},{24,28},{28,32},{32,36}... | collective-permute-start | bytes 835592 | tf_op jit(solution)/shard_map/ppermute | solution.py:28
  40.1 10.6 %collective-permute-done.1.refs_4_ = bf16[256,512]{1,0:T(8,128)(2,1)S(1)} collective-permute-done((bf16[256,512]{1,0:T(8,128)(2,1)}, bf16[256,512]{1,0:T(8,128)(2,1)S(1)}, u32[]{:S(2)}, u32[]{:S(2)}) %collective-permute-start.1) | collective-permute-done | bytes 262176 | tf_op jit(solution)/shard_map/ppermute | solution.py:28
  50.6 5.0 %collective-permute-start.3 = (bf16[256,512]{1,0:T(8,128)(2,1)S(1)}, bf16[256,512]{1,0:T(8,128)(2,1)S(1)}, u32[]{:S(2)}, u32[]{:S(2)}) collective-permute-start(bf16[256,512]{1,0:T(8,128)(2,1)S(1)} %collective-permute-done.1.refs_4_), channel_id=1, source_target_pairs={{0,4},{4,8},{8,12},{12,16},{16,20},{20,24},{24,28},{28,32},{32,36}... | collective-permute-start | bytes 786440 | tf_op jit(solution)/shard_map/ppermute | solution.py:28
  55.7 20.3 %collective-permute-done.3.refs_6_ = bf16[256,512]{1,0:T(8,128)(2,1)S(1)} collective-permute-done((bf16[256,512]{1,0:T(8,128)(2,1)S(1)}, bf16[256,512]{1,0:T(8,128)(2,1)S(1)}, u32[]{:S(2)}, u32[]{:S(2)}) %collective-permute-start.3) | collective-permute-done | bytes 262176 | tf_op jit(solution)/shard_map/ppermute | solution.py:28
  76.8 5.1 %attention.1 = (bf16[256,512]{1,0:T(8,128)(2,1)}, bf16[272,512]{1,0:T(8,128)(2,1)}) custom-call(s32[2]{0:T(128)} %lengths_ref.1, f32[1,512]{1,0:T(1,128)} %bitcast.36, bf16[256,512]{1,0:T(8,128)(2,1)} %refs_0_.1, bf16[272,512]{1,0:T(8,128)(2,1)} %copy-done.3, bf16[256,512]{1,0:T(8,128)(2,1)} %refs_2_.1, bf16[272,512]{1,0:T(8,128)(2,1)} %copy-done.4, ...), custom_call_target="tpu_custom_call" | custom-call | flops 402653184 | bytes 3145728 | tf_op jit(solution)/shard_map/attention/pallas_call | solution.py:108
  81.9 5.0 %collective-permute-start.7 = (bf16[272,512]{1,0:T(8,128)(2,1)}, bf16[272,512]{1,0:T(8,128)(2,1)S(1)}, u32[]{:S(2)}, u32[]{:S(2)}) collective-permute-start(bf16[272,512]{1,0:T(8,128)(2,1)} %get-tuple-element.10.refs_0_), channel_id=1, source_target_pairs={{0,4},{4,0},{8,12},{12,8},{1,5},{5,1},{9,13},{13,9},{2,6},{6,2},{1... | collective-permute-start | bytes 835592 | tf_op jit(solution)/shard_map/ppermute | solution.py:38
  88.8 9.4 %collective-permute-done.7.refs_4_ = bf16[272,512]{1,0:T(8,128)(2,1)S(1)} collective-permute-done((bf16[272,512]{1,0:T(8,128)(2,1)}, bf16[272,512]{1,0:T(8,128)(2,1)S(1)}, u32[]{:S(2)}, u32[]{:S(2)}) %collective-permute-start.7) | collective-permute-done | bytes 278560 | tf_op jit(solution)/shard_map/ppermute | solution.py:38
  100.1 3.0 %collective-permute-start.4 = (bf16[272,512]{1,0:T(8,128)(2,1)}, bf16[272,512]{1,0:T(8,128)(2,1)S(1)}, u32[]{:S(2)}, u32[]{:S(2)}) collective-permute-start(bf16[272,512]{1,0:T(8,128)(2,1)} %get-tuple-element.10.refs_0_), channel_id=1, source_target_pairs={{0,1},{1,0},{2,3},{3,2},{4,5},{5,4},{6,7},{7,6},{8,9},{9,8},{10,11... | collective-permute-start | bytes 835592 | tf_op jit(solution)/shard_map/ppermute | solution.py:38
  105.1 2.4 %collective-permute-start.6 = (bf16[272,512]{1,0:T(8,128)(2,1)S(1)}, bf16[272,512]{1,0:T(8,128)(2,1)S(1)}, u32[]{:S(2)}, u32[]{:S(2)}) collective-permute-start(bf16[272,512]{1,0:T(8,128)(2,1)S(1)} %collective-permute-done.5.refs_2_), channel_id=1, source_target_pairs={{0,1},{1,0},{2,3},{3,2},{4,5},{5,4},{6,7},{7,6},{8,9},{9,8},{10,11... | collective-permute-start | bytes 835592 | tf_op jit(solution)/shard_map/ppermute | solution.py:38
  107.5 3.6 %collective-permute-start.10 = (bf16[272,512]{1,0:T(8,128)(2,1)S(1)}, bf16[272,512]{1,0:T(8,128)(2,1)S(1)}, u32[]{:S(2)}, u32[]{:S(2)}) collective-permute-start(bf16[272,512]{1,0:T(8,128)(2,1)S(1)} %collective-permute-done.9.refs_6_), channel_id=1, source_target_pairs={{0,1},{1,0},{2,3},{3,2},{4,5},{5,4},{6,7},{7,6},{8,9},{9,8},{10,11... | collective-permute-start | bytes 835592 | tf_op jit(solution)/shard_map/ppermute | solution.py:38
  115.5 23.7 %all-gather.3.cloned.1.call-done = bf16[128,48,512]{2,1,0:T(8,128)(2,1)} async-done(((bf16[4,48,512]{2,1,0:T(8,128)(2,1)}), bf16[128,48,512]{2,1,0:T(8,128)(2,1)}) %all-gather.3.cloned.1.call-update) | async-done | bytes 6291472 | tf_op jit(solution)/shard_map/all_gather | solution.py:276
  139.3 6.9 %hidden.1 = (bf16[512,512]{1,0:T(8,128)(2,1)}, bf16[2,256,512]{2,1,0:T(8,128)(2,1)}, bf16[2,256,512]{2,1,0:T(8,128)(2,1)}) custom-call(s32[8]{0:T(128)} %stack.50.place_ref, bf16[2,512,1024]{2,1,0:T(8,128)(2,1)} %copy-done, bf16[32,4,48,512]{3,2,1,0:T(8,128)(2,1)} %bitcast.29), custom_call_target="tpu_custom_call" | custom-call | flops 2684354560 | bytes 10485760 | tf_op jit(solution)/shard_map/hidden/pallas_call | solution.py:222
  146.2 3.0 %collective-permute-start.16 = (bf16[2,256,512]{2,1,0:T(8,128)(2,1)}, bf16[2,256,512]{2,1,0:T(8,128)(2,1)S(1)}, u32[]{:S(2)}, u32[]{:S(2)}) collective-permute-start(bf16[2,256,512]{2,1,0:T(8,128)(2,1)} %get-tuple-element.15), channel_id=1, source_target_pairs={{0,1},{1,0},{2,3},{3,2},{4,5},{5,4},{6,7},{7,6},{8,9},{9,8},{10,11... | collective-permute-start | bytes 1572872 | tf_op jit(solution)/shard_map/ppermute | solution.py:38
  151.1 3.7 %keep.1 = (bf16[2,256,512]{2,1,0:T(8,128)(2,1)}, bf16[2,256,512]{2,1,0:T(8,128)(2,1)}) custom-call(s32[8]{0:T(128)} %stack.50.place_ref, bf16[512,512]{1,0:T(8,128)(2,1)} %get-tuple-element.11.hidden_hbm, bf16[32,4,48,512]{3,2,1,0:T(8,128)(2,1)} %bitcast.30), custom_call_target="tpu_custom_call" | custom-call | flops 536870912 | bytes 3145728 | tf_op jit(solution)/shard_map/keep/pallas_call | solution.py:239
  155.8 3.1 %collective-permute-start.17 = (bf16[256,512]{1,0:T(8,128)(2,1)S(1)}, bf16[256,512]{1,0:T(8,128)(2,1)S(1)}, u32[]{:S(2)}, u32[]{:S(2)}) collective-permute-start(bf16[256,512]{1,0:T(8,128)(2,1)S(1)} %fusion.4), channel_id=1, source_target_pairs={{0,2},{2,0},{1,3},{3,1},{4,6},{6,4},{5,7},{7,5},{8,10},{10,8},{9,1... | collective-permute-start | bytes 786440 | tf_op jit(solution)/shard_map/ppermute | solution.py:38
  160.0 2.2 %collective-permute-start.15 = (bf16[256,512]{1,0:T(8,128)(2,1)S(1)}, bf16[256,512]{1,0:T(8,128)(2,1)S(1)}, u32[]{:S(2)}, u32[]{:S(2)}) collective-permute-start(bf16[256,512]{1,0:T(8,128)(2,1)S(1)} %fusion.3), channel_id=1, source_target_pairs={{0,2},{2,0},{1,3},{3,1},{4,6},{6,4},{5,7},{7,5},{8,10},{10,8},{9,1... | collective-permute-start | bytes 786440 | tf_op jit(solution)/shard_map/ppermute | solution.py:38
  162.1 2.9 %collective-permute-done.17 = bf16[256,512]{1,0:T(8,128)(2,1)S(1)} collective-permute-done((bf16[256,512]{1,0:T(8,128)(2,1)S(1)}, bf16[256,512]{1,0:T(8,128)(2,1)S(1)}, u32[]{:S(2)}, u32[]{:S(2)}) %collective-permute-start.17) | collective-permute-done | bytes 262176 | tf_op jit(solution)/shard_map/ppermute | solution.py:38
  166.1 4.0 %collective-permute-start.18 = (bf16[256,512]{1,0:T(8,128)(2,1)S(1)}, bf16[256,512]{1,0:T(8,128)(2,1)S(1)}, u32[]{:S(2)}, u32[]{:S(2)}) collective-permute-start(bf16[256,512]{1,0:T(8,128)(2,1)S(1)} %fusion), channel_id=1, source_target_pairs={{0,4},{4,0},{8,12},{12,8},{1,5},{5,1},{9,13},{13,9},{2,6},{6,2},{1... | collective-permute-start | bytes 786440 | tf_op jit(solution)/shard_map/ppermute | solution.py:38
  170.7 10.2 %collective-permute-done.18 = bf16[256,512]{1,0:T(8,128)(2,1)S(1)} collective-permute-done((bf16[256,512]{1,0:T(8,128)(2,1)S(1)}, bf16[256,512]{1,0:T(8,128)(2,1)S(1)}, u32[]{:S(2)}, u32[]{:S(2)}) %collective-permute-start.18) | collective-permute-done | bytes 262176 | tf_op jit(solution)/shard_map/ppermute | solution.py:38
  (52 shorter events, 24.7 us)
Async XLA Ops:
  7.2 132.1 %all-gather.3.cloned.1.call-start = ((), (), s32[]{:S(2)}) async-start(), calls=%async_computation | async-start | bytes 6488064 | tf_op jit(solution)/shard_map/all_gather | solution.py:276
  8.0 14.5 %collective-permute-start.13 = (bf16[48,512]{1,0:T(8,128)(2,1)S(1)}, bf16[48,512]{1,0:T(8,128)(2,1)S(1)}, u32[]{:S(2)}, u32[]{:S(2)}) collective-permute-start(bf16[48,512]{1,0:T(8,128)(2,1)S(1)} %get-tuple-element.17), channel_id=1, source_target_pairs={{0,12},{4,0},{8,4},{12,8},{1,13},{5,1},{9,5},{13,9},{2,14},{6,2},{... | collective-permute-start | bytes 147464 | tf_op jit(solution)/shard_map/ppermute | solution.py:33
  14.7 8.7 %collective-permute-start.12 = (bf16[48,512]{1,0:T(8,128)(2,1)S(1)}, bf16[48,512]{1,0:T(8,128)(2,1)S(1)}, u32[]{:S(2)}, u32[]{:S(2)}) collective-permute-start(bf16[48,512]{1,0:T(8,128)(2,1)S(1)} %get-tuple-element.16), channel_id=1, source_target_pairs={{0,8},{4,12},{8,0},{12,4},{1,9},{5,13},{9,1},{13,5},{2,10},{6,14},... | collective-permute-start | bytes 147464 | tf_op jit(solution)/shard_map/ppermute | solution.py:33
  18.3 7.0 %collective-permute-start.11 = (bf16[48,512]{1,0:T(8,128)(2,1)S(1)}, bf16[48,512]{1,0:T(8,128)(2,1)S(1)}, u32[]{:S(2)}, u32[]{:S(2)}) collective-permute-start(bf16[48,512]{1,0:T(8,128)(2,1)S(1)} %get-tuple-element.17), channel_id=1, source_target_pairs={{0,4},{4,8},{8,12},{12,0},{1,5},{5,9},{9,13},{13,1},{2,6},{6,10},{... | collective-permute-start | bytes 147464 | tf_op jit(solution)/shard_map/ppermute | solution.py:33
  27.9 48.1 %copy-start.3 = (bf16[272,512]{1,0:T(8,128)(2,1)}, bf16[272,512]{1,0:T(8,128)(2,1)S(1)}, u32[]{:S(2)}) copy-start(bf16[272,512]{1,0:T(8,128)(2,1)S(1)} %pad_maximum_fusion.refs_1_) | copy-start | bytes 835588
  27.9 7.9 %collective-permute-start = (bf16[272,512]{1,0:T(8,128)(2,1)S(1)}, bf16[272,512]{1,0:T(8,128)(2,1)S(1)}, u32[]{:S(2)}, u32[]{:S(2)}) collective-permute-start(bf16[272,512]{1,0:T(8,128)(2,1)S(1)} %pad_maximum_fusion.refs_1_), channel_id=1, source_target_pairs={{0,4},{4,8},{8,12},{12,16},{16,20},{20,24},{24,28},{28,32},{32,36}... | collective-permute-start | bytes 835592 | tf_op jit(solution)/shard_map/ppermute | solution.py:28
  30.9 19.7 %collective-permute-start.1 = (bf16[256,512]{1,0:T(8,128)(2,1)}, bf16[256,512]{1,0:T(8,128)(2,1)S(1)}, u32[]{:S(2)}, u32[]{:S(2)}) collective-permute-start(bf16[256,512]{1,0:T(8,128)(2,1)} %refs_2_.1), channel_id=1, source_target_pairs={{0,4},{4,8},{8,12},{12,16},{16,20},{20,24},{24,28},{28,32},{32,36}... | collective-permute-start | bytes 786440 | tf_op jit(solution)/shard_map/ppermute | solution.py:28
  35.9 40.2 %copy-start.4 = (bf16[272,512]{1,0:T(8,128)(2,1)}, bf16[272,512]{1,0:T(8,128)(2,1)S(1)}, u32[]{:S(2)}) copy-start(bf16[272,512]{1,0:T(8,128)(2,1)S(1)} %collective-permute-done.refs_3_) | copy-start | bytes 835588
  35.9 40.1 %collective-permute-start.2 = (bf16[272,512]{1,0:T(8,128)(2,1)S(1)}, bf16[272,512]{1,0:T(8,128)(2,1)S(1)}, u32[]{:S(2)}, u32[]{:S(2)}) collective-permute-start(bf16[272,512]{1,0:T(8,128)(2,1)S(1)} %collective-permute-done.refs_3_), channel_id=1, source_target_pairs={{0,4},{4,8},{8,12},{12,16},{16,20},{20,24},{24,28},{28,32},{32,36}... | collective-permute-start | bytes 835592 | tf_op jit(solution)/shard_map/ppermute | solution.py:28
  50.6 25.4 %collective-permute-start.3 = (bf16[256,512]{1,0:T(8,128)(2,1)S(1)}, bf16[256,512]{1,0:T(8,128)(2,1)S(1)}, u32[]{:S(2)}, u32[]{:S(2)}) collective-permute-start(bf16[256,512]{1,0:T(8,128)(2,1)S(1)} %collective-permute-done.1.refs_4_), channel_id=1, source_target_pairs={{0,4},{4,8},{8,12},{12,16},{16,20},{20,24},{24,28},{28,32},{32,36}... | collective-permute-start | bytes 786440 | tf_op jit(solution)/shard_map/ppermute | solution.py:28
  81.9 16.3 %collective-permute-start.7 = (bf16[272,512]{1,0:T(8,128)(2,1)}, bf16[272,512]{1,0:T(8,128)(2,1)S(1)}, u32[]{:S(2)}, u32[]{:S(2)}) collective-permute-start(bf16[272,512]{1,0:T(8,128)(2,1)} %get-tuple-element.10.refs_0_), channel_id=1, source_target_pairs={{0,4},{4,0},{8,12},{12,8},{1,5},{5,1},{9,13},{13,9},{2,6},{6,2},{1... | collective-permute-start | bytes 835592 | tf_op jit(solution)/shard_map/ppermute | solution.py:38
  86.9 18.2 %collective-permute-start.5 = (bf16[272,512]{1,0:T(8,128)(2,1)}, bf16[272,512]{1,0:T(8,128)(2,1)S(1)}, u32[]{:S(2)}, u32[]{:S(2)}) collective-permute-start(bf16[272,512]{1,0:T(8,128)(2,1)} %get-tuple-element.10.refs_0_), channel_id=1, source_target_pairs={{0,2},{2,0},{1,3},{3,1},{4,6},{6,4},{5,7},{7,5},{8,10},{10,8},{9,1... | collective-permute-start | bytes 835592 | tf_op jit(solution)/shard_map/ppermute | solution.py:38
  98.2 9.3 %collective-permute-start.9 = (bf16[272,512]{1,0:T(8,128)(2,1)S(1)}, bf16[272,512]{1,0:T(8,128)(2,1)S(1)}, u32[]{:S(2)}, u32[]{:S(2)}) collective-permute-start(bf16[272,512]{1,0:T(8,128)(2,1)S(1)} %collective-permute-done.7.refs_4_), channel_id=1, source_target_pairs={{0,2},{2,0},{1,3},{3,1},{4,6},{6,4},{5,7},{7,5},{8,10},{10,8},{9,1... | collective-permute-start | bytes 835592 | tf_op jit(solution)/shard_map/ppermute | solution.py:38
  100.1 11.6 %collective-permute-start.4 = (bf16[272,512]{1,0:T(8,128)(2,1)}, bf16[272,512]{1,0:T(8,128)(2,1)S(1)}, u32[]{:S(2)}, u32[]{:S(2)}) collective-permute-start(bf16[272,512]{1,0:T(8,128)(2,1)} %get-tuple-element.10.refs_0_), channel_id=1, source_target_pairs={{0,1},{1,0},{2,3},{3,2},{4,5},{5,4},{6,7},{7,6},{8,9},{9,8},{10,11... | collective-permute-start | bytes 835592 | tf_op jit(solution)/shard_map/ppermute | solution.py:38
  103.1 8.6 %collective-permute-start.8 = (bf16[272,512]{1,0:T(8,128)(2,1)S(1)}, bf16[272,512]{1,0:T(8,128)(2,1)S(1)}, u32[]{:S(2)}, u32[]{:S(2)}) collective-permute-start(bf16[272,512]{1,0:T(8,128)(2,1)S(1)} %collective-permute-done.7.refs_4_), channel_id=1, source_target_pairs={{0,1},{1,0},{2,3},{3,2},{4,5},{5,4},{6,7},{7,6},{8,9},{9,8},{10,11... | collective-permute-start | bytes 835592 | tf_op jit(solution)/shard_map/ppermute | solution.py:38
  105.1 6.6 %collective-permute-start.6 = (bf16[272,512]{1,0:T(8,128)(2,1)S(1)}, bf16[272,512]{1,0:T(8,128)(2,1)S(1)}, u32[]{:S(2)}, u32[]{:S(2)}) collective-permute-start(bf16[272,512]{1,0:T(8,128)(2,1)S(1)} %collective-permute-done.5.refs_2_), channel_id=1, source_target_pairs={{0,1},{1,0},{2,3},{3,2},{4,5},{5,4},{6,7},{7,6},{8,9},{9,8},{10,11... | collective-permute-start | bytes 835592 | tf_op jit(solution)/shard_map/ppermute | solution.py:38
  107.5 4.7 %collective-permute-start.10 = (bf16[272,512]{1,0:T(8,128)(2,1)S(1)}, bf16[272,512]{1,0:T(8,128)(2,1)S(1)}, u32[]{:S(2)}, u32[]{:S(2)}) collective-permute-start(bf16[272,512]{1,0:T(8,128)(2,1)S(1)} %collective-permute-done.9.refs_6_), channel_id=1, source_target_pairs={{0,1},{1,0},{2,3},{3,2},{4,5},{5,4},{6,7},{7,6},{8,9},{9,8},{10,11... | collective-permute-start | bytes 835592 | tf_op jit(solution)/shard_map/ppermute | solution.py:38
  146.1 34.8 %copy-start.2 = (f32[256,512]{1,0:T(8,128)S(1)}, f32[256,512]{1,0:T(8,128)}, u32[]{:S(2)}) copy-start(f32[256,512]{1,0:T(8,128)} %refs_7_.1) | copy-start | bytes 1572868
  146.1 34.8 %copy-start.6 = (bf16[256,512]{1,0:T(8,128)(2,1)S(1)}, bf16[256,512]{1,0:T(8,128)(2,1)}, u32[]{:S(2)}) copy-start(bf16[256,512]{1,0:T(8,128)(2,1)} %get-tuple-element.7) | copy-start | bytes 786436
  146.2 8.6 %collective-permute-start.16 = (bf16[2,256,512]{2,1,0:T(8,128)(2,1)}, bf16[2,256,512]{2,1,0:T(8,128)(2,1)S(1)}, u32[]{:S(2)}, u32[]{:S(2)}) collective-permute-start(bf16[2,256,512]{2,1,0:T(8,128)(2,1)} %get-tuple-element.15), channel_id=1, source_target_pairs={{0,1},{1,0},{2,3},{3,2},{4,5},{5,4},{6,7},{7,6},{8,9},{9,8},{10,11... | collective-permute-start | bytes 1572872 | tf_op jit(solution)/shard_map/ppermute | solution.py:38
  149.2 9.8 %collective-permute-start.14 = (bf16[2,256,512]{2,1,0:T(8,128)(2,1)}, bf16[2,256,512]{2,1,0:T(8,128)(2,1)S(1)}, u32[]{:S(2)}, u32[]{:S(2)}) collective-permute-start(bf16[2,256,512]{2,1,0:T(8,128)(2,1)} %get-tuple-element.13), channel_id=1, source_target_pairs={{0,1},{1,0},{2,3},{3,2},{4,5},{5,4},{6,7},{7,6},{8,9},{9,8},{10,11... | collective-permute-start | bytes 1572872 | tf_op jit(solution)/shard_map/ppermute | solution.py:38
  155.8 9.3 %collective-permute-start.17 = (bf16[256,512]{1,0:T(8,128)(2,1)S(1)}, bf16[256,512]{1,0:T(8,128)(2,1)S(1)}, u32[]{:S(2)}, u32[]{:S(2)}) collective-permute-start(bf16[256,512]{1,0:T(8,128)(2,1)S(1)} %fusion.4), channel_id=1, source_target_pairs={{0,2},{2,0},{1,3},{3,1},{4,6},{6,4},{5,7},{7,5},{8,10},{10,8},{9,1... | collective-permute-start | bytes 786440 | tf_op jit(solution)/shard_map/ppermute | solution.py:38
  160.0 10.7 %collective-permute-start.15 = (bf16[256,512]{1,0:T(8,128)(2,1)S(1)}, bf16[256,512]{1,0:T(8,128)(2,1)S(1)}, u32[]{:S(2)}, u32[]{:S(2)}) collective-permute-start(bf16[256,512]{1,0:T(8,128)(2,1)S(1)} %fusion.3), channel_id=1, source_target_pairs={{0,2},{2,0},{1,3},{3,1},{4,6},{6,4},{5,7},{7,5},{8,10},{10,8},{9,1... | collective-permute-start | bytes 786440 | tf_op jit(solution)/shard_map/ppermute | solution.py:38
  166.1 14.8 %collective-permute-start.18 = (bf16[256,512]{1,0:T(8,128)(2,1)S(1)}, bf16[256,512]{1,0:T(8,128)(2,1)S(1)}, u32[]{:S(2)}, u32[]{:S(2)}) collective-permute-start(bf16[256,512]{1,0:T(8,128)(2,1)S(1)} %fusion), channel_id=1, source_target_pairs={{0,4},{4,0},{8,12},{12,8},{1,5},{5,1},{9,13},{13,9},{2,6},{6,2},{1... | collective-permute-start | bytes 786440 | tf_op jit(solution)/shard_map/ppermute | solution.py:38
  (5 other events, 29.2 us)
Sparse Core Ops, SparseCore 0:
  26.1 113.0 all-gather.2

commit v9 on v5

--- a/solution.py
+++ b/solution.py
@@ -126,7 +126,7 @@
 
 
 def normalize_kernel(*refs):
-    parts, outs = refs[:8], refs[8:]
+    parts, out = refs[:8], refs[8]
     for g in range(2):
         square = jnp.zeros((ROWS, 1), F32)
         for p in range(4):
@@ -137,20 +137,21 @@
             extra = parts[4 * g + p][pl.ds(ROWS, EXTRA), :].astype(F32)
             gain = extra[0:1] + extra[1:2] + extra[2:3]
             value = parts[4 * g + p][pl.ds(0, ROWS), :].astype(F32)
-            outs[g][p] = (value * inverse * gain).astype(BF16)
+            out[p, pl.ds(g * ROWS, ROWS), :] = (value * inverse * gain).astype(BF16)
 
 
 def normalize(parts):
     return pl.pallas_call(
         normalize_kernel,
-        out_shape=[jax.ShapeDtypeStruct((4, ROWS, TP_WIDTH), BF16)] * 2,
+        out_shape=jax.ShapeDtypeStruct((4, 2 * ROWS, TP_WIDTH), BF16),
         compiler_params=pltpu.CompilerParams(vmem_limit_bytes=32 << 20),
         cost_estimate=pl.CostEstimate(flops=8 * ROWS * D, bytes_accessed=4 << 20, transcendentals=0),
         name="normalize",
     )(*parts)
 
 
-def feed_forward_kernel(place_ref, x_ref, w_ref, keep_ref, send_ref, acc_ref):
+def feed_forward_kernel(place_ref, x_ref, w_ref, *refs):
+    outs, acc_ref = refs[:4], refs[4]
     step = pl.program_id(0)
 
     def block(p, kind):
@@ -165,8 +166,8 @@
         ]
         return jnp.concatenate(pieces, axis=1).reshape(TP_WIDTH, UNIT_BLOCK)
 
-    gate = jnp.zeros((ROWS, UNIT_BLOCK), F32)
-    up = jnp.zeros((ROWS, UNIT_BLOCK), F32)
+    gate = jnp.zeros((2 * ROWS, UNIT_BLOCK), F32)
+    up = jnp.zeros((2 * ROWS, UNIT_BLOCK), F32)
     for p in range(4):
         gate += jnp.dot(x_ref[p], block(p, 0), preferred_element_type=F32)
         up += jnp.dot(x_ref[p], block(p, 1), preferred_element_type=F32)
@@ -185,8 +186,10 @@
     @pl.when(step == 1)
     def _():
         for i, p in enumerate((2, 0)):
-            send_ref[i] = (acc_ref[p + 1] + down(p + 1)).astype(BF16)
-            keep_ref[i] = (acc_ref[p] + down(p)).astype(BF16)
+            for away in range(2):
+                total = (acc_ref[p + away] + down(p + away)).astype(BF16)
+                for g in range(2):
+                    outs[2 * g + away][i] = total[g * ROWS : (g + 1) * ROWS]
 
 
 def feed_forward(place, x, weights):
@@ -195,20 +198,20 @@
     assert units == 2 * UNIT_BLOCK
     return pl.pallas_call(
         feed_forward_kernel,
-        out_shape=[jax.ShapeDtypeStruct((2, ROWS, TP_WIDTH), BF16)] * 2,
+        out_shape=[jax.ShapeDtypeStruct((2, ROWS, TP_WIDTH), BF16)] * 4,
         grid_spec=pltpu.PrefetchScalarGridSpec(
             num_scalar_prefetch=1,
             grid=(2,),
             in_specs=[
-                pl.BlockSpec((4, ROWS, TP_WIDTH), lambda i, o: (0, 0, 0)),
+                pl.BlockSpec((4, 2 * ROWS, TP_WIDTH), lambda i, o: (0, 0, 0)),
                 pl.BlockSpec((32, 4, 48, UNIT_BLOCK), lambda i, o: (0, 0, 0, i)),
             ],
-            out_specs=[pair] * 2,
-            scratch_shapes=[pltpu.VMEM((4, ROWS, TP_WIDTH), F32)],
-        ),
-        compiler_params=pltpu.CompilerParams(vmem_limit_bytes=58 << 20),
+            out_specs=[pair] * 4,
+            scratch_shapes=[pltpu.VMEM((4, 2 * ROWS, TP_WIDTH), F32)],
+        ),
+        compiler_params=pltpu.CompilerParams(vmem_limit_bytes=48 << 20),
         cost_estimate=pl.CostEstimate(
-            flops=6 * ROWS * D * units, bytes_accessed=8 << 20, transcendentals=ROWS * units
+            flops=12 * ROWS * D * units, bytes_accessed=10 << 20, transcendentals=2 * ROWS * units
         ),
         name="feed_forward",
     )(place, x, weights)
@@ -256,10 +259,9 @@
     own = 2 * lax.axis_index("yl") + lax.axis_index("c")
     place = [own, own ^ 1, own ^ 2, own ^ 3] + [(yh - y) & 3 for y in range(4)]
     place = jnp.stack(place).astype(jnp.int32)
-    own_x, partner_x = normalize(parts)
-    partner_keep, partner_send = feed_forward(place, partner_x, weights)
-    own_x, partner_send = lax.optimization_barrier((own_x, partner_send))
-    own_keep, own_send = feed_forward(place, own_x, weights)
+    own_keep, own_send, partner_keep, partner_send = feed_forward(
+        place, normalize(parts), weights
+    )
 
     def add(left, right):
         return left.astype(F32) + right.astype(F32)

time: 191 us -> 184 us (0.963)
  Pallas kernels: 18.7 us -> 12.5 us
    pallas_call x2 -> x1, Pallas kernels: 12.7 us -> 6.52 us  [feed_forward(): pl.pallas_call(feed_forward_kernel, out_shape=[jax.ShapeDtypeStruct((2, R...]
    unnamed x22 -> x24, local copies, waits for them, and re-layouts: 3.78 us -> 5.09 us
  transfers between devices with their start and end apart: 20 -> 20, of which waited for: 10 -> 10; matrix products, arithmetic and copies ran while one was open for 2% -> 1% of each run, Pallas kernels for 7% -> 3%
where the time goes in v9:
time: 184 us; the launch traced here: 182 us
  waiting for transfers between devices  80.2 us (44%)
  starting transfers between devices  65.5 us (36%)
  between operations  14.4 us (8%)
  Pallas kernels  12.5 us (7%)
  local copies, waits for them, and re-layouts  5.35 us (3%)
  other arithmetic  4.52 us (2%)
    ppermute x12, starting transfers between devices, swap(): return lax.ppermute(value, axis, [(i, i ^ 1) for i in range(size)])  33.8 us
    ppermute x4, waiting for transfers between devices, from_behind(): return lax.ppermute(value, SEQ, [(i, i + by) for i in range(size - by)])  30.9 us
    ppermute x12, waiting for transfers between devices, swap(): return lax.ppermute(value, axis, [(i, i ^ 1) for i in range(size)])  24 us
    all_gather x1, waiting for transfers between devices, on_device(): weights = lax.all_gather(near, ('x', 'z'), axis=0)  22.5 us
    ppermute x4, starting transfers between devices, from_behind(): return lax.ppermute(value, SEQ, [(i, i + by) for i in range(size - by)])  17.1 us
    ppermute x3, starting transfers between devices, around(): lax.ppermute(value, axis, [(i, (i + by) % size) for i in range(size)])  14.5 us
    pallas_call x1, Pallas kernels, feed_forward(): pl.pallas_call(feed_forward_kernel, out_shape=[jax.ShapeDtypeStruct((2, R...  6.52 us
    unnamed x24, local copies, waits for them, and re-layouts  5.09 us
  transfers between devices with their start and end apart: 20, of which 10 were waited for; matrix products, arithmetic and copies ran while one was open for 1% of the time, Pallas kernels for 3%

profile of v9, /device:TPU:1, one launch (start us, length us, event | category | flops | bytes accessed | tf_op | source)
XLA Modules:
  0.0 182.4 jit_solution(1596123665734065934)
XLA Ops:
  8.0 6.7 %collective-permute-start.13 = (bf16[48,512]{1,0:T(8,128)(2,1)S(1)}, bf16[48,512]{1,0:T(8,128)(2,1)S(1)}, u32[]{:S(2)}, u32[]{:S(2)}) collective-permute-start(bf16[48,512]{1,0:T(8,128)(2,1)S(1)} %get-tuple-element.15), channel_id=1, source_target_pairs={{0,12},{4,0},{8,4},{12,8},{1,13},{5,1},{9,5},{13,9},{2,14},{6,2},{... | collective-permute-start | bytes 147464 | tf_op jit(solution)/shard_map/ppermute | solution.py:33
  14.7 3.5 %collective-permute-start.12 = (bf16[48,512]{1,0:T(8,128)(2,1)S(1)}, bf16[48,512]{1,0:T(8,128)(2,1)S(1)}, u32[]{:S(2)}, u32[]{:S(2)}) collective-permute-start(bf16[48,512]{1,0:T(8,128)(2,1)S(1)} %get-tuple-element.14), channel_id=1, source_target_pairs={{0,8},{4,12},{8,0},{12,4},{1,9},{5,13},{9,1},{13,5},{2,10},{6,14},... | collective-permute-start | bytes 147464 | tf_op jit(solution)/shard_map/ppermute | solution.py:33
  18.3 4.2 %collective-permute-start.11 = (bf16[48,512]{1,0:T(8,128)(2,1)S(1)}, bf16[48,512]{1,0:T(8,128)(2,1)S(1)}, u32[]{:S(2)}, u32[]{:S(2)}) collective-permute-start(bf16[48,512]{1,0:T(8,128)(2,1)S(1)} %get-tuple-element.15), channel_id=1, source_target_pairs={{0,4},{4,8},{8,12},{12,0},{1,5},{5,9},{9,13},{13,1},{2,6},{6,10},{... | collective-permute-start | bytes 147464 | tf_op jit(solution)/shard_map/ppermute | solution.py:33
  28.0 3.0 %collective-permute-start = (bf16[272,512]{1,0:T(8,128)(2,1)S(1)}, bf16[272,512]{1,0:T(8,128)(2,1)S(1)}, u32[]{:S(2)}, u32[]{:S(2)}) collective-permute-start(bf16[272,512]{1,0:T(8,128)(2,1)S(1)} %pad_maximum_fusion.refs_1_), channel_id=1, source_target_pairs={{0,4},{4,8},{8,12},{12,16},{16,20},{20,24},{24,28},{28,32},{32,36}... | collective-permute-start | bytes 835592 | tf_op jit(solution)/shard_map/ppermute | solution.py:28
  31.0 4.9 %collective-permute-start.1 = (bf16[256,512]{1,0:T(8,128)(2,1)}, bf16[256,512]{1,0:T(8,128)(2,1)S(1)}, u32[]{:S(2)}, u32[]{:S(2)}) collective-permute-start(bf16[256,512]{1,0:T(8,128)(2,1)} %refs_2_.1), channel_id=1, source_target_pairs={{0,4},{4,8},{8,12},{12,16},{16,20},{20,24},{24,28},{28,32},{32,36}... | collective-permute-start | bytes 786440 | tf_op jit(solution)/shard_map/ppermute | solution.py:28
  35.9 4.2 %collective-permute-start.2 = (bf16[272,512]{1,0:T(8,128)(2,1)S(1)}, bf16[272,512]{1,0:T(8,128)(2,1)S(1)}, u32[]{:S(2)}, u32[]{:S(2)}) collective-permute-start(bf16[272,512]{1,0:T(8,128)(2,1)S(1)} %collective-permute-done.refs_3_), channel_id=1, source_target_pairs={{0,4},{4,8},{8,12},{12,16},{16,20},{20,24},{24,28},{28,32},{32,36}... | collective-permute-start | bytes 835592 | tf_op jit(solution)/shard_map/ppermute | solution.py:28
  40.1 10.6 %collective-permute-done.1.refs_4_ = bf16[256,512]{1,0:T(8,128)(2,1)S(1)} collective-permute-done((bf16[256,512]{1,0:T(8,128)(2,1)}, bf16[256,512]{1,0:T(8,128)(2,1)S(1)}, u32[]{:S(2)}, u32[]{:S(2)}) %collective-permute-start.1) | collective-permute-done | bytes 262176 | tf_op jit(solution)/shard_map/ppermute | solution.py:28
  50.7 5.0 %collective-permute-start.3 = (bf16[256,512]{1,0:T(8,128)(2,1)S(1)}, bf16[256,512]{1,0:T(8,128)(2,1)S(1)}, u32[]{:S(2)}, u32[]{:S(2)}) collective-permute-start(bf16[256,512]{1,0:T(8,128)(2,1)S(1)} %collective-permute-done.1.refs_4_), channel_id=1, source_target_pairs={{0,4},{4,8},{8,12},{12,16},{16,20},{20,24},{24,28},{28,32},{32,36}... | collective-permute-start | bytes 786440 | tf_op jit(solution)/shard_map/ppermute | solution.py:28
  55.7 20.3 %collective-permute-done.3.refs_6_ = bf16[256,512]{1,0:T(8,128)(2,1)S(1)} collective-permute-done((bf16[256,512]{1,0:T(8,128)(2,1)S(1)}, bf16[256,512]{1,0:T(8,128)(2,1)S(1)}, u32[]{:S(2)}, u32[]{:S(2)}) %collective-permute-start.3) | collective-permute-done | bytes 262176 | tf_op jit(solution)/shard_map/ppermute | solution.py:28
  76.8 5.1 %attention.1 = (bf16[256,512]{1,0:T(8,128)(2,1)}, bf16[272,512]{1,0:T(8,128)(2,1)}) custom-call(s32[2]{0:T(128)} %lengths_ref.1, f32[1,512]{1,0:T(1,128)} %bitcast.34, bf16[256,512]{1,0:T(8,128)(2,1)} %refs_0_.1, bf16[272,512]{1,0:T(8,128)(2,1)} %copy-done.6, bf16[256,512]{1,0:T(8,128)(2,1)} %refs_2_.1, bf16[272,512]{1,0:T(8,128)(2,1)} %copy-done.7, ...), custom_call_target="tpu_custom_call" | custom-call | flops 402653184 | bytes 3145728 | tf_op jit(solution)/shard_map/attention/pallas_call | solution.py:108
  81.9 5.0 %collective-permute-start.7 = (bf16[272,512]{1,0:T(8,128)(2,1)}, bf16[272,512]{1,0:T(8,128)(2,1)S(1)}, u32[]{:S(2)}, u32[]{:S(2)}) collective-permute-start(bf16[272,512]{1,0:T(8,128)(2,1)} %get-tuple-element.9.refs_0_), channel_id=1, source_target_pairs={{0,4},{4,0},{8,12},{12,8},{1,5},{5,1},{9,13},{13,9},{2,6},{6,2},{1... | collective-permute-start | bytes 835592 | tf_op jit(solution)/shard_map/ppermute | solution.py:38
  88.9 9.4 %collective-permute-done.7.refs_4_ = bf16[272,512]{1,0:T(8,128)(2,1)S(1)} collective-permute-done((bf16[272,512]{1,0:T(8,128)(2,1)}, bf16[272,512]{1,0:T(8,128)(2,1)S(1)}, u32[]{:S(2)}, u32[]{:S(2)}) %collective-permute-start.7) | collective-permute-done | bytes 278560 | tf_op jit(solution)/shard_map/ppermute | solution.py:38
  100.2 3.0 %collective-permute-start.4 = (bf16[272,512]{1,0:T(8,128)(2,1)}, bf16[272,512]{1,0:T(8,128)(2,1)S(1)}, u32[]{:S(2)}, u32[]{:S(2)}) collective-permute-start(bf16[272,512]{1,0:T(8,128)(2,1)} %get-tuple-element.9.refs_0_), channel_id=1, source_target_pairs={{0,1},{1,0},{2,3},{3,2},{4,5},{5,4},{6,7},{7,6},{8,9},{9,8},{10,11... | collective-permute-start | bytes 835592 | tf_op jit(solution)/shard_map/ppermute | solution.py:38
  105.1 2.4 %collective-permute-start.6 = (bf16[272,512]{1,0:T(8,128)(2,1)S(1)}, bf16[272,512]{1,0:T(8,128)(2,1)S(1)}, u32[]{:S(2)}, u32[]{:S(2)}) collective-permute-start(bf16[272,512]{1,0:T(8,128)(2,1)S(1)} %collective-permute-done.5.refs_2_), channel_id=1, source_target_pairs={{0,1},{1,0},{2,3},{3,2},{4,5},{5,4},{6,7},{7,6},{8,9},{9,8},{10,11... | collective-permute-start | bytes 835592 | tf_op jit(solution)/shard_map/ppermute | solution.py:38
  107.5 3.5 %collective-permute-start.10 = (bf16[272,512]{1,0:T(8,128)(2,1)S(1)}, bf16[272,512]{1,0:T(8,128)(2,1)S(1)}, u32[]{:S(2)}, u32[]{:S(2)}) collective-permute-start(bf16[272,512]{1,0:T(8,128)(2,1)S(1)} %collective-permute-done.9.refs_6_), channel_id=1, source_target_pairs={{0,1},{1,0},{2,3},{3,2},{4,5},{5,4},{6,7},{7,6},{8,9},{9,8},{10,11... | collective-permute-start | bytes 835592 | tf_op jit(solution)/shard_map/ppermute | solution.py:38
  116.8 22.5 %all-gather.3.cloned.1.call-done = bf16[128,48,512]{2,1,0:T(8,128)(2,1)} async-done(((bf16[4,48,512]{2,1,0:T(8,128)(2,1)}), bf16[128,48,512]{2,1,0:T(8,128)(2,1)}) %all-gather.3.cloned.1.call-update) | async-done | bytes 6291472 | tf_op jit(solution)/shard_map/all_gather | solution.py:241
  139.3 6.5 %feed_forward.1 = (bf16[2,256,512]{2,1,0:T(8,128)(2,1)S(1)}, bf16[2,256,512]{2,1,0:T(8,128)(2,1)S(1)}, bf16[2,256,512]{2,1,0:T(8,128)(2,1)S(1)}, bf16[2,256,512]{2,1,0:T(8,128)(2,1)S(1)}) custom-call(s32[8]{0:T(128)S(1)} %stack.50.place_ref, bf16[4,512,512]{2,1,0:T(8,128)(2,1)S(1)} %normalize.1.x_ref, bf16[32,4,48,512]{3,2,1,0:T(8,128)(2,1)} %bitcast.35), custom_call_target="tpu_custom_call" | custom-call | flops 3221225472 | bytes 10485760 | tf_op jit(solution)/shard_map/feed_forward/pallas_call | solution.py:199
  145.8 2.9 %collective-permute-start.16 = (bf16[2,256,512]{2,1,0:T(8,128)(2,1)S(1)}, bf16[2,256,512]{2,1,0:T(8,128)(2,1)S(1)}, u32[]{:S(2)}, u32[]{:S(2)}) collective-permute-start(bf16[2,256,512]{2,1,0:T(8,128)(2,1)S(1)} %get-tuple-element.13), channel_id=1, source_target_pairs={{0,1},{1,0},{2,3},{3,2},{4,5},{5,4},{6,7},{7,6},{8,9},{9,8},{10,11... | collective-permute-start | bytes 1572872 | tf_op jit(solution)/shard_map/ppermute | solution.py:38
  148.7 1.9 %collective-permute-start.14 = (bf16[2,256,512]{2,1,0:T(8,128)(2,1)S(1)}, bf16[2,256,512]{2,1,0:T(8,128)(2,1)S(1)}, u32[]{:S(2)}, u32[]{:S(2)}) collective-permute-start(bf16[2,256,512]{2,1,0:T(8,128)(2,1)S(1)} %get-tuple-element.11), channel_id=1, source_target_pairs={{0,1},{1,0},{2,3},{3,2},{4,5},{5,4},{6,7},{7,6},{8,9},{9,8},{10,11... | collective-permute-start | bytes 1572872 | tf_op jit(solution)/shard_map/ppermute | solution.py:38
  150.7 3.1 %collective-permute-start.17 = (bf16[256,512]{1,0:T(8,128)(2,1)S(1)}, bf16[256,512]{1,0:T(8,128)(2,1)S(1)}, u32[]{:S(2)}, u32[]{:S(2)}) collective-permute-start(bf16[256,512]{1,0:T(8,128)(2,1)S(1)} %fusion.4), channel_id=1, source_target_pairs={{0,2},{2,0},{1,3},{3,1},{4,6},{6,4},{5,7},{7,5},{8,10},{10,8},{9,1... | collective-permute-start | bytes 786440 | tf_op jit(solution)/shard_map/ppermute | solution.py:38
  153.9 2.2 %collective-permute-start.15 = (bf16[256,512]{1,0:T(8,128)(2,1)S(1)}, bf16[256,512]{1,0:T(8,128)(2,1)S(1)}, u32[]{:S(2)}, u32[]{:S(2)}) collective-permute-start(bf16[256,512]{1,0:T(8,128)(2,1)S(1)} %fusion.3), channel_id=1, source_target_pairs={{0,2},{2,0},{1,3},{3,1},{4,6},{6,4},{5,7},{7,5},{8,10},{10,8},{9,1... | collective-permute-start | bytes 786440 | tf_op jit(solution)/shard_map/ppermute | solution.py:38
  156.1 3.9 %collective-permute-done.17 = bf16[256,512]{1,0:T(8,128)(2,1)S(1)} collective-permute-done((bf16[256,512]{1,0:T(8,128)(2,1)S(1)}, bf16[256,512]{1,0:T(8,128)(2,1)S(1)}, u32[]{:S(2)}, u32[]{:S(2)}) %collective-permute-start.17) | collective-permute-done | bytes 262176 | tf_op jit(solution)/shard_map/ppermute | solution.py:38
  160.1 4.0 %collective-permute-start.18 = (bf16[256,512]{1,0:T(8,128)(2,1)S(1)}, bf16[256,512]{1,0:T(8,128)(2,1)S(1)}, u32[]{:S(2)}, u32[]{:S(2)}) collective-permute-start(bf16[256,512]{1,0:T(8,128)(2,1)S(1)} %fusion), channel_id=1, source_target_pairs={{0,4},{4,0},{8,12},{12,8},{1,5},{5,1},{9,13},{13,9},{2,6},{6,2},{1... | collective-permute-start | bytes 786440 | tf_op jit(solution)/shard_map/ppermute | solution.py:38
  165.6 8.9 %collective-permute-done.18 = bf16[256,512]{1,0:T(8,128)(2,1)S(1)} collective-permute-done((bf16[256,512]{1,0:T(8,128)(2,1)S(1)}, bf16[256,512]{1,0:T(8,128)(2,1)S(1)}, u32[]{:S(2)}, u32[]{:S(2)}) %collective-permute-start.18) | collective-permute-done | bytes 262176 | tf_op jit(solution)/shard_map/ppermute | solution.py:38
  (57 shorter events, 21.2 us)
Async XLA Ops:
  7.2 132.1 %all-gather.3.cloned.1.call-start = ((), (), s32[]{:S(2)}) async-start(), calls=%async_computation | async-start | bytes 6488064 | tf_op jit(solution)/shard_map/all_gather | solution.py:241
  8.0 14.5 %collective-permute-start.13 = (bf16[48,512]{1,0:T(8,128)(2,1)S(1)}, bf16[48,512]{1,0:T(8,128)(2,1)S(1)}, u32[]{:S(2)}, u32[]{:S(2)}) collective-permute-start(bf16[48,512]{1,0:T(8,128)(2,1)S(1)} %get-tuple-element.15), channel_id=1, source_target_pairs={{0,12},{4,0},{8,4},{12,8},{1,13},{5,1},{9,5},{13,9},{2,14},{6,2},{... | collective-permute-start | bytes 147464 | tf_op jit(solution)/shard_map/ppermute | solution.py:33
  14.7 8.7 %collective-permute-start.12 = (bf16[48,512]{1,0:T(8,128)(2,1)S(1)}, bf16[48,512]{1,0:T(8,128)(2,1)S(1)}, u32[]{:S(2)}, u32[]{:S(2)}) collective-permute-start(bf16[48,512]{1,0:T(8,128)(2,1)S(1)} %get-tuple-element.14), channel_id=1, source_target_pairs={{0,8},{4,12},{8,0},{12,4},{1,9},{5,13},{9,1},{13,5},{2,10},{6,14},... | collective-permute-start | bytes 147464 | tf_op jit(solution)/shard_map/ppermute | solution.py:33
  18.3 7.0 %collective-permute-start.11 = (bf16[48,512]{1,0:T(8,128)(2,1)S(1)}, bf16[48,512]{1,0:T(8,128)(2,1)S(1)}, u32[]{:S(2)}, u32[]{:S(2)}) collective-permute-start(bf16[48,512]{1,0:T(8,128)(2,1)S(1)} %get-tuple-element.15), channel_id=1, source_target_pairs={{0,4},{4,8},{8,12},{12,0},{1,5},{5,9},{9,13},{13,1},{2,6},{6,10},{... | collective-permute-start | bytes 147464 | tf_op jit(solution)/shard_map/ppermute | solution.py:33
  28.0 48.1 %copy-start.6 = (bf16[272,512]{1,0:T(8,128)(2,1)}, bf16[272,512]{1,0:T(8,128)(2,1)S(1)}, u32[]{:S(2)}) copy-start(bf16[272,512]{1,0:T(8,128)(2,1)S(1)} %pad_maximum_fusion.refs_1_) | copy-start | bytes 835588
  28.0 7.9 %collective-permute-start = (bf16[272,512]{1,0:T(8,128)(2,1)S(1)}, bf16[272,512]{1,0:T(8,128)(2,1)S(1)}, u32[]{:S(2)}, u32[]{:S(2)}) collective-permute-start(bf16[272,512]{1,0:T(8,128)(2,1)S(1)} %pad_maximum_fusion.refs_1_), channel_id=1, source_target_pairs={{0,4},{4,8},{8,12},{12,16},{16,20},{20,24},{24,28},{28,32},{32,36}... | collective-permute-start | bytes 835592 | tf_op jit(solution)/shard_map/ppermute | solution.py:28
  31.0 19.7 %collective-permute-start.1 = (bf16[256,512]{1,0:T(8,128)(2,1)}, bf16[256,512]{1,0:T(8,128)(2,1)S(1)}, u32[]{:S(2)}, u32[]{:S(2)}) collective-permute-start(bf16[256,512]{1,0:T(8,128)(2,1)} %refs_2_.1), channel_id=1, source_target_pairs={{0,4},{4,8},{8,12},{12,16},{16,20},{20,24},{24,28},{28,32},{32,36}... | collective-permute-start | bytes 786440 | tf_op jit(solution)/shard_map/ppermute | solution.py:28
  35.9 40.2 %copy-start.7 = (bf16[272,512]{1,0:T(8,128)(2,1)}, bf16[272,512]{1,0:T(8,128)(2,1)S(1)}, u32[]{:S(2)}) copy-start(bf16[272,512]{1,0:T(8,128)(2,1)S(1)} %collective-permute-done.refs_3_) | copy-start | bytes 835588
  35.9 40.1 %collective-permute-start.2 = (bf16[272,512]{1,0:T(8,128)(2,1)S(1)}, bf16[272,512]{1,0:T(8,128)(2,1)S(1)}, u32[]{:S(2)}, u32[]{:S(2)}) collective-permute-start(bf16[272,512]{1,0:T(8,128)(2,1)S(1)} %collective-permute-done.refs_3_), channel_id=1, source_target_pairs={{0,4},{4,8},{8,12},{12,16},{16,20},{20,24},{24,28},{28,32},{32,36}... | collective-permute-start | bytes 835592 | tf_op jit(solution)/shard_map/ppermute | solution.py:28
  50.7 25.4 %collective-permute-start.3 = (bf16[256,512]{1,0:T(8,128)(2,1)S(1)}, bf16[256,512]{1,0:T(8,128)(2,1)S(1)}, u32[]{:S(2)}, u32[]{:S(2)}) collective-permute-start(bf16[256,512]{1,0:T(8,128)(2,1)S(1)} %collective-permute-done.1.refs_4_), channel_id=1, source_target_pairs={{0,4},{4,8},{8,12},{12,16},{16,20},{20,24},{24,28},{28,32},{32,36}... | collective-permute-start | bytes 786440 | tf_op jit(solution)/shard_map/ppermute | solution.py:28
  81.9 16.3 %collective-permute-start.7 = (bf16[272,512]{1,0:T(8,128)(2,1)}, bf16[272,512]{1,0:T(8,128)(2,1)S(1)}, u32[]{:S(2)}, u32[]{:S(2)}) collective-permute-start(bf16[272,512]{1,0:T(8,128)(2,1)} %get-tuple-element.9.refs_0_), channel_id=1, source_target_pairs={{0,4},{4,0},{8,12},{12,8},{1,5},{5,1},{9,13},{13,9},{2,6},{6,2},{1... | collective-permute-start | bytes 835592 | tf_op jit(solution)/shard_map/ppermute | solution.py:38
  86.9 18.2 %collective-permute-start.5 = (bf16[272,512]{1,0:T(8,128)(2,1)}, bf16[272,512]{1,0:T(8,128)(2,1)S(1)}, u32[]{:S(2)}, u32[]{:S(2)}) collective-permute-start(bf16[272,512]{1,0:T(8,128)(2,1)} %get-tuple-element.9.refs_0_), channel_id=1, source_target_pairs={{0,2},{2,0},{1,3},{3,1},{4,6},{6,4},{5,7},{7,5},{8,10},{10,8},{9,1... | collective-permute-start | bytes 835592 | tf_op jit(solution)/shard_map/ppermute | solution.py:38
  98.2 9.3 %collective-permute-start.9 = (bf16[272,512]{1,0:T(8,128)(2,1)S(1)}, bf16[272,512]{1,0:T(8,128)(2,1)S(1)}, u32[]{:S(2)}, u32[]{:S(2)}) collective-permute-start(bf16[272,512]{1,0:T(8,128)(2,1)S(1)} %collective-permute-done.7.refs_4_), channel_id=1, source_target_pairs={{0,2},{2,0},{1,3},{3,1},{4,6},{6,4},{5,7},{7,5},{8,10},{10,8},{9,1... | collective-permute-start | bytes 835592 | tf_op jit(solution)/shard_map/ppermute | solution.py:38
  100.2 11.0 %collective-permute-start.4 = (bf16[272,512]{1,0:T(8,128)(2,1)}, bf16[272,512]{1,0:T(8,128)(2,1)S(1)}, u32[]{:S(2)}, u32[]{:S(2)}) collective-permute-start(bf16[272,512]{1,0:T(8,128)(2,1)} %get-tuple-element.9.refs_0_), channel_id=1, source_target_pairs={{0,1},{1,0},{2,3},{3,2},{4,5},{5,4},{6,7},{7,6},{8,9},{9,8},{10,11... | collective-permute-start | bytes 835592 | tf_op jit(solution)/shard_map/ppermute | solution.py:38
  103.2 8.7 %collective-permute-start.8 = (bf16[272,512]{1,0:T(8,128)(2,1)S(1)}, bf16[272,512]{1,0:T(8,128)(2,1)S(1)}, u32[]{:S(2)}, u32[]{:S(2)}) collective-permute-start(bf16[272,512]{1,0:T(8,128)(2,1)S(1)} %collective-permute-done.7.refs_4_), channel_id=1, source_target_pairs={{0,1},{1,0},{2,3},{3,2},{4,5},{5,4},{6,7},{7,6},{8,9},{9,8},{10,11... | collective-permute-start | bytes 835592 | tf_op jit(solution)/shard_map/ppermute | solution.py:38
  105.1 6.1 %collective-permute-start.6 = (bf16[272,512]{1,0:T(8,128)(2,1)S(1)}, bf16[272,512]{1,0:T(8,128)(2,1)S(1)}, u32[]{:S(2)}, u32[]{:S(2)}) collective-permute-start(bf16[272,512]{1,0:T(8,128)(2,1)S(1)} %collective-permute-done.5.refs_2_), channel_id=1, source_target_pairs={{0,1},{1,0},{2,3},{3,2},{4,5},{5,4},{6,7},{7,6},{8,9},{9,8},{10,11... | collective-permute-start | bytes 835592 | tf_op jit(solution)/shard_map/ppermute | solution.py:38
  107.5 4.7 %collective-permute-start.10 = (bf16[272,512]{1,0:T(8,128)(2,1)S(1)}, bf16[272,512]{1,0:T(8,128)(2,1)S(1)}, u32[]{:S(2)}, u32[]{:S(2)}) collective-permute-start(bf16[272,512]{1,0:T(8,128)(2,1)S(1)} %collective-permute-done.9.refs_6_), channel_id=1, source_target_pairs={{0,1},{1,0},{2,3},{3,2},{4,5},{5,4},{6,7},{7,6},{8,9},{9,8},{10,11... | collective-permute-start | bytes 835592 | tf_op jit(solution)/shard_map/ppermute | solution.py:38
  139.3 35.2 %copy-start.5 = (f32[256,512]{1,0:T(8,128)S(1)}, f32[256,512]{1,0:T(8,128)}, u32[]{:S(2)}) copy-start(f32[256,512]{1,0:T(8,128)} %refs_7_.1) | copy-start | bytes 1572868
  139.3 35.2 %copy-start.9 = (bf16[256,512]{1,0:T(8,128)(2,1)S(1)}, bf16[256,512]{1,0:T(8,128)(2,1)}, u32[]{:S(2)}) copy-start(bf16[256,512]{1,0:T(8,128)(2,1)} %get-tuple-element.6) | copy-start | bytes 786436
  145.8 4.8 %collective-permute-start.16 = (bf16[2,256,512]{2,1,0:T(8,128)(2,1)S(1)}, bf16[2,256,512]{2,1,0:T(8,128)(2,1)S(1)}, u32[]{:S(2)}, u32[]{:S(2)}) collective-permute-start(bf16[2,256,512]{2,1,0:T(8,128)(2,1)S(1)} %get-tuple-element.13), channel_id=1, source_target_pairs={{0,1},{1,0},{2,3},{3,2},{4,5},{5,4},{6,7},{7,6},{8,9},{9,8},{10,11... | collective-permute-start | bytes 1572872 | tf_op jit(solution)/shard_map/ppermute | solution.py:38
  148.7 5.1 %collective-permute-start.14 = (bf16[2,256,512]{2,1,0:T(8,128)(2,1)S(1)}, bf16[2,256,512]{2,1,0:T(8,128)(2,1)S(1)}, u32[]{:S(2)}, u32[]{:S(2)}) collective-permute-start(bf16[2,256,512]{2,1,0:T(8,128)(2,1)S(1)} %get-tuple-element.11), channel_id=1, source_target_pairs={{0,1},{1,0},{2,3},{3,2},{4,5},{5,4},{6,7},{7,6},{8,9},{9,8},{10,11... | collective-permute-start | bytes 1572872 | tf_op jit(solution)/shard_map/ppermute | solution.py:38
  150.7 9.3 %collective-permute-start.17 = (bf16[256,512]{1,0:T(8,128)(2,1)S(1)}, bf16[256,512]{1,0:T(8,128)(2,1)S(1)}, u32[]{:S(2)}, u32[]{:S(2)}) collective-permute-start(bf16[256,512]{1,0:T(8,128)(2,1)S(1)} %fusion.4), channel_id=1, source_target_pairs={{0,2},{2,0},{1,3},{3,1},{4,6},{6,4},{5,7},{7,5},{8,10},{10,8},{9,1... | collective-permute-start | bytes 786440 | tf_op jit(solution)/shard_map/ppermute | solution.py:38
  153.9 11.7 %collective-permute-start.15 = (bf16[256,512]{1,0:T(8,128)(2,1)S(1)}, bf16[256,512]{1,0:T(8,128)(2,1)S(1)}, u32[]{:S(2)}, u32[]{:S(2)}) collective-permute-start(bf16[256,512]{1,0:T(8,128)(2,1)S(1)} %fusion.3), channel_id=1, source_target_pairs={{0,2},{2,0},{1,3},{3,1},{4,6},{6,4},{5,7},{7,5},{8,10},{10,8},{9,1... | collective-permute-start | bytes 786440 | tf_op jit(solution)/shard_map/ppermute | solution.py:38
  160.1 14.4 %collective-permute-start.18 = (bf16[256,512]{1,0:T(8,128)(2,1)S(1)}, bf16[256,512]{1,0:T(8,128)(2,1)S(1)}, u32[]{:S(2)}, u32[]{:S(2)}) collective-permute-start(bf16[256,512]{1,0:T(8,128)(2,1)S(1)} %fusion), channel_id=1, source_target_pairs={{0,4},{4,0},{8,12},{12,8},{1,5},{5,1},{9,13},{13,9},{2,6},{6,2},{1... | collective-permute-start | bytes 786440 | tf_op jit(solution)/shard_map/ppermute | solution.py:38
  (8 other events, 31.2 us)
Sparse Core Ops, SparseCore 0:
  26.2 113.0 all-gather.2

commit v10 on v9

--- a/solution.py
+++ b/solution.py
@@ -26,11 +26,6 @@
 def from_behind(value, by):
     size = lax.axis_size(SEQ)
     return lax.ppermute(value, SEQ, [(i, i + by) for i in range(size - by)])
-
-
-def around(value, axis, by):
-    size = lax.axis_size(axis)
-    return lax.ppermute(value, axis, [(i, (i + by) % size) for i in range(size)])
 
 
 def swap(value, axis):
@@ -158,7 +153,7 @@
         pieces = [
             w_ref[
                 pl.ds(place_ref[p] * 8, 8),
-                pl.ds(place_ref[4 + y], 1),
+                pl.ds(y, 1),
                 pl.ds(kind * 16, 16),
                 :,
             ]
@@ -228,16 +223,11 @@
     up_weight,
     down_weight,
 ):
-    yh = lax.axis_index("yh")
     half = gate_weight.shape[1] // 2
 
     packed = jnp.concatenate([gate_weight, up_weight, down_weight.T], axis=0)
-    parity = yh & 1
-    mine = lax.dynamic_slice_in_dim(packed, parity * half, half, 1)
-    other = lax.dynamic_slice_in_dim(packed, (1 - parity) * half, half, 1)
-    near = jnp.stack(
-        [mine, around(other, "yh", 1), around(mine, "yh", 2), around(other, "yh", 3)]
-    )
+    halves = [packed[:, :half], packed[:, half:]]
+    near = lax.all_to_all(jnp.stack(halves * 2), "yh", 0, 0)
     weights = lax.all_gather(near, ("x", "z"), axis=0)
 
     tail = jnp.broadcast_to(
@@ -257,8 +247,7 @@
         chip = swap(start, "yl")
         parts += [start, swap(start, "c"), chip, swap(chip, "c")]
     own = 2 * lax.axis_index("yl") + lax.axis_index("c")
-    place = [own, own ^ 1, own ^ 2, own ^ 3] + [(yh - y) & 3 for y in range(4)]
-    place = jnp.stack(place).astype(jnp.int32)
+    place = jnp.stack([own, own ^ 1, own ^ 2, own ^ 3]).astype(jnp.int32)
     own_keep, own_send, partner_keep, partner_send = feed_forward(
         place, normalize(parts), weights
     )

time: 184 us -> 177 us (0.962)
  waiting for transfers between devices: 80.2 us -> 45.5 us
  blocking collectives: 0 us -> 16 us
  starting transfers between devices: 65.5 us -> 78.1 us
    ppermute x12, starting transfers between devices: 33.8 us -> 61.3 us  [swap(): return lax.ppermute(value, axis, [(i, i ^ 1) for i in range(size)])]
    ppermute x4, waiting for transfers between devices: 30.9 us -> 13.6 us  [from_behind(): return lax.ppermute(value, SEQ, [(i, i + by) for i in range(size - by)])]
    all_to_all x0 -> x1, blocking collectives: none -> 16 us  [on_device(): near = lax.all_to_all(jnp.stack(halves * 2), 'yh', 0, 0)]
    ppermute x3 -> x0, starting transfers between devices: 14.5 us -> none  [around(): lax.ppermute(value, axis, [(i, (i + by) % size) for i in range(size)])]
    ppermute x12, waiting for transfers between devices: 24 us -> 15 us  [swap(): return lax.ppermute(value, axis, [(i, i ^ 1) for i in range(size)])]
    all_gather x1, waiting for transfers between devices: 22.5 us -> 16.8 us  [on_device(): weights = lax.all_gather(near, ('x', 'z'), axis=0)]
    ppermute x3 -> x0, waiting for transfers between devices: 2.75 us -> none  [around(): lax.ppermute(value, axis, [(i, (i + by) % size) for i in range(size)])]
  transfers between devices with their start and end apart: 20 -> 17, of which waited for: 10 -> 8; matrix products, arithmetic and copies ran while one was open for 1% -> 1% of each run, Pallas kernels for 3% -> 3%
where the time goes in v10:
time: 177 us; the launch traced here: 176 us
  starting transfers between devices  78.1 us (44%)
  waiting for transfers between devices  45.5 us (26%)
  blocking collectives  16 us (9%)
  between operations  14.3 us (8%)
  Pallas kernels  12.5 us (7%)
  local copies, waits for them, and re-layouts  5.33 us (3%)
  other arithmetic  3.87 us (2%)
    ppermute x12, starting transfers between devices, swap(): return lax.ppermute(value, axis, [(i, i ^ 1) for i in range(size)])  61.3 us
    all_gather x1, waiting for transfers between devices, on_device(): weights = lax.all_gather(near, ('x', 'z'), axis=0)  16.8 us
    ppermute x4, starting transfers between devices, from_behind(): return lax.ppermute(value, SEQ, [(i, i + by) for i in range(size - by)])  16.7 us
    all_to_all x1, blocking collectives, on_device(): near = lax.all_to_all(jnp.stack(halves * 2), 'yh', 0, 0)  16 us
    ppermute x12, waiting for transfers between devices, swap(): return lax.ppermute(value, axis, [(i, i ^ 1) for i in range(size)])  15 us
    ppermute x4, waiting for transfers between devices, from_behind(): return lax.ppermute(value, SEQ, [(i, i + by) for i in range(size - by)])  13.6 us
    pallas_call x1, Pallas kernels, feed_forward(): pl.pallas_call(feed_forward_kernel, out_shape=[jax.ShapeDtypeStruct((2, R...  6.5 us
    unnamed x24, local copies, waits for them, and re-layouts  5.15 us
  transfers between devices with their start and end apart: 17, of which 8 were waited for; matrix products, arithmetic and copies ran while one was open for 1% of the time, Pallas kernels for 3%

profile of v10, /device:TPU:1, one launch (start us, length us, event | category | flops | bytes accessed | tf_op | source)
XLA Modules:
  0.0 175.5 jit_solution(17222368998887043488)
XLA Ops:
  8.1 16.0 %all_to_all.5 = bf16[4,48,512]{2,1,0:T(8,128)(2,1)} all-to-all(bf16[4,48,512]{2,1,0:T(8,128)(2,1)S(1)} %pad_maximum_fusion.1), channel_id=1, replica_groups=mesh['x'=4,'z'=8,'yh'=4,'yl'=2,'c'=2] {'yh'}, dimensions={0} | all-to-all | bytes 393216 | tf_op jit(solution)/shard_map/all_to_all | solution.py:230
  25.9 3.1 %collective-permute-start = (bf16[272,512]{1,0:T(8,128)(2,1)S(1)}, bf16[272,512]{1,0:T(8,128)(2,1)S(1)}, u32[]{:S(2)}, u32[]{:S(2)}) collective-permute-start(bf16[272,512]{1,0:T(8,128)(2,1)S(1)} %pad_maximum_fusion.refs_1_), channel_id=1, source_target_pairs={{0,4},{4,8},{8,12},{12,16},{16,20},{20,24},{24,28},{28,32},{32,36}... | collective-permute-start | bytes 835592 | tf_op jit(solution)/shard_map/ppermute | solution.py:28
  29.0 2.5 %collective-permute-start.1 = (bf16[256,512]{1,0:T(8,128)(2,1)}, bf16[256,512]{1,0:T(8,128)(2,1)S(1)}, u32[]{:S(2)}, u32[]{:S(2)}) collective-permute-start(bf16[256,512]{1,0:T(8,128)(2,1)} %refs_2_.1), channel_id=1, source_target_pairs={{0,4},{4,8},{8,12},{12,16},{16,20},{20,24},{24,28},{28,32},{32,36}... | collective-permute-start | bytes 786440 | tf_op jit(solution)/shard_map/ppermute | solution.py:28
  32.6 6.1 %collective-permute-start.2 = (bf16[272,512]{1,0:T(8,128)(2,1)S(1)}, bf16[272,512]{1,0:T(8,128)(2,1)S(1)}, u32[]{:S(2)}, u32[]{:S(2)}) collective-permute-start(bf16[272,512]{1,0:T(8,128)(2,1)S(1)} %collective-permute-done.refs_3_), channel_id=1, source_target_pairs={{0,4},{4,8},{8,12},{12,16},{16,20},{20,24},{24,28},{28,32},{32,36}... | collective-permute-start | bytes 835592 | tf_op jit(solution)/shard_map/ppermute | solution.py:28
  38.7 1.9 %collective-permute-done.1.refs_4_ = bf16[256,512]{1,0:T(8,128)(2,1)S(1)} collective-permute-done((bf16[256,512]{1,0:T(8,128)(2,1)}, bf16[256,512]{1,0:T(8,128)(2,1)S(1)}, u32[]{:S(2)}, u32[]{:S(2)}) %collective-permute-start.1) | collective-permute-done | bytes 262176 | tf_op jit(solution)/shard_map/ppermute | solution.py:28
  40.6 5.0 %collective-permute-start.3 = (bf16[256,512]{1,0:T(8,128)(2,1)S(1)}, bf16[256,512]{1,0:T(8,128)(2,1)S(1)}, u32[]{:S(2)}, u32[]{:S(2)}) collective-permute-start(bf16[256,512]{1,0:T(8,128)(2,1)S(1)} %collective-permute-done.1.refs_4_), channel_id=1, source_target_pairs={{0,4},{4,8},{8,12},{12,16},{16,20},{20,24},{24,28},{28,32},{32,36}... | collective-permute-start | bytes 786440 | tf_op jit(solution)/shard_map/ppermute | solution.py:28
  45.6 10.7 %collective-permute-done.3.refs_6_ = bf16[256,512]{1,0:T(8,128)(2,1)S(1)} collective-permute-done((bf16[256,512]{1,0:T(8,128)(2,1)S(1)}, bf16[256,512]{1,0:T(8,128)(2,1)S(1)}, u32[]{:S(2)}, u32[]{:S(2)}) %collective-permute-start.3) | collective-permute-done | bytes 262176 | tf_op jit(solution)/shard_map/ppermute | solution.py:28
  57.1 5.1 %attention.1 = (bf16[256,512]{1,0:T(8,128)(2,1)}, bf16[272,512]{1,0:T(8,128)(2,1)}) custom-call(s32[2]{0:T(128)} %lengths_ref.1, f32[1,512]{1,0:T(1,128)} %bitcast.26, bf16[256,512]{1,0:T(8,128)(2,1)} %refs_0_.1, bf16[272,512]{1,0:T(8,128)(2,1)} %copy-done.6, bf16[256,512]{1,0:T(8,128)(2,1)} %refs_2_.1, bf16[272,512]{1,0:T(8,128)(2,1)} %copy-done.7, ...), custom_call_target="tpu_custom_call" | custom-call | flops 402653184 | bytes 3145728 | tf_op jit(solution)/shard_map/attention/pallas_call | solution.py:103
  62.2 5.0 %collective-permute-start.7 = (bf16[272,512]{1,0:T(8,128)(2,1)}, bf16[272,512]{1,0:T(8,128)(2,1)S(1)}, u32[]{:S(2)}, u32[]{:S(2)}) collective-permute-start(bf16[272,512]{1,0:T(8,128)(2,1)} %get-tuple-element.9.refs_0_), channel_id=1, source_target_pairs={{0,4},{4,0},{8,12},{12,8},{1,5},{5,1},{9,13},{13,9},{2,6},{6,2},{1... | collective-permute-start | bytes 835592 | tf_op jit(solution)/shard_map/ppermute | solution.py:33
  67.3 24.7 %collective-permute-start.5 = (bf16[272,512]{1,0:T(8,128)(2,1)}, bf16[272,512]{1,0:T(8,128)(2,1)S(1)}, u32[]{:S(2)}, u32[]{:S(2)}) collective-permute-start(bf16[272,512]{1,0:T(8,128)(2,1)} %get-tuple-element.9.refs_0_), channel_id=1, source_target_pairs={{0,2},{2,0},{1,3},{3,1},{4,6},{6,4},{5,7},{7,5},{8,10},{10,8},{9,1... | collective-permute-start | bytes 835592 | tf_op jit(solution)/shard_map/ppermute | solution.py:33
  92.0 6.1 %collective-permute-start.9 = (bf16[272,512]{1,0:T(8,128)(2,1)S(1)}, bf16[272,512]{1,0:T(8,128)(2,1)S(1)}, u32[]{:S(2)}, u32[]{:S(2)}) collective-permute-start(bf16[272,512]{1,0:T(8,128)(2,1)S(1)} %collective-permute-done.7.refs_4_), channel_id=1, source_target_pairs={{0,2},{2,0},{1,3},{3,1},{4,6},{6,4},{5,7},{7,5},{8,10},{10,8},{9,1... | collective-permute-start | bytes 835592 | tf_op jit(solution)/shard_map/ppermute | solution.py:33
  98.1 5.1 %collective-permute-start.4 = (bf16[272,512]{1,0:T(8,128)(2,1)}, bf16[272,512]{1,0:T(8,128)(2,1)S(1)}, u32[]{:S(2)}, u32[]{:S(2)}) collective-permute-start(bf16[272,512]{1,0:T(8,128)(2,1)} %get-tuple-element.9.refs_0_), channel_id=1, source_target_pairs={{0,1},{1,0},{2,3},{3,2},{4,5},{5,4},{6,7},{7,6},{8,9},{9,8},{10,11... | collective-permute-start | bytes 835592 | tf_op jit(solution)/shard_map/ppermute | solution.py:33
  103.2 1.9 %collective-permute-start.8 = (bf16[272,512]{1,0:T(8,128)(2,1)S(1)}, bf16[272,512]{1,0:T(8,128)(2,1)S(1)}, u32[]{:S(2)}, u32[]{:S(2)}) collective-permute-start(bf16[272,512]{1,0:T(8,128)(2,1)S(1)} %collective-permute-done.7.refs_4_), channel_id=1, source_target_pairs={{0,1},{1,0},{2,3},{3,2},{4,5},{5,4},{6,7},{7,6},{8,9},{9,8},{10,11... | collective-permute-start | bytes 835592 | tf_op jit(solution)/shard_map/ppermute | solution.py:33
  105.1 2.4 %collective-permute-start.6 = (bf16[272,512]{1,0:T(8,128)(2,1)S(1)}, bf16[272,512]{1,0:T(8,128)(2,1)S(1)}, u32[]{:S(2)}, u32[]{:S(2)}) collective-permute-start(bf16[272,512]{1,0:T(8,128)(2,1)S(1)} %collective-permute-done.5.refs_2_), channel_id=1, source_target_pairs={{0,1},{1,0},{2,3},{3,2},{4,5},{5,4},{6,7},{7,6},{8,9},{9,8},{10,11... | collective-permute-start | bytes 835592 | tf_op jit(solution)/shard_map/ppermute | solution.py:33
  107.6 1.9 %collective-permute-start.10 = (bf16[272,512]{1,0:T(8,128)(2,1)S(1)}, bf16[272,512]{1,0:T(8,128)(2,1)S(1)}, u32[]{:S(2)}, u32[]{:S(2)}) collective-permute-start(bf16[272,512]{1,0:T(8,128)(2,1)S(1)} %collective-permute-done.9.refs_6_), channel_id=1, source_target_pairs={{0,1},{1,0},{2,3},{3,2},{4,5},{5,4},{6,7},{7,6},{8,9},{9,8},{10,11... | collective-permute-start | bytes 835592 | tf_op jit(solution)/shard_map/ppermute | solution.py:33
  115.6 16.8 %all-gather.3.cloned.1.call-done = bf16[128,48,512]{2,1,0:T(8,128)(2,1)} async-done(((bf16[4,48,512]{2,1,0:T(8,128)(2,1)}), bf16[128,48,512]{2,1,0:T(8,128)(2,1)}) %all-gather.3.cloned.1.call-update) | async-done | bytes 6291472 | tf_op jit(solution)/shard_map/all_gather | solution.py:231
  132.4 6.5 %feed_forward.1 = (bf16[2,256,512]{2,1,0:T(8,128)(2,1)S(1)}, bf16[2,256,512]{2,1,0:T(8,128)(2,1)S(1)}, bf16[2,256,512]{2,1,0:T(8,128)(2,1)S(1)}, bf16[2,256,512]{2,1,0:T(8,128)(2,1)S(1)}) custom-call(s32[4]{0:T(128)S(1)} %pad_add_fusion.place_ref, bf16[4,512,512]{2,1,0:T(8,128)(2,1)S(1)} %normalize.1.x_ref, bf16[32,4,48,512]{3,2,1,0:T(8,128)(2,1)} %bitcast.27), custom_call_target="tpu_custom_call" | custom-call | flops 3221225472 | bytes 10485760 | tf_op jit(solution)/shard_map/feed_forward/pallas_call | solution.py:194
  139.0 2.9 %collective-permute-start.13 = (bf16[2,256,512]{2,1,0:T(8,128)(2,1)S(1)}, bf16[2,256,512]{2,1,0:T(8,128)(2,1)S(1)}, u32[]{:S(2)}, u32[]{:S(2)}) collective-permute-start(bf16[2,256,512]{2,1,0:T(8,128)(2,1)S(1)} %get-tuple-element.13), channel_id=1, source_target_pairs={{0,1},{1,0},{2,3},{3,2},{4,5},{5,4},{6,7},{7,6},{8,9},{9,8},{10,11... | collective-permute-start | bytes 1572872 | tf_op jit(solution)/shard_map/ppermute | solution.py:33
  141.8 1.9 %collective-permute-start.11 = (bf16[2,256,512]{2,1,0:T(8,128)(2,1)S(1)}, bf16[2,256,512]{2,1,0:T(8,128)(2,1)S(1)}, u32[]{:S(2)}, u32[]{:S(2)}) collective-permute-start(bf16[2,256,512]{2,1,0:T(8,128)(2,1)S(1)} %get-tuple-element.11), channel_id=1, source_target_pairs={{0,1},{1,0},{2,3},{3,2},{4,5},{5,4},{6,7},{7,6},{8,9},{9,8},{10,11... | collective-permute-start | bytes 1572872 | tf_op jit(solution)/shard_map/ppermute | solution.py:33
  143.8 3.1 %collective-permute-start.14 = (bf16[256,512]{1,0:T(8,128)(2,1)S(1)}, bf16[256,512]{1,0:T(8,128)(2,1)S(1)}, u32[]{:S(2)}, u32[]{:S(2)}) collective-permute-start(bf16[256,512]{1,0:T(8,128)(2,1)S(1)} %fusion.4), channel_id=1, source_target_pairs={{0,2},{2,0},{1,3},{3,1},{4,6},{6,4},{5,7},{7,5},{8,10},{10,8},{9,1... | collective-permute-start | bytes 786440 | tf_op jit(solution)/shard_map/ppermute | solution.py:33
  147.0 2.2 %collective-permute-start.12 = (bf16[256,512]{1,0:T(8,128)(2,1)S(1)}, bf16[256,512]{1,0:T(8,128)(2,1)S(1)}, u32[]{:S(2)}, u32[]{:S(2)}) collective-permute-start(bf16[256,512]{1,0:T(8,128)(2,1)S(1)} %fusion.3), channel_id=1, source_target_pairs={{0,2},{2,0},{1,3},{3,1},{4,6},{6,4},{5,7},{7,5},{8,10},{10,8},{9,1... | collective-permute-start | bytes 786440 | tf_op jit(solution)/shard_map/ppermute | solution.py:33
  149.2 3.9 %collective-permute-done.14 = bf16[256,512]{1,0:T(8,128)(2,1)S(1)} collective-permute-done((bf16[256,512]{1,0:T(8,128)(2,1)S(1)}, bf16[256,512]{1,0:T(8,128)(2,1)S(1)}, u32[]{:S(2)}, u32[]{:S(2)}) %collective-permute-start.14) | collective-permute-done | bytes 262176 | tf_op jit(solution)/shard_map/ppermute | solution.py:33
  153.2 4.0 %collective-permute-start.15 = (bf16[256,512]{1,0:T(8,128)(2,1)S(1)}, bf16[256,512]{1,0:T(8,128)(2,1)S(1)}, u32[]{:S(2)}, u32[]{:S(2)}) collective-permute-start(bf16[256,512]{1,0:T(8,128)(2,1)S(1)} %fusion), channel_id=1, source_target_pairs={{0,4},{4,0},{8,12},{12,8},{1,5},{5,1},{9,13},{13,9},{2,6},{6,2},{1... | collective-permute-start | bytes 786440 | tf_op jit(solution)/shard_map/ppermute | solution.py:33
  158.7 8.9 %collective-permute-done.15 = bf16[256,512]{1,0:T(8,128)(2,1)S(1)} collective-permute-done((bf16[256,512]{1,0:T(8,128)(2,1)S(1)}, bf16[256,512]{1,0:T(8,128)(2,1)S(1)}, u32[]{:S(2)}, u32[]{:S(2)}) %collective-permute-start.15) | collective-permute-done | bytes 262176 | tf_op jit(solution)/shard_map/ppermute | solution.py:33
  (52 shorter events, 13.4 us)
Async XLA Ops:
  7.2 125.3 %all-gather.3.cloned.1.call-start = ((), (), s32[]{:S(2)}) async-start(), calls=%async_computation.1 | async-start | bytes 6488064 | tf_op jit(solution)/shard_map/all_gather | solution.py:231
  25.9 30.4 %copy-start.6 = (bf16[272,512]{1,0:T(8,128)(2,1)}, bf16[272,512]{1,0:T(8,128)(2,1)S(1)}, u32[]{:S(2)}) copy-start(bf16[272,512]{1,0:T(8,128)(2,1)S(1)} %pad_maximum_fusion.refs_1_) | copy-start | bytes 835588
  25.9 6.6 %collective-permute-start = (bf16[272,512]{1,0:T(8,128)(2,1)S(1)}, bf16[272,512]{1,0:T(8,128)(2,1)S(1)}, u32[]{:S(2)}, u32[]{:S(2)}) collective-permute-start(bf16[272,512]{1,0:T(8,128)(2,1)S(1)} %pad_maximum_fusion.refs_1_), channel_id=1, source_target_pairs={{0,4},{4,8},{8,12},{12,16},{16,20},{20,24},{24,28},{28,32},{32,36}... | collective-permute-start | bytes 835592 | tf_op jit(solution)/shard_map/ppermute | solution.py:28
  29.0 11.5 %collective-permute-start.1 = (bf16[256,512]{1,0:T(8,128)(2,1)}, bf16[256,512]{1,0:T(8,128)(2,1)S(1)}, u32[]{:S(2)}, u32[]{:S(2)}) collective-permute-start(bf16[256,512]{1,0:T(8,128)(2,1)} %refs_2_.1), channel_id=1, source_target_pairs={{0,4},{4,8},{8,12},{12,16},{16,20},{20,24},{24,28},{28,32},{32,36}... | collective-permute-start | bytes 786440 | tf_op jit(solution)/shard_map/ppermute | solution.py:28
  32.6 23.8 %copy-start.7 = (bf16[272,512]{1,0:T(8,128)(2,1)}, bf16[272,512]{1,0:T(8,128)(2,1)S(1)}, u32[]{:S(2)}) copy-start(bf16[272,512]{1,0:T(8,128)(2,1)S(1)} %collective-permute-done.refs_3_) | copy-start | bytes 835588
  32.6 23.8 %collective-permute-start.2 = (bf16[272,512]{1,0:T(8,128)(2,1)S(1)}, bf16[272,512]{1,0:T(8,128)(2,1)S(1)}, u32[]{:S(2)}, u32[]{:S(2)}) collective-permute-start(bf16[272,512]{1,0:T(8,128)(2,1)S(1)} %collective-permute-done.refs_3_), channel_id=1, source_target_pairs={{0,4},{4,8},{8,12},{12,16},{16,20},{20,24},{24,28},{28,32},{32,36}... | collective-permute-start | bytes 835592 | tf_op jit(solution)/shard_map/ppermute | solution.py:28
  40.6 15.8 %copy-start.10 = (bf16[256,512]{1,0:T(8,128)(2,1)}, bf16[256,512]{1,0:T(8,128)(2,1)S(1)}, u32[]{:S(2)}) copy-start(bf16[256,512]{1,0:T(8,128)(2,1)S(1)} %collective-permute-done.1.refs_4_) | copy-start | bytes 786436
  40.6 15.7 %collective-permute-start.3 = (bf16[256,512]{1,0:T(8,128)(2,1)S(1)}, bf16[256,512]{1,0:T(8,128)(2,1)S(1)}, u32[]{:S(2)}, u32[]{:S(2)}) collective-permute-start(bf16[256,512]{1,0:T(8,128)(2,1)S(1)} %collective-permute-done.1.refs_4_), channel_id=1, source_target_pairs={{0,4},{4,8},{8,12},{12,16},{16,20},{20,24},{24,28},{28,32},{32,36}... | collective-permute-start | bytes 786440 | tf_op jit(solution)/shard_map/ppermute | solution.py:28
  62.2 29.8 %collective-permute-start.7 = (bf16[272,512]{1,0:T(8,128)(2,1)}, bf16[272,512]{1,0:T(8,128)(2,1)S(1)}, u32[]{:S(2)}, u32[]{:S(2)}) collective-permute-start(bf16[272,512]{1,0:T(8,128)(2,1)} %get-tuple-element.9.refs_0_), channel_id=1, source_target_pairs={{0,4},{4,0},{8,12},{12,8},{1,5},{5,1},{9,13},{13,9},{2,6},{6,2},{1... | collective-permute-start | bytes 835592 | tf_op jit(solution)/shard_map/ppermute | solution.py:33
  67.3 37.9 %collective-permute-start.5 = (bf16[272,512]{1,0:T(8,128)(2,1)}, bf16[272,512]{1,0:T(8,128)(2,1)S(1)}, u32[]{:S(2)}, u32[]{:S(2)}) collective-permute-start(bf16[272,512]{1,0:T(8,128)(2,1)} %get-tuple-element.9.refs_0_), channel_id=1, source_target_pairs={{0,2},{2,0},{1,3},{3,1},{4,6},{6,4},{5,7},{7,5},{8,10},{10,8},{9,1... | collective-permute-start | bytes 835592 | tf_op jit(solution)/shard_map/ppermute | solution.py:33
  92.0 15.6 %collective-permute-start.9 = (bf16[272,512]{1,0:T(8,128)(2,1)S(1)}, bf16[272,512]{1,0:T(8,128)(2,1)S(1)}, u32[]{:S(2)}, u32[]{:S(2)}) collective-permute-start(bf16[272,512]{1,0:T(8,128)(2,1)S(1)} %collective-permute-done.7.refs_4_), channel_id=1, source_target_pairs={{0,2},{2,0},{1,3},{3,1},{4,6},{6,4},{5,7},{7,5},{8,10},{10,8},{9,1... | collective-permute-start | bytes 835592 | tf_op jit(solution)/shard_map/ppermute | solution.py:33
  98.1 11.5 %collective-permute-start.4 = (bf16[272,512]{1,0:T(8,128)(2,1)}, bf16[272,512]{1,0:T(8,128)(2,1)S(1)}, u32[]{:S(2)}, u32[]{:S(2)}) collective-permute-start(bf16[272,512]{1,0:T(8,128)(2,1)} %get-tuple-element.9.refs_0_), channel_id=1, source_target_pairs={{0,1},{1,0},{2,3},{3,2},{4,5},{5,4},{6,7},{7,6},{8,9},{9,8},{10,11... | collective-permute-start | bytes 835592 | tf_op jit(solution)/shard_map/ppermute | solution.py:33
  103.2 7.1 %collective-permute-start.8 = (bf16[272,512]{1,0:T(8,128)(2,1)S(1)}, bf16[272,512]{1,0:T(8,128)(2,1)S(1)}, u32[]{:S(2)}, u32[]{:S(2)}) collective-permute-start(bf16[272,512]{1,0:T(8,128)(2,1)S(1)} %collective-permute-done.7.refs_4_), channel_id=1, source_target_pairs={{0,1},{1,0},{2,3},{3,2},{4,5},{5,4},{6,7},{7,6},{8,9},{9,8},{10,11... | collective-permute-start | bytes 835592 | tf_op jit(solution)/shard_map/ppermute | solution.py:33
  105.1 4.4 %collective-permute-start.6 = (bf16[272,512]{1,0:T(8,128)(2,1)S(1)}, bf16[272,512]{1,0:T(8,128)(2,1)S(1)}, u32[]{:S(2)}, u32[]{:S(2)}) collective-permute-start(bf16[272,512]{1,0:T(8,128)(2,1)S(1)} %collective-permute-done.5.refs_2_), channel_id=1, source_target_pairs={{0,1},{1,0},{2,3},{3,2},{4,5},{5,4},{6,7},{7,6},{8,9},{9,8},{10,11... | collective-permute-start | bytes 835592 | tf_op jit(solution)/shard_map/ppermute | solution.py:33
  107.6 3.5 %collective-permute-start.10 = (bf16[272,512]{1,0:T(8,128)(2,1)S(1)}, bf16[272,512]{1,0:T(8,128)(2,1)S(1)}, u32[]{:S(2)}, u32[]{:S(2)}) collective-permute-start(bf16[272,512]{1,0:T(8,128)(2,1)S(1)} %collective-permute-done.9.refs_6_), channel_id=1, source_target_pairs={{0,1},{1,0},{2,3},{3,2},{4,5},{5,4},{6,7},{7,6},{8,9},{9,8},{10,11... | collective-permute-start | bytes 835592 | tf_op jit(solution)/shard_map/ppermute | solution.py:33
  111.8 1.0 copy-start
  112.7 1.0 copy-start.2
  132.4 35.2 %copy-start.5 = (f32[256,512]{1,0:T(8,128)S(1)}, f32[256,512]{1,0:T(8,128)}, u32[]{:S(2)}) copy-start(f32[256,512]{1,0:T(8,128)} %refs_7_.1) | copy-start | bytes 1572868
  132.4 35.2 %copy-start.9 = (bf16[256,512]{1,0:T(8,128)(2,1)S(1)}, bf16[256,512]{1,0:T(8,128)(2,1)}, u32[]{:S(2)}) copy-start(bf16[256,512]{1,0:T(8,128)(2,1)} %get-tuple-element.6) | copy-start | bytes 786436
  139.0 4.8 %collective-permute-start.13 = (bf16[2,256,512]{2,1,0:T(8,128)(2,1)S(1)}, bf16[2,256,512]{2,1,0:T(8,128)(2,1)S(1)}, u32[]{:S(2)}, u32[]{:S(2)}) collective-permute-start(bf16[2,256,512]{2,1,0:T(8,128)(2,1)S(1)} %get-tuple-element.13), channel_id=1, source_target_pairs={{0,1},{1,0},{2,3},{3,2},{4,5},{5,4},{6,7},{7,6},{8,9},{9,8},{10,11... | collective-permute-start | bytes 1572872 | tf_op jit(solution)/shard_map/ppermute | solution.py:33
  141.8 5.1 %collective-permute-start.11 = (bf16[2,256,512]{2,1,0:T(8,128)(2,1)S(1)}, bf16[2,256,512]{2,1,0:T(8,128)(2,1)S(1)}, u32[]{:S(2)}, u32[]{:S(2)}) collective-permute-start(bf16[2,256,512]{2,1,0:T(8,128)(2,1)S(1)} %get-tuple-element.11), channel_id=1, source_target_pairs={{0,1},{1,0},{2,3},{3,2},{4,5},{5,4},{6,7},{7,6},{8,9},{9,8},{10,11... | collective-permute-start | bytes 1572872 | tf_op jit(solution)/shard_map/ppermute | solution.py:33
  143.8 9.3 %collective-permute-start.14 = (bf16[256,512]{1,0:T(8,128)(2,1)S(1)}, bf16[256,512]{1,0:T(8,128)(2,1)S(1)}, u32[]{:S(2)}, u32[]{:S(2)}) collective-permute-start(bf16[256,512]{1,0:T(8,128)(2,1)S(1)} %fusion.4), channel_id=1, source_target_pairs={{0,2},{2,0},{1,3},{3,1},{4,6},{6,4},{5,7},{7,5},{8,10},{10,8},{9,1... | collective-permute-start | bytes 786440 | tf_op jit(solution)/shard_map/ppermute | solution.py:33
  147.0 11.7 %collective-permute-start.12 = (bf16[256,512]{1,0:T(8,128)(2,1)S(1)}, bf16[256,512]{1,0:T(8,128)(2,1)S(1)}, u32[]{:S(2)}, u32[]{:S(2)}) collective-permute-start(bf16[256,512]{1,0:T(8,128)(2,1)S(1)} %fusion.3), channel_id=1, source_target_pairs={{0,2},{2,0},{1,3},{3,1},{4,6},{6,4},{5,7},{7,5},{8,10},{10,8},{9,1... | collective-permute-start | bytes 786440 | tf_op jit(solution)/shard_map/ppermute | solution.py:33
  153.2 14.4 %collective-permute-start.15 = (bf16[256,512]{1,0:T(8,128)(2,1)S(1)}, bf16[256,512]{1,0:T(8,128)(2,1)S(1)}, u32[]{:S(2)}, u32[]{:S(2)}) collective-permute-start(bf16[256,512]{1,0:T(8,128)(2,1)S(1)} %fusion), channel_id=1, source_target_pairs={{0,4},{4,0},{8,12},{12,8},{1,5},{5,1},{9,13},{13,9},{2,6},{6,2},{1... | collective-permute-start | bytes 786440 | tf_op jit(solution)/shard_map/ppermute | solution.py:33
  (5 other events, 3.9 us)
Sparse Core Ops, SparseCore 0:
  24.2 108.2 all-gather.2

commit v11 on v10

--- a/solution.py
+++ b/solution.py
@@ -258,8 +258,11 @@
     partner_got = swap(partner_send, "c")
     own_got = swap(own_send, "c")
     partner_far = swap(add(partner_keep[0], partner_got[0]).astype(BF16), "yl")
-    own_far = swap(add(own_keep[0], own_got[0]).astype(BF16), "yl")
-    back = swap((add(partner_keep[1], partner_got[1]) + partner_far.astype(F32)).astype(BF16), "yh")
+    back = (add(partner_keep[1], partner_got[1]) + partner_far.astype(F32)).astype(BF16)
+    own_far = add(own_keep[0], own_got[0]).astype(BF16)
+    back, own_far = lax.optimization_barrier((back, own_far))
+    back = swap(back, "yh")
+    own_far = swap(own_far, "yl")
     summed = add(own_keep[1], own_got[1]) + own_far.astype(F32) + back.astype(F32)
     mixed = residual_in + attended.astype(F32) + summed
     return attended, mixed

time: 177 us -> 179 us (1.011)
  no operation moved by 1% of the time
where the time goes in v11:
time: 179 us; the launch traced here: 178 us
  starting transfers between devices  79 us (44%)
  waiting for transfers between devices  46.9 us (26%)
  blocking collectives  16 us (9%)
  between operations  14.3 us (8%)
  Pallas kernels  12.5 us (7%)
  local copies, waits for them, and re-layouts  5.33 us (3%)
  other arithmetic  3.87 us (2%)
    ppermute x12, starting transfers between devices, swap(): return lax.ppermute(value, axis, [(i, i ^ 1) for i in range(size)])  62.3 us
    all_gather x1, waiting for transfers between devices, on_device(): weights = lax.all_gather(near, ('x', 'z'), axis=0)  16.8 us
    ppermute x4, starting transfers between devices, from_behind(): return lax.ppermute(value, SEQ, [(i, i + by) for i in range(size - by)])  16.7 us
    ppermute x12, waiting for transfers between devices, swap(): return lax.ppermute(value, axis, [(i, i ^ 1) for i in range(size)])  16.5 us
    all_to_all x1, blocking collectives, on_device(): near = lax.all_to_all(jnp.stack(halves * 2), 'yh', 0, 0)  16 us
    ppermute x4, waiting for transfers between devices, from_behind(): return lax.ppermute(value, SEQ, [(i, i + by) for i in range(size - by)])  13.6 us
    pallas_call x1, Pallas kernels, feed_forward(): pl.pallas_call(feed_forward_kernel, out_shape=[jax.ShapeDtypeStruct((2, R...  6.5 us
    unnamed x24, local copies, waits for them, and re-layouts  5.15 us
  transfers between devices with their start and end apart: 17, of which 8 were waited for; matrix products, arithmetic and copies ran while one was open for 1% of the time, Pallas kernels for 3%

profile of v11, /device:TPU:1, one launch (start us, length us, event | category | flops | bytes accessed | tf_op | source)
XLA Modules:
  0.0 178.0 jit_solution(4047420931478759856)
XLA Ops:
  8.1 16.0 %all_to_all.5 = bf16[4,48,512]{2,1,0:T(8,128)(2,1)} all-to-all(bf16[4,48,512]{2,1,0:T(8,128)(2,1)S(1)} %pad_maximum_fusion.1), channel_id=1, replica_groups=mesh['x'=4,'z'=8,'yh'=4,'yl'=2,'c'=2] {'yh'}, dimensions={0} | all-to-all | bytes 393216 | tf_op jit(solution)/shard_map/all_to_all | solution.py:230
  25.9 3.1 %collective-permute-start = (bf16[272,512]{1,0:T(8,128)(2,1)S(1)}, bf16[272,512]{1,0:T(8,128)(2,1)S(1)}, u32[]{:S(2)}, u32[]{:S(2)}) collective-permute-start(bf16[272,512]{1,0:T(8,128)(2,1)S(1)} %pad_maximum_fusion.refs_1_), channel_id=1, source_target_pairs={{0,4},{4,8},{8,12},{12,16},{16,20},{20,24},{24,28},{28,32},{32,36}... | collective-permute-start | bytes 835592 | tf_op jit(solution)/shard_map/ppermute | solution.py:28
  29.0 2.5 %collective-permute-start.1 = (bf16[256,512]{1,0:T(8,128)(2,1)}, bf16[256,512]{1,0:T(8,128)(2,1)S(1)}, u32[]{:S(2)}, u32[]{:S(2)}) collective-permute-start(bf16[256,512]{1,0:T(8,128)(2,1)} %refs_2_.1), channel_id=1, source_target_pairs={{0,4},{4,8},{8,12},{12,16},{16,20},{20,24},{24,28},{28,32},{32,36}... | collective-permute-start | bytes 786440 | tf_op jit(solution)/shard_map/ppermute | solution.py:28
  32.6 6.1 %collective-permute-start.2 = (bf16[272,512]{1,0:T(8,128)(2,1)S(1)}, bf16[272,512]{1,0:T(8,128)(2,1)S(1)}, u32[]{:S(2)}, u32[]{:S(2)}) collective-permute-start(bf16[272,512]{1,0:T(8,128)(2,1)S(1)} %collective-permute-done.refs_3_), channel_id=1, source_target_pairs={{0,4},{4,8},{8,12},{12,16},{16,20},{20,24},{24,28},{28,32},{32,36}... | collective-permute-start | bytes 835592 | tf_op jit(solution)/shard_map/ppermute | solution.py:28
  38.7 1.9 %collective-permute-done.1.refs_4_ = bf16[256,512]{1,0:T(8,128)(2,1)S(1)} collective-permute-done((bf16[256,512]{1,0:T(8,128)(2,1)}, bf16[256,512]{1,0:T(8,128)(2,1)S(1)}, u32[]{:S(2)}, u32[]{:S(2)}) %collective-permute-start.1) | collective-permute-done | bytes 262176 | tf_op jit(solution)/shard_map/ppermute | solution.py:28
  40.6 5.0 %collective-permute-start.3 = (bf16[256,512]{1,0:T(8,128)(2,1)S(1)}, bf16[256,512]{1,0:T(8,128)(2,1)S(1)}, u32[]{:S(2)}, u32[]{:S(2)}) collective-permute-start(bf16[256,512]{1,0:T(8,128)(2,1)S(1)} %collective-permute-done.1.refs_4_), channel_id=1, source_target_pairs={{0,4},{4,8},{8,12},{12,16},{16,20},{20,24},{24,28},{28,32},{32,36}... | collective-permute-start | bytes 786440 | tf_op jit(solution)/shard_map/ppermute | solution.py:28
  45.6 10.7 %collective-permute-done.3.refs_6_ = bf16[256,512]{1,0:T(8,128)(2,1)S(1)} collective-permute-done((bf16[256,512]{1,0:T(8,128)(2,1)S(1)}, bf16[256,512]{1,0:T(8,128)(2,1)S(1)}, u32[]{:S(2)}, u32[]{:S(2)}) %collective-permute-start.3) | collective-permute-done | bytes 262176 | tf_op jit(solution)/shard_map/ppermute | solution.py:28
  57.1 5.1 %attention.1 = (bf16[256,512]{1,0:T(8,128)(2,1)}, bf16[272,512]{1,0:T(8,128)(2,1)}) custom-call(s32[2]{0:T(128)} %lengths_ref.1, f32[1,512]{1,0:T(1,128)} %bitcast.26, bf16[256,512]{1,0:T(8,128)(2,1)} %refs_0_.1, bf16[272,512]{1,0:T(8,128)(2,1)} %copy-done.6, bf16[256,512]{1,0:T(8,128)(2,1)} %refs_2_.1, bf16[272,512]{1,0:T(8,128)(2,1)} %copy-done.7, ...), custom_call_target="tpu_custom_call" | custom-call | flops 402653184 | bytes 3145728 | tf_op jit(solution)/shard_map/attention/pallas_call | solution.py:103
  62.2 5.0 %collective-permute-start.7 = (bf16[272,512]{1,0:T(8,128)(2,1)}, bf16[272,512]{1,0:T(8,128)(2,1)S(1)}, u32[]{:S(2)}, u32[]{:S(2)}) collective-permute-start(bf16[272,512]{1,0:T(8,128)(2,1)} %get-tuple-element.11.refs_0_), channel_id=1, source_target_pairs={{0,4},{4,0},{8,12},{12,8},{1,5},{5,1},{9,13},{13,9},{2,6},{6,2},{1... | collective-permute-start | bytes 835592 | tf_op jit(solution)/shard_map/ppermute | solution.py:33
  67.3 24.7 %collective-permute-start.5 = (bf16[272,512]{1,0:T(8,128)(2,1)}, bf16[272,512]{1,0:T(8,128)(2,1)S(1)}, u32[]{:S(2)}, u32[]{:S(2)}) collective-permute-start(bf16[272,512]{1,0:T(8,128)(2,1)} %get-tuple-element.11.refs_0_), channel_id=1, source_target_pairs={{0,2},{2,0},{1,3},{3,1},{4,6},{6,4},{5,7},{7,5},{8,10},{10,8},{9,1... | collective-permute-start | bytes 835592 | tf_op jit(solution)/shard_map/ppermute | solution.py:33
  92.0 6.1 %collective-permute-start.9 = (bf16[272,512]{1,0:T(8,128)(2,1)S(1)}, bf16[272,512]{1,0:T(8,128)(2,1)S(1)}, u32[]{:S(2)}, u32[]{:S(2)}) collective-permute-start(bf16[272,512]{1,0:T(8,128)(2,1)S(1)} %collective-permute-done.7.refs_4_), channel_id=1, source_target_pairs={{0,2},{2,0},{1,3},{3,1},{4,6},{6,4},{5,7},{7,5},{8,10},{10,8},{9,1... | collective-permute-start | bytes 835592 | tf_op jit(solution)/shard_map/ppermute | solution.py:33
  98.1 5.1 %collective-permute-start.4 = (bf16[272,512]{1,0:T(8,128)(2,1)}, bf16[272,512]{1,0:T(8,128)(2,1)S(1)}, u32[]{:S(2)}, u32[]{:S(2)}) collective-permute-start(bf16[272,512]{1,0:T(8,128)(2,1)} %get-tuple-element.11.refs_0_), channel_id=1, source_target_pairs={{0,1},{1,0},{2,3},{3,2},{4,5},{5,4},{6,7},{7,6},{8,9},{9,8},{10,11... | collective-permute-start | bytes 835592 | tf_op jit(solution)/shard_map/ppermute | solution.py:33
  103.2 1.9 %collective-permute-start.8 = (bf16[272,512]{1,0:T(8,128)(2,1)S(1)}, bf16[272,512]{1,0:T(8,128)(2,1)S(1)}, u32[]{:S(2)}, u32[]{:S(2)}) collective-permute-start(bf16[272,512]{1,0:T(8,128)(2,1)S(1)} %collective-permute-done.7.refs_4_), channel_id=1, source_target_pairs={{0,1},{1,0},{2,3},{3,2},{4,5},{5,4},{6,7},{7,6},{8,9},{9,8},{10,11... | collective-permute-start | bytes 835592 | tf_op jit(solution)/shard_map/ppermute | solution.py:33
  105.1 2.4 %collective-permute-start.6 = (bf16[272,512]{1,0:T(8,128)(2,1)S(1)}, bf16[272,512]{1,0:T(8,128)(2,1)S(1)}, u32[]{:S(2)}, u32[]{:S(2)}) collective-permute-start(bf16[272,512]{1,0:T(8,128)(2,1)S(1)} %collective-permute-done.5.refs_2_), channel_id=1, source_target_pairs={{0,1},{1,0},{2,3},{3,2},{4,5},{5,4},{6,7},{7,6},{8,9},{9,8},{10,11... | collective-permute-start | bytes 835592 | tf_op jit(solution)/shard_map/ppermute | solution.py:33
  107.6 1.9 %collective-permute-start.10 = (bf16[272,512]{1,0:T(8,128)(2,1)S(1)}, bf16[272,512]{1,0:T(8,128)(2,1)S(1)}, u32[]{:S(2)}, u32[]{:S(2)}) collective-permute-start(bf16[272,512]{1,0:T(8,128)(2,1)S(1)} %collective-permute-done.9.refs_6_), channel_id=1, source_target_pairs={{0,1},{1,0},{2,3},{3,2},{4,5},{5,4},{6,7},{7,6},{8,9},{9,8},{10,11... | collective-permute-start | bytes 835592 | tf_op jit(solution)/shard_map/ppermute | solution.py:33
  115.6 16.8 %all-gather.3.cloned.1.call-done = bf16[128,48,512]{2,1,0:T(8,128)(2,1)} async-done(((bf16[4,48,512]{2,1,0:T(8,128)(2,1)}), bf16[128,48,512]{2,1,0:T(8,128)(2,1)}) %all-gather.3.cloned.1.call-update) | async-done | bytes 6291472 | tf_op jit(solution)/shard_map/all_gather | solution.py:231
  132.4 6.5 %feed_forward.1 = (bf16[2,256,512]{2,1,0:T(8,128)(2,1)S(1)}, bf16[2,256,512]{2,1,0:T(8,128)(2,1)S(1)}, bf16[2,256,512]{2,1,0:T(8,128)(2,1)S(1)}, bf16[2,256,512]{2,1,0:T(8,128)(2,1)S(1)}) custom-call(s32[4]{0:T(128)S(1)} %pad_add_fusion.place_ref, bf16[4,512,512]{2,1,0:T(8,128)(2,1)S(1)} %normalize.1.x_ref, bf16[32,4,48,512]{3,2,1,0:T(8,128)(2,1)} %bitcast.27), custom_call_target="tpu_custom_call" | custom-call | flops 3221225472 | bytes 10485760 | tf_op jit(solution)/shard_map/feed_forward/pallas_call | solution.py:194
  139.0 2.9 %collective-permute-start.12 = (bf16[2,256,512]{2,1,0:T(8,128)(2,1)S(1)}, bf16[2,256,512]{2,1,0:T(8,128)(2,1)S(1)}, u32[]{:S(2)}, u32[]{:S(2)}) collective-permute-start(bf16[2,256,512]{2,1,0:T(8,128)(2,1)S(1)} %get-tuple-element.15), channel_id=1, source_target_pairs={{0,1},{1,0},{2,3},{3,2},{4,5},{5,4},{6,7},{7,6},{8,9},{9,8},{10,11... | collective-permute-start | bytes 1572872 | tf_op jit(solution)/shard_map/ppermute | solution.py:33
  141.8 1.9 %collective-permute-start.11 = (bf16[2,256,512]{2,1,0:T(8,128)(2,1)S(1)}, bf16[2,256,512]{2,1,0:T(8,128)(2,1)S(1)}, u32[]{:S(2)}, u32[]{:S(2)}) collective-permute-start(bf16[2,256,512]{2,1,0:T(8,128)(2,1)S(1)} %get-tuple-element.13), channel_id=1, source_target_pairs={{0,1},{1,0},{2,3},{3,2},{4,5},{5,4},{6,7},{7,6},{8,9},{9,8},{10,11... | collective-permute-start | bytes 1572872 | tf_op jit(solution)/shard_map/ppermute | solution.py:33
  143.8 3.1 %collective-permute-start.13 = (bf16[256,512]{1,0:T(8,128)(2,1)S(1)}, bf16[256,512]{1,0:T(8,128)(2,1)S(1)}, u32[]{:S(2)}, u32[]{:S(2)}) collective-permute-start(bf16[256,512]{1,0:T(8,128)(2,1)S(1)} %fusion.3), channel_id=1, source_target_pairs={{0,2},{2,0},{1,3},{3,1},{4,6},{6,4},{5,7},{7,5},{8,10},{10,8},{9,1... | collective-permute-start | bytes 786440 | tf_op jit(solution)/shard_map/ppermute | solution.py:33
  147.0 6.1 %collective-permute-done.13 = bf16[256,512]{1,0:T(8,128)(2,1)S(1)} collective-permute-done((bf16[256,512]{1,0:T(8,128)(2,1)S(1)}, bf16[256,512]{1,0:T(8,128)(2,1)S(1)}, u32[]{:S(2)}, u32[]{:S(2)}) %collective-permute-start.13) | collective-permute-done | bytes 262176 | tf_op jit(solution)/shard_map/ppermute | solution.py:33
  153.2 4.0 %collective-permute-start.15 = (bf16[256,512]{1,0:T(8,128)(2,1)S(1)}, bf16[256,512]{1,0:T(8,128)(2,1)S(1)}, u32[]{:S(2)}, u32[]{:S(2)}) collective-permute-start(bf16[256,512]{1,0:T(8,128)(2,1)S(1)} %fusion), channel_id=1, source_target_pairs={{0,4},{4,0},{8,12},{12,8},{1,5},{5,1},{9,13},{13,9},{2,6},{6,2},{1... | collective-permute-start | bytes 786440 | tf_op jit(solution)/shard_map/ppermute | solution.py:33
  157.3 3.1 %collective-permute-start.14 = (bf16[256,512]{1,0:T(8,128)(2,1)S(1)}, bf16[256,512]{1,0:T(8,128)(2,1)S(1)}, u32[]{:S(2)}, u32[]{:S(2)}) collective-permute-start(bf16[256,512]{1,0:T(8,128)(2,1)S(1)} %fusion.4), channel_id=1, source_target_pairs={{0,2},{2,0},{1,3},{3,1},{4,6},{6,4},{5,7},{7,5},{8,10},{10,8},{9,1... | collective-permute-start | bytes 786440 | tf_op jit(solution)/shard_map/ppermute | solution.py:33
  160.4 8.5 %collective-permute-done.15 = bf16[256,512]{1,0:T(8,128)(2,1)S(1)} collective-permute-done((bf16[256,512]{1,0:T(8,128)(2,1)S(1)}, bf16[256,512]{1,0:T(8,128)(2,1)S(1)}, u32[]{:S(2)}, u32[]{:S(2)}) %collective-permute-start.15) | collective-permute-done | bytes 262176 | tf_op jit(solution)/shard_map/ppermute | solution.py:33
  (52 shorter events, 13.2 us)
Async XLA Ops:
  7.2 125.3 %all-gather.3.cloned.1.call-start = ((), (), s32[]{:S(2)}) async-start(), calls=%async_computation.1 | async-start | bytes 6488064 | tf_op jit(solution)/shard_map/all_gather | solution.py:231
  25.9 30.4 %copy-start.6 = (bf16[272,512]{1,0:T(8,128)(2,1)}, bf16[272,512]{1,0:T(8,128)(2,1)S(1)}, u32[]{:S(2)}) copy-start(bf16[272,512]{1,0:T(8,128)(2,1)S(1)} %pad_maximum_fusion.refs_1_) | copy-start | bytes 835588
  25.9 6.6 %collective-permute-start = (bf16[272,512]{1,0:T(8,128)(2,1)S(1)}, bf16[272,512]{1,0:T(8,128)(2,1)S(1)}, u32[]{:S(2)}, u32[]{:S(2)}) collective-permute-start(bf16[272,512]{1,0:T(8,128)(2,1)S(1)} %pad_maximum_fusion.refs_1_), channel_id=1, source_target_pairs={{0,4},{4,8},{8,12},{12,16},{16,20},{20,24},{24,28},{28,32},{32,36}... | collective-permute-start | bytes 835592 | tf_op jit(solution)/shard_map/ppermute | solution.py:28
  29.0 11.5 %collective-permute-start.1 = (bf16[256,512]{1,0:T(8,128)(2,1)}, bf16[256,512]{1,0:T(8,128)(2,1)S(1)}, u32[]{:S(2)}, u32[]{:S(2)}) collective-permute-start(bf16[256,512]{1,0:T(8,128)(2,1)} %refs_2_.1), channel_id=1, source_target_pairs={{0,4},{4,8},{8,12},{12,16},{16,20},{20,24},{24,28},{28,32},{32,36}... | collective-permute-start | bytes 786440 | tf_op jit(solution)/shard_map/ppermute | solution.py:28
  32.6 23.8 %copy-start.7 = (bf16[272,512]{1,0:T(8,128)(2,1)}, bf16[272,512]{1,0:T(8,128)(2,1)S(1)}, u32[]{:S(2)}) copy-start(bf16[272,512]{1,0:T(8,128)(2,1)S(1)} %collective-permute-done.refs_3_) | copy-start | bytes 835588
  32.6 23.8 %collective-permute-start.2 = (bf16[272,512]{1,0:T(8,128)(2,1)S(1)}, bf16[272,512]{1,0:T(8,128)(2,1)S(1)}, u32[]{:S(2)}, u32[]{:S(2)}) collective-permute-start(bf16[272,512]{1,0:T(8,128)(2,1)S(1)} %collective-permute-done.refs_3_), channel_id=1, source_target_pairs={{0,4},{4,8},{8,12},{12,16},{16,20},{20,24},{24,28},{28,32},{32,36}... | collective-permute-start | bytes 835592 | tf_op jit(solution)/shard_map/ppermute | solution.py:28
  40.6 15.8 %copy-start.10 = (bf16[256,512]{1,0:T(8,128)(2,1)}, bf16[256,512]{1,0:T(8,128)(2,1)S(1)}, u32[]{:S(2)}) copy-start(bf16[256,512]{1,0:T(8,128)(2,1)S(1)} %collective-permute-done.1.refs_4_) | copy-start | bytes 786436
  40.6 15.7 %collective-permute-start.3 = (bf16[256,512]{1,0:T(8,128)(2,1)S(1)}, bf16[256,512]{1,0:T(8,128)(2,1)S(1)}, u32[]{:S(2)}, u32[]{:S(2)}) collective-permute-start(bf16[256,512]{1,0:T(8,128)(2,1)S(1)} %collective-permute-done.1.refs_4_), channel_id=1, source_target_pairs={{0,4},{4,8},{8,12},{12,16},{16,20},{20,24},{24,28},{28,32},{32,36}... | collective-permute-start | bytes 786440 | tf_op jit(solution)/shard_map/ppermute | solution.py:28
  62.2 29.8 %collective-permute-start.7 = (bf16[272,512]{1,0:T(8,128)(2,1)}, bf16[272,512]{1,0:T(8,128)(2,1)S(1)}, u32[]{:S(2)}, u32[]{:S(2)}) collective-permute-start(bf16[272,512]{1,0:T(8,128)(2,1)} %get-tuple-element.11.refs_0_), channel_id=1, source_target_pairs={{0,4},{4,0},{8,12},{12,8},{1,5},{5,1},{9,13},{13,9},{2,6},{6,2},{1... | collective-permute-start | bytes 835592 | tf_op jit(solution)/shard_map/ppermute | solution.py:33
  67.3 37.9 %collective-permute-start.5 = (bf16[272,512]{1,0:T(8,128)(2,1)}, bf16[272,512]{1,0:T(8,128)(2,1)S(1)}, u32[]{:S(2)}, u32[]{:S(2)}) collective-permute-start(bf16[272,512]{1,0:T(8,128)(2,1)} %get-tuple-element.11.refs_0_), channel_id=1, source_target_pairs={{0,2},{2,0},{1,3},{3,1},{4,6},{6,4},{5,7},{7,5},{8,10},{10,8},{9,1... | collective-permute-start | bytes 835592 | tf_op jit(solution)/shard_map/ppermute | solution.py:33
  92.0 15.6 %collective-permute-start.9 = (bf16[272,512]{1,0:T(8,128)(2,1)S(1)}, bf16[272,512]{1,0:T(8,128)(2,1)S(1)}, u32[]{:S(2)}, u32[]{:S(2)}) collective-permute-start(bf16[272,512]{1,0:T(8,128)(2,1)S(1)} %collective-permute-done.7.refs_4_), channel_id=1, source_target_pairs={{0,2},{2,0},{1,3},{3,1},{4,6},{6,4},{5,7},{7,5},{8,10},{10,8},{9,1... | collective-permute-start | bytes 835592 | tf_op jit(solution)/shard_map/ppermute | solution.py:33
  98.1 11.5 %collective-permute-start.4 = (bf16[272,512]{1,0:T(8,128)(2,1)}, bf16[272,512]{1,0:T(8,128)(2,1)S(1)}, u32[]{:S(2)}, u32[]{:S(2)}) collective-permute-start(bf16[272,512]{1,0:T(8,128)(2,1)} %get-tuple-element.11.refs_0_), channel_id=1, source_target_pairs={{0,1},{1,0},{2,3},{3,2},{4,5},{5,4},{6,7},{7,6},{8,9},{9,8},{10,11... | collective-permute-start | bytes 835592 | tf_op jit(solution)/shard_map/ppermute | solution.py:33
  103.2 7.1 %collective-permute-start.8 = (bf16[272,512]{1,0:T(8,128)(2,1)S(1)}, bf16[272,512]{1,0:T(8,128)(2,1)S(1)}, u32[]{:S(2)}, u32[]{:S(2)}) collective-permute-start(bf16[272,512]{1,0:T(8,128)(2,1)S(1)} %collective-permute-done.7.refs_4_), channel_id=1, source_target_pairs={{0,1},{1,0},{2,3},{3,2},{4,5},{5,4},{6,7},{7,6},{8,9},{9,8},{10,11... | collective-permute-start | bytes 835592 | tf_op jit(solution)/shard_map/ppermute | solution.py:33
  105.1 4.4 %collective-permute-start.6 = (bf16[272,512]{1,0:T(8,128)(2,1)S(1)}, bf16[272,512]{1,0:T(8,128)(2,1)S(1)}, u32[]{:S(2)}, u32[]{:S(2)}) collective-permute-start(bf16[272,512]{1,0:T(8,128)(2,1)S(1)} %collective-permute-done.5.refs_2_), channel_id=1, source_target_pairs={{0,1},{1,0},{2,3},{3,2},{4,5},{5,4},{6,7},{7,6},{8,9},{9,8},{10,11... | collective-permute-start | bytes 835592 | tf_op jit(solution)/shard_map/ppermute | solution.py:33
  107.6 3.5 %collective-permute-start.10 = (bf16[272,512]{1,0:T(8,128)(2,1)S(1)}, bf16[272,512]{1,0:T(8,128)(2,1)S(1)}, u32[]{:S(2)}, u32[]{:S(2)}) collective-permute-start(bf16[272,512]{1,0:T(8,128)(2,1)S(1)} %collective-permute-done.9.refs_6_), channel_id=1, source_target_pairs={{0,1},{1,0},{2,3},{3,2},{4,5},{5,4},{6,7},{7,6},{8,9},{9,8},{10,11... | collective-permute-start | bytes 835592 | tf_op jit(solution)/shard_map/ppermute | solution.py:33
  111.8 1.0 copy-start
  112.7 1.0 copy-start.2
  132.4 37.6 %copy-start.5 = (f32[256,512]{1,0:T(8,128)S(1)}, f32[256,512]{1,0:T(8,128)}, u32[]{:S(2)}) copy-start(f32[256,512]{1,0:T(8,128)} %refs_7_.1) | copy-start | bytes 1572868
  132.4 37.7 %copy-start.9 = (bf16[256,512]{1,0:T(8,128)(2,1)S(1)}, bf16[256,512]{1,0:T(8,128)(2,1)}, u32[]{:S(2)}) copy-start(bf16[256,512]{1,0:T(8,128)(2,1)} %get-tuple-element.8) | copy-start | bytes 786436
  139.0 4.8 %collective-permute-start.12 = (bf16[2,256,512]{2,1,0:T(8,128)(2,1)S(1)}, bf16[2,256,512]{2,1,0:T(8,128)(2,1)S(1)}, u32[]{:S(2)}, u32[]{:S(2)}) collective-permute-start(bf16[2,256,512]{2,1,0:T(8,128)(2,1)S(1)} %get-tuple-element.15), channel_id=1, source_target_pairs={{0,1},{1,0},{2,3},{3,2},{4,5},{5,4},{6,7},{7,6},{8,9},{9,8},{10,11... | collective-permute-start | bytes 1572872 | tf_op jit(solution)/shard_map/ppermute | solution.py:33
  141.8 5.1 %collective-permute-start.11 = (bf16[2,256,512]{2,1,0:T(8,128)(2,1)S(1)}, bf16[2,256,512]{2,1,0:T(8,128)(2,1)S(1)}, u32[]{:S(2)}, u32[]{:S(2)}) collective-permute-start(bf16[2,256,512]{2,1,0:T(8,128)(2,1)S(1)} %get-tuple-element.13), channel_id=1, source_target_pairs={{0,1},{1,0},{2,3},{3,2},{4,5},{5,4},{6,7},{7,6},{8,9},{9,8},{10,11... | collective-permute-start | bytes 1572872 | tf_op jit(solution)/shard_map/ppermute | solution.py:33
  143.8 9.3 %collective-permute-start.13 = (bf16[256,512]{1,0:T(8,128)(2,1)S(1)}, bf16[256,512]{1,0:T(8,128)(2,1)S(1)}, u32[]{:S(2)}, u32[]{:S(2)}) collective-permute-start(bf16[256,512]{1,0:T(8,128)(2,1)S(1)} %fusion.3), channel_id=1, source_target_pairs={{0,2},{2,0},{1,3},{3,1},{4,6},{6,4},{5,7},{7,5},{8,10},{10,8},{9,1... | collective-permute-start | bytes 786440 | tf_op jit(solution)/shard_map/ppermute | solution.py:33
  153.2 15.7 %collective-permute-start.15 = (bf16[256,512]{1,0:T(8,128)(2,1)S(1)}, bf16[256,512]{1,0:T(8,128)(2,1)S(1)}, u32[]{:S(2)}, u32[]{:S(2)}) collective-permute-start(bf16[256,512]{1,0:T(8,128)(2,1)S(1)} %fusion), channel_id=1, source_target_pairs={{0,4},{4,0},{8,12},{12,8},{1,5},{5,1},{9,13},{13,9},{2,6},{6,2},{1... | collective-permute-start | bytes 786440 | tf_op jit(solution)/shard_map/ppermute | solution.py:33
  157.3 12.8 %collective-permute-start.14 = (bf16[256,512]{1,0:T(8,128)(2,1)S(1)}, bf16[256,512]{1,0:T(8,128)(2,1)S(1)}, u32[]{:S(2)}, u32[]{:S(2)}) collective-permute-start(bf16[256,512]{1,0:T(8,128)(2,1)S(1)} %fusion.4), channel_id=1, source_target_pairs={{0,2},{2,0},{1,3},{3,1},{4,6},{6,4},{5,7},{7,5},{8,10},{10,8},{9,1... | collective-permute-start | bytes 786440 | tf_op jit(solution)/shard_map/ppermute | solution.py:33
  (5 other events, 3.9 us)
Sparse Core Ops, SparseCore 0:
  24.2 108.2 all-gather.2
